TPU v7x, 32 devices: a whole 2x2x4 slice. The times are simulated.
32 devices in a mesh: dp: 8 (over z, core), seq: 4 (over y, x).
Axes of the slice: x: 2, y: 2, z: 4, core: 2. Of those that a mesh axis runs over, the one named last changes fastest.
Arguments:
- block_in: bfloat16 [3, 8, 2048, 512], P(None, 'dp', 'seq'), may hold values from -6 to 6
- routes: int32 [3, 8, 2048, 2], P(None, 'dp', 'seq'), may hold values from 0 to 7, all different within a row
- segments: int32 [3, 8, 2048], P(None, 'dp'), may hold values from 0 to 7, never falling along the last dimension, each value on 1 to 1536 neighbouring positions
- cotangent: bfloat16 [3, 8, 2048, 512], P(None, 'dp', 'seq'), may hold values from -6 to 6
- ln1_gain: bfloat16 [512], P(('dp', 'seq')), may hold values from 0.5 to 1.5
- ln1_bias: bfloat16 [512], P(('dp', 'seq')), may hold values from -0.5 to 0.5
- query_weight: bfloat16 [512, 512], P(('dp', 'seq')), may hold values from -0.25 to 0.25
- kv_weight: bfloat16 [512, 128], P(('dp', 'seq')), may hold values from -0.25 to 0.25
- router_weight: bfloat16 [512, 8], P(('dp', 'seq')), may hold values from -0.25 to 0.25
- out_weight: bfloat16 [512, 512], P(('dp', 'seq')), may hold values from -4 to 4
- ln2_gain: bfloat16 [512], P(('dp', 'seq')), may hold values from 0.5 to 1.5
- ln2_bias: bfloat16 [512], P(('dp', 'seq')), may hold values from -0.5 to 0.5
- up_weight: bfloat16 [512, 2048], P(('dp', 'seq')), may hold values from -0.25 to 0.25
- up_bias: bfloat16 [2048], P(('dp', 'seq')), may hold values from -0.5 to 0.5
- down_weight: bfloat16 [2048, 512], P(('dp', 'seq')), may hold values from -0.1875 to 0.1875
- down_bias: bfloat16 [512], P(('dp', 'seq')), may hold values from -0.5 to 0.5
Outputs:
- block_out: bfloat16 [3, 8, 2048, 512], P(None, 'dp', 'seq')
- grad_in: float32 [3, 8, 2048, 512], P(None, 'dp', 'seq')
- grad_ln1_gain: float32 [512], P(('dp', 'seq'))
- grad_ln1_bias: float32 [512], P(('dp', 'seq'))
- grad_query_weight: float32 [512, 512], P(('dp', 'seq'))
- grad_kv_weight: float32 [512, 128], P(('dp', 'seq'))
- grad_router_weight: float32 [512, 8], P(('dp', 'seq'))
- grad_out_weight: float32 [512, 512], P(('dp', 'seq'))
- grad_ln2_gain: float32 [512], P(('dp', 'seq'))
- grad_ln2_bias: float32 [512], P(('dp', 'seq'))
- grad_up_weight: float32 [512, 2048], P(('dp', 'seq'))
- grad_up_bias: float32 [2048], P(('dp', 'seq'))
- grad_down_weight: float32 [2048, 512], P(('dp', 'seq'))
- grad_down_bias: float32 [512], P(('dp', 'seq'))
Inputs may be any that keep to these rules, and one draw needn't show every extreme that they name: `routes`: each token names two different experts; every expert is named by some token. `segments`: within a sequence the ids never fall; a document has 1 to 1536 tokens, and one has exactly 1536.
All inputs are finite; a program needn't handle non-finite values.
Results may differ from a plain program's by a relative error of at most 0.015.
Values may be sent and summed in bfloat16 or wider, within the bound.
No kernel may reach another device: no remote copies, remote signals or barrier semaphores. Data moves between devices by JAX's collectives and lax.ppermute only.
A program may use at most 192 MiB of HBM per device.

v0:
```python
import jax
import jax.numpy as jnp
from jax import lax
from jax.sharding import PartitionSpec as P

EPS = 1e-05


def passed_along(value, axis, steps):
    count = lax.axis_size(axis)
    leading, last = (max(0, -steps), min(count, count - steps))
    return lax.ppermute(value, axis, [(source, source + steps) for source in range(leading, last)])


def normalize(values):
    centered = values - jnp.mean(values, -1, keepdims=True)
    inv_dev = lax.rsqrt(jnp.mean(centered * centered, -1, keepdims=True) + EPS)
    return (centered * inv_dev, inv_dev)


def norm_back(grad_norm, gain, normed, inv_dev):
    scaled = grad_norm * gain.astype(jnp.float32)
    return inv_dev * (
        scaled
        - jnp.mean(scaled, -1, keepdims=True)
        - normed * jnp.mean(scaled * normed, -1, keepdims=True)
    )


def dense(left, right):
    return jnp.dot(left, right, preferred_element_type=jnp.float32)


def dense_tn(left, right):
    return lax.dot_general(
        left, right, (((0,), (0,)), ((), ())), preferred_element_type=jnp.float32
    )


def dense_nt(left, right):
    return lax.dot_general(
        left, right, (((1,), (1,)), ((), ())), preferred_element_type=jnp.float32
    )


def masked_scores(queries, keyvals, allowed, score_scale, head_size):
    keys = keyvals[:, :head_size]
    raw = jnp.einsum("hqd,kd->hqk", queries, keys, preferred_element_type=jnp.float32) * score_scale
    return jnp.where(allowed[None], raw, -1e30)


def attend_group(queries, keyvals, allowed, score_scale, head_size):
    scores = masked_scores(queries, keyvals, allowed, score_scale, head_size)
    peak = jnp.max(scores, -1, keepdims=True)
    expo = jnp.exp(scores - peak)
    totals = jnp.sum(expo, -1, keepdims=True)
    probs = expo / totals
    values = keyvals[:, head_size:]
    outcome = jnp.einsum(
        "hqk,kd->hqd", probs.astype(jnp.bfloat16), values, preferred_element_type=jnp.float32
    )
    return (outcome, peak[..., 0] + jnp.log(totals[..., 0]))


def attend_back(queries, keyvals, allowed, log_sums, grad_out, score_scale, head_size):
    scores = masked_scores(queries, keyvals, allowed, score_scale, head_size)
    probs = jnp.exp(scores - log_sums[..., None])
    keys = keyvals[:, :head_size]
    values = keyvals[:, head_size:]
    grad_probs = jnp.einsum("hqd,kd->hqk", grad_out, values, preferred_element_type=jnp.float32)
    inner = jnp.sum(grad_probs * probs, -1, keepdims=True)
    grad_scores = (probs * (grad_probs - inner)).astype(jnp.bfloat16)
    grad_query = (
        jnp.einsum("hqk,kd->hqd", grad_scores, keys, preferred_element_type=jnp.float32)
        * score_scale
    )
    grad_key = (
        jnp.einsum("hqk,hqd->kd", grad_scores, queries, preferred_element_type=jnp.float32)
        * score_scale
    )
    grad_value = jnp.einsum(
        "hqk,hqd->kd", probs.astype(jnp.bfloat16), grad_out, preferred_element_type=jnp.float32
    )
    return (grad_query, jnp.concatenate([grad_key, grad_value], -1))


def on_device(
    block_in,
    routes,
    segments,
    cotangent,
    ln1_gain,
    ln1_bias,
    query_weight,
    kv_weight,
    router_weight,
    out_weight,
    ln2_gain,
    ln2_bias,
    up_weight,
    up_bias,
    down_weight,
    down_bias,
):
    micro_count, seq_count, local_len, width = block_in.shape
    full_len = segments.shape[2]
    experts = router_weight.shape[1]
    head_size = kv_weight.shape[1] // 2
    token_rows = seq_count * local_len
    group_heads = min(experts, max(1, 512 // local_len))
    group_count = experts // group_heads
    score_scale = head_size ** (-0.5)
    spread = lax.axis_size(("dp", "seq"))
    longest = full_len * 3 // 4
    reach = min(lax.axis_size("seq"), (longest - 2) // local_len + 2)
    own_shard = lax.axis_index("seq")
    start_pos = own_shard * local_len
    query_pos = start_pos + jnp.arange(local_len, dtype=jnp.int32)
    causal = query_pos[:, None] >= jnp.arange(full_len, dtype=jnp.int32)[None, :]
    expert_ids = jnp.arange(experts, dtype=jnp.int32)
    shard_list = (
        ln1_gain,
        ln1_bias,
        query_weight,
        kv_weight,
        router_weight,
        out_weight,
        ln2_gain,
        ln2_bias,
        up_weight,
        up_bias,
        down_weight,
        down_bias,
    )
    totals = [
        jnp.zeros((piece.shape[0] * spread,) + piece.shape[1:], jnp.float32) for piece in shard_list
    ]
    outputs = []
    input_grads = []
    for micro_index in range(micro_count):
        fetched = (
            lax.all_gather(ln1_gain, ("dp", "seq"), axis=0, tiled=True),
            lax.all_gather(ln1_bias, ("dp", "seq"), axis=0, tiled=True),
            lax.all_gather(query_weight, ("dp", "seq"), axis=0, tiled=True),
            lax.all_gather(kv_weight, ("dp", "seq"), axis=0, tiled=True),
            lax.all_gather(router_weight, ("dp", "seq"), axis=0, tiled=True),
            lax.all_gather(out_weight, ("dp", "seq"), axis=0, tiled=True),
            lax.all_gather(ln2_gain, ("dp", "seq"), axis=0, tiled=True),
            lax.all_gather(ln2_bias, ("dp", "seq"), axis=0, tiled=True),
            lax.all_gather(up_weight, ("dp", "seq"), axis=0, tiled=True),
            lax.all_gather(up_bias, ("dp", "seq"), axis=0, tiled=True),
            lax.all_gather(down_weight, ("dp", "seq"), axis=0, tiled=True),
            lax.all_gather(down_bias, ("dp", "seq"), axis=0, tiled=True),
        )
        (
            gain_one,
            shift_one,
            query_full,
            keyval_full,
            router_full,
            output_full,
            gain_two,
            shift_two,
            up_full,
            upshift_full,
            down_full,
            downshift_full,
        ) = fetched
        tokens = block_in[micro_index].reshape(token_rows, width).astype(jnp.float32)
        normed_one, inv_one = normalize(tokens)
        hidden_low = (
            normed_one * gain_one.astype(jnp.float32) + shift_one.astype(jnp.float32)
        ).astype(jnp.bfloat16)
        hidden_wide = hidden_low.astype(jnp.float32)
        logits = dense(hidden_low, router_full)
        route_rows = routes[micro_index].reshape(token_rows, 2)
        pick_first = (route_rows[:, 0:1] == expert_ids).astype(jnp.float32)
        pick_second = (route_rows[:, 1:2] == expert_ids).astype(jnp.float32)
        first = jnp.sum(logits * pick_first, -1, keepdims=True)
        second = jnp.sum(logits * pick_second, -1, keepdims=True)
        peak = jnp.maximum(first, second)
        exp_first = jnp.exp(first - peak)
        exp_second = jnp.exp(second - peak)
        gate_first = exp_first / (exp_first + exp_second)
        gate_second = exp_second / (exp_first + exp_second)
        gates = gate_first * pick_first + gate_second * pick_second
        queries = dense(hidden_low, query_full).astype(jnp.bfloat16)
        keyvals = dense(hidden_low, keyval_full).astype(jnp.bfloat16)
        keyvals_all = lax.all_gather(
            keyvals.reshape(seq_count, local_len, 2 * head_size), "seq", axis=1, tiled=True
        )
        seg_rows = segments[micro_index]
        seg_local = lax.dynamic_slice_in_dim(seg_rows, start_pos, local_len, 1)
        allowed = (seg_local[:, :, None] == seg_rows[:, None, :]) & causal[None]
        query_groups = queries.reshape(
            seq_count, local_len, group_count, group_heads, head_size
        ).transpose(0, 2, 3, 1, 4)

        def forward_sequence(item):
            seq_queries, seq_keyvals, seq_allowed = item
            return lax.map(
                lambda group_query: attend_group(
                    group_query, seq_keyvals, seq_allowed, score_scale, head_size
                ),
                seq_queries,
            )

        mixed_groups, log_sums = lax.map(forward_sequence, (query_groups, keyvals_all, allowed))
        mixed = mixed_groups.transpose(0, 3, 1, 2, 4).reshape(token_rows, experts, head_size)
        routed = (
            (gates[:, :, None] * mixed)
            .astype(jnp.bfloat16)
            .reshape(token_rows, experts * head_size)
        )
        middle = tokens + dense(routed, output_full)
        normed_two, inv_two = normalize(middle)
        second_low = (
            normed_two * gain_two.astype(jnp.float32) + shift_two.astype(jnp.float32)
        ).astype(jnp.bfloat16)
        pre_act = dense(second_low, up_full) + upshift_full.astype(jnp.float32)
        sigma = jax.nn.sigmoid(pre_act)
        active = (pre_act * sigma).astype(jnp.bfloat16)
        branch = dense(active, down_full) + downshift_full.astype(jnp.float32)
        outputs.append((middle + branch).astype(jnp.bfloat16).reshape(seq_count, local_len, width))
        back_weights = (
            lax.all_gather(ln1_gain, ("dp", "seq"), axis=0, tiled=True),
            lax.all_gather(ln1_bias, ("dp", "seq"), axis=0, tiled=True),
            lax.all_gather(query_weight, ("dp", "seq"), axis=0, tiled=True),
            lax.all_gather(kv_weight, ("dp", "seq"), axis=0, tiled=True),
            lax.all_gather(router_weight, ("dp", "seq"), axis=0, tiled=True),
            lax.all_gather(out_weight, ("dp", "seq"), axis=0, tiled=True),
            lax.all_gather(ln2_gain, ("dp", "seq"), axis=0, tiled=True),
            lax.all_gather(ln2_bias, ("dp", "seq"), axis=0, tiled=True),
            lax.all_gather(up_weight, ("dp", "seq"), axis=0, tiled=True),
            lax.all_gather(up_bias, ("dp", "seq"), axis=0, tiled=True),
            lax.all_gather(down_weight, ("dp", "seq"), axis=0, tiled=True),
            lax.all_gather(down_bias, ("dp", "seq"), axis=0, tiled=True),
        )
        (
            gain_one,
            shift_one,
            query_full,
            keyval_full,
            router_full,
            output_full,
            gain_two,
            shift_two,
            up_full,
            upshift_full,
            down_full,
            downshift_full,
        ) = back_weights
        grad_out = cotangent[micro_index].reshape(token_rows, width)
        grad_wide = grad_out.astype(jnp.float32)
        grad_active = dense_nt(grad_out, down_full).astype(jnp.bfloat16).astype(jnp.float32)
        grad_pre = (grad_active * (sigma * (1.0 + pre_act * (1.0 - sigma)))).astype(jnp.bfloat16)
        grad_second = dense_nt(grad_pre, up_full)
        grad_middle = grad_wide + norm_back(grad_second, gain_two, normed_two, inv_two)
        grad_att = grad_middle.astype(jnp.bfloat16)
        grad_routed = (
            dense_nt(grad_att, output_full)
            .astype(jnp.bfloat16)
            .reshape(token_rows, experts, head_size)
            .astype(jnp.float32)
        )
        grad_gates = jnp.sum(grad_routed * mixed, -1)
        grad_mixed = (gates[:, :, None] * grad_routed).astype(jnp.bfloat16)
        grad_first = jnp.sum(grad_gates * pick_first, -1, keepdims=True)
        grad_other = jnp.sum(grad_gates * pick_second, -1, keepdims=True)
        common = gate_first * grad_first + gate_second * grad_other
        grad_logits = (
            gate_first * (grad_first - common) * pick_first
            + gate_second * (grad_other - common) * pick_second
        )
        grad_groups = grad_mixed.reshape(
            seq_count, local_len, group_count, group_heads, head_size
        ).transpose(0, 2, 3, 1, 4)

        def backward_sequence(item):
            seq_queries, seq_keyvals, seq_allowed, seq_logs, seq_grads = item

            def group_step(carry, group_item):
                group_query, group_log, group_grad = group_item
                grad_query, grad_keyval = attend_back(
                    group_query,
                    seq_keyvals,
                    seq_allowed,
                    group_log,
                    group_grad,
                    score_scale,
                    head_size,
                )
                return (carry + grad_keyval, grad_query)

            return lax.scan(
                group_step,
                jnp.zeros((full_len, 2 * head_size), jnp.float32),
                (seq_queries, seq_logs, seq_grads),
            )

        keyval_terms, query_terms = lax.map(
            backward_sequence, (query_groups, keyvals_all, allowed, log_sums, grad_groups)
        )
        summed = jnp.zeros((seq_count, local_len, 2 * head_size), jnp.float32)
        for offset in range(reach):
            target = jnp.maximum(own_shard - offset, 0) * local_len
            piece = lax.dynamic_slice_in_dim(keyval_terms, target, local_len, 1)
            summed = summed + passed_along(piece.astype(jnp.bfloat16), "seq", -offset).astype(
                piece.dtype
            )
        grad_keyvals = summed.astype(jnp.bfloat16).reshape(token_rows, 2 * head_size)
        grad_queries = (
            query_terms.transpose(0, 3, 1, 2, 4)
            .reshape(token_rows, experts * head_size)
            .astype(jnp.bfloat16)
        )
        grad_hidden = (
            dense_nt(grad_queries, query_full)
            + dense_nt(grad_keyvals, keyval_full)
            + jnp.dot(
                grad_logits, router_full.astype(jnp.float32).T, precision=lax.Precision.HIGHEST
            )
        )
        grad_tokens = grad_middle + norm_back(grad_hidden, gain_one, normed_one, inv_one)
        input_grads.append(grad_tokens.reshape(seq_count, local_len, width))
        grad_router = lax.dot_general(
            hidden_wide,
            grad_logits,
            (((0,), (0,)), ((), ())),
            precision=lax.Precision.HIGHEST,
            preferred_element_type=jnp.float32,
        )
        new_terms = (
            jnp.sum(grad_hidden * normed_one, 0),
            jnp.sum(grad_hidden, 0),
            dense_tn(hidden_low, grad_queries),
            dense_tn(hidden_low, grad_keyvals),
            grad_router,
            dense_tn(routed, grad_att),
            jnp.sum(grad_second * normed_two, 0),
            jnp.sum(grad_second, 0),
            dense_tn(second_low, grad_pre),
            jnp.sum(grad_pre.astype(jnp.float32), 0),
            dense_tn(active, grad_out),
            jnp.sum(grad_wide, 0),
        )
        totals = [older + newer for older, newer in zip(totals, new_terms)]
    reduced = (
        lax.psum_scatter(totals[0], ("dp", "seq"), scatter_dimension=0, tiled=True),
        lax.psum_scatter(totals[1], ("dp", "seq"), scatter_dimension=0, tiled=True),
        lax.psum_scatter(totals[2], ("dp", "seq"), scatter_dimension=0, tiled=True),
        lax.psum_scatter(totals[3], ("dp", "seq"), scatter_dimension=0, tiled=True),
        lax.psum_scatter(totals[4], ("dp", "seq"), scatter_dimension=0, tiled=True),
        lax.psum_scatter(totals[5], ("dp", "seq"), scatter_dimension=0, tiled=True),
        lax.psum_scatter(totals[6], ("dp", "seq"), scatter_dimension=0, tiled=True),
        lax.psum_scatter(totals[7], ("dp", "seq"), scatter_dimension=0, tiled=True),
        lax.psum_scatter(totals[8], ("dp", "seq"), scatter_dimension=0, tiled=True),
        lax.psum_scatter(totals[9], ("dp", "seq"), scatter_dimension=0, tiled=True),
        lax.psum_scatter(totals[10], ("dp", "seq"), scatter_dimension=0, tiled=True),
        lax.psum_scatter(totals[11], ("dp", "seq"), scatter_dimension=0, tiled=True),
    )
    return (
        jnp.stack(outputs),
        jnp.stack(input_grads),
        reduced[0],
        reduced[1],
        reduced[2],
        reduced[3],
        reduced[4],
        reduced[5],
        reduced[6],
        reduced[7],
        reduced[8],
        reduced[9],
        reduced[10],
        reduced[11],
    )


def solution(mesh):
    placed = (
        P(None, "dp", "seq", None),
        P(None, "dp", "seq", None),
        P(None, "dp", None),
        P(None, "dp", "seq", None),
        P(("dp", "seq")),
        P(("dp", "seq")),
        P(("dp", "seq"), None),
        P(("dp", "seq"), None),
        P(("dp", "seq"), None),
        P(("dp", "seq"), None),
        P(("dp", "seq")),
        P(("dp", "seq")),
        P(("dp", "seq"), None),
        P(("dp", "seq")),
        P(("dp", "seq"), None),
        P(("dp", "seq")),
    )
    return jax.shard_map(
        on_device,
        mesh=mesh,
        in_specs=placed,
        out_specs=(
            P(None, "dp", "seq", None),
            P(None, "dp", "seq", None),
            P(("dp", "seq")),
            P(("dp", "seq")),
            P(("dp", "seq"), None),
            P(("dp", "seq"), None),
            P(("dp", "seq"), None),
            P(("dp", "seq"), None),
            P(("dp", "seq")),
            P(("dp", "seq")),
            P(("dp", "seq"), None),
            P(("dp", "seq")),
            P(("dp", "seq"), None),
            P(("dp", "seq")),
        ),
        check_vma=False,
    )
```

profile of v0, /device:TPU:0, one launch (start us, length us, event | category | flops | bytes accessed | tf_op | source)
XLA Modules:
  0.0 1616.8 jit_solution(4586670554735094862)
XLA Ops:
  13.4 42.3 %all-reduce.13 = (bf16[512]{0:T(512)(128)(2,1)S(1)}, bf16[512]{0:T(512)(128)(2,1)S(1)}, bf16[512]{0:T(512)(128)(2,1)}, bf16[512]{0:T(512)(128)(2,1)}, bf16[512]{0:T(512)(128)(2,1)}, /*index=5*/bf16[2048]{0:T(1024)(128)(2,1)}) all-reduce(bf16[512]{0:T(512)(128)(2,1)S(1)} %dynamic-update-slice.1, ...), channel_id=1, replica_groups=mesh['dp'=8,'seq'=4] {'dp','seq'}, use_global_device_ids=true, to_apply=%add.1 | all-reduce | flops 4608 | bytes 18432
  56.3 70.3 %all_gather.33 = bf16[512,512]{1,0:T(8,128)(2,1)S(1)} all-gather(bf16[16,512]{1,0:T(8,128)(2,1)S(1)} %copy-done.138), channel_id=1, replica_groups=mesh['dp'=8,'seq'=4] {'dp','seq'}, dimensions={0}, use_global_device_ids=true | all-gather | bytes 540672 | tf_op jit(solution)/shard_map/all_gather | solution.py:144
  126.5 64.2 %all_gather.34 = bf16[512,128]{1,0:T(8,128)(2,1)S(1)} all-gather(bf16[16,128]{1,0:T(8,128)(2,1)S(1)} %copy-done.157), channel_id=1, replica_groups=mesh['dp'=8,'seq'=4] {'dp','seq'}, dimensions={0}, use_global_device_ids=true | all-gather | bytes 135168 | tf_op jit(solution)/shard_map/all_gather | solution.py:145
  198.8 66.1 %all-gather.3 = bf16[32,16,8]{1,2,0:T(8,128)(2,1)S(1)} all-gather(bf16[1,16,8]{1,2,0:T(8,128)(2,1)} %bitcast.588), channel_id=1, replica_groups=mesh['dp'=8,'seq'=4] {'dp','seq'}, dimensions={0}, use_global_device_ids=true | all-gather | bytes 8448 | tf_op jit(solution)/shard_map/all_gather | solution.py:146
  267.4 9.4 all-gather
  279.3 37.9 %while.132 = (s32[]{:T(128)}, f32[8,1,512,64]{2,3,1,0:T(8,128)}, f32[8,1,512]{2,1,0:T(1,128)S(1)}, bf16[8,1,512,64]{3,2,1,0:T(8,128)(2,1)}, bf16[2048,128]{1,0:T...) while((s32[]{:T(128)}, f32[8,1,512,64]{2,3,1,0:T(8,128)}, ...), condition=%wide.region_7.8_spmd.clone, body=%wide.region_4.7_spmd.clone.sunk | while | flops 279969280 | bytes 13927521 | solution.py:201
  319.3 10.0 all-gather.1
  330.4 37.9 %while.133 = (s32[]{:T(128)}, f32[8,1,512,64]{2,3,1,0:T(8,128)}, f32[8,1,512]{2,1,0:T(1,128)S(1)}, bf16[8,1,512,64]{3,2,1,0:T(8,128)(2,1)}, bf16[2048,128]{1,0:T...) while((s32[]{:T(128)}, f32[8,1,512,64]{2,3,1,0:T(8,128)}, ...), condition=%wide.region_17.18_spmd.clone, body=%wide.region_14.17_spmd.clone.sunk | while | flops 279969280 | bytes 13927521 | solution.py:201
  371.5 9.4 all-gather.2
  383.8 42.6 %while.134 = (s32[]{:T(128)}, f32[8,1,512,64]{2,3,1,0:T(8,128)}, f32[8,1,512]{2,1,0:T(1,128)}, bf16[8,1,512,64]{3,2,1,0:T(8,128)(2,1)}, bf16[2048,128]{1,0:T(8,1...) while((s32[]{:T(128)}, f32[8,1,512,64]{2,3,1,0:T(8,128)}, ...), condition=%wide.region_27.28_spmd.clone, body=%wide.region_24.27_spmd.clone.sunk | while | flops 279969280 | bytes 13928029 | solution.py:201
  426.4 2.7 fusion.290
  444.7 67.9 %all_gather.36 = bf16[512,512]{1,0:T(8,128)(2,1)S(1)} all-gather(bf16[16,512]{1,0:T(8,128)(2,1)S(1)} %copy-done.139), channel_id=1, replica_groups=mesh['dp'=8,'seq'=4] {'dp','seq'}, dimensions={0}, use_global_device_ids=true | all-gather | bytes 540672 | tf_op jit(solution)/shard_map/all_gather | solution.py:147
  517.1 5.2 fusion.286
  522.2 5.8 convert_reduce_fusion
  528.0 2.8 fusion.300
  530.9 2.5 copy.118
  535.6 3.1 fusion.283
  538.8 5.4 convert_reduce_fusion.2
  544.2 2.9 fusion.301
  547.0 2.6 copy.106
  549.6 3.5 fusion.285
  553.1 4.5 convert_reduce_fusion.1
  557.6 2.8 fusion.302
  560.5 2.6 copy.112
  563.2 4.0 convert_reduce_fusion.6
  569.8 2.7 fusion.185
  573.6 3.0 fusion.184
  576.7 2.7 fusion.183
  585.7 97.1 %while.135 = (s32[]{:T(128)}, f32[2048,128]{0,1:T(8,128)}, bf16[8,1,512,64]{2,3,1,0:T(8,128)(2,1)}, bf16[8,1,512,64]{3,2,1,0:T(8,128)(2,1)}, bf16[2048,128]{1,0:...) while((s32[]{:T(128)}, f32[2048,128]{0,1:T(8,128)}, ...), condition=%wide.region_34.35_spmd.clone, body=%wide.region_32.34_spmd.clone.sunk | while | flops 684621312 | bytes 37905024 | solution.py:295
  689.2 102.5 %while.136 = (s32[]{:T(128)}, f32[2048,128]{0,1:T(8,128)}, bf16[8,1,512,64]{2,3,1,0:T(8,128)(2,1)}, bf16[8,1,512,64]{3,2,1,0:T(8,128)(2,1)}, bf16[2048,128]{1,0:...) while((s32[]{:T(128)}, f32[2048,128]{0,1:T(8,128)}, ...), condition=%wide.region_44.45_spmd.clone, body=%wide.region_42.44_spmd.clone.sunk | while | flops 684621312 | bytes 37905024 | solution.py:295
  710.7 2.5 maximum_add_fusion.7
  723.5 2.5 maximum_add_fusion.7
  736.4 2.5 maximum_add_fusion.7
  802.5 102.6 %while.137 = (s32[]{:T(128)}, f32[2048,128]{0,1:T(8,128)}, bf16[8,1,512,64]{2,3,1,0:T(8,128)(2,1)}, bf16[8,1,512,64]{3,2,1,0:T(8,128)(2,1)}, bf16[2048,128]{1,0:...) while((s32[]{:T(128)}, f32[2048,128]{0,1:T(8,128)}, ...), condition=%wide.region_54.55_spmd.clone, body=%wide.region_52.54_spmd.clone.sunk | while | flops 684621312 | bytes 37905024 | solution.py:295
  928.6 2.5 convolution_add_fusion.3
  936.2 3.1 fusion.282
  941.2 3.3 add_add_fusion.1
  945.2 3.9 fusion.197
  951.5 3.9 add_add_fusion
  955.5 4.7 fusion.140
  982.4 3.1 fusion.148
  987.8 38.1 %all-reduce.12 = (f32[512]{0:T(512)S(1)}, f32[512]{0:T(512)S(1)}, f32[512]{0:T(512)S(1)}, f32[512]{0:T(512)S(1)}, f32[2048]{0:T(1024)S(1)}, /*index=5*/f32[512]{0:T(512)S(1)}) all-reduce(f32[512]{0:T(512)S(1)} %add_add_fusion.7, f32[512]{0:T(512)S(1)} %add_add_fusion.6, ...), channel_id=5, replica_groups=mesh['dp'=8,'seq'=4] {'dp','seq'}, use_global_device_ids=true, to_apply=%region_63.64.clone | all-reduce | flops 4608 | bytes 36864
  1028.9 2.5 fusion.156
  1034.7 24.4 %reduce-scatter.11.cloned.1.call-done = f32[16,128]{1,0:T(8,128)} async-done(((f32[512,128]{1,0:T(8,128)}), f32[16,128]{1,0:T(8,128)}) %reduce-scatter.11.cloned.1.call-update) | async-done | bytes 8208 | tf_op jit(solution)/shard_map/reduce_scatter | solution.py:352
  1059.1 134.1 %reduce-scatter.13.cloned.1.call-done = f32[16,512]{1,0:T(8,128)} async-done(((f32[512,512]{1,0:T(8,128)}), f32[16,512]{1,0:T(8,128)}) %reduce-scatter.13.cloned.1.call-update) | async-done | bytes 32784 | tf_op jit(solution)/shard_map/reduce_scatter | solution.py:354
  1193.1 134.1 %reduce-scatter.9.cloned.1.call-done = f32[16,512]{1,0:T(8,128)} async-done(((f32[512,512]{1,0:T(8,128)}), f32[16,512]{1,0:T(8,128)}) %reduce-scatter.9.cloned.1.call-update) | async-done | bytes 32784 | tf_op jit(solution)/shard_map/reduce_scatter | solution.py:351
  1327.3 140.5 %reduce-scatter.15.cloned.1.call-done = f32[16,2048]{1,0:T(8,128)} async-done(((f32[512,2048]{1,0:T(8,128)}), f32[16,2048]{1,0:T(8,128)}) %reduce-scatter.15.cloned.1.call-update) | async-done | bytes 131088 | tf_op jit(solution)/shard_map/reduce_scatter | solution.py:357
  1467.8 142.0 %reduce-scatter.17.cloned.1.call-done = f32[64,512]{1,0:T(8,128)} async-done(((f32[2048,512]{1,0:T(8,128)}), f32[64,512]{1,0:T(8,128)}) %reduce-scatter.17.cloned.1.call-update) | async-done | bytes 131088 | tf_op jit(solution)/shard_map/reduce_scatter | solution.py:359
  (877 shorter events, 553.3 us)
Async XLA Ops:
  7.2 509.8 %all-gather.7.cloned.1.call-start = ((), (), s32[]{:S(2)}) async-start(), calls=%async_computation.6 | async-start | bytes 2162688 | tf_op jit(solution)/shard_map/all_gather | solution.py:150
  8.0 514.3 %all-gather.9.cloned.1.call-start = ((), (), s32[]{:S(2)}) async-start(), calls=%async_computation.7 | async-start | bytes 2162688 | tf_op jit(solution)/shard_map/all_gather | solution.py:152
  8.7 970.5 %reduce-scatter.19.cloned.1.call-start = ((), (), s32[]{:S(2)}) async-start(), calls=%async_computation.13 | async-start | bytes 270336
  10.8 115.7 %copy-start.157 = (bf16[16,128]{1,0:T(8,128)(2,1)S(1)}, bf16[16,128]{1,0:T(8,128)(2,1)}, u32[]{:S(2)}) copy-start(bf16[16,128]{1,0:T(8,128)(2,1)} %param.35) | copy-start | bytes 12292
  11.1 503.5 %copy-start.18 = (bf16[1,1,512,512]{2,3,1,0:T(8,128)(2,1)}, bf16[1,1,512,512]{2,3,1,0:T(8,128)(2,1)S(1)}, u32[]{:S(2)}) copy-start(bf16[1,1,512,512]{2,3,1,0:T(8,128)(2,1)S(1)} %copy.143) | copy-start | bytes 1572868
  11.2 180.2 %copy-start.113 = (f32[512]{0:T(512)}, f32[512]{0:T(512)S(1)}, u32[]{:S(2)}) copy-start(f32[512]{0:T(512)S(1)} %broadcast_multiply_fusion.15) | copy-start | bytes 6148
  11.6 504.6 %copy-start.11 = (bf16[1,1,512,512]{2,3,1,0:T(8,128)(2,1)}, bf16[1,1,512,512]{2,3,1,0:T(8,128)(2,1)S(1)}, u32[]{:S(2)}) copy-start(bf16[1,1,512,512]{2,3,1,0:T(8,128)(2,1)S(1)} %copy.144) | copy-start | bytes 1572868
  11.7 182.0 %copy-start.107 = (f32[512]{0:T(512)}, f32[512]{0:T(512)S(1)}, u32[]{:S(2)}) copy-start(f32[512]{0:T(512)S(1)} %broadcast_multiply_fusion.13) | copy-start | bytes 6148
  55.7 139.3 %copy-start.110 = (f32[512]{0:T(512)}, f32[512]{0:T(512)S(1)}, u32[]{:S(2)}) copy-start(f32[512]{0:T(512)S(1)} %convert_element_type.503) | copy-start | bytes 6148
  55.7 139.3 %copy-start.122 = (f32[512]{0:T(512)}, f32[512]{0:T(512)S(1)}, u32[]{:S(2)}) copy-start(f32[512]{0:T(512)S(1)} %convert_element_type.504) | copy-start | bytes 6148
  55.9 456.7 %copy-start.24 = (bf16[1,1,512,512]{2,3,1,0:T(8,128)(2,1)}, bf16[1,1,512,512]{2,3,1,0:T(8,128)(2,1)S(1)}, u32[]{:S(2)}) copy-start(bf16[1,1,512,512]{2,3,1,0:T(8,128)(2,1)S(1)} %copy.142) | copy-start | bytes 1572868
  56.1 139.0 %copy-start.120 = (f32[512]{0:T(512)}, f32[512]{0:T(512)S(1)}, u32[]{:S(2)}) copy-start(f32[512]{0:T(512)S(1)} %broadcast_multiply_fusion.17) | copy-start | bytes 6148
  56.3 138.8 %copy-start.128 = (f32[512]{0:T(512)}, f32[512]{0:T(512)S(1)}, u32[]{:S(2)}) copy-start(f32[512]{0:T(512)S(1)} %add_rsqrt_fusion.5) | copy-start | bytes 6148
  126.5 70.2 %copy-start.14 = (bf16[512,512]{1,0:T(8,128)(2,1)}, bf16[512,512]{1,0:T(8,128)(2,1)S(1)}, u32[]{:S(2)}) copy-start(bf16[512,512]{1,0:T(8,128)(2,1)S(1)} %all_gather.33) | copy-start | bytes 1572868
  191.4 250.9 %copy-start.33 = (bf16[512,512]{0,1:T(8,128)(2,1)}, bf16[512,512]{0,1:T(8,128)(2,1)S(1)}, u32[]{:S(2)}) copy-start(bf16[512,512]{0,1:T(8,128)(2,1)S(1)} %get-tuple-element.809) | copy-start | bytes 1572868
  197.1 68.0 %copy-start.39 = (bf16[8,1,512,64]{2,3,1,0:T(8,128)(2,1)}, bf16[8,1,512,64]{2,3,1,0:T(8,128)(2,1)S(1)}, u32[]{:S(2)}) copy-start(bf16[8,1,512,64]{2,3,1,0:T(8,128)(2,1)S(1)} %fusion.292) | copy-start | bytes 1572868
  265.1 177.2 %copy-start.78 = (bf16[512,8]{0,1:T(8,128)(2,1)}, bf16[512,8]{0,1:T(8,128)(2,1)S(1)}, u32[]{:S(2)}) copy-start(bf16[512,8]{0,1:T(8,128)(2,1)S(1)} %reshape.1278) | copy-start | bytes 24580
  317.3 255.2 %copy-start.74 = (f32[512]{0:T(512)}, f32[512]{0:T(512)S(1)}, u32[]{:S(2)}) copy-start(f32[512]{0:T(512)S(1)} %convert_element_type.509) | copy-start | bytes 6148
  317.3 232.3 %copy-start.76 = (f32[512]{0:T(512)}, f32[512]{0:T(512)S(1)}, u32[]{:S(2)}) copy-start(f32[512]{0:T(512)S(1)} %convert_element_type.510) | copy-start | bytes 6148
  435.3 144.1 %copy-start.105 = (s32[512,1]{0,1:T(1,128)}, s32[512,1]{0,1:T(1,128)S(1)}, u32[]{:S(2)}) copy-start(s32[512,1]{0,1:T(1,128)S(1)} %get-tuple-element.805) | copy-start | bytes 6148
  435.3 144.1 %copy-start.106 = (s32[512,1]{0,1:T(1,128)}, s32[512,1]{0,1:T(1,128)S(1)}, u32[]{:S(2)}) copy-start(s32[512,1]{0,1:T(1,128)S(1)} %get-tuple-element.806) | copy-start | bytes 6148
  435.3 144.7 %copy-start.101 = (s32[512,1]{0,1:T(1,128)}, s32[512,1]{0,1:T(1,128)S(1)}, u32[]{:S(2)}) copy-start(s32[512,1]{0,1:T(1,128)S(1)} %get-tuple-element.858) | copy-start | bytes 6148
  435.4 144.7 %copy-start.103 = (s32[512,1]{0,1:T(1,128)}, s32[512,1]{0,1:T(1,128)S(1)}, u32[]{:S(2)}) copy-start(s32[512,1]{0,1:T(1,128)S(1)} %get-tuple-element.859) | copy-start | bytes 6148
  442.3 138.3 %copy-start.97 = (s32[512,1]{0,1:T(1,128)}, s32[512,1]{0,1:T(1,128)S(1)}, u32[]{:S(2)}) copy-start(s32[512,1]{0,1:T(1,128)S(1)} %get-tuple-element.816) | copy-start | bytes 6148
  442.3 138.3 %copy-start.99 = (s32[512,1]{0,1:T(1,128)}, s32[512,1]{0,1:T(1,128)S(1)}, u32[]{:S(2)}) copy-start(s32[512,1]{0,1:T(1,128)S(1)} %get-tuple-element.817) | copy-start | bytes 6148
  444.7 69.8 %copy-start.44 = (bf16[512,512]{0,1:T(8,128)(2,1)S(1)}, bf16[512,512]{0,1:T(8,128)(2,1)}, u32[]{:S(2)}) copy-start(bf16[512,512]{0,1:T(8,128)(2,1)} %fusion.187) | copy-start | bytes 1572868
  444.7 71.5 %copy-start.46 = (bf16[512,512]{0,1:T(8,128)(2,1)S(1)}, bf16[512,512]{0,1:T(8,128)(2,1)}, u32[]{:S(2)}) copy-start(bf16[512,512]{0,1:T(8,128)(2,1)} %fusion.186) | copy-start | bytes 1572868
  515.1 57.4 %copy-start.82 = (f32[512]{0:T(512)}, f32[512]{0:T(512)S(1)}, u32[]{:S(2)}) copy-start(f32[512]{0:T(512)S(1)} %broadcast_multiply_fusion.14) | copy-start | bytes 6148
  517.0 55.5 %copy-start.84 = (f32[512]{0:T(512)}, f32[512]{0:T(512)S(1)}, u32[]{:S(2)}) copy-start(f32[512]{0:T(512)S(1)} %add_rsqrt_fusion.2) | copy-start | bytes 6148
  582.0 477.0 %reduce-scatter.11.cloned.1.call-start = ((), (), s32[]{:S(2)}) async-start(), calls=%async_computation.9 | async-start | bytes 270336 | tf_op jit(solution)/shard_map/reduce_scatter | solution.py:352
  685.0 229.6 %collective-permute-start = (bf16[1,512,128]{1,2,0:T(8,128)(2,1)}, bf16[1,512,128]{1,2,0:T(8,128)(2,1)S(1)}, u32[]{:S(2)}, u32[]{:S(2)}) collective-permute-start(bf16[1,512,128]{1,2,0:T(8,128)(2,1)} %get-tuple-element.770), channel_id=1, source_target_pairs={{0,0},{1,1},{2,2},{3,3},{4,4},{5,5},{6,6},{7,7},{8,8},{9,9},{10,10... | collective-permute-start | bytes 393224 | tf_op jit(solution)/shard_map/ppermute | solution.py:12
  794.0 112.8 %collective-permute-start.4 = (bf16[1,512,128]{1,2,0:T(8,128)(2,1)}, bf16[1,512,128]{1,2,0:T(8,128)(2,1)S(1)}, u32[]{:S(2)}, u32[]{:S(2)}) collective-permute-start(bf16[1,512,128]{1,2,0:T(8,128)(2,1)} %get-tuple-element.777), channel_id=1, source_target_pairs={{0,0},{1,1},{2,2},{3,3},{4,4},{5,5},{6,6},{7,7},{8,8},{9,9},{10,10... | collective-permute-start | bytes 393224 | tf_op jit(solution)/shard_map/ppermute | solution.py:12
  794.9 113.2 %collective-permute-start.5 = (bf16[1,512,128]{1,2,0:T(8,128)(2,1)}, bf16[1,512,128]{1,2,0:T(8,128)(2,1)S(1)}, u32[]{:S(2)}, u32[]{:S(2)}) collective-permute-start(bf16[1,512,128]{1,2,0:T(8,128)(2,1)} %get-tuple-element.778), channel_id=1, source_target_pairs={{1,0},{2,1},{3,2},{5,4},{6,5},{7,6},{9,8},{10,9},{11,10},{13,12},{... | collective-permute-start | bytes 393224 | tf_op jit(solution)/shard_map/ppermute | solution.py:12
  796.2 113.2 %collective-permute-start.6 = (bf16[1,512,128]{1,2,0:T(8,128)(2,1)}, bf16[1,512,128]{1,2,0:T(8,128)(2,1)}, u32[]{:S(2)}, u32[]{:S(2)}) collective-permute-start(bf16[1,512,128]{1,2,0:T(8,128)(2,1)} %get-tuple-element.780), channel_id=1, source_target_pairs={{2,0},{3,1},{6,4},{7,5},{10,8},{11,9},{14,12},{15,13},{18,16},{19,... | collective-permute-start | bytes 393224 | tf_op jit(solution)/shard_map/ppermute | solution.py:12
  797.5 113.2 %collective-permute-start.7 = (bf16[1,512,128]{1,2,0:T(8,128)(2,1)}, bf16[1,512,128]{1,2,0:T(8,128)(2,1)}, u32[]{:S(2)}, u32[]{:S(2)}) collective-permute-start(bf16[1,512,128]{1,2,0:T(8,128)(2,1)} %get-tuple-element.779), channel_id=1, source_target_pairs={{3,0},{7,4},{11,8},{15,12},{19,16},{23,20},{27,24},{31,28}} | collective-permute-start | bytes 393224 | tf_op jit(solution)/shard_map/ppermute | solution.py:12
  802.5 110.6 %copy-start.111 = (f32[512]{0:T(512)S(1)}, f32[512]{0:T(512)}, u32[]{:S(2)}) copy-start(f32[512]{0:T(512)} %copy-done.110) | copy-start | bytes 6148
  802.5 110.6 %copy-start.114 = (f32[512]{0:T(512)S(1)}, f32[512]{0:T(512)}, u32[]{:S(2)}) copy-start(f32[512]{0:T(512)} %copy-done.113) | copy-start | bytes 6148
  906.8 9.1 collective-permute-start.1
  908.1 9.0 collective-permute-start.2
  909.4 11.6 collective-permute-start.3
  910.7 11.8 collective-permute-start.10
  914.6 10.0 collective-permute-start.11
  915.9 8.7 collective-permute-start.8
  917.1 8.1 collective-permute-start.9
  926.4 266.7 %reduce-scatter.13.cloned.1.call-start = ((), (), s32[]{:S(2)}) async-start(), calls=%async_computation.10 | async-start | bytes 1081344 | tf_op jit(solution)/shard_map/reduce_scatter | solution.py:354
  931.2 396.1 %reduce-scatter.9.cloned.1.call-start = ((), (), s32[]{:S(2)}) async-start(), calls=%async_computation.8 | async-start | bytes 1081344 | tf_op jit(solution)/shard_map/reduce_scatter | solution.py:351
  936.0 531.7 %reduce-scatter.15.cloned.1.call-start = ((), (), s32[]{:S(2)}) async-start(), calls=%async_computation.11 | async-start | bytes 4325376 | tf_op jit(solution)/shard_map/reduce_scatter | solution.py:357
  944.5 665.2 %reduce-scatter.17.cloned.1.call-start = ((), (), s32[]{:S(2)}) async-start(), calls=%async_computation.12 | async-start | bytes 4325376 | tf_op jit(solution)/shard_map/reduce_scatter | solution.py:359
  (151 other events, 1312.5 us)
Sparse Core Ops, SparseCore 0:
  10.9 59.5 all-gather.6
  73.4 56.1 all-gather.8
  582.2 130.7 reduce-scatter.18
  926.5 132.4 reduce-scatter.10
  1061.7 131.3 reduce-scatter.12
  1195.9 131.3 reduce-scatter.8
  1330.1 137.6 reduce-scatter.14
  1470.6 139.0 reduce-scatter.16
where the time goes:
time: 1630 us; the launch traced here: 1620 us
  waiting for transfers between devices  583 us (36%)
  matrix products  430 us (26%)
  blocking collectives  378 us (23%)
  other arithmetic  118 us (7%)
  local copies, waits for them, and re-layouts  76.8 us (5%)
  between operations  16.7 us (1%)
    reduce_scatter x1, waiting for transfers between devices, on_device(): lax.psum_scatter(totals[10], ('dp', 'seq'), scatter_dimension=0, tiled=True)  142 us
    reduce_scatter x1, waiting for transfers between devices, on_device(): lax.psum_scatter(totals[8], ('dp', 'seq'), scatter_dimension=0, tiled=True)  140 us
    reduce_scatter x1, waiting for transfers between devices, on_device(): lax.psum_scatter(totals[2], ('dp', 'seq'), scatter_dimension=0, tiled=True)  134 us
    reduce_scatter x1, waiting for transfers between devices, on_device(): lax.psum_scatter(totals[5], ('dp', 'seq'), scatter_dimension=0, tiled=True)  134 us
    dot_general x48, matrix products, masked_scores(): jnp.einsum('hqd,kd->hqk', queries, keys, preferred_element_type=jnp.float32)  109 us
    unnamed x2, blocking collectives  80.4 us
    all_gather x1, blocking collectives, on_device(): lax.all_gather(query_weight, ('dp', 'seq'), axis=0, tiled=True)  70.3 us
    all_gather x1, blocking collectives, on_device(): lax.all_gather(out_weight, ('dp', 'seq'), axis=0, tiled=True)  67.9 us
  transfers between devices with their start and end apart: 20, of which 9 were waited for; matrix products, arithmetic and copies ran while one was open for 35% of the time, Pallas kernels for 0%

commit v1 on v0

v1 whole, which is shorter than its diff:
```python
import functools

import jax
import jax.numpy as jnp
from jax import lax
from jax.experimental import pallas as pl
from jax.experimental.pallas import tpu as pltpu
from jax.sharding import PartitionSpec as P

EPS = 1e-05
LANES = 128
VMEM_LIMIT = 56 * 1024 * 1024
BF16 = jnp.bfloat16
F32 = jnp.float32


def call_params():
    return pltpu.CompilerParams(vmem_limit_bytes=VMEM_LIMIT)


def cost(flops, bytes_accessed, transcendentals=0):
    return pl.CostEstimate(
        flops=int(flops), bytes_accessed=int(bytes_accessed), transcendentals=int(transcendentals)
    )


def dot_nn(left, right):
    return lax.dot_general(left, right, (((1,), (0,)), ((), ())), preferred_element_type=F32)


def dot_nt(left, right):
    return lax.dot_general(left, right, (((1,), (1,)), ((), ())), preferred_element_type=F32)


def lanes_of(rows, width):
    return lax.broadcasted_iota(jnp.int32, (rows, width), 1)


def fold_matrix(width, head, shift):
    source = lax.broadcasted_iota(jnp.int32, (width, LANES), 0)
    target = lax.broadcasted_iota(jnp.int32, (width, LANES), 1)
    return jnp.where(target == shift + lax.rem(source, head), 1.0, 0.0).astype(BF16)


def unfold_matrix(width, head, shift):
    source = lax.broadcasted_iota(jnp.int32, (LANES, width), 1)
    target = lax.broadcasted_iota(jnp.int32, (LANES, width), 0)
    return jnp.where(target == shift + lax.rem(source, head), 1.0, 0.0).astype(BF16)


def rows_of(columns, picked):
    row = lax.broadcasted_iota(jnp.int32, (8, LANES), 0)
    lane = lax.broadcasted_iota(jnp.int32, (8, LANES), 1)
    chosen = jnp.zeros((8, LANES), F32)
    for at, column in enumerate(picked):
        chosen = jnp.where((row == at) & (lane == column), 1.0, chosen)
    return dot_nt(chosen.astype(BF16), columns)


def normalize(values):
    centered = values - jnp.mean(values, -1, keepdims=True)
    inv_dev = lax.rsqrt(jnp.mean(centered * centered, -1, keepdims=True) + EPS)
    return centered * inv_dev, inv_dev


def norm_back(grad, gain, normed, inv_dev):
    scaled = grad * gain
    return inv_dev * (
        scaled
        - jnp.mean(scaled, -1, keepdims=True)
        - normed * jnp.mean(scaled * normed, -1, keepdims=True)
    )


def pre_kernel(experts, head, x_ref, routes_ref, weight_ref, hidden_ref, kv_ref, q_ref, gate_ref):
    width = x_ref.shape[1]
    inner = experts * head
    extras = weight_ref[:, inner + LANES :]
    vectors = rows_of(extras, (experts, experts + 1))
    normed, _ = normalize(x_ref[...].astype(F32))
    hidden = (normed * vectors[0:1] + vectors[1:2]).astype(BF16)
    hidden_ref[...] = hidden
    big = dot_nn(hidden, weight_ref[...])
    rows = big.shape[0]
    kv_ref[...] = big[:, inner : inner + LANES].astype(BF16)
    logits = big[:, inner + LANES :]
    lane = lanes_of(rows, LANES)
    first, second = routes_ref[:, 0:1], routes_ref[:, 1:2]
    logit_one = jnp.sum(jnp.where(lane == first, logits, 0.0), -1, keepdims=True)
    logit_two = jnp.sum(jnp.where(lane == second, logits, 0.0), -1, keepdims=True)
    peak = jnp.maximum(logit_one, logit_two)
    exp_one = jnp.exp(logit_one - peak)
    exp_two = jnp.exp(logit_two - peak)
    total = exp_one + exp_two
    gate_ref[...] = jnp.where(lane == 0, exp_one / total, jnp.where(lane == 1, exp_two / total, 0.0))
    queries = (big[:, :inner] * (head**-0.5)).astype(BF16)
    owner = lax.div(lanes_of(rows, inner), head)
    fold = fold_matrix(inner, head, 0)
    zero = jnp.zeros_like(queries)
    q_ref[0] = dot_nn(jnp.where(owner == first, queries, zero), fold).astype(BF16)
    q_ref[1] = dot_nn(jnp.where(owner == second, queries, zero), fold).astype(BF16)


def masked(scores, start, key_at, query_at):
    keys = key_at + lax.broadcasted_iota(jnp.int32, scores.shape, 0)
    queries = query_at + lax.rem(
        lax.broadcasted_iota(jnp.int32, (1, scores.shape[1]), 1), scores.shape[1] // 2
    )
    return jnp.where((keys >= start) & (keys <= queries), scores, -1e30)


def attend_kernel(
    reach, chunk, head, low_ref, q_ref, start_ref, *rest
):
    pieces = rest[:reach]
    mixed_ref, lse_ref, kv_buf, vt_buf, peak_ref, total_ref, acc_ref = rest[reach:]
    seq, tile = pl.program_id(0), pl.program_id(1)
    local = pieces[0].shape[1]
    tokens = q_ref.shape[1]
    per_piece = local // chunk

    @pl.when(tile == 0)
    def _():
        for at in range(reach):
            for part in range(per_piece):
                block = pieces[at][0, part * chunk : (part + 1) * chunk, :]
                kv_buf[at * per_piece + part] = block
                row = lax.broadcasted_iota(jnp.int32, (LANES, chunk), 0)
                vt_buf[at * per_piece + part] = jnp.where(
                    row >= head, block.astype(F32).T, 0.0
                ).astype(BF16)

    queries = jnp.concatenate([q_ref[0], q_ref[1]], 0)
    start = start_ref[0]
    start = jnp.concatenate([start, start], 1)
    query_at = (reach - 1) * local + tile * tokens
    peak_ref[...] = jnp.full_like(peak_ref, -1e30)
    total_ref[...] = jnp.zeros_like(total_ref)
    acc_ref[...] = jnp.zeros_like(acc_ref)

    def step(at, carry):
        scores = masked(dot_nt(kv_buf[at], queries), start, at * chunk, query_at)
        peak = jnp.maximum(peak_ref[...], jnp.max(scores, 0, keepdims=True))
        fade = jnp.exp(peak_ref[...] - peak)
        expo = jnp.exp(scores - peak)
        total_ref[...] = total_ref[...] * fade + jnp.sum(expo, 0, keepdims=True)
        acc_ref[...] = acc_ref[...] * fade + dot_nn(vt_buf[at], expo.astype(BF16))
        peak_ref[...] = peak
        return carry

    low = low_ref[seq * pl.num_programs(1) + tile]
    high = (query_at + tokens - 1) // chunk + 1
    lax.fori_loop(low, high, step, 0)
    mixed = (acc_ref[...] / total_ref[...]).T
    mixed_ref[0] = mixed[:tokens]
    mixed_ref[1] = mixed[tokens:]
    lse_ref[0] = peak_ref[...] + jnp.log(total_ref[...])


def mid_kernel(
    experts,
    head,
    ff_chunk,
    x_ref,
    dy_ref,
    routes_ref,
    gate_ref,
    mixed_ref,
    weight_ref,
    down_ref,
    out_ref,
    grad_mid_ref,
    grad_mixed_ref,
    grad_logit_ref,
    d_weight_ref,
    d_down_ref,
    acc_out,
    acc_up,
    acc_down,
    acc_vec,
    acc_upb,
    branch_ref,
    gsec_ref,
):
    step, last = pl.program_id(0), pl.num_programs(0) - 1
    rows, width = x_ref.shape
    inner = experts * head
    ff = down_ref.shape[0]

    @pl.when(step == 0)
    def _():
        acc_out[...] = jnp.zeros_like(acc_out)
        acc_up[...] = jnp.zeros_like(acc_up)
        acc_down[...] = jnp.zeros_like(acc_down)
        acc_vec[...] = jnp.zeros_like(acc_vec)
        acc_upb[...] = jnp.zeros_like(acc_upb)

    vectors = rows_of(weight_ref[:, width + ff :], (0, 1, 2))
    gain, shift, down_bias = vectors[0:1], vectors[1:2], vectors[2:3]
    first, second = routes_ref[:, 0:1], routes_ref[:, 1:2]
    gate_one, gate_two = gate_ref[:, 0:1], gate_ref[:, 1:2]
    owner = lax.div(lanes_of(rows, inner), head)
    unfold = unfold_matrix(inner, head, head)
    fold = fold_matrix(inner, head, head)
    mixed_one, mixed_two = mixed_ref[0], mixed_ref[1]
    routed_one = dot_nn((gate_one * mixed_one).astype(BF16), unfold)
    routed_two = dot_nn((gate_two * mixed_two).astype(BF16), unfold)
    routed = jnp.where(
        owner == first, routed_one, jnp.where(owner == second, routed_two, 0.0)
    )
    middle = x_ref[...].astype(F32) + dot_nn(routed.astype(BF16), weight_ref[:, :width])
    normed, inv_dev = normalize(middle)
    second_low = (normed * gain + shift).astype(BF16)
    second_t = (normed * gain + shift).T.astype(BF16)
    dy = dy_ref[...]
    dy_wide = dy.astype(F32)
    dy_t = dy_wide.T.astype(BF16)
    branch_ref[...] = middle + down_bias
    gsec_ref[...] = jnp.zeros_like(gsec_ref)

    def ff_step(at, carry):
        lo = pl.multiple_of(at * ff_chunk, ff_chunk)
        up = weight_ref[:, pl.ds(width + lo, ff_chunk)]
        down = down_ref[pl.ds(lo, ff_chunk), :width]
        up_bias = rows_of(down_ref[pl.ds(lo, ff_chunk), width:], (0,))[0:1]
        pre_act = dot_nn(second_low, up) + up_bias
        sigma = 1.0 / (1.0 + jnp.exp(-pre_act))
        active = (pre_act * sigma).astype(BF16)
        branch_ref[...] += dot_nn(active, down)
        grad_active = dot_nt(dy, down).astype(BF16).astype(F32)
        grad_pre = grad_active * (sigma * (1.0 + pre_act * (1.0 - sigma)))
        grad_low = grad_pre.astype(BF16)
        gsec_ref[...] += dot_nt(grad_low, up)
        acc_down[:, pl.ds(lo, ff_chunk)] += dot_nn(dy_t, active)
        acc_up[:, pl.ds(lo, ff_chunk)] += dot_nn(second_t, grad_low)
        acc_upb[0:1, pl.ds(lo, ff_chunk)] += jnp.sum(grad_low.astype(F32), 0, keepdims=True)
        return carry

    lax.fori_loop(0, ff // ff_chunk, ff_step, 0)
    out_ref[...] = branch_ref[...].astype(BF16)
    gsec = gsec_ref[...]
    acc_vec[0:1] += jnp.sum(gsec * normed, 0, keepdims=True)
    acc_vec[1:2] += jnp.sum(gsec, 0, keepdims=True)
    acc_vec[2:3] += jnp.sum(dy_wide, 0, keepdims=True)
    grad_mid = dy_wide + norm_back(gsec, gain, normed, inv_dev)
    grad_mid_ref[...] = grad_mid
    grad_att = grad_mid.astype(BF16)
    acc_out[...] += dot_nn(routed.T.astype(BF16), grad_att)
    grad_routed = dot_nt(grad_att, weight_ref[:, :width]).astype(BF16)
    zero = jnp.zeros_like(grad_routed)
    picked_one = dot_nn(jnp.where(owner == first, grad_routed, zero), fold)
    picked_two = dot_nn(jnp.where(owner == second, grad_routed, zero), fold)
    grad_mixed_ref[0] = (gate_one * picked_one).astype(BF16)
    grad_mixed_ref[1] = (gate_two * picked_two).astype(BF16)
    grad_one = jnp.sum(picked_one * mixed_one, -1, keepdims=True)
    grad_two = jnp.sum(picked_two * mixed_two, -1, keepdims=True)
    common = gate_one * grad_one + gate_two * grad_two
    lane = lanes_of(rows, LANES)
    grad_logit_ref[...] = jnp.where(
        lane == first,
        gate_one * (grad_one - common),
        jnp.where(lane == second, gate_two * (grad_two - common), 0.0),
    )

    @pl.when(step == last)
    def _():
        d_weight_ref[:, :width] = acc_out[...].astype(BF16)
        d_weight_ref[:, width : width + ff] = acc_up[...].astype(BF16)
        d_weight_ref[:, width + ff :] = acc_vec[...].T.astype(BF16)
        for lo in range(0, ff, 512):
            d_down_ref[lo : lo + 512, :width] = acc_down[:, lo : lo + 512].T.astype(BF16)
            d_down_ref[lo : lo + 512, width:] = acc_upb[:, lo : lo + 512].T.astype(BF16)


def attend_back_kernel(
    reach, chunk, head, low_ref, q_ref, grad_ref, mixed_ref, lse_ref, start_ref, *rest
):
    pieces = rest[:reach]
    grad_q_ref = rest[reach]
    outs = rest[reach + 1 : 2 * reach + 1]
    kv_buf, kt_buf, acc_kv, acc_q = rest[2 * reach + 1 :]
    seq, tile = pl.program_id(0), pl.program_id(1)
    local = pieces[0].shape[1]
    tokens = q_ref.shape[1]
    per_piece = local // chunk

    @pl.when(tile == 0)
    def _():
        acc_kv[...] = jnp.zeros_like(acc_kv)
        for at in range(reach):
            for part in range(per_piece):
                block = pieces[at][0, part * chunk : (part + 1) * chunk, :]
                kv_buf[at * per_piece + part] = block
                kt_buf[at * per_piece + part] = block.astype(F32).T.astype(BF16)

    queries = jnp.concatenate([q_ref[0], q_ref[1]], 0)
    grads = jnp.concatenate([grad_ref[0], grad_ref[1]], 0)
    mixed = jnp.concatenate([mixed_ref[0], mixed_ref[1]], 0)
    inner = jnp.sum((grads.astype(F32) * mixed).T, 0, keepdims=True)
    start = start_ref[0]
    start = jnp.concatenate([start, start], 1)
    lse = lse_ref[0]
    query_at = (reach - 1) * local + tile * tokens
    acc_q[...] = jnp.zeros_like(acc_q)

    def step(at, carry):
        keyval = kv_buf[at]
        scores = masked(dot_nt(keyval, queries), start, at * chunk, query_at)
        probs = jnp.exp(scores - lse)
        grad_probs = dot_nt(keyval, grads)
        grad_scores = (probs * (grad_probs - inner)).astype(BF16)
        acc_kv[at] += dot_nn(grad_scores, queries) + dot_nn(probs.astype(BF16), grads)
        acc_q[...] += dot_nn(kt_buf[at], grad_scores)
        return carry

    low = low_ref[seq * pl.num_programs(1) + tile]
    high = (query_at + tokens - 1) // chunk + 1
    lax.fori_loop(low, high, step, 0)
    row = lax.broadcasted_iota(jnp.int32, acc_q.shape, 0)
    grad_q = (jnp.where(row < head, acc_q[...], 0.0) * (head**-0.5)).T.astype(BF16)
    grad_q_ref[0] = grad_q[:tokens]
    grad_q_ref[1] = grad_q[tokens:]

    @pl.when(tile == pl.num_programs(1) - 1)
    def _():
        for at in range(reach):
            for part in range(per_piece):
                block = acc_kv[at * per_piece + part]
                outs[at][0, part * chunk : (part + 1) * chunk, :] = block.astype(outs[at].dtype)


def last_kernel(
    experts,
    head,
    count,
    x_ref,
    hidden_ref,
    routes_ref,
    grad_q_ref,
    grad_logit_ref,
    grad_mid_ref,
    weight_ref,
    *rest,
):
    pieces = rest[:count]
    grad_in_ref, d_weight_ref, acc_ref, acc_vec = rest[count:]
    step, last = pl.program_id(0), pl.num_programs(0) - 1
    rows, width = x_ref.shape
    inner = experts * head

    @pl.when(step == 0)
    def _():
        acc_ref[...] = jnp.zeros_like(acc_ref)
        acc_vec[...] = jnp.zeros_like(acc_vec)

    gain = rows_of(weight_ref[:, inner + LANES :], (experts,))[0:1]
    normed, inv_dev = normalize(x_ref[...].astype(F32))
    first, second = routes_ref[:, 0:1], routes_ref[:, 1:2]
    owner = lax.div(lanes_of(rows, inner), head)
    unfold = unfold_matrix(inner, head, 0)
    grad_queries = jnp.where(
        owner == first,
        dot_nn(grad_q_ref[0], unfold),
        jnp.where(owner == second, dot_nn(grad_q_ref[1], unfold), 0.0),
    ).astype(BF16)
    summed = pieces[0][...]
    for piece in pieces[1:]:
        summed = summed + piece[...].astype(F32)
    grad_keyvals = summed.astype(BF16)
    grad_logits = grad_logit_ref[...]
    logit_high = grad_logits.astype(BF16)
    logit_low = (grad_logits - logit_high.astype(F32)).astype(BF16)
    router = weight_ref[:, inner + LANES :]
    grad_hidden = (
        dot_nt(grad_queries, weight_ref[:, :inner])
        + dot_nt(grad_keyvals, weight_ref[:, inner : inner + LANES])
        + dot_nt(logit_high, router)
        + dot_nt(logit_low, router)
    )
    grad_in_ref[...] = grad_mid_ref[...] + norm_back(grad_hidden, gain, normed, inv_dev)
    hidden_t = hidden_ref[...].astype(F32).T.astype(BF16)
    acc_ref[:, :inner] += dot_nn(hidden_t, grad_queries)
    acc_ref[:, inner : inner + LANES] += dot_nn(hidden_t, grad_keyvals)
    acc_ref[:, inner + LANES :] += dot_nn(hidden_t, logit_high) + dot_nn(hidden_t, logit_low)
    acc_vec[experts : experts + 1] += jnp.sum(grad_hidden * normed, 0, keepdims=True)
    acc_vec[experts + 1 : experts + 2] += jnp.sum(grad_hidden, 0, keepdims=True)

    @pl.when(step == last)
    def _():
        d_weight_ref[:, : inner + LANES] = acc_ref[:, : inner + LANES].astype(BF16)
        d_weight_ref[:, inner + LANES :] = (acc_ref[:, inner + LANES :] + acc_vec[...].T).astype(
            BF16
        )


def whole_spec(shape):
    zeros = (0,) * len(shape)
    return pl.BlockSpec(shape, lambda *_: zeros, pipeline_mode=pl.Buffered(1))


def row_spec(rows, columns):
    return pl.BlockSpec((rows, columns), lambda i, *_: (i, 0))


def pair_spec(rows):
    return pl.BlockSpec((2, rows, LANES), lambda i, *_: (0, i, 0))


def swapped(value, axis, mask):
    count = lax.axis_size(axis)
    return lax.ppermute(value, axis, [(at, at ^ mask) for at in range(count)])


def passed_along(value, axis, steps):
    count = lax.axis_size(axis)
    leading, last = (max(0, -steps), min(count, count - steps))
    return lax.ppermute(value, axis, [(source, source + steps) for source in range(leading, last)])


def gathered(shard):
    dp, seq = lax.axis_size("dp"), lax.axis_size("seq")
    along = [shard] + [swapped(shard, "dp", 2 * at) for at in range(1, dp // 2)]
    held = jnp.stack(along)
    across = [held] + [swapped(held, "seq", at) for at in range(1, seq)]
    held = jnp.stack(across)
    held = jnp.stack([held, swapped(held, "dp", 1)])
    dp_me, seq_me = lax.axis_index("dp"), lax.axis_index("seq")
    held = jnp.moveaxis(held, 2, 0)
    z_me, core_me = dp_me // 2, dp_me % 2
    for dim, me in ((0, z_me), (1, core_me), (2, seq_me)):
        size = held.shape[dim]
        order = jnp.arange(size, dtype=jnp.int32) ^ me
        held = jnp.take(held, order, axis=dim)
    return held.reshape((dp * seq * shard.shape[0],) + shard.shape[1:])


def halved(value, dim, bit, axis, mask):
    keep = lax.dynamic_index_in_dim(value, bit, dim, keepdims=False)
    send = lax.dynamic_index_in_dim(value, 1 - bit, dim, keepdims=False)
    return keep + swapped(send, axis, mask)


def scattered(value):
    dp, seq = lax.axis_size("dp"), lax.axis_size("seq")
    rows = value.shape[0] // (dp * seq)
    dp_bits, seq_bits = dp.bit_length() - 1, seq.bit_length() - 1
    bits = [("dp", 1 << at) for at in reversed(range(dp_bits))]
    bits += [("seq", 1 << at) for at in reversed(range(seq_bits))]
    held = value.reshape([2] * len(bits) + [rows, value.shape[1]])
    order = [("dp", 1)]
    order += [("seq", 1 << at) for at in range(seq_bits)]
    order += [("dp", 1 << at) for at in range(1, dp_bits)]
    for axis, mask in order:
        dim = bits.index((axis, mask))
        bit = (lax.axis_index(axis) // mask) % 2
        held = halved(held, dim, bit, axis, mask)
        bits.pop(dim)
    return held


def on_device(
    block_in,
    routes,
    segments,
    cotangent,
    ln1_gain,
    ln1_bias,
    query_weight,
    kv_weight,
    router_weight,
    out_weight,
    ln2_gain,
    ln2_bias,
    up_weight,
    up_bias,
    down_weight,
    down_bias,
):
    micro_count, seq_count, local_len, width = block_in.shape
    full_len = segments.shape[2]
    experts = router_weight.shape[1]
    head = kv_weight.shape[1] // 2
    inner = experts * head
    ff = up_weight.shape[1]
    shards = lax.axis_size("seq")
    batch = micro_count * seq_count
    rows_all = batch * local_len
    tile = 512
    longest = full_len * 3 // 4
    reach = min(shards, (longest - 2) // local_len + 2)
    own_shard = lax.axis_index("seq")
    start_pos = own_shard * local_len

    def column(vector):
        return vector[:, None]

    def padded(value, columns):
        return jnp.pad(value, ((0, 0), (0, columns - value.shape[1])))

    group_a = gathered(
        jnp.concatenate(
            [
                query_weight,
                kv_weight,
                padded(
                    jnp.concatenate([router_weight, column(ln1_gain), column(ln1_bias)], 1), LANES
                ),
            ],
            1,
        )
    )
    group_b = gathered(
        jnp.concatenate(
            [
                out_weight,
                up_weight,
                padded(
                    jnp.concatenate([column(ln2_gain), column(ln2_bias), column(down_bias)], 1),
                    LANES,
                ),
            ],
            1,
        )
    )
    group_c = gathered(jnp.concatenate([down_weight, padded(column(up_bias), LANES)], 1))

    tokens = block_in.reshape(rows_all, width)
    grad_out = cotangent.reshape(rows_all, width)
    route_rows = routes.reshape(rows_all, 2)

    seg_rows = segments.reshape(batch, full_len)
    seg_local = lax.dynamic_slice_in_dim(seg_rows, start_pos, local_len, 1)
    doc_start = jnp.sum(
        (seg_rows[:, None, :] < seg_local[:, :, None]).astype(jnp.int32), -1, dtype=jnp.int32
    )
    doc_start = jnp.maximum(doc_start - (own_shard - (reach - 1)) * local_len, 0)
    query_tile = min(local_len, 256)
    chunk = min(local_len, 256)
    tiles = local_len // query_tile
    low_chunks = (doc_start.reshape(batch * tiles, query_tile)[:, 0] // chunk).astype(jnp.int32)
    starts = doc_start.reshape(batch, 1, local_len)

    steps = rows_all // tile
    a_cols, b_cols, c_cols = inner + 2 * LANES, width + ff + LANES, width + LANES
    hidden, keyvals, queries, gates = pl.pallas_call(
        functools.partial(pre_kernel, experts, head),
        grid=(steps,),
        in_specs=[row_spec(tile, width), row_spec(tile, 2), whole_spec((width, a_cols))],
        out_specs=[
            row_spec(tile, width),
            row_spec(tile, LANES),
            pair_spec(tile),
            row_spec(tile, LANES),
        ],
        out_shape=[
            jax.ShapeDtypeStruct((rows_all, width), BF16),
            jax.ShapeDtypeStruct((rows_all, LANES), BF16),
            jax.ShapeDtypeStruct((2, rows_all, LANES), BF16),
            jax.ShapeDtypeStruct((rows_all, LANES), F32),
        ],
        compiler_params=call_params(),
        cost_estimate=cost(2 * rows_all * width * (a_cols + 512), rows_all * width * 8),
        name="pre",
    )(tokens, route_rows, group_a)

    own_pieces = keyvals.reshape(batch, local_len, LANES)
    pieces = [own_pieces] + [passed_along(own_pieces, "seq", back) for back in range(1, reach)]
    pieces = pieces[::-1]

    buffer_chunks = reach * local_len // chunk
    piece_spec = pl.BlockSpec((1, local_len, LANES), lambda b, t, *_: (b, 0, 0))
    q_spec = pl.BlockSpec((2, query_tile, LANES), lambda b, t, *_: (0, b * tiles + t, 0))
    start_spec = pl.BlockSpec((1, 1, query_tile), lambda b, t, *_: (b, 0, t))
    lse_spec = pl.BlockSpec((1, 1, 2 * query_tile), lambda b, t, *_: (b * tiles + t, 0, 0))
    lse_shape = jax.ShapeDtypeStruct((batch * tiles, 1, 2 * query_tile), F32)
    pairs = 2 * rows_all * full_len
    mixed, lse = pl.pallas_call(
        functools.partial(attend_kernel, reach, chunk, head),
        grid_spec=pltpu.PrefetchScalarGridSpec(
            num_scalar_prefetch=1,
            grid=(batch, tiles),
            in_specs=[q_spec, start_spec] + [piece_spec] * reach,
            out_specs=[q_spec, lse_spec],
            scratch_shapes=[
                pltpu.VMEM((buffer_chunks, chunk, LANES), BF16),
                pltpu.VMEM((buffer_chunks, LANES, chunk), BF16),
                pltpu.VMEM((1, 2 * query_tile), F32),
                pltpu.VMEM((1, 2 * query_tile), F32),
                pltpu.VMEM((LANES, 2 * query_tile), F32),
            ],
        ),
        out_shape=[jax.ShapeDtypeStruct((2, rows_all, LANES), F32), lse_shape],
        compiler_params=call_params(),
        cost_estimate=cost(4 * pairs * LANES, rows_all * LANES * 16, pairs),
        name="attend",
    )(low_chunks, queries, starts, *pieces)

    block_out, grad_mid, grad_mixed, grad_logits, d_b, d_c = pl.pallas_call(
        functools.partial(mid_kernel, experts, head, 512),
        grid=(steps,),
        in_specs=[
            row_spec(tile, width),
            row_spec(tile, width),
            row_spec(tile, 2),
            row_spec(tile, LANES),
            pair_spec(tile),
            whole_spec((width, b_cols)),
            whole_spec((ff, c_cols)),
        ],
        out_specs=[
            row_spec(tile, width),
            row_spec(tile, width),
            pair_spec(tile),
            row_spec(tile, LANES),
            whole_spec((width, b_cols)),
            whole_spec((ff, c_cols)),
        ],
        out_shape=[
            jax.ShapeDtypeStruct((rows_all, width), BF16),
            jax.ShapeDtypeStruct((rows_all, width), F32),
            jax.ShapeDtypeStruct((2, rows_all, LANES), BF16),
            jax.ShapeDtypeStruct((rows_all, LANES), F32),
            jax.ShapeDtypeStruct((width, b_cols), BF16),
            jax.ShapeDtypeStruct((ff, c_cols), BF16),
        ],
        scratch_shapes=[
            pltpu.VMEM((inner, width), F32),
            pltpu.VMEM((width, ff), F32),
            pltpu.VMEM((width, ff), F32),
            pltpu.VMEM((LANES, width), F32),
            pltpu.VMEM((LANES, ff), F32),
            pltpu.VMEM((tile, width), F32),
            pltpu.VMEM((tile, width), F32),
        ],
        compiler_params=call_params(),
        cost_estimate=cost(6 * rows_all * width * (2 * ff + width), rows_all * width * 16),
        name="mid",
    )(tokens, grad_out, route_rows, gates, mixed, group_b, group_c)
    own_b = scattered(d_b)
    own_c = scattered(d_c)

    grad_spec = pl.BlockSpec((1, local_len, LANES), lambda b, t, *_: (b, 0, 0))
    back = pl.pallas_call(
        functools.partial(attend_back_kernel, reach, chunk, head),
        grid_spec=pltpu.PrefetchScalarGridSpec(
            num_scalar_prefetch=1,
            grid=(batch, tiles),
            in_specs=[q_spec, q_spec, q_spec, lse_spec, start_spec] + [piece_spec] * reach,
            out_specs=[q_spec] + [grad_spec] * reach,
            scratch_shapes=[
                pltpu.VMEM((buffer_chunks, chunk, LANES), BF16),
                pltpu.VMEM((buffer_chunks, LANES, chunk), BF16),
                pltpu.VMEM((buffer_chunks, chunk, LANES), F32),
                pltpu.VMEM((LANES, 2 * query_tile), F32),
            ],
        ),
        out_shape=[jax.ShapeDtypeStruct((2, rows_all, LANES), BF16)]
        + [
            jax.ShapeDtypeStruct((batch, local_len, LANES), BF16 if at < reach - 1 else F32)
            for at in range(reach)
        ],
        compiler_params=call_params(),
        cost_estimate=cost(10 * pairs * LANES, rows_all * LANES * 32, pairs),
        name="attend_back",
    )(low_chunks, queries, grad_mixed, mixed, lse, starts, *pieces)
    grad_queries, grad_pieces = back[0], back[1:]
    returned = [grad_pieces[reach - 1].reshape(rows_all, LANES)]
    for steps_back in range(1, reach):
        piece = passed_along(grad_pieces[reach - 1 - steps_back], "seq", -steps_back)
        returned.append(piece.reshape(rows_all, LANES))

    grad_in, d_a = pl.pallas_call(
        functools.partial(last_kernel, experts, head, reach),
        grid=(steps,),
        in_specs=[
            row_spec(tile, width),
            row_spec(tile, width),
            row_spec(tile, 2),
            pair_spec(tile),
            row_spec(tile, LANES),
            row_spec(tile, width),
            whole_spec((width, a_cols)),
        ]
        + [row_spec(tile, LANES)] * reach,
        out_specs=[row_spec(tile, width), whole_spec((width, a_cols))],
        out_shape=[
            jax.ShapeDtypeStruct((rows_all, width), F32),
            jax.ShapeDtypeStruct((width, a_cols), BF16),
        ],
        scratch_shapes=[pltpu.VMEM((width, a_cols), F32), pltpu.VMEM((LANES, width), F32)],
        compiler_params=call_params(),
        cost_estimate=cost(4 * rows_all * width * a_cols, rows_all * width * 12),
        name="last",
    )(tokens, hidden, route_rows, grad_queries, grad_logits, grad_mid, group_a, *returned)
    own_a = scattered(d_a)

    own_a, own_b, own_c = (value.astype(F32) for value in (own_a, own_b, own_c))
    extra = own_a[:, inner + LANES :]
    return (
        block_out.reshape(block_in.shape),
        grad_in.reshape(block_in.shape),
        extra[:, experts],
        extra[:, experts + 1],
        own_a[:, :inner],
        own_a[:, inner : inner + 2 * head],
        extra[:, :experts],
        own_b[:, :width],
        own_b[:, width + ff],
        own_b[:, width + ff + 1],
        own_b[:, width : width + ff],
        own_c[:, width],
        own_c[:, :width],
        own_b[:, width + ff + 2],
    )


def solution(mesh):
    rows = P(("dp", "seq"), None)
    vector = P(("dp", "seq"))
    data = P(None, "dp", "seq", None)
    weights = (
        vector,
        vector,
        rows,
        rows,
        rows,
        rows,
        vector,
        vector,
        rows,
        vector,
        rows,
        vector,
    )
    return jax.shard_map(
        on_device,
        mesh=mesh,
        in_specs=(data, data, P(None, "dp", None), data) + weights,
        out_specs=(data, data) + weights,
        check_vma=False,
    )
```

time: 1630 us -> 323 us (0.20)
  waiting for transfers between devices: 583 us -> 110 us
  matrix products: 430 us -> 0 us
  blocking collectives: 378 us -> 0 us
  other arithmetic: 118 us -> 34.7 us
  Pallas kernels: 0 us -> 81.4 us
  starting transfers between devices: 14.1 us -> 54.3 us
  local copies, waits for them, and re-layouts: 76.8 us -> 40.2 us
    reduce_scatter x5 -> x0, waiting for transfers between devices: 575 us -> none  [the longest x1 142 us: on_device(): lax.psum_scatter(totals[10], ('dp', 'seq'), scatter_dimension=0, tiled=True)]
    dot_general x222 -> x0, matrix products: 430 us -> none  [the longest x48 109 us: masked_scores(): jnp.einsum('hqd,kd->hqk', queries, keys, preferred_element_type=jnp.float32)]
    all_gather x7 -> x0, blocking collectives: 297 us -> none  [the longest x1 70.3 us: on_device(): lax.all_gather(query_weight, ('dp', 'seq'), axis=0, tiled=True)]
    pallas_call x0 -> x5, Pallas kernels: none -> 81.4 us  [the longest x1 44.4 us: on_device(): pl.pallas_call(functools.partial(mid_kernel, experts, head, 512), grid=(s...]
    unnamed x2 -> x0, blocking collectives: 80.4 us -> none
    ppermute x0 -> x36, waiting for transfers between devices: none -> 59.8 us  [swapped(): return lax.ppermute(value, axis, [(at, at ^ mask) for at in range(count)])]
    add x58 -> x12, other arithmetic: 62.1 us -> 4.41 us  [halved(): return keep + swapped(send, axis, mask)]
    ppermute x12 -> x6, waiting for transfers between devices: 6.37 us -> 50.7 us  [passed_along(): lax.ppermute(value, axis, [(source, source + steps) for source in range(l...]
  transfers between devices with their start and end apart: 20 -> 42, of which waited for: 9 -> 18; matrix products, arithmetic and copies ran while one was open for 35% -> 15% of each run, Pallas kernels for 0% -> 5%
where the time goes in v1:
time: 323 us; the launch traced here: 322 us
  waiting for transfers between devices  110 us (34%)
  Pallas kernels  81.4 us (25%)
  starting transfers between devices  54.3 us (17%)
  local copies, waits for them, and re-layouts  40.2 us (12%)
  other arithmetic  34.7 us (11%)
    ppermute x36, waiting for transfers between devices, swapped(): return lax.ppermute(value, axis, [(at, at ^ mask) for at in range(count)])  59.8 us
    ppermute x6, waiting for transfers between devices, passed_along(): lax.ppermute(value, axis, [(source, source + steps) for source in range(l...  50.7 us
    pallas_call x1, Pallas kernels, on_device(): pl.pallas_call(functools.partial(mid_kernel, experts, head, 512), grid=(s...  44.4 us
    ppermute x36, starting transfers between devices, swapped(): return lax.ppermute(value, axis, [(at, at ^ mask) for at in range(count)])  43.1 us
    gather x12, local copies, waits for them, and re-layouts, gathered(): held = jnp.take(held, order, axis=dim)  18.7 us
    select_n x12, other arithmetic, gathered(): held = jnp.take(held, order, axis=dim)  15.4 us
    ppermute x6, starting transfers between devices, passed_along(): lax.ppermute(value, axis, [(source, source + steps) for source in range(l...  11.2 us
    pallas_call x1, Pallas kernels, on_device(): pl.pallas_call(functools.partial(attend_back_kernel, reach, chunk, head),...  10.9 us
  transfers between devices with their start and end apart: 42, of which 18 were waited for; matrix products, arithmetic and copies ran while one was open for 15% of the time, Pallas kernels for 5%

profile of v1, /device:TPU:0, one launch (start us, length us, event | category | flops | bytes accessed | tf_op | source)
XLA Modules:
  0.0 322.3 jit_solution(11112252755234075263)
XLA Ops:
  2.3 3.1 collective-permute-start.10
  5.4 2.6 collective-permute-start.11
  10.0 3.9 %collective-permute-start.2 = (bf16[16,768]{1,0:T(8,128)(2,1)S(1)}, bf16[16,768]{1,0:T(8,128)(2,1)S(1)}, u32[]{:S(2)}, u32[]{:S(2)}) collective-permute-start(bf16[16,768]{1,0:T(8,128)(2,1)S(1)} %get-tuple-element.164), channel_id=1, source_target_pairs={{0,24},{4,28},{8,16},{12,20},{16,8},{20,12},{24,0},{28,4},{1,25},{... | collective-permute-start | bytes 73736 | tf_op jit(solution)/shard_map/ppermute | solution.py:411
  18.8 1.9 copy.112
  21.4 3.8 %collective-permute-start.19 = (bf16[64,640]{1,0:T(8,128)(2,1)S(1)}, bf16[64,640]{1,0:T(8,128)(2,1)S(1)}, u32[]{:S(2)}, u32[]{:S(2)}) collective-permute-start(bf16[64,640]{1,0:T(8,128)(2,1)S(1)} %get-tuple-element.162), channel_id=1, source_target_pairs={{0,24},{4,28},{8,16},{12,20},{16,8},{20,12},{24,0},{28,4},{1,25},{... | collective-permute-start | bytes 245768 | tf_op jit(solution)/shard_map/ppermute | solution.py:411
  32.0 2.1 collective-permute-start.12
  35.1 2.0 collective-permute-done.5
  37.6 2.7 collective-permute-start.22
  41.6 3.2 %collective-permute-done.20 = bf16[4,64,640]{2,1,0:T(8,128)(2,1)S(1)} collective-permute-done((bf16[4,64,640]{2,1,0:T(8,128)(2,1)S(1)}, bf16[4,64,640]{2,1,0:T(8,128)(2,1)S(1)}, u32[]{:S(2)}, u32[]{:S(2)}) %collective-permute-start.20) | collective-permute-done | bytes 327712 | tf_op jit(solution)/shard_map/ppermute | solution.py:411
  45.8 4.3 %collective-permute-done.21 = bf16[4,64,640]{2,1,0:T(8,128)(2,1)S(1)} collective-permute-done((bf16[4,64,640]{2,1,0:T(8,128)(2,1)S(1)}, bf16[4,64,640]{2,1,0:T(8,128)(2,1)S(1)}, u32[]{:S(2)}, u32[]{:S(2)}) %collective-permute-start.21) | collective-permute-done | bytes 327712 | tf_op jit(solution)/shard_map/ppermute | solution.py:411
  57.4 6.0 %pre.1 = (bf16[1536,512]{1,0:T(8,128)(2,1)}, bf16[1536,128]{1,0:T(8,128)(2,1)}, bf16[2,1536,128]{2,1,0:T(8,128)(2,1)}, f32[1536,128]{1,0:T(8,128)}) custom-call(bf16[1536,512]{1,0:T(8,128)(2,1)} %bitcast.180, s32[1536,2]{1,0:T(8,128)} %bitcast.174, bf16[512,768]{1,0:T(8,128)(2,1)} %bitcast_select_fusion.2.weight_ref), custom_call_target="tpu_custom_call" | custom-call | flops 2013265920 | bytes 6291456 | tf_op jit(solution)/shard_map/pre/pallas_call | solution.py:545
  63.5 3.3 %collective-permute-start.7 = (bf16[3,512,128]{2,1,0:T(8,128)(2,1)}, bf16[3,512,128]{2,1,0:T(8,128)(2,1)S(1)}, u32[]{:S(2)}, u32[]{:S(2)}) collective-permute-start(bf16[3,512,128]{2,1,0:T(8,128)(2,1)} %bitcast.216), channel_id=1, source_target_pairs={{0,3},{4,7},{8,11},{12,15},{16,19},{20,23},{24,27},{28,31}} | collective-permute-start | bytes 1179656 | tf_op jit(solution)/shard_map/ppermute | solution.py:417
  68.1 2.7 collective-permute-start.9
  72.1 3.0 fusion.20
  76.5 9.3 %collective-permute-done.8.rest_1_ = bf16[3,512,128]{2,1,0:T(8,128)(2,1)S(1)} collective-permute-done((bf16[3,512,128]{2,1,0:T(8,128)(2,1)}, bf16[3,512,128]{2,1,0:T(8,128)(2,1)S(1)}, u32[]{:S(2)}, u32[]{:S(2)}) %collective-permute-start.8) | collective-permute-done | bytes 393248 | tf_op jit(solution)/shard_map/ppermute | solution.py:417
  86.7 9.3 %attend.1 = (f32[2,1536,128]{2,1,0:T(8,128)}, f32[6,1,512]{2,1,0:T(1,128)}) custom-call(s32[6]{0:T(128)} %and_select_fusion.low_ref, bf16[2,1536,128]{2,1,0:T(8,128)(2,1)} %get-tuple-element.34.q_ref, s32[3,1,512]{2,1,0:T(1,128)} %max.23.start_ref, bf16[3,512,128]{2,1,0:T(8,128)(2,1)} %copy-done.8, bf16[3,512,128]{2,1,0:T(8,128)(2,1)} %copy-done.9, ...), custom_call_target="tpu_custom_call" | custom-call | flops 3221225472 | bytes 3145728 | tf_op jit(solution)/shard_map/attend/pallas_call | solution.py:577
  98.8 2.4 gather_fusion.6
  101.1 2.1 broadcast_select_fusion.1
  103.2 2.4 gather_fusion.7
  105.6 3.6 %select_bitcast_fusion.1 = bf16[4,2,4,64,640]{4,3,2,0,1:T(8,128)(2,1)} fusion(bf16[2,4,4,64,640]{4,3,2,1,0:T(8,128)(2,1)} %gather_fusion.7, pred[2]{0:T(512)(128)(4,1)S(1)} %compare_and_fusion.1), kind=kLoop, calls=%fused_computation.16 | loop fusion | flops 1310720 | bytes 5242882 | tf_op jit(solution)/shard_map/jit(_take)/select_n | solution.py:433
  109.1 2.8 gather_fusion.8
  112.2 2.0 bitcast_select_fusion.1.down_ref
  115.8 2.4 gather_fusion.3
  118.2 2.1 broadcast_select_fusion
  120.3 2.4 gather_fusion.4
  122.6 2.1 select_bitcast_fusion
  124.8 2.4 gather_fusion.5
  127.1 2.0 copy.117
  129.2 2.1 bitcast_select_fusion.weight_ref
  131.3 44.4 %mid.1 = (bf16[1536,512]{1,0:T(8,128)(2,1)}, f32[1536,512]{1,0:T(8,128)}, bf16[2,1536,128]{2,1,0:T(8,128)(2,1)}, f32[1536,128]{1,0:T(8,128)}, bf16[512,2688]{1,0:T(8,128)(2,1)}, /*index=5*/bf16[2048,640]{1,0:T(8,128)(2,1)}) custom-call(bf16[1536,512]{1,0:T(8,128)(2,1)} %bitcast.181, bf16[1536,512]{1,0:T(8,128)(2,1)} %bitcast.215, s32[1536,2]{1,0:T(8,128)} %bitcast.175, ...), custom_call_target="tpu_custom_call" | custom-call | flops 21743271936 | bytes 12582912 | tf_op jit(solution)/shard_map/mid/pallas_call | solution.py:598
  175.7 10.9 %attend_back.1 = (bf16[2,1536,128]{2,1,0:T(8,128)(2,1)}, bf16[3,512,128]{2,1,0:T(8,128)(2,1)}, bf16[3,512,128]{2,1,0:T(8,128)(2,1)}, bf16[3,512,128]{2,1,0:T(8,128)(2,1)}, f32[3,512,128]{2,1,0:T(8,128)}) custom-call(s32[6]{0:T(128)} %and_select_fusion.low_ref, bf16[2,1536,128]{2,1,0:T(8,128)(2,1)} %get-tuple-element.34.q_ref, ...), custom_call_target="tpu_custom_call" | custom-call | flops 8053063680 | bytes 6291456 | tf_op jit(solution)/shard_map/attend_back/pallas_call | solution.py:643
  190.5 16.3 %collective-permute-done.24 = bf16[3,512,128]{2,1,0:T(8,128)(2,1)S(1)} collective-permute-done((bf16[3,512,128]{2,1,0:T(8,128)(2,1)}, bf16[3,512,128]{2,1,0:T(8,128)(2,1)S(1)}, u32[]{:S(2)}, u32[]{:S(2)}) %collective-permute-start.24) | collective-permute-done | bytes 393248 | tf_op jit(solution)/shard_map/ppermute | solution.py:417
  206.8 23.6 %collective-permute-done.25 = bf16[3,512,128]{2,1,0:T(8,128)(2,1)S(1)} collective-permute-done((bf16[3,512,128]{2,1,0:T(8,128)(2,1)}, bf16[3,512,128]{2,1,0:T(8,128)(2,1)S(1)}, u32[]{:S(2)}, u32[]{:S(2)}) %collective-permute-start.25) | collective-permute-done | bytes 393248 | tf_op jit(solution)/shard_map/ppermute | solution.py:417
  231.3 10.7 %last.1 = (f32[1536,512]{1,0:T(8,128)}, bf16[512,768]{1,0:T(8,128)(2,1)}) custom-call(bf16[1536,512]{1,0:T(8,128)(2,1)} %bitcast.182, bf16[1536,512]{1,0:T(8,128)(2,1)} %get-tuple-element.38.hidden_ref, s32[1536,2]{1,0:T(8,128)} %bitcast.176, bf16[2,1536,128]{2,1,0:T(8,128)(2,1)} %get-tuple-element.41.grad_q_ref, ...), custom_call_target="tpu_custom_call" | custom-call | flops 2415919104 | bytes 9437184 | tf_op jit(solution)/shard_map/last/pallas_call | solution.py:672
  243.3 2.0 constant_dynamic-slice_fusion.1
  249.4 4.6 %collective-permute-done.28 = bf16[2,2,2,16,768]{4,3,2,1,0:T(8,128)(2,1)S(1)} collective-permute-done((bf16[2,2,2,16,768]{4,3,2,1,0:T(8,128)(2,1)S(1)}, bf16[2,2,2,16,768]{4,3,2,1,0:T(8,128)(2,1)S(1)}, u32[]{:S(2)}, u32[]{:S(2)}) %collective-permute-start.28) | collective-permute-done | bytes 196640 | tf_op jit(solution)/shard_map/ppermute | solution.py:411
  254.1 4.6 %collective-permute-done.29 = bf16[2,2,16,768]{3,2,1,0:T(8,128)(2,1)S(1)} collective-permute-done((bf16[2,2,16,768]{3,2,1,0:T(8,128)(2,1)S(1)}, bf16[2,2,16,768]{3,2,1,0:T(8,128)(2,1)S(1)}, u32[]{:S(2)}, u32[]{:S(2)}) %collective-permute-start.29) | collective-permute-done | bytes 98336 | tf_op jit(solution)/shard_map/ppermute | solution.py:411
  258.8 2.0 collective-permute-start.30
  260.8 2.2 collective-permute-done.30
  262.9 4.4 %collective-permute-start.31 = (bf16[16,768]{1,0:T(8,128)(2,1)S(1)}, bf16[16,768]{1,0:T(8,128)(2,1)S(1)}, u32[]{:S(2)}, u32[]{:S(2)}) collective-permute-start(bf16[16,768]{1,0:T(8,128)(2,1)S(1)} %dynamic-slice_bitcast_fusion.11), channel_id=1, source_target_pairs={{0,16},{4,20},{8,24},{12,28},{16,0},{20,4},{24,8},{28,12},{1,17},{... | collective-permute-start | bytes 73736 | tf_op jit(solution)/shard_map/ppermute | solution.py:411
  271.6 2.0 collective-permute-start.33
  276.1 11.6 %collective-permute-done.38 = bf16[2,2,2,64,640]{4,3,2,1,0:T(8,128)(2,1)S(1)} collective-permute-done((bf16[2,2,2,64,640]{4,3,2,1,0:T(8,128)(2,1)}, bf16[2,2,2,64,640]{4,3,2,1,0:T(8,128)(2,1)S(1)}, u32[]{:S(2)}, u32[]{:S(2)}) %collective-permute-start.38) | collective-permute-done | bytes 655392 | tf_op jit(solution)/shard_map/ppermute | solution.py:411
  289.0 9.2 %collective-permute-done.33 = bf16[2,2,2,16,2688]{4,3,2,1,0:T(8,128)(2,1)S(1)} collective-permute-done((bf16[2,2,2,16,2688]{4,3,2,1,0:T(8,128)(2,1)S(1)}, bf16[2,2,2,16,2688]{4,3,2,1,0:T(8,128)(2,1)S(1)}, u32[]{:S(2)}, u32[]{:S(2)}) %collective-permute-start.33) | collective-permute-done | bytes 688160 | tf_op jit(solution)/shard_map/ppermute | solution.py:411
  298.8 1.8 collective-permute-start.40
  300.6 5.1 %collective-permute-done.34 = bf16[2,2,16,2688]{3,2,1,0:T(8,128)(2,1)S(1)} collective-permute-done((bf16[2,2,16,2688]{3,2,1,0:T(8,128)(2,1)S(1)}, bf16[2,2,16,2688]{3,2,1,0:T(8,128)(2,1)S(1)}, u32[]{:S(2)}, u32[]{:S(2)}) %collective-permute-start.34) | collective-permute-done | bytes 344096 | tf_op jit(solution)/shard_map/ppermute | solution.py:411
  306.2 1.8 collective-permute-start.35
  308.0 5.9 %collective-permute-done.41 = bf16[64,640]{1,0:T(8,128)(2,1)S(1)} collective-permute-done((bf16[64,640]{1,0:T(8,128)(2,1)S(1)}, bf16[64,640]{1,0:T(8,128)(2,1)S(1)}, u32[]{:S(2)}, u32[]{:S(2)}) %collective-permute-start.41) | collective-permute-done | bytes 81952 | tf_op jit(solution)/shard_map/ppermute | solution.py:411
  316.1 4.2 %collective-permute-done.36 = bf16[16,2688]{1,0:T(8,128)(2,1)S(1)} collective-permute-done((bf16[16,2688]{1,0:T(8,128)(2,1)S(1)}, bf16[16,2688]{1,0:T(8,128)(2,1)S(1)}, u32[]{:S(2)}, u32[]{:S(2)}) %collective-permute-start.36) | collective-permute-done | bytes 86048 | tf_op jit(solution)/shard_map/ppermute | solution.py:411
  (167 shorter events, 59.9 us)
Async XLA Ops:
  2.3 35.3 %collective-permute-start.10 = (bf16[16,2688]{1,0:T(8,128)(2,1)S(1)}, bf16[16,2688]{1,0:T(8,128)(2,1)S(1)}, u32[]{:S(2)}, u32[]{:S(2)}) collective-permute-start(bf16[16,2688]{1,0:T(8,128)(2,1)S(1)} %get-tuple-element.160), channel_id=1, source_target_pairs={{0,8},{4,12},{8,0},{12,4},{16,24},{20,28},{24,16},{28,20},{1,9},{5... | collective-permute-start | bytes 258056 | tf_op jit(solution)/shard_map/ppermute | solution.py:411
  5.4 35.0 %collective-permute-start.11 = (bf16[16,2688]{1,0:T(8,128)(2,1)S(1)}, bf16[16,2688]{1,0:T(8,128)(2,1)S(1)}, u32[]{:S(2)}, u32[]{:S(2)}) collective-permute-start(bf16[16,2688]{1,0:T(8,128)(2,1)S(1)} %get-tuple-element.160), channel_id=1, source_target_pairs={{0,16},{4,20},{8,24},{12,28},{16,0},{20,4},{24,8},{28,12},{1,17},{... | collective-permute-start | bytes 258056 | tf_op jit(solution)/shard_map/ppermute | solution.py:411
  9.5 11.3 %collective-permute-start = (bf16[16,768]{1,0:T(8,128)(2,1)S(1)}, bf16[16,768]{1,0:T(8,128)(2,1)S(1)}, u32[]{:S(2)}, u32[]{:S(2)}) collective-permute-start(bf16[16,768]{1,0:T(8,128)(2,1)S(1)} %get-tuple-element.164), channel_id=1, source_target_pairs={{0,8},{4,12},{8,0},{12,4},{16,24},{20,28},{24,16},{28,20},{1,9},{5... | collective-permute-start | bytes 73736 | tf_op jit(solution)/shard_map/ppermute | solution.py:411
  10.0 10.9 %collective-permute-start.1 = (bf16[16,768]{1,0:T(8,128)(2,1)S(1)}, bf16[16,768]{1,0:T(8,128)(2,1)S(1)}, u32[]{:S(2)}, u32[]{:S(2)}) collective-permute-start(bf16[16,768]{1,0:T(8,128)(2,1)S(1)} %get-tuple-element.164), channel_id=1, source_target_pairs={{0,16},{4,20},{8,24},{12,28},{16,0},{20,4},{24,8},{28,12},{1,17},{... | collective-permute-start | bytes 73736 | tf_op jit(solution)/shard_map/ppermute | solution.py:411
  10.0 11.4 %collective-permute-start.2 = (bf16[16,768]{1,0:T(8,128)(2,1)S(1)}, bf16[16,768]{1,0:T(8,128)(2,1)S(1)}, u32[]{:S(2)}, u32[]{:S(2)}) collective-permute-start(bf16[16,768]{1,0:T(8,128)(2,1)S(1)} %get-tuple-element.164), channel_id=1, source_target_pairs={{0,24},{4,28},{8,16},{12,20},{16,8},{20,12},{24,0},{28,4},{1,25},{... | collective-permute-start | bytes 73736 | tf_op jit(solution)/shard_map/ppermute | solution.py:411
  20.8 5.4 %collective-permute-start.17 = (bf16[64,640]{1,0:T(8,128)(2,1)S(1)}, bf16[64,640]{1,0:T(8,128)(2,1)S(1)}, u32[]{:S(2)}, u32[]{:S(2)}) collective-permute-start(bf16[64,640]{1,0:T(8,128)(2,1)S(1)} %get-tuple-element.162), channel_id=1, source_target_pairs={{0,8},{4,12},{8,0},{12,4},{16,24},{20,28},{24,16},{28,20},{1,9},{5... | collective-permute-start | bytes 245768 | tf_op jit(solution)/shard_map/ppermute | solution.py:411
  20.8 8.1 %collective-permute-start.18 = (bf16[64,640]{1,0:T(8,128)(2,1)S(1)}, bf16[64,640]{1,0:T(8,128)(2,1)S(1)}, u32[]{:S(2)}, u32[]{:S(2)}) collective-permute-start(bf16[64,640]{1,0:T(8,128)(2,1)S(1)} %get-tuple-element.162), channel_id=1, source_target_pairs={{0,16},{4,20},{8,24},{12,28},{16,0},{20,4},{24,8},{28,12},{1,17},{... | collective-permute-start | bytes 245768 | tf_op jit(solution)/shard_map/ppermute | solution.py:411
  21.4 9.1 %collective-permute-start.19 = (bf16[64,640]{1,0:T(8,128)(2,1)S(1)}, bf16[64,640]{1,0:T(8,128)(2,1)S(1)}, u32[]{:S(2)}, u32[]{:S(2)}) collective-permute-start(bf16[64,640]{1,0:T(8,128)(2,1)S(1)} %get-tuple-element.162), channel_id=1, source_target_pairs={{0,24},{4,28},{8,16},{12,20},{16,8},{20,12},{24,0},{28,4},{1,25},{... | collective-permute-start | bytes 245768 | tf_op jit(solution)/shard_map/ppermute | solution.py:411
  26.3 5.7 %collective-permute-start.3 = (bf16[4,16,768]{2,1,0:T(8,128)(2,1)S(1)}, bf16[4,16,768]{2,1,0:T(8,128)(2,1)S(1)}, u32[]{:S(2)}, u32[]{:S(2)}) collective-permute-start(bf16[4,16,768]{2,1,0:T(8,128)(2,1)S(1)} %get-tuple-element.158), channel_id=1, source_target_pairs={{0,1},{1,0},{2,3},{3,2},{4,5},{5,4},{6,7},{7,6},{8,9},{9,8},{10,11... | collective-permute-start | bytes 294920 | tf_op jit(solution)/shard_map/ppermute | solution.py:411
  29.0 5.2 %collective-permute-start.4 = (bf16[4,16,768]{2,1,0:T(8,128)(2,1)S(1)}, bf16[4,16,768]{2,1,0:T(8,128)(2,1)S(1)}, u32[]{:S(2)}, u32[]{:S(2)}) collective-permute-start(bf16[4,16,768]{2,1,0:T(8,128)(2,1)S(1)} %get-tuple-element.158), channel_id=1, source_target_pairs={{0,2},{1,3},{2,0},{3,1},{4,6},{5,7},{6,4},{7,5},{8,10},{9,11},{10,... | collective-permute-start | bytes 294920 | tf_op jit(solution)/shard_map/ppermute | solution.py:411
  30.5 6.6 %collective-permute-start.5 = (bf16[4,16,768]{2,1,0:T(8,128)(2,1)S(1)}, bf16[4,16,768]{2,1,0:T(8,128)(2,1)S(1)}, u32[]{:S(2)}, u32[]{:S(2)}) collective-permute-start(bf16[4,16,768]{2,1,0:T(8,128)(2,1)S(1)} %get-tuple-element.158), channel_id=1, source_target_pairs={{0,3},{1,2},{2,1},{3,0},{4,7},{5,6},{6,5},{7,4},{8,11},{9,10},{10,... | collective-permute-start | bytes 294920 | tf_op jit(solution)/shard_map/ppermute | solution.py:411
  32.0 8.3 %collective-permute-start.12 = (bf16[16,2688]{1,0:T(8,128)(2,1)S(1)}, bf16[16,2688]{1,0:T(8,128)(2,1)S(1)}, u32[]{:S(2)}, u32[]{:S(2)}) collective-permute-start(bf16[16,2688]{1,0:T(8,128)(2,1)S(1)} %get-tuple-element.160), channel_id=1, source_target_pairs={{0,24},{4,28},{8,16},{12,20},{16,8},{20,12},{24,0},{28,4},{1,25},{... | collective-permute-start | bytes 258056 | tf_op jit(solution)/shard_map/ppermute | solution.py:411
  34.2 10.6 %collective-permute-start.20 = (bf16[4,64,640]{2,1,0:T(8,128)(2,1)S(1)}, bf16[4,64,640]{2,1,0:T(8,128)(2,1)S(1)}, u32[]{:S(2)}, u32[]{:S(2)}) collective-permute-start(bf16[4,64,640]{2,1,0:T(8,128)(2,1)S(1)} %get-tuple-element.156), channel_id=1, source_target_pairs={{0,1},{1,0},{2,3},{3,2},{4,5},{5,4},{6,7},{7,6},{8,9},{9,8},{10,11... | collective-permute-start | bytes 983048 | tf_op jit(solution)/shard_map/ppermute | solution.py:411
  37.1 12.9 %collective-permute-start.21 = (bf16[4,64,640]{2,1,0:T(8,128)(2,1)S(1)}, bf16[4,64,640]{2,1,0:T(8,128)(2,1)S(1)}, u32[]{:S(2)}, u32[]{:S(2)}) collective-permute-start(bf16[4,64,640]{2,1,0:T(8,128)(2,1)S(1)} %get-tuple-element.156), channel_id=1, source_target_pairs={{0,2},{1,3},{2,0},{3,1},{4,6},{5,7},{6,4},{7,5},{8,10},{9,11},{10,... | collective-permute-start | bytes 983048 | tf_op jit(solution)/shard_map/ppermute | solution.py:411
  37.6 14.7 %collective-permute-start.22 = (bf16[4,64,640]{2,1,0:T(8,128)(2,1)S(1)}, bf16[4,64,640]{2,1,0:T(8,128)(2,1)S(1)}, u32[]{:S(2)}, u32[]{:S(2)}) collective-permute-start(bf16[4,64,640]{2,1,0:T(8,128)(2,1)S(1)} %get-tuple-element.156), channel_id=1, source_target_pairs={{0,3},{1,2},{2,1},{3,0},{4,7},{5,6},{6,5},{7,4},{8,11},{9,10},{10,... | collective-permute-start | bytes 983048 | tf_op jit(solution)/shard_map/ppermute | solution.py:411
  40.3 13.7 %collective-permute-start.6 = (bf16[4,4,16,768]{3,2,1,0:T(8,128)(2,1)S(1)}, bf16[4,4,16,768]{3,2,1,0:T(8,128)(2,1)S(1)}, u32[]{:S(2)}, u32[]{:S(2)}) collective-permute-start(bf16[4,4,16,768]{3,2,1,0:T(8,128)(2,1)S(1)} %get-tuple-element.152), channel_id=1, source_target_pairs={{0,4},{4,0},{8,12},{12,8},{16,20},{20,16},{24,28},{28,24},{1,5},{5... | collective-permute-start | bytes 1179656 | tf_op jit(solution)/shard_map/ppermute | solution.py:411
  41.2 25.6 %collective-permute-start.13 = (bf16[4,16,2688]{2,1,0:T(8,128)(2,1)}, bf16[4,16,2688]{2,1,0:T(8,128)(2,1)}, u32[]{:S(2)}, u32[]{:S(2)}) collective-permute-start(bf16[4,16,2688]{2,1,0:T(8,128)(2,1)} %get-tuple-element.154), channel_id=1, source_target_pairs={{0,1},{1,0},{2,3},{3,2},{4,5},{5,4},{6,7},{7,6},{8,9},{9,8},{10,11... | collective-permute-start | bytes 1032200 | tf_op jit(solution)/shard_map/ppermute | solution.py:411
  44.8 23.3 %collective-permute-start.14 = (bf16[4,16,2688]{2,1,0:T(8,128)(2,1)}, bf16[4,16,2688]{2,1,0:T(8,128)(2,1)}, u32[]{:S(2)}, u32[]{:S(2)}) collective-permute-start(bf16[4,16,2688]{2,1,0:T(8,128)(2,1)} %get-tuple-element.154), channel_id=1, source_target_pairs={{0,2},{1,3},{2,0},{3,1},{4,6},{5,7},{6,4},{7,5},{8,10},{9,11},{10,... | collective-permute-start | bytes 1032200 | tf_op jit(solution)/shard_map/ppermute | solution.py:411
  50.1 22.0 %collective-permute-start.15 = (bf16[4,16,2688]{2,1,0:T(8,128)(2,1)}, bf16[4,16,2688]{2,1,0:T(8,128)(2,1)}, u32[]{:S(2)}, u32[]{:S(2)}) collective-permute-start(bf16[4,16,2688]{2,1,0:T(8,128)(2,1)} %get-tuple-element.154), channel_id=1, source_target_pairs={{0,3},{1,2},{2,1},{3,0},{4,7},{5,6},{6,5},{7,4},{8,11},{9,10},{10,... | collective-permute-start | bytes 1032200 | tf_op jit(solution)/shard_map/ppermute | solution.py:411
  54.1 42.0 %collective-permute-start.23 = (bf16[4,4,64,640]{3,2,1,0:T(8,128)(2,1)}, bf16[4,4,64,640]{3,2,1,0:T(8,128)(2,1)S(1)}, u32[]{:S(2)}, u32[]{:S(2)}) collective-permute-start(bf16[4,4,64,640]{3,2,1,0:T(8,128)(2,1)} %get-tuple-element.148), channel_id=1, source_target_pairs={{0,4},{4,0},{8,12},{12,8},{16,20},{20,16},{24,28},{28,24},{1,5},{5... | collective-permute-start | bytes 3932168 | tf_op jit(solution)/shard_map/ppermute | solution.py:411
  63.5 13.1 %collective-permute-start.7 = (bf16[3,512,128]{2,1,0:T(8,128)(2,1)}, bf16[3,512,128]{2,1,0:T(8,128)(2,1)S(1)}, u32[]{:S(2)}, u32[]{:S(2)}) collective-permute-start(bf16[3,512,128]{2,1,0:T(8,128)(2,1)} %bitcast.216), channel_id=1, source_target_pairs={{0,3},{4,7},{8,11},{12,15},{16,19},{20,23},{24,27},{28,31}} | collective-permute-start | bytes 1179656 | tf_op jit(solution)/shard_map/ppermute | solution.py:417
  66.8 19.1 %collective-permute-start.8 = (bf16[3,512,128]{2,1,0:T(8,128)(2,1)}, bf16[3,512,128]{2,1,0:T(8,128)(2,1)S(1)}, u32[]{:S(2)}, u32[]{:S(2)}) collective-permute-start(bf16[3,512,128]{2,1,0:T(8,128)(2,1)} %bitcast.217), channel_id=1, source_target_pairs={{0,2},{1,3},{4,6},{5,7},{8,10},{9,11},{12,14},{13,15},{16,18},{17,... | collective-permute-start | bytes 1179656 | tf_op jit(solution)/shard_map/ppermute | solution.py:417
  68.1 17.7 %collective-permute-start.9 = (bf16[3,512,128]{2,1,0:T(8,128)(2,1)}, bf16[3,512,128]{2,1,0:T(8,128)(2,1)S(1)}, u32[]{:S(2)}, u32[]{:S(2)}) collective-permute-start(bf16[3,512,128]{2,1,0:T(8,128)(2,1)} %bitcast.218), channel_id=1, source_target_pairs={{0,1},{1,2},{2,3},{4,5},{5,6},{6,7},{8,9},{9,10},{10,11},{12,13},{... | collective-permute-start | bytes 1179656 | tf_op jit(solution)/shard_map/ppermute | solution.py:417
  75.0 39.1 %collective-permute-start.16 = (bf16[4,4,16,2688]{3,2,1,0:T(8,128)(2,1)}, bf16[4,4,16,2688]{3,2,1,0:T(8,128)(2,1)}, u32[]{:S(2)}, u32[]{:S(2)}) collective-permute-start(bf16[4,4,16,2688]{3,2,1,0:T(8,128)(2,1)} %get-tuple-element.146), channel_id=1, source_target_pairs={{0,4},{4,0},{8,12},{12,8},{16,20},{20,16},{24,28},{28,24},{1,5},{5... | collective-permute-start | bytes 4128776 | tf_op jit(solution)/shard_map/ppermute | solution.py:411
  76.5 9.3 %copy-start.8 = (bf16[3,512,128]{2,1,0:T(8,128)(2,1)}, bf16[3,512,128]{2,1,0:T(8,128)(2,1)S(1)}, u32[]{:S(2)}) copy-start(bf16[3,512,128]{2,1,0:T(8,128)(2,1)S(1)} %collective-permute-done.7.rest_0_) | copy-start | bytes 1179652
  86.7 10.4 %copy-start.1 = (bf16[1,4,4,64,640]{4,3,2,1,0:T(8,128)(2,1)S(1)}, bf16[1,4,4,64,640]{4,3,2,1,0:T(8,128)(2,1)}, u32[]{:S(2)}) copy-start(bf16[1,4,4,64,640]{4,3,2,1,0:T(8,128)(2,1)} %get-tuple-element.147) | copy-start | bytes 3932164
  112.2 2.0 copy-start
  186.6 20.2 %collective-permute-start.24 = (bf16[3,512,128]{2,1,0:T(8,128)(2,1)}, bf16[3,512,128]{2,1,0:T(8,128)(2,1)S(1)}, u32[]{:S(2)}, u32[]{:S(2)}) collective-permute-start(bf16[3,512,128]{2,1,0:T(8,128)(2,1)} %get-tuple-element.45), channel_id=1, source_target_pairs={{1,0},{2,1},{3,2},{5,4},{6,5},{7,6},{9,8},{10,9},{11,10},{13,12},{... | collective-permute-start | bytes 1179656 | tf_op jit(solution)/shard_map/ppermute | solution.py:417
  187.9 42.5 %collective-permute-start.25 = (bf16[3,512,128]{2,1,0:T(8,128)(2,1)}, bf16[3,512,128]{2,1,0:T(8,128)(2,1)S(1)}, u32[]{:S(2)}, u32[]{:S(2)}) collective-permute-start(bf16[3,512,128]{2,1,0:T(8,128)(2,1)} %get-tuple-element.46), channel_id=1, source_target_pairs={{2,0},{3,1},{6,4},{7,5},{10,8},{11,9},{14,12},{15,13},{18,16},{19,... | collective-permute-start | bytes 1179656 | tf_op jit(solution)/shard_map/ppermute | solution.py:417
  189.2 41.2 %collective-permute-start.26 = (bf16[3,512,128]{2,1,0:T(8,128)(2,1)}, bf16[3,512,128]{2,1,0:T(8,128)(2,1)S(1)}, u32[]{:S(2)}, u32[]{:S(2)}) collective-permute-start(bf16[3,512,128]{2,1,0:T(8,128)(2,1)} %get-tuple-element.47), channel_id=1, source_target_pairs={{3,0},{7,4},{11,8},{15,12},{19,16},{23,20},{27,24},{31,28}} | collective-permute-start | bytes 1179656 | tf_op jit(solution)/shard_map/ppermute | solution.py:417
  206.8 23.6 %copy-start.5 = (bf16[3,512,128]{2,1,0:T(8,128)(2,1)}, bf16[3,512,128]{2,1,0:T(8,128)(2,1)S(1)}, u32[]{:S(2)}) copy-start(bf16[3,512,128]{2,1,0:T(8,128)(2,1)S(1)} %collective-permute-done.24) | copy-start | bytes 1179652
  243.2 3.8 %collective-permute-start.27 = (bf16[2,2,2,2,16,768]{5,4,2,1,0,3:T(8,128)(2,1)S(1)}, bf16[2,2,2,2,16,768]{5,4,2,1,0,3:T(8,128)(2,1)S(1)}, u32[]{:S(2)}, u32[]{:S(2)}) collective-permute-start(bf16[2,2,2,2,16,768]{5,4,2,1,0,3:T(8,128)(2,1)S(1)} %bitcast.189), channel_id=1, source_target_pairs={{0,4},{4,0},{8,12},{12,8},{16,20},{20,16},{24,28},{28,24},{1,5},{5... | collective-permute-start | bytes 1179656 | tf_op jit(solution)/shard_map/ppermute | solution.py:411
  245.3 2.3 copy-start.3
  246.5 20.9 %collective-permute-start.37 = (bf16[2,2,2,2,64,640]{5,4,2,1,0,3:T(8,128)(2,1)}, bf16[2,2,2,2,64,640]{5,4,2,1,0,3:T(8,128)(2,1)}, u32[]{:S(2)}, u32[]{:S(2)}) collective-permute-start(bf16[2,2,2,2,64,640]{5,4,2,1,0,3:T(8,128)(2,1)} %bitcast.168), channel_id=1, source_target_pairs={{0,4},{4,0},{8,12},{12,8},{16,20},{20,16},{24,28},{28,24},{1,5},{5... | collective-permute-start | bytes 3932168 | tf_op jit(solution)/shard_map/ppermute | solution.py:411
  247.0 6.9 %collective-permute-start.28 = (bf16[2,2,2,16,768]{4,3,2,1,0:T(8,128)(2,1)S(1)}, bf16[2,2,2,16,768]{4,3,2,1,0:T(8,128)(2,1)S(1)}, u32[]{:S(2)}, u32[]{:S(2)}) collective-permute-start(bf16[2,2,2,16,768]{4,3,2,1,0:T(8,128)(2,1)S(1)} %dynamic-slice_bitcast_fusion.4), channel_id=1, source_target_pairs={{0,1},{1,0},{2,3},{3,2},{4,5},{5,4},{6,7},{7,6},{8,9},{9,8},{10,11... | collective-permute-start | bytes 589832 | tf_op jit(solution)/shard_map/ppermute | solution.py:411
  249.0 21.0 %collective-permute-start.32 = (bf16[2,2,2,2,16,2688]{5,4,2,1,0,3:T(8,128)(2,1)}, bf16[2,2,2,2,16,2688]{5,4,2,1,0,3:T(8,128)(2,1)}, u32[]{:S(2)}, u32[]{:S(2)}) collective-permute-start(bf16[2,2,2,2,16,2688]{5,4,2,1,0,3:T(8,128)(2,1)} %bitcast.167), channel_id=1, source_target_pairs={{0,4},{4,0},{8,12},{12,8},{16,20},{20,16},{24,28},{28,24},{1,5},{5... | collective-permute-start | bytes 4128776 | tf_op jit(solution)/shard_map/ppermute | solution.py:411
  254.0 4.7 %collective-permute-start.29 = (bf16[2,2,16,768]{3,2,1,0:T(8,128)(2,1)S(1)}, bf16[2,2,16,768]{3,2,1,0:T(8,128)(2,1)S(1)}, u32[]{:S(2)}, u32[]{:S(2)}) collective-permute-start(bf16[2,2,16,768]{3,2,1,0:T(8,128)(2,1)S(1)} %dynamic-slice_bitcast_fusion.7), channel_id=1, source_target_pairs={{0,2},{1,3},{2,0},{3,1},{4,6},{5,7},{6,4},{7,5},{8,10},{9,11},{10,... | collective-permute-start | bytes 294920 | tf_op jit(solution)/shard_map/ppermute | solution.py:411
  258.8 4.2 %collective-permute-start.30 = (bf16[2,16,768]{2,1,0:T(8,128)(2,1)S(1)}, bf16[2,16,768]{2,1,0:T(8,128)(2,1)S(1)}, u32[]{:S(2)}, u32[]{:S(2)}) collective-permute-start(bf16[2,16,768]{2,1,0:T(8,128)(2,1)S(1)} %dynamic-slice_bitcast_fusion.10), channel_id=1, source_target_pairs={{0,8},{4,12},{8,0},{12,4},{16,24},{20,28},{24,16},{28,20},{1,9},{5... | collective-permute-start | bytes 147464 | tf_op jit(solution)/shard_map/ppermute | solution.py:411
  262.9 10.6 %collective-permute-start.31 = (bf16[16,768]{1,0:T(8,128)(2,1)S(1)}, bf16[16,768]{1,0:T(8,128)(2,1)S(1)}, u32[]{:S(2)}, u32[]{:S(2)}) collective-permute-start(bf16[16,768]{1,0:T(8,128)(2,1)S(1)} %dynamic-slice_bitcast_fusion.11), channel_id=1, source_target_pairs={{0,16},{4,20},{8,24},{12,28},{16,0},{20,4},{24,8},{28,12},{1,17},{... | collective-permute-start | bytes 73736 | tf_op jit(solution)/shard_map/ppermute | solution.py:411
  268.9 2.6 copy-start.2
  269.9 17.9 %collective-permute-start.38 = (bf16[2,2,2,64,640]{4,3,2,1,0:T(8,128)(2,1)}, bf16[2,2,2,64,640]{4,3,2,1,0:T(8,128)(2,1)S(1)}, u32[]{:S(2)}, u32[]{:S(2)}) collective-permute-start(bf16[2,2,2,64,640]{4,3,2,1,0:T(8,128)(2,1)} %dynamic-slice_bitcast_fusion.1), channel_id=1, source_target_pairs={{0,1},{1,0},{2,3},{3,2},{4,5},{5,4},{6,7},{7,6},{8,9},{9,8},{10,11... | collective-permute-start | bytes 1966088 | tf_op jit(solution)/shard_map/ppermute | solution.py:411
  271.6 26.7 %collective-permute-start.33 = (bf16[2,2,2,16,2688]{4,3,2,1,0:T(8,128)(2,1)S(1)}, bf16[2,2,2,16,2688]{4,3,2,1,0:T(8,128)(2,1)S(1)}, u32[]{:S(2)}, u32[]{:S(2)}) collective-permute-start(bf16[2,2,2,16,2688]{4,3,2,1,0:T(8,128)(2,1)S(1)} %dynamic-slice_bitcast_fusion), channel_id=1, source_target_pairs={{0,1},{1,0},{2,3},{3,2},{4,5},{5,4},{6,7},{7,6},{8,9},{9,8},{10,11... | collective-permute-start | bytes 2064392 | tf_op jit(solution)/shard_map/ppermute | solution.py:411
  289.0 9.8 %collective-permute-start.39 = (bf16[2,2,64,640]{3,2,1,0:T(8,128)(2,1)S(1)}, bf16[2,2,64,640]{3,2,1,0:T(8,128)(2,1)S(1)}, u32[]{:S(2)}, u32[]{:S(2)}) collective-permute-start(bf16[2,2,64,640]{3,2,1,0:T(8,128)(2,1)S(1)} %dynamic-slice_bitcast_fusion.3), channel_id=1, source_target_pairs={{0,2},{1,3},{2,0},{3,1},{4,6},{5,7},{6,4},{7,5},{8,10},{9,11},{10,... | collective-permute-start | bytes 983048 | tf_op jit(solution)/shard_map/ppermute | solution.py:411
  298.4 7.3 %collective-permute-start.34 = (bf16[2,2,16,2688]{3,2,1,0:T(8,128)(2,1)S(1)}, bf16[2,2,16,2688]{3,2,1,0:T(8,128)(2,1)S(1)}, u32[]{:S(2)}, u32[]{:S(2)}) collective-permute-start(bf16[2,2,16,2688]{3,2,1,0:T(8,128)(2,1)S(1)} %dynamic-slice_bitcast_fusion.2), channel_id=1, source_target_pairs={{0,2},{1,3},{2,0},{3,1},{4,6},{5,7},{6,4},{7,5},{8,10},{9,11},{10,... | collective-permute-start | bytes 1032200 | tf_op jit(solution)/shard_map/ppermute | solution.py:411
  298.8 6.9 %collective-permute-start.40 = (bf16[2,64,640]{2,1,0:T(8,128)(2,1)S(1)}, bf16[2,64,640]{2,1,0:T(8,128)(2,1)S(1)}, u32[]{:S(2)}, u32[]{:S(2)}) collective-permute-start(bf16[2,64,640]{2,1,0:T(8,128)(2,1)S(1)} %dynamic-slice_bitcast_fusion.6), channel_id=1, source_target_pairs={{0,8},{4,12},{8,0},{12,4},{16,24},{20,28},{24,16},{28,20},{1,9},{5... | collective-permute-start | bytes 491528 | tf_op jit(solution)/shard_map/ppermute | solution.py:411
  305.8 8.1 %collective-permute-start.41 = (bf16[64,640]{1,0:T(8,128)(2,1)S(1)}, bf16[64,640]{1,0:T(8,128)(2,1)S(1)}, u32[]{:S(2)}, u32[]{:S(2)}) collective-permute-start(bf16[64,640]{1,0:T(8,128)(2,1)S(1)} %dynamic-slice_bitcast_fusion.9), channel_id=1, source_target_pairs={{0,16},{4,20},{8,24},{12,28},{16,0},{20,4},{24,8},{28,12},{1,17},{... | collective-permute-start | bytes 245768 | tf_op jit(solution)/shard_map/ppermute | solution.py:411
  306.2 8.4 %collective-permute-start.35 = (bf16[2,16,2688]{2,1,0:T(8,128)(2,1)S(1)}, bf16[2,16,2688]{2,1,0:T(8,128)(2,1)S(1)}, u32[]{:S(2)}, u32[]{:S(2)}) collective-permute-start(bf16[2,16,2688]{2,1,0:T(8,128)(2,1)S(1)} %dynamic-slice_bitcast_fusion.5), channel_id=1, source_target_pairs={{0,8},{4,12},{8,0},{12,4},{16,24},{20,28},{24,16},{28,20},{1,9},{5... | collective-permute-start | bytes 516104 | tf_op jit(solution)/shard_map/ppermute | solution.py:411
  314.6 5.7 %collective-permute-start.36 = (bf16[16,2688]{1,0:T(8,128)(2,1)S(1)}, bf16[16,2688]{1,0:T(8,128)(2,1)S(1)}, u32[]{:S(2)}, u32[]{:S(2)}) collective-permute-start(bf16[16,2688]{1,0:T(8,128)(2,1)S(1)} %dynamic-slice_bitcast_fusion.8), channel_id=1, source_target_pairs={{0,16},{4,20},{8,24},{12,28},{16,0},{20,4},{24,8},{28,12},{1,17},{... | collective-permute-start | bytes 258056 | tf_op jit(solution)/shard_map/ppermute | solution.py:411
  (5 other events, 4.3 us)

commit v2 on v1

v2 whole, which is shorter than its diff:
```python
import functools

import jax
import jax.numpy as jnp
from jax import lax
from jax.experimental import pallas as pl
from jax.experimental.pallas import tpu as pltpu
from jax.sharding import PartitionSpec as P

EPS = 1e-05
LANES = 128
VMEM_LIMIT = 56 * 1024 * 1024
BF16 = jnp.bfloat16
F32 = jnp.float32


def call_params():
    return pltpu.CompilerParams(vmem_limit_bytes=VMEM_LIMIT)


def cost(flops, bytes_accessed, transcendentals=0):
    return pl.CostEstimate(
        flops=int(flops), bytes_accessed=int(bytes_accessed), transcendentals=int(transcendentals)
    )


def dot_nn(left, right):
    return lax.dot_general(left, right, (((1,), (0,)), ((), ())), preferred_element_type=F32)


def dot_nt(left, right):
    return lax.dot_general(left, right, (((1,), (1,)), ((), ())), preferred_element_type=F32)


def lanes_of(rows, width):
    return lax.broadcasted_iota(jnp.int32, (rows, width), 1)


def fold_matrix(width, head, shift):
    source = lax.broadcasted_iota(jnp.int32, (width, LANES), 0)
    target = lax.broadcasted_iota(jnp.int32, (width, LANES), 1)
    return jnp.where(target == shift + lax.rem(source, head), 1.0, 0.0).astype(BF16)


def unfold_matrix(width, head, shift):
    source = lax.broadcasted_iota(jnp.int32, (LANES, width), 1)
    target = lax.broadcasted_iota(jnp.int32, (LANES, width), 0)
    return jnp.where(target == shift + lax.rem(source, head), 1.0, 0.0).astype(BF16)


def rows_of(columns, picked):
    row = lax.broadcasted_iota(jnp.int32, (8, LANES), 0)
    lane = lax.broadcasted_iota(jnp.int32, (8, LANES), 1)
    chosen = jnp.zeros((8, LANES), F32)
    for at, column in enumerate(picked):
        chosen = jnp.where((row == at) & (lane == column), 1.0, chosen)
    return dot_nt(chosen.astype(BF16), columns)


def normalize(values):
    centered = values - jnp.mean(values, -1, keepdims=True)
    inv_dev = lax.rsqrt(jnp.mean(centered * centered, -1, keepdims=True) + EPS)
    return centered * inv_dev, inv_dev


def norm_back(grad, gain, normed, inv_dev):
    scaled = grad * gain
    return inv_dev * (
        scaled
        - jnp.mean(scaled, -1, keepdims=True)
        - normed * jnp.mean(scaled * normed, -1, keepdims=True)
    )


def pre_kernel(experts, head, x_ref, routes_ref, weight_ref, hidden_ref, kv_ref, q_ref, gate_ref):
    width = x_ref.shape[1]
    inner = experts * head
    extras = weight_ref[:, inner + LANES :]
    vectors = rows_of(extras, (experts, experts + 1))
    normed, _ = normalize(x_ref[...].astype(F32))
    hidden = (normed * vectors[0:1] + vectors[1:2]).astype(BF16)
    hidden_ref[...] = hidden
    big = dot_nn(hidden, weight_ref[...])
    rows = big.shape[0]
    kv_ref[...] = big[:, inner : inner + LANES].astype(BF16)
    logits = big[:, inner + LANES :]
    lane = lanes_of(rows, LANES)
    first, second = routes_ref[:, 0:1], routes_ref[:, 1:2]
    logit_one = jnp.sum(jnp.where(lane == first, logits, 0.0), -1, keepdims=True)
    logit_two = jnp.sum(jnp.where(lane == second, logits, 0.0), -1, keepdims=True)
    peak = jnp.maximum(logit_one, logit_two)
    exp_one = jnp.exp(logit_one - peak)
    exp_two = jnp.exp(logit_two - peak)
    total = exp_one + exp_two
    gate_ref[...] = jnp.where(lane == 0, exp_one / total, jnp.where(lane == 1, exp_two / total, 0.0))
    queries = (big[:, :inner] * (head**-0.5)).astype(BF16)
    owner = lax.div(lanes_of(rows, inner), head)
    fold = fold_matrix(inner, head, 0)
    zero = jnp.zeros_like(queries)
    q_ref[0] = dot_nn(jnp.where(owner == first, queries, zero), fold).astype(BF16)
    q_ref[1] = dot_nn(jnp.where(owner == second, queries, zero), fold).astype(BF16)


def masked(scores, start, key_at, query_at):
    keys = key_at + lax.broadcasted_iota(jnp.int32, scores.shape, 0)
    queries = query_at + lax.rem(
        lax.broadcasted_iota(jnp.int32, (1, scores.shape[1]), 1), scores.shape[1] // 2
    )
    return jnp.where((keys >= start) & (keys <= queries), scores, -1e30)


def over_chunks(step, bounds_ref, seq, chunk, query_at, tokens):
    low = bounds_ref[2 * seq] // chunk
    high = (query_at + tokens - 1) // chunk + 1
    clear_high = (query_at + 1) // chunk
    clear_low = jnp.minimum((bounds_ref[2 * seq + 1] + chunk - 1) // chunk, clear_high)

    def with_mask(at, carry):
        step(at, True)
        return carry

    def without_mask(at, carry):
        step(at, False)
        return carry

    lax.fori_loop(low, clear_low, with_mask, 0)
    lax.fori_loop(clear_low, clear_high, without_mask, 0)
    lax.fori_loop(clear_high, high, with_mask, 0)


def attend_kernel(reach, chunk, head, bounds_ref, q_ref, start_ref, *rest):
    pieces = rest[:reach]
    mixed_ref, lse_ref, kv_buf, vt_buf, peak_ref, total_ref, acc_ref = rest[reach:]
    seq = pl.program_id(0)
    local = pieces[0].shape[1]
    per_piece = local // chunk
    for at in range(reach):
        for part in range(per_piece):
            block = pieces[at][0, part * chunk : (part + 1) * chunk, :]
            kv_buf[at * per_piece + part] = block
            row = lax.broadcasted_iota(jnp.int32, (LANES, chunk), 0)
            vt_buf[at * per_piece + part] = jnp.where(
                row >= head, block.astype(F32).T, 0.0
            ).astype(BF16)

    queries = jnp.concatenate([q_ref[0], q_ref[1]], 0)
    start = start_ref[0]
    start = jnp.concatenate([start, start], 1)
    query_at = (reach - 1) * local
    peak_ref[...] = jnp.full_like(peak_ref, -1e30)
    total_ref[...] = jnp.zeros_like(total_ref)
    acc_ref[...] = jnp.zeros_like(acc_ref)

    def step(at, needs_mask):
        scores = dot_nt(kv_buf[at], queries)
        if needs_mask:
            scores = masked(scores, start, at * chunk, query_at)
        peak = jnp.maximum(peak_ref[...], jnp.max(scores, 0, keepdims=True))
        fade = jnp.exp(peak_ref[...] - peak)
        expo = jnp.exp(scores - peak)
        total_ref[...] = total_ref[...] * fade + jnp.sum(expo, 0, keepdims=True)
        acc_ref[...] = acc_ref[...] * fade + dot_nn(vt_buf[at], expo.astype(BF16))
        peak_ref[...] = peak

    over_chunks(step, bounds_ref, seq, chunk, query_at, local)
    mixed = (acc_ref[...] / total_ref[...]).T
    mixed_ref[0] = mixed[:local]
    mixed_ref[1] = mixed[local:]
    lse_ref[0] = peak_ref[...] + jnp.log(total_ref[...])


def mid_kernel(
    experts,
    head,
    x_ref,
    dy_ref,
    routes_ref,
    gate_ref,
    mixed_ref,
    vector_ref,
    down_ref,
    up_ref,
    wo_ref,
    out_ref,
    grad_mid_ref,
    grad_mixed_ref,
    grad_logit_ref,
    grads_ref,
    acc_out,
    acc_up,
    acc_down,
    acc_vec,
    acc_upb,
    branch_ref,
    gsec_ref,
):
    step, last = pl.program_id(0), pl.num_programs(0) - 1
    rows, width = x_ref.shape
    inner = experts * head
    owners, own_rows = wo_ref.shape[:2]
    ff_rows = down_ref.shape[1]
    ff = owners * ff_rows
    blocks = ff // width

    @pl.when(step == 0)
    def _():
        acc_out[...] = jnp.zeros_like(acc_out)
        acc_up[...] = jnp.zeros_like(acc_up)
        acc_down[...] = jnp.zeros_like(acc_down)
        acc_vec[...] = jnp.zeros_like(acc_vec)
        acc_upb[...] = jnp.zeros_like(acc_upb)

    gain, shift = vector_ref[1:2, :width], vector_ref[2:3, :width]
    down_bias = vector_ref[3:4, :width]
    first, second = routes_ref[:, 0:1], routes_ref[:, 1:2]
    gate_one, gate_two = gate_ref[:, 0:1], gate_ref[:, 1:2]
    owner = lax.div(lanes_of(rows, inner), head)
    unfold = unfold_matrix(inner, head, head)
    fold = fold_matrix(inner, head, head)
    wo = wo_ref[...].reshape(inner, width)
    mixed_one, mixed_two = mixed_ref[0], mixed_ref[1]
    routed_one = dot_nn((gate_one * mixed_one).astype(BF16), unfold)
    routed_two = dot_nn((gate_two * mixed_two).astype(BF16), unfold)
    routed = jnp.where(
        owner == first, routed_one, jnp.where(owner == second, routed_two, 0.0)
    )
    middle = x_ref[...].astype(F32) + dot_nn(routed.astype(BF16), wo)
    normed, inv_dev = normalize(middle)
    second_wide = normed * gain + shift
    second_low = second_wide.astype(BF16)
    second_t = second_wide.T.astype(BF16)
    dy = dy_ref[...]
    dy_wide = dy.astype(F32)
    dy_t = dy_wide.T.astype(BF16)
    branch_ref[...] = middle + down_bias
    gsec_ref[...] = jnp.zeros_like(gsec_ref)
    per_block = width // ff_rows if owners > 1 else 1

    def down_block(at):
        if owners > 1:
            return down_ref[at * per_block : (at + 1) * per_block].reshape(width, width)
        return down_ref[0, at * width : (at + 1) * width, :]

    for at in range(blocks):
        lo = at * width
        up = up_ref[:, at * own_rows : (at + 1) * own_rows, :].reshape(width, width)
        down = down_block(at)
        pre_act = dot_nn(second_low, up) + vector_ref[0:1, lo : lo + width]
        sigma = 1.0 / (1.0 + jnp.exp(-pre_act))
        active = (pre_act * sigma).astype(BF16)
        branch_ref[...] += dot_nn(active, down)
        grad_active = dot_nt(dy, down).astype(BF16).astype(F32)
        grad_pre = grad_active * (sigma * (1.0 + pre_act * (1.0 - sigma)))
        grad_low = grad_pre.astype(BF16)
        gsec_ref[...] += dot_nt(grad_low, up)
        acc_down[:, lo : lo + width] += dot_nn(dy_t, active)
        acc_up[:, lo : lo + width] += dot_nn(second_t, grad_low)
        acc_upb[8:9, lo : lo + width] += jnp.sum(grad_low.astype(F32), 0, keepdims=True)

    out_ref[...] = branch_ref[...].astype(BF16)
    gsec = gsec_ref[...]
    acc_vec[0:1] += jnp.sum(gsec * normed, 0, keepdims=True)
    acc_vec[1:2] += jnp.sum(gsec, 0, keepdims=True)
    acc_vec[2:3] += jnp.sum(dy_wide, 0, keepdims=True)
    grad_mid = dy_wide + norm_back(gsec, gain, normed, inv_dev)
    grad_mid_ref[...] = grad_mid
    grad_att = grad_mid.astype(BF16)
    acc_out[...] += dot_nn(routed.T.astype(BF16), grad_att)
    grad_routed = dot_nt(grad_att, wo).astype(BF16)
    zero = jnp.zeros_like(grad_routed)
    picked_one = dot_nn(jnp.where(owner == first, grad_routed, zero), fold)
    picked_two = dot_nn(jnp.where(owner == second, grad_routed, zero), fold)
    grad_mixed_ref[0] = (gate_one * picked_one).astype(BF16)
    grad_mixed_ref[1] = (gate_two * picked_two).astype(BF16)
    grad_one = jnp.sum(picked_one * mixed_one, -1, keepdims=True)
    grad_two = jnp.sum(picked_two * mixed_two, -1, keepdims=True)
    common = gate_one * grad_one + gate_two * grad_two
    lane = lanes_of(rows, LANES)
    grad_logit_ref[...] = jnp.where(
        lane == first,
        gate_one * (grad_one - common),
        jnp.where(lane == second, gate_two * (grad_two - common), 0.0),
    )

    @pl.when(step == last)
    def _():
        up_at, out_at = ff_rows, ff_rows + blocks * own_rows
        for at in range(blocks):
            lo = at * width
            turned = acc_down[:, lo : lo + width].T.astype(BF16)
            if owners > 1:
                grads_ref[at * per_block : (at + 1) * per_block, :ff_rows, :] = turned.reshape(
                    per_block, ff_rows, width
                )
            else:
                grads_ref[0, lo : lo + width, :] = turned
            grads_ref[:, up_at + at * own_rows : up_at + (at + 1) * own_rows, :] = (
                acc_up[:, lo : lo + width].astype(BF16).reshape(owners, own_rows, width)
            )
        grads_ref[:, out_at : out_at + own_rows, :] = (
            acc_out[...].astype(BF16).reshape(owners, own_rows, width)
        )
        extra = acc_upb[...].T.astype(BF16).reshape(owners, blocks, own_rows, LANES)
        for at in range(blocks):
            part = extra[:, at]
            if at == 0:
                part = part + acc_vec[...].T.astype(BF16).reshape(owners, own_rows, LANES)
            grads_ref[:, out_at + own_rows :, at * LANES : (at + 1) * LANES] = part


def attend_back_kernel(
    reach, chunk, head, micro, chained, bounds_ref, q_ref, grad_ref, mixed_ref, lse_ref, start_ref, *rest
):
    pieces = rest[:reach]
    rest = rest[reach + chained :]
    grad_q_ref = rest[0]
    outs = rest[1 : reach + 1]
    kv_buf, kt_buf, acc_kv, acc_q = rest[reach + 1 :]
    seq = micro * pl.num_programs(0) + pl.program_id(0)
    local = pieces[0].shape[1]
    per_piece = local // chunk
    acc_kv[...] = jnp.zeros_like(acc_kv)
    for at in range(reach):
        for part in range(per_piece):
            block = pieces[at][0, part * chunk : (part + 1) * chunk, :]
            kv_buf[at * per_piece + part] = block
            kt_buf[at * per_piece + part] = block.astype(F32).T.astype(BF16)

    queries = jnp.concatenate([q_ref[0], q_ref[1]], 0)
    grads = jnp.concatenate([grad_ref[0], grad_ref[1]], 0)
    mixed = jnp.concatenate([mixed_ref[0], mixed_ref[1]], 0)
    inner = jnp.sum((grads.astype(F32) * mixed).T, 0, keepdims=True)
    start = start_ref[0]
    start = jnp.concatenate([start, start], 1)
    lse = lse_ref[0]
    query_at = (reach - 1) * local
    acc_q[...] = jnp.zeros_like(acc_q)

    def step(at, needs_mask):
        keyval = kv_buf[at]
        scores = dot_nt(keyval, queries)
        if needs_mask:
            scores = masked(scores, start, at * chunk, query_at)
        probs = jnp.exp(scores - lse)
        grad_probs = dot_nt(keyval, grads)
        grad_scores = (probs * (grad_probs - inner)).astype(BF16)
        acc_kv[at] += dot_nn(grad_scores, queries) + dot_nn(probs.astype(BF16), grads)
        acc_q[...] += dot_nn(kt_buf[at], grad_scores)

    over_chunks(step, bounds_ref, seq, chunk, query_at, local)
    row = lax.broadcasted_iota(jnp.int32, acc_q.shape, 0)
    grad_q = (jnp.where(row < head, acc_q[...], 0.0) * (head**-0.5)).T.astype(BF16)
    grad_q_ref[0] = grad_q[:local]
    grad_q_ref[1] = grad_q[local:]
    for at in range(reach):
        for part in range(per_piece):
            block = acc_kv[at * per_piece + part]
            outs[at][0, part * chunk : (part + 1) * chunk, :] = block.astype(outs[at].dtype)


def query_grad_kernel(
    experts,
    head,
    hidden_ref,
    routes_ref,
    grad_q_ref,
    grad_logit_ref,
    weight_ref,
    partial_ref,
    d_query_ref,
    d_router_ref,
    acc_query,
    acc_router,
):
    step, last = pl.program_id(0), pl.num_programs(0) - 1
    rows, width = hidden_ref.shape
    inner = experts * head

    @pl.when(step == 0)
    def _():
        acc_query[...] = jnp.zeros_like(acc_query)
        acc_router[...] = jnp.zeros_like(acc_router)

    first, second = routes_ref[:, 0:1], routes_ref[:, 1:2]
    owner = lax.div(lanes_of(rows, inner), head)
    unfold = unfold_matrix(inner, head, 0)
    grad_queries = jnp.where(
        owner == first,
        dot_nn(grad_q_ref[0], unfold),
        jnp.where(owner == second, dot_nn(grad_q_ref[1], unfold), 0.0),
    ).astype(BF16)
    grad_logits = grad_logit_ref[...]
    logit_high = grad_logits.astype(BF16)
    logit_low = (grad_logits - logit_high.astype(F32)).astype(BF16)
    router = weight_ref[:, inner + LANES :]
    partial_ref[...] = (
        dot_nt(grad_queries, weight_ref[:, :inner])
        + dot_nt(logit_high, router)
        + dot_nt(logit_low, router)
    )
    hidden_t = hidden_ref[...].astype(F32).T.astype(BF16)
    acc_query[...] += dot_nn(hidden_t, grad_queries)
    acc_router[...] += dot_nn(hidden_t, logit_high) + dot_nn(hidden_t, logit_low)

    @pl.when(step == last)
    def _():
        d_query_ref[...] = acc_query[...].astype(BF16)
        d_router_ref[...] = acc_router[...]


def last_kernel(
    experts,
    head,
    reach,
    micro_count,
    x_ref,
    hidden_ref,
    partial_ref,
    grad_mid_ref,
    router_ref,
    weight_ref,
    *rest,
):
    pieces = rest[: reach * micro_count]
    grad_in_ref, d_small_ref, acc_kv, acc_vec, summed_ref = rest[reach * micro_count :]
    step, last = pl.program_id(0), pl.num_programs(0) - 1
    rows, width = x_ref.shape
    inner = experts * head

    @pl.when(step == 0)
    def _():
        acc_kv[...] = jnp.zeros_like(acc_kv)
        acc_vec[...] = jnp.zeros_like(acc_vec)

    for micro in range(micro_count):

        @pl.when(step == micro)
        def _():
            mine = pieces[micro * reach : (micro + 1) * reach]
            summed = mine[0][...]
            for piece in mine[1:]:
                summed = summed + piece[...].astype(F32)
            summed_ref[...] = summed.astype(BF16)

    gain = rows_of(weight_ref[:, inner + LANES :], (experts,))[0:1]
    normed, inv_dev = normalize(x_ref[...].astype(F32))
    grad_keyvals = summed_ref[...]
    grad_hidden = partial_ref[...] + dot_nt(grad_keyvals, weight_ref[:, inner : inner + LANES])
    grad_in_ref[...] = grad_mid_ref[...] + norm_back(grad_hidden, gain, normed, inv_dev)
    hidden_t = hidden_ref[...].astype(F32).T.astype(BF16)
    acc_kv[...] += dot_nn(hidden_t, grad_keyvals)
    acc_vec[experts : experts + 1] += jnp.sum(grad_hidden * normed, 0, keepdims=True)
    acc_vec[experts + 1 : experts + 2] += jnp.sum(grad_hidden, 0, keepdims=True)

    @pl.when(step == last)
    def _():
        d_small_ref[:, :LANES] = acc_kv[...].astype(BF16)
        d_small_ref[:, LANES:] = (router_ref[...] + acc_vec[...].T).astype(BF16)


def whole_spec(shape):
    zeros = (0,) * len(shape)
    return pl.BlockSpec(shape, lambda *_: zeros, pipeline_mode=pl.Buffered(1))


def row_spec(rows, columns):
    return pl.BlockSpec((rows, columns), lambda i, *_: (i, 0))


def pair_spec(rows):
    return pl.BlockSpec((2, rows, LANES), lambda i, *_: (0, i, 0))


def swapped(value, axis, mask):
    count = lax.axis_size(axis)
    return lax.ppermute(value, axis, [(at, at ^ mask) for at in range(count)])


def passed_along(value, axis, steps):
    count = lax.axis_size(axis)
    leading, last = (max(0, -steps), min(count, count - steps))
    return lax.ppermute(value, axis, [(source, source + steps) for source in range(leading, last)])


def gathered(shard):
    dp, seq = lax.axis_size("dp"), lax.axis_size("seq")
    along = [shard] + [swapped(shard, "dp", 2 * at) for at in range(1, dp // 2)]
    held = jnp.stack(along)
    across = [held] + [swapped(held, "seq", at) for at in range(1, seq)]
    held = jnp.stack(across)
    held = jnp.stack([held, swapped(held, "dp", 1)])
    dp_me, seq_me = lax.axis_index("dp"), lax.axis_index("seq")
    held = jnp.moveaxis(held, 2, 0)
    for dim, me in ((0, dp_me // 2), (1, dp_me % 2), (2, seq_me)):
        order = jnp.arange(held.shape[dim], dtype=jnp.int32) ^ me
        held = jnp.take(held, order, axis=dim)
    return held.reshape((dp * seq * shard.shape[0],) + shard.shape[1:])


def at_index(value, index, dim):
    return lax.dynamic_index_in_dim(value, index, dim, keepdims=False)


def core_halved(value):
    core = lax.axis_index("dp") % 2
    return at_index(value, core, 1) + swapped(at_index(value, 1 - core, 1), "dp", 1)


def seq_halved(value, dim, mask):
    bit = (lax.axis_index("seq") // mask) % 2
    return at_index(value, bit, dim) + swapped(at_index(value, 1 - bit, dim), "seq", mask)


def summed_direct(value, dim, axis, scale):
    me = lax.axis_index(axis) // scale
    total = at_index(value, me, dim).astype(F32)
    for at in range(1, value.shape[dim]):
        total = total + swapped(at_index(value, me ^ at, dim), axis, at * scale).astype(F32)
    return total


def small_scattered(value):
    dp, seq = lax.axis_size("dp"), lax.axis_size("seq")
    held = value.reshape(dp // 2, 2, seq, value.shape[0] // (dp * seq), value.shape[1])
    held = core_halved(held)
    held = summed_direct(held, 1, "seq", 1).astype(BF16)
    return summed_direct(held, 0, "dp", 2)


def together(*values):
    return lax.optimization_barrier(values)


def on_device(
    block_in,
    routes,
    segments,
    cotangent,
    ln1_gain,
    ln1_bias,
    query_weight,
    kv_weight,
    router_weight,
    out_weight,
    ln2_gain,
    ln2_bias,
    up_weight,
    up_bias,
    down_weight,
    down_bias,
):
    micro_count, seq_count, local_len, width = block_in.shape
    full_len = segments.shape[2]
    experts = router_weight.shape[1]
    head = kv_weight.shape[1] // 2
    inner = experts * head
    ff = up_weight.shape[1]
    dp, shards = lax.axis_size("dp"), lax.axis_size("seq")
    devices = dp * shards
    own_rows, ff_rows, blocks = width // devices, ff // devices, ff // width
    aligned = own_rows % 16 == 0
    batch = micro_count * seq_count
    rows_all = batch * local_len
    tile = seq_count * local_len
    longest = full_len * 3 // 4
    reach = min(shards, (longest - 2) // local_len + 2)
    own_shard = lax.axis_index("seq")
    start_pos = own_shard * local_len

    def column(vector):
        return vector[:, None]

    def padded(value, columns):
        return jnp.pad(value, ((0, 0), (0, columns - value.shape[1])))

    extra = [router_weight, column(ln1_gain), column(ln1_bias), column(ln2_gain)]
    extra += [column(ln2_bias), column(down_bias), up_bias.reshape(own_rows, blocks)]
    packed_a = jnp.concatenate(
        [query_weight, kv_weight, padded(jnp.concatenate(extra, 1), LANES)], 1
    )
    group_a = gathered(packed_a)
    packed_b = jnp.concatenate(
        [down_weight]
        + [up_weight[:, at * width : (at + 1) * width] for at in range(blocks)]
        + [out_weight],
        0,
    )
    group_b = lax.all_gather(packed_b, ("dp", "seq"), axis=0, tiled=False)
    up_at, out_at = ff_rows, ff_rows + blocks * own_rows
    if aligned:
        nb, rb, fb = devices, own_rows, ff_rows
        weights = [group_b, group_b, group_b]
        weight_specs = [
            pl.BlockSpec((nb, ff_rows, width), lambda *_: (0, 0, 0), pipeline_mode=pl.Buffered(1)),
            pl.BlockSpec(
                (nb, blocks * own_rows, width), lambda *_: (0, 1, 0), pipeline_mode=pl.Buffered(1)
            ),
            pl.BlockSpec(
                (nb, own_rows, width),
                lambda *_: (0, out_at // own_rows, 0),
                pipeline_mode=pl.Buffered(1),
            ),
        ]
    else:
        nb, rb, fb = 1, width, ff
        up_all = group_b[:, up_at:out_at].reshape(devices, blocks, own_rows, width)
        weights = [
            group_b[:, :ff_rows].reshape(1, ff, width),
            jnp.moveaxis(up_all, 0, 1).reshape(1, ff, width),
            group_b[:, out_at:].reshape(1, width, width),
        ]
        weight_specs = [whole_spec(value.shape) for value in weights]

    tokens = block_in.reshape(rows_all, width)
    grad_out = cotangent.reshape(rows_all, width)
    route_rows = routes.reshape(rows_all, 2)

    seg_rows = segments.reshape(batch, full_len)
    seg_local = lax.dynamic_slice_in_dim(seg_rows, start_pos, local_len, 1)
    doc_start = jnp.sum(
        (seg_rows[:, None, :] < seg_local[:, :, None]).astype(jnp.int32), -1, dtype=jnp.int32
    )
    doc_start = jnp.maximum(doc_start - (own_shard - (reach - 1)) * local_len, 0)
    chunk = min(local_len, 256)
    bounds = jnp.stack([doc_start[:, 0], doc_start[:, -1]], 1).reshape(2 * batch)
    starts = doc_start.reshape(batch, 1, local_len)

    steps = micro_count
    a_cols = inner + 2 * LANES
    hidden, keyvals, queries, gates = pl.pallas_call(
        functools.partial(pre_kernel, experts, head),
        grid=(steps,),
        in_specs=[row_spec(tile, width), row_spec(tile, 2), whole_spec((width, a_cols))],
        out_specs=[
            row_spec(tile, width),
            row_spec(tile, LANES),
            pair_spec(tile),
            row_spec(tile, LANES),
        ],
        out_shape=[
            jax.ShapeDtypeStruct((rows_all, width), BF16),
            jax.ShapeDtypeStruct((rows_all, LANES), BF16),
            jax.ShapeDtypeStruct((2, rows_all, LANES), BF16),
            jax.ShapeDtypeStruct((rows_all, LANES), F32),
        ],
        compiler_params=call_params(),
        cost_estimate=cost(2 * rows_all * width * (a_cols + 512), rows_all * width * 8),
        name="pre",
    )(tokens, route_rows, group_a)

    own_pieces = keyvals.reshape(batch, local_len, LANES)
    pieces = [own_pieces] + [passed_along(own_pieces, "seq", back) for back in range(1, reach)]
    pieces = pieces[::-1]

    columns = group_a[:, inner + LANES :].astype(F32)
    small = jnp.pad(columns[:, experts + 2 : experts + 5].T, ((0, 4), (0, ff - width)))
    up_row = columns[:, experts + 5 : experts + 5 + blocks].reshape(1, ff)
    vectors = jnp.concatenate([up_row, small], 0)

    buffer_chunks = reach * local_len // chunk
    piece_spec = pl.BlockSpec((1, local_len, LANES), lambda b, *_: (b, 0, 0))
    q_spec = pl.BlockSpec((2, local_len, LANES), lambda b, *_: (0, b, 0))
    start_spec = pl.BlockSpec((1, 1, local_len), lambda b, *_: (b, 0, 0))
    lse_spec = pl.BlockSpec((1, 1, 2 * local_len), lambda b, *_: (b, 0, 0))
    pairs = rows_all * full_len
    mixed, lse = pl.pallas_call(
        functools.partial(attend_kernel, reach, chunk, head),
        grid_spec=pltpu.PrefetchScalarGridSpec(
            num_scalar_prefetch=1,
            grid=(batch,),
            in_specs=[q_spec, start_spec] + [piece_spec] * reach,
            out_specs=[q_spec, lse_spec],
            scratch_shapes=[
                pltpu.VMEM((buffer_chunks, chunk, LANES), BF16),
                pltpu.VMEM((buffer_chunks, LANES, chunk), BF16),
                pltpu.VMEM((1, 2 * local_len), F32),
                pltpu.VMEM((1, 2 * local_len), F32),
                pltpu.VMEM((LANES, 2 * local_len), F32),
            ],
        ),
        out_shape=[
            jax.ShapeDtypeStruct((2, rows_all, LANES), F32),
            jax.ShapeDtypeStruct((batch, 1, 2 * local_len), F32),
        ],
        compiler_params=call_params(),
        cost_estimate=cost(4 * pairs * LANES, rows_all * LANES * 16, pairs),
        name="attend",
    )(bounds, queries, starts, *pieces)

    grad_rows = ff_rows + (blocks + 2) * own_rows if aligned else ff + (blocks + 2) * width
    block_out, grad_mid, grad_mixed, grad_logits, grads_b = pl.pallas_call(
        functools.partial(mid_kernel, experts, head),
        grid=(steps,),
        in_specs=[
            row_spec(tile, width),
            row_spec(tile, width),
            row_spec(tile, 2),
            row_spec(tile, LANES),
            pair_spec(tile),
            whole_spec((8, ff)),
        ]
        + weight_specs,
        out_specs=[
            row_spec(tile, width),
            row_spec(tile, width),
            pair_spec(tile),
            row_spec(tile, LANES),
            whole_spec((nb, grad_rows, width)),
        ],
        out_shape=[
            jax.ShapeDtypeStruct((rows_all, width), BF16),
            jax.ShapeDtypeStruct((rows_all, width), F32),
            jax.ShapeDtypeStruct((2, rows_all, LANES), BF16),
            jax.ShapeDtypeStruct((rows_all, LANES), F32),
            jax.ShapeDtypeStruct((nb, grad_rows, width), BF16),
        ],
        scratch_shapes=[
            pltpu.VMEM((inner, width), F32),
            pltpu.VMEM((width, ff), F32),
            pltpu.VMEM((width, ff), F32),
            pltpu.VMEM((LANES, width), F32),
            pltpu.VMEM((LANES, ff), F32),
            pltpu.VMEM((tile, width), F32),
            pltpu.VMEM((tile, width), F32),
        ],
        compiler_params=call_params(),
        cost_estimate=cost(6 * rows_all * width * (2 * ff + width), rows_all * width * 16),
        name="mid",
    )(tokens, grad_out, route_rows, gates, mixed, vectors, *weights)

    if not aligned:
        parts = grads_b[0]
        down_part = parts[:ff].reshape(devices, ff_rows, width)
        up_part = parts[ff : 2 * ff].reshape(blocks, devices, own_rows, width)
        up_part = jnp.moveaxis(up_part, 0, 1).reshape(devices, blocks * own_rows, width)
        out_part = parts[2 * ff : 2 * ff + width].reshape(devices, own_rows, width)
        tail = parts[2 * ff + width :]
        rows_up = tail.reshape(width, blocks, LANES)[:, :, 8].T.reshape(devices, own_rows, blocks)
        rows_vec = tail[:, :8].reshape(devices, own_rows, 8)
        rows_up = jnp.moveaxis(rows_up.reshape(devices, blocks, own_rows), 1, 2)
        tail = jnp.zeros((devices, own_rows, blocks, LANES), BF16)
        tail = tail.at[:, :, :, 8].set(rows_up).at[:, :, 0, :8].set(rows_vec)
        tail = tail.reshape(devices, own_rows, width)
        grads_b = jnp.concatenate([down_part, up_part, out_part, tail], 1)

    held = grads_b.reshape((dp // 2, 2, shards) + grads_b.shape[1:])
    held = core_halved(held)
    bits = shards.bit_length() - 1
    order = [1 << at for at in range(bits)]
    orders = (order, order[bits // 2 :] + order[: bits // 2])
    half_rows = held.shape[2] // 2
    halves = [
        held.reshape((dp // 2,) + (2,) * bits + held.shape[2:])[..., :half_rows, :],
        held.reshape((dp // 2,) + (2,) * bits + held.shape[2:])[..., half_rows:, :],
    ]
    remaining = [list(reversed(order)), list(reversed(order))]

    def halving(stage):
        for part in range(2):
            mask = orders[part][stage]
            dim = 1 + remaining[part].index(mask)
            remaining[part].remove(mask)
            halves[part] = seq_halved(halves[part], dim, mask)

    back_params = dict(compiler_params=call_params(), name="attend_back")
    grad_queries = None
    returned = []
    stage = 0
    for micro in range(micro_count):

        def at_micro(block, dims):
            base = micro * seq_count
            if dims == "b":
                return pl.BlockSpec(block, lambda b, *_: (base + b, 0, 0))
            return pl.BlockSpec(block, lambda b, *_: (0, base + b, 0))

        q_at = at_micro((2, local_len, LANES), "q")
        in_specs = [
            q_at,
            q_at,
            q_at,
            at_micro((1, 1, 2 * local_len), "b"),
            at_micro((1, 1, local_len), "b"),
        ]
        in_specs += [at_micro((1, local_len, LANES), "b")] * reach
        operands = [queries, grad_mixed, mixed, lse, starts, *pieces]
        bounds_now = bounds
        aliases = {}
        if micro:
            in_specs.append(pl.BlockSpec(memory_space=pl.ANY))
            if stage == 0:
                bounds_now, halves[0], halves[1] = together(bounds, halves[0], halves[1])
            if stage < bits:
                halving(stage)
                stage += 1
            operands.append(grad_queries)
            aliases = {len(operands): 0}
        back = pl.pallas_call(
            functools.partial(attend_back_kernel, reach, chunk, head, micro, int(micro > 0)),
            grid_spec=pltpu.PrefetchScalarGridSpec(
                num_scalar_prefetch=1,
                grid=(seq_count,),
                in_specs=in_specs,
                out_specs=[q_at] + [piece_spec] * reach,
                scratch_shapes=[
                    pltpu.VMEM((buffer_chunks, chunk, LANES), BF16),
                    pltpu.VMEM((buffer_chunks, LANES, chunk), BF16),
                    pltpu.VMEM((buffer_chunks, chunk, LANES), F32),
                    pltpu.VMEM((LANES, 2 * local_len), F32),
                ],
            ),
            out_shape=[jax.ShapeDtypeStruct((2, rows_all, LANES), BF16)]
            + [
                jax.ShapeDtypeStruct(
                    (seq_count, local_len, LANES), BF16 if at < reach - 1 else F32
                )
                for at in range(reach)
            ],
            input_output_aliases=aliases,
            cost_estimate=cost(
                10 * pairs * LANES // micro_count, tile * LANES * 32, pairs // micro_count
            ),
            **back_params,
        )(bounds_now, *operands)
        grad_queries, grad_pieces = back[0], back[1:]
        returned.append(grad_pieces[reach - 1].reshape(tile, LANES))
        for steps_back in range(1, reach):
            piece = passed_along(grad_pieces[reach - 1 - steps_back], "seq", -steps_back)
            returned.append(piece.reshape(tile, LANES))

    partial_hidden, d_query, d_router = pl.pallas_call(
        functools.partial(query_grad_kernel, experts, head),
        grid=(steps,),
        in_specs=[
            row_spec(tile, width),
            row_spec(tile, 2),
            pair_spec(tile),
            row_spec(tile, LANES),
            whole_spec((width, a_cols)),
        ],
        out_specs=[
            row_spec(tile, width),
            whole_spec((width, inner)),
            whole_spec((width, LANES)),
        ],
        out_shape=[
            jax.ShapeDtypeStruct((rows_all, width), F32),
            jax.ShapeDtypeStruct((width, inner), BF16),
            jax.ShapeDtypeStruct((width, LANES), F32),
        ],
        scratch_shapes=[pltpu.VMEM((width, inner), F32), pltpu.VMEM((width, LANES), F32)],
        compiler_params=call_params(),
        cost_estimate=cost(4 * rows_all * width * a_cols, rows_all * width * 12),
        name="query_grad",
    )(hidden, route_rows, grad_queries, grad_logits, group_a)

    while stage < bits:
        halving(stage)
        stage += 1
    own_b = jnp.concatenate(halves, 1)
    own_b = summed_direct(own_b, 0, "dp", 2)
    own_query = small_scattered(d_query)

    grad_in, d_small = pl.pallas_call(
        functools.partial(last_kernel, experts, head, reach, micro_count),
        grid=(steps,),
        in_specs=[
            row_spec(tile, width),
            row_spec(tile, width),
            row_spec(tile, width),
            row_spec(tile, width),
            whole_spec((width, LANES)),
            whole_spec((width, a_cols)),
        ]
        + [whole_spec((tile, LANES))] * (reach * micro_count),
        out_specs=[row_spec(tile, width), whole_spec((width, 2 * LANES))],
        out_shape=[
            jax.ShapeDtypeStruct((rows_all, width), F32),
            jax.ShapeDtypeStruct((width, 2 * LANES), BF16),
        ],
        scratch_shapes=[
            pltpu.VMEM((width, LANES), F32),
            pltpu.VMEM((LANES, width), F32),
            pltpu.VMEM((tile, LANES), BF16),
        ],
        compiler_params=call_params(),
        cost_estimate=cost(4 * rows_all * width * LANES, rows_all * width * 16),
        name="last",
    )(tokens, hidden, partial_hidden, grad_mid, d_router, group_a, *returned)
    own_small = small_scattered(d_small)

    tail = own_b[out_at + own_rows :]
    grad_up = jnp.concatenate(
        [own_b[up_at + at * own_rows : up_at + (at + 1) * own_rows] for at in range(blocks)], 1
    )
    grad_up_bias = jnp.concatenate([tail[:, at * LANES + 8] for at in range(blocks)])
    return (
        block_out.reshape(block_in.shape),
        grad_in.reshape(block_in.shape),
        own_small[:, LANES + experts],
        own_small[:, LANES + experts + 1],
        own_query,
        own_small[:, : 2 * head],
        own_small[:, LANES : LANES + experts],
        own_b[out_at : out_at + own_rows],
        tail[:, 0],
        tail[:, 1],
        grad_up,
        grad_up_bias,
        own_b[:ff_rows],
        tail[:, 2],
    )


def solution(mesh):
    rows = P(("dp", "seq"), None)
    vector = P(("dp", "seq"))
    data = P(None, "dp", "seq", None)
    weights = (
        vector,
        vector,
        rows,
        rows,
        rows,
        rows,
        vector,
        vector,
        rows,
        vector,
        rows,
        vector,
    )
    return jax.shard_map(
        on_device,
        mesh=mesh,
        in_specs=(data, data, P(None, "dp", None), data) + weights,
        out_specs=(data, data) + weights,
        check_vma=False,
    )
```

time: 323 us -> 286 us (0.89); the launches traced: 322 us -> 281 us
  waiting for transfers between devices: 110 us -> 58 us
  starting transfers between devices: 54.3 us -> 79 us
  other arithmetic: 34.7 us -> 12.9 us
  between operations: 1.3 us -> 14.9 us
  local copies, waits for them, and re-layouts: 40.2 us -> 26.8 us
  Pallas kernels: 81.4 us -> 89.1 us
    ppermute x36 -> x29, waiting for transfers between devices: 59.8 us -> 29.5 us  [swapped(): return lax.ppermute(value, axis, [(at, at ^ mask) for at in range(count)])]
    ppermute x6 -> x12, waiting for transfers between devices: 50.7 us -> 28.4 us  [passed_along(): lax.ppermute(value, axis, [(source, source + steps) for source in range(l...]
    ppermute x36 -> x29, starting transfers between devices: 43.1 us -> 60.8 us  [swapped(): return lax.ppermute(value, axis, [(at, at ^ mask) for at in range(count)])]
    gather x12 -> x4, local copies, waits for them, and re-layouts: 18.7 us -> 1.86 us  [gathered(): held = jnp.take(held, order, axis=dim)]
    select_n x12 -> x6, other arithmetic: 15.4 us -> 1.34 us  [gathered(): held = jnp.take(held, order, axis=dim)]
    pallas_call x3 -> x6, Pallas kernels: 66 us -> 74.2 us  [the longest x1 40.6 us: on_device(): pl.pallas_call(functools.partial(mid_kernel, experts, head), grid=(steps,...]
    ppermute x6 -> x12, starting transfers between devices: 11.2 us -> 18.1 us  [passed_along(): lax.ppermute(value, axis, [(source, source + steps) for source in range(l...]
    dynamic_slice x6 -> x2, local copies, waits for them, and re-layouts: 5.82 us -> 0.05 us  [at_index(): return lax.dynamic_index_in_dim(value, index, dim, keepdims=False)]
  transfers between devices with their start and end apart: 42 -> 42, of which waited for: 18 -> 17; matrix products, arithmetic and copies ran while one was open for 15% -> 9% of each run, Pallas kernels for 5% -> 17%
where the time goes in v2:
time: 286 us; the launch traced here: 281 us
  Pallas kernels  89.1 us (31%)
  starting transfers between devices  79 us (28%)
  waiting for transfers between devices  58 us (20%)
  local copies, waits for them, and re-layouts  26.8 us (9%)
  between operations  14.9 us (5%)
  other arithmetic  12.9 us (5%)
    ppermute x29, starting transfers between devices, swapped(): return lax.ppermute(value, axis, [(at, at ^ mask) for at in range(count)])  60.8 us
    pallas_call x1, Pallas kernels, on_device(): pl.pallas_call(functools.partial(mid_kernel, experts, head), grid=(steps,...  40.6 us
    ppermute x29, waiting for transfers between devices, swapped(): return lax.ppermute(value, axis, [(at, at ^ mask) for at in range(count)])  29.5 us
    ppermute x12, waiting for transfers between devices, passed_along(): lax.ppermute(value, axis, [(source, source + steps) for source in range(l...  28.4 us
    ppermute x12, starting transfers between devices, passed_along(): lax.ppermute(value, axis, [(source, source + steps) for source in range(l...  18.1 us
    pallas_call x3, Pallas kernels, on_device(): pl.pallas_call(functools.partial(attend_back_kernel, reach, chunk, head,...  16.8 us
    unnamed x41, local copies, waits for them, and re-layouts  9.5 us
    pallas_call x1, Pallas kernels, on_device(): pl.pallas_call(functools.partial(last_kernel, experts, head, reach, micro...  9.06 us
  transfers between devices with their start and end apart: 42, of which 17 were waited for; matrix products, arithmetic and copies ran while one was open for 9% of the time, Pallas kernels for 17%

profile of v2, /device:TPU:0, one launch (start us, length us, event | category | flops | bytes accessed | tf_op | source)
XLA Modules:
  0.0 280.7 jit_solution(7513724590966093432)
XLA Ops:
  13.2 1.5 concatenate.21
  15.6 4.0 %collective-permute-start.1 = (bf16[16,768]{1,0:T(8,128)(2,1)S(1)}, bf16[16,768]{1,0:T(8,128)(2,1)S(1)}, u32[]{:S(2)}, u32[]{:S(2)}) collective-permute-start(bf16[16,768]{1,0:T(8,128)(2,1)S(1)} %get-tuple-element.190), channel_id=1, source_target_pairs={{0,16},{4,20},{8,24},{12,28},{16,0},{20,4},{24,8},{28,12},{1,17},{... | collective-permute-start | bytes 73736 | tf_op jit(solution)/shard_map/ppermute | solution.py:476
  19.6 1.3 collective-permute-start.2
  22.6 1.5 convert_reduce_fusion
  25.1 1.9 copy.77
  27.7 1.6 collective-permute-start.3
  29.2 1.5 collective-permute-start.4
  31.2 1.5 collective-permute-done.3
  32.7 2.1 collective-permute-done.4
  34.9 1.4 collective-permute-done.5
  36.5 1.7 collective-permute-done.6
  41.4 6.0 %pre.1 = (bf16[1536,512]{1,0:T(8,128)(2,1)}, bf16[1536,128]{1,0:T(8,128)(2,1)}, bf16[2,1536,128]{2,1,0:T(8,128)(2,1)}, f32[1536,128]{1,0:T(8,128)}) custom-call(bf16[1536,512]{1,0:T(8,128)(2,1)} %bitcast.148, s32[1536,2]{1,0:T(8,128)} %bitcast.158, bf16[512,768]{1,0:T(8,128)(2,1)} %bitcast_select_fusion.weight_ref), custom_call_target="tpu_custom_call" | custom-call | flops 2013265920 | bytes 6291456 | tf_op jit(solution)/shard_map/pre/pallas_call | solution.py:630
  47.4 2.5 collective-permute-start.7
  50.0 1.3 collective-permute-start.8
  51.3 2.5 collective-permute-start.9
  55.9 4.2 %collective-permute-done.7.rest_0_ = bf16[3,512,128]{2,1,0:T(8,128)(2,1)S(1)} collective-permute-done((bf16[3,512,128]{2,1,0:T(8,128)(2,1)}, bf16[3,512,128]{2,1,0:T(8,128)(2,1)S(1)}, u32[]{:S(2)}, u32[]{:S(2)}) %collective-permute-start.7) | collective-permute-done | bytes 393248 | tf_op jit(solution)/shard_map/ppermute | solution.py:482
  60.1 15.6 %collective-permute-done.8.rest_1_ = bf16[3,512,128]{2,1,0:T(8,128)(2,1)S(1)} collective-permute-done((bf16[3,512,128]{2,1,0:T(8,128)(2,1)}, bf16[3,512,128]{2,1,0:T(8,128)(2,1)S(1)}, u32[]{:S(2)}, u32[]{:S(2)}) %collective-permute-start.8) | collective-permute-done | bytes 393248 | tf_op jit(solution)/shard_map/ppermute | solution.py:482
  76.6 8.9 %attend.1 = (f32[2,1536,128]{2,1,0:T(8,128)}, f32[3,1,1024]{2,1,0:T(1,128)}) custom-call(s32[6]{0:T(128)} %reshape.203.bounds_ref, bf16[2,1536,128]{2,1,0:T(8,128)(2,1)} %get-tuple-element.49.q_ref, s32[3,1,512]{2,1,0:T(1,128)} %max.18.start_ref, bf16[3,512,128]{2,1,0:T(8,128)(2,1)} %copy-done, bf16[3,512,128]{2,1,0:T(8,128)(2,1)} %copy-done.1, ...), custom_call_target="tpu_custom_call" | custom-call | flops 1610612736 | bytes 3145728 | tf_op jit(solution)/shard_map/attend/pallas_call | solution.py:666
  85.6 40.6 %mid.1 = (bf16[1536,512]{1,0:T(8,128)(2,1)}, f32[1536,512]{1,0:T(8,128)}, bf16[2,1536,128]{2,1,0:T(8,128)(2,1)}, f32[1536,128]{1,0:T(8,128)}, bf16[32,160,512]{2,1,0:T(8,128)(2,1)}) custom-call(bf16[1536,512]{1,0:T(8,128)(2,1)} %bitcast.149, bf16[1536,512]{1,0:T(8,128)(2,1)} %bitcast.195, s32[1536,2]{1,0:T(8,128)} %bitcast.159, ...), custom_call_target="tpu_custom_call" | custom-call | flops 21743271936 | bytes 12582912 | tf_op jit(solution)/shard_map/mid/pallas_call | solution.py:691
  126.2 3.5 %dynamic-slice_bitcast_fusion = bf16[4,4,160,512]{3,2,1,0:T(8,128)(2,1)} fusion(bf16[4,2,4,160,512]{4,3,2,1,0:T(8,128)(2,1)} %bitcast.145, s32[]{:T(128)S(6)} %select_n.189), kind=kLoop, calls=%fused_computation.5 | loop fusion | bytes 5242884 | tf_op jit(solution)/shard_map/jit(dynamic_index_in_dim)/squeeze | solution.py:501
  129.7 5.7 %attend_back.3 = (bf16[2,1536,128]{2,1,0:T(8,128)(2,1)}, bf16[1,512,128]{2,1,0:T(8,128)(2,1)}, bf16[1,512,128]{2,1,0:T(8,128)(2,1)}, bf16[1,512,128]{2,1,0:T(8,128)(2,1)}, f32[1,512,128]{2,1,0:T(8,128)}) custom-call(s32[6]{0:T(128)} %reshape.203.bounds_ref, bf16[2,1536,128]{2,1,0:T(8,128)(2,1)} %get-tuple-element.49.q_ref, ...), custom_call_target="tpu_custom_call" | custom-call | flops 1342177280 | bytes 2097152 | tf_op jit(solution)/shard_map/attend_back/pallas_call | solution.py:798
  136.7 1.3 collective-permute-start.12
  138.0 1.3 collective-permute-start.13
  139.3 2.0 bitcast_add_fusion
  141.5 5.5 %attend_back.4 = (bf16[2,1536,128]{2,1,0:T(8,128)(2,1)}, bf16[1,512,128]{2,1,0:T(8,128)(2,1)}, bf16[1,512,128]{2,1,0:T(8,128)(2,1)}, bf16[1,512,128]{2,1,0:T(8,128)(2,1)}, f32[1,512,128]{2,1,0:T(8,128)}) custom-call(s32[6]{0:T(128)} %reshape.203.bounds_ref, bf16[2,1536,128]{2,1,0:T(8,128)(2,1)} %get-tuple-element.49.q_ref, ...), custom_call_target="tpu_custom_call", output_to_operand_aliasing={{0}: (10, {})} | custom-call | flops 1342177280 | bytes 2097152 | tf_op jit(solution)/shard_map/attend_back/pallas_call | solution.py:798
  147.0 5.5 %attend_back.5 = (bf16[2,1536,128]{2,1,0:T(8,128)(2,1)}, bf16[1,512,128]{2,1,0:T(8,128)(2,1)}, bf16[1,512,128]{2,1,0:T(8,128)(2,1)}, bf16[1,512,128]{2,1,0:T(8,128)(2,1)}, f32[1,512,128]{2,1,0:T(8,128)}) custom-call(s32[6]{0:T(128)} %reshape.203.bounds_ref, bf16[2,1536,128]{2,1,0:T(8,128)(2,1)} %get-tuple-element.49.q_ref, ...), custom_call_target="tpu_custom_call", output_to_operand_aliasing={{0}: (10, {})} | custom-call | flops 1342177280 | bytes 2097152 | tf_op jit(solution)/shard_map/attend_back/pallas_call | solution.py:798
  155.3 1.3 collective-permute-start.19
  157.9 5.3 %collective-permute-done.13 = bf16[1,512,128]{2,1,0:T(8,128)(2,1)S(1)} collective-permute-done((bf16[1,512,128]{2,1,0:T(8,128)(2,1)}, bf16[1,512,128]{2,1,0:T(8,128)(2,1)S(1)}, u32[]{:S(2)}, u32[]{:S(2)}) %collective-permute-start.13) | collective-permute-done | bytes 131104 | tf_op jit(solution)/shard_map/ppermute | solution.py:482
  164.5 2.0 collective-permute-done.17
  166.5 1.5 collective-permute-start.16
  168.0 7.7 %query_grad.1 = (f32[1536,512]{1,0:T(8,128)}, bf16[512,512]{1,0:T(8,128)(2,1)}, f32[512,128]{1,0:T(8,128)}) custom-call(bf16[1536,512]{1,0:T(8,128)(2,1)} %get-tuple-element.53.hidden_ref, s32[1536,2]{1,0:T(8,128)} %bitcast.160, bf16[2,1536,128]{2,1,0:T(8,128)(2,1)} %get-tuple-element.60.grad_q_ref, f32[1536,128]{1,0:T(8,128)} %get-tuple-element.61.grad_logit_ref, ...), custom_call_target="tpu_custom_call" | custom-call | flops 2415919104 | bytes 9437184 | tf_op jit(solution)/shard_map/query_grad/pallas_call | solution.py:831
  177.0 19.8 %collective-permute-start.36 = (bf16[4,2,80,512]{3,2,1,0:T(8,128)(2,1)S(1)}, bf16[4,2,80,512]{3,2,1,0:T(8,128)(2,1)}, u32[]{:S(2)}, u32[]{:S(2)}) collective-permute-start(bf16[4,2,80,512]{3,2,1,0:T(8,128)(2,1)S(1)} %dynamic-slice_bitcast_fusion.1), channel_id=1, source_target_pairs={{0,2},{1,3},{2,0},{3,1},{4,6},{5,7},{6,4},{7,5},{8,10},{9,11},{10,... | collective-permute-start | bytes 1966088 | tf_op jit(solution)/shard_map/ppermute | solution.py:476
  197.6 9.1 %last.1 = (f32[1536,512]{1,0:T(8,128)}, bf16[512,256]{1,0:T(8,128)(2,1)}) custom-call(bf16[1536,512]{1,0:T(8,128)(2,1)} %bitcast.150, bf16[1536,512]{1,0:T(8,128)(2,1)} %get-tuple-element.53.hidden_ref, f32[1536,512]{1,0:T(8,128)} %get-tuple-element.62.partial_ref, f32[1536,512]{1,0:T(8,128)} %get-tuple-element.63.grad_mid_ref, ...), custom_call_target="tpu_custom_call" | custom-call | flops 402653184 | bytes 12582912 | tf_op jit(solution)/shard_map/last/pallas_call | solution.py:864
  208.6 1.9 collective-permute-start.34
  212.2 2.1 collective-permute-start.23
  214.3 12.7 %collective-permute-done.21 = bf16[4,16,256]{2,1,0:T(8,128)(2,1)S(1)} collective-permute-done((bf16[4,16,256]{2,1,0:T(8,128)(2,1)S(1)}, bf16[4,16,256]{2,1,0:T(8,128)(2,1)S(1)}, u32[]{:S(2)}, u32[]{:S(2)}) %collective-permute-start.21) | collective-permute-done | bytes 32800 | tf_op jit(solution)/shard_map/ppermute | solution.py:476
  227.1 2.8 %collective-permute-start.24 = (bf16[16,256]{1,0:T(8,128)(2,1)S(1)}, bf16[16,256]{1,0:T(8,128)(2,1)S(1)}, u32[]{:S(2)}, u32[]{:S(2)}) collective-permute-start(bf16[16,256]{1,0:T(8,128)(2,1)S(1)} %get-tuple-element.186), channel_id=1, source_target_pairs={{0,8},{4,12},{8,0},{12,4},{16,24},{20,28},{24,16},{28,20},{1,9},{5... | collective-permute-start | bytes 24584 | tf_op jit(solution)/shard_map/ppermute | solution.py:476
  229.9 5.1 %collective-permute-start.25 = (bf16[16,256]{1,0:T(8,128)(2,1)S(1)}, bf16[16,256]{1,0:T(8,128)(2,1)S(1)}, u32[]{:S(2)}, u32[]{:S(2)}) collective-permute-start(bf16[16,256]{1,0:T(8,128)(2,1)S(1)} %get-tuple-element.188), channel_id=1, source_target_pairs={{0,16},{4,20},{8,24},{12,28},{16,0},{20,4},{24,8},{28,12},{1,17},{... | collective-permute-start | bytes 24584 | tf_op jit(solution)/shard_map/ppermute | solution.py:476
  235.7 1.9 collective-permute-start.28
  237.6 1.8 collective-permute-start.29
  240.4 3.1 %collective-permute-start.30 = (bf16[4,16,512]{2,1,0:T(8,128)(2,1)}, bf16[4,16,512]{2,1,0:T(8,128)(2,1)}, u32[]{:S(2)}, u32[]{:S(2)}) collective-permute-start(bf16[4,16,512]{2,1,0:T(8,128)(2,1)} %get-tuple-element.176), channel_id=1, source_target_pairs={{0,3},{1,2},{2,1},{3,0},{4,7},{5,6},{6,5},{7,4},{8,11},{9,10},{10,... | collective-permute-start | bytes 196616 | tf_op jit(solution)/shard_map/ppermute | solution.py:476
  248.3 1.7 collective-permute-start.37
  251.2 1.9 collective-permute-start.35
  253.8 3.8 %collective-permute-start.33 = (bf16[16,512]{1,0:T(8,128)(2,1)S(1)}, bf16[16,512]{1,0:T(8,128)(2,1)S(1)}, u32[]{:S(2)}, u32[]{:S(2)}) collective-permute-start(bf16[16,512]{1,0:T(8,128)(2,1)S(1)} %get-tuple-element.184), channel_id=1, source_target_pairs={{0,24},{4,28},{8,16},{12,20},{16,8},{20,12},{24,0},{28,4},{1,25},{... | collective-permute-start | bytes 49160 | tf_op jit(solution)/shard_map/ppermute | solution.py:476
  258.5 1.7 collective-permute-start.39
  260.2 2.7 collective-permute-start.40
  263.6 2.5 collective-permute-done.38
  266.0 4.2 %collective-permute-done.39 = bf16[160,512]{1,0:T(8,128)(2,1)S(1)} collective-permute-done((bf16[160,512]{1,0:T(8,128)(2,1)S(1)}, bf16[160,512]{1,0:T(8,128)(2,1)S(1)}, u32[]{:S(2)}, u32[]{:S(2)}) %collective-permute-start.39) | collective-permute-done | bytes 163872 | tf_op jit(solution)/shard_map/ppermute | solution.py:476
  (156 shorter events, 42.6 us)
Async XLA Ops:
  7.2 78.4 %all-gather.3.cloned.1.call-start = ((), (), s32[]{:S(2)}) async-start(), calls=%async_computation | async-start | bytes 4866048 | tf_op jit(solution)/shard_map/all_gather | solution.py:588
  15.6 12.1 %collective-permute-start.1 = (bf16[16,768]{1,0:T(8,128)(2,1)S(1)}, bf16[16,768]{1,0:T(8,128)(2,1)S(1)}, u32[]{:S(2)}, u32[]{:S(2)}) collective-permute-start(bf16[16,768]{1,0:T(8,128)(2,1)S(1)} %get-tuple-element.190), channel_id=1, source_target_pairs={{0,16},{4,20},{8,24},{12,28},{16,0},{20,4},{24,8},{28,12},{1,17},{... | collective-permute-start | bytes 73736 | tf_op jit(solution)/shard_map/ppermute | solution.py:476
  19.6 8.0 %collective-permute-start.2 = (bf16[16,768]{1,0:T(8,128)(2,1)S(1)}, bf16[16,768]{1,0:T(8,128)(2,1)S(1)}, u32[]{:S(2)}, u32[]{:S(2)}) collective-permute-start(bf16[16,768]{1,0:T(8,128)(2,1)S(1)} %get-tuple-element.190), channel_id=1, source_target_pairs={{0,24},{4,28},{8,16},{12,20},{16,8},{20,12},{24,0},{28,4},{1,25},{... | collective-permute-start | bytes 73736 | tf_op jit(solution)/shard_map/ppermute | solution.py:476
  20.9 6.7 %collective-permute-start = (bf16[16,768]{1,0:T(8,128)(2,1)S(1)}, bf16[16,768]{1,0:T(8,128)(2,1)S(1)}, u32[]{:S(2)}, u32[]{:S(2)}) collective-permute-start(bf16[16,768]{1,0:T(8,128)(2,1)S(1)} %get-tuple-element.190), channel_id=1, source_target_pairs={{0,8},{4,12},{8,0},{12,4},{16,24},{20,28},{24,16},{28,20},{1,9},{5... | collective-permute-start | bytes 73736 | tf_op jit(solution)/shard_map/ppermute | solution.py:476
  27.7 5.1 %collective-permute-start.3 = (bf16[4,16,768]{2,1,0:T(8,128)(2,1)S(1)}, bf16[4,16,768]{2,1,0:T(8,128)(2,1)S(1)}, u32[]{:S(2)}, u32[]{:S(2)}) collective-permute-start(bf16[4,16,768]{2,1,0:T(8,128)(2,1)S(1)} %get-tuple-element.182), channel_id=1, source_target_pairs={{0,1},{1,0},{2,3},{3,2},{4,5},{5,4},{6,7},{7,6},{8,9},{9,8},{10,11... | collective-permute-start | bytes 294920 | tf_op jit(solution)/shard_map/ppermute | solution.py:476
  29.2 5.7 %collective-permute-start.4 = (bf16[4,16,768]{2,1,0:T(8,128)(2,1)S(1)}, bf16[4,16,768]{2,1,0:T(8,128)(2,1)S(1)}, u32[]{:S(2)}, u32[]{:S(2)}) collective-permute-start(bf16[4,16,768]{2,1,0:T(8,128)(2,1)S(1)} %get-tuple-element.182), channel_id=1, source_target_pairs={{0,2},{1,3},{2,0},{3,1},{4,6},{5,7},{6,4},{7,5},{8,10},{9,11},{10,... | collective-permute-start | bytes 294920 | tf_op jit(solution)/shard_map/ppermute | solution.py:476
  30.7 5.5 %collective-permute-start.5 = (bf16[4,16,768]{2,1,0:T(8,128)(2,1)S(1)}, bf16[4,16,768]{2,1,0:T(8,128)(2,1)S(1)}, u32[]{:S(2)}, u32[]{:S(2)}) collective-permute-start(bf16[4,16,768]{2,1,0:T(8,128)(2,1)S(1)} %get-tuple-element.182), channel_id=1, source_target_pairs={{0,3},{1,2},{2,1},{3,0},{4,7},{5,6},{6,5},{7,4},{8,11},{9,10},{10,... | collective-permute-start | bytes 294920 | tf_op jit(solution)/shard_map/ppermute | solution.py:476
  36.3 1.8 collective-permute-start.6
  47.4 12.7 %collective-permute-start.7 = (bf16[3,512,128]{2,1,0:T(8,128)(2,1)}, bf16[3,512,128]{2,1,0:T(8,128)(2,1)S(1)}, u32[]{:S(2)}, u32[]{:S(2)}) collective-permute-start(bf16[3,512,128]{2,1,0:T(8,128)(2,1)} %bitcast.151), channel_id=1, source_target_pairs={{0,3},{4,7},{8,11},{12,15},{16,19},{20,23},{24,27},{28,31}} | collective-permute-start | bytes 1179656 | tf_op jit(solution)/shard_map/ppermute | solution.py:482
  50.0 25.8 %collective-permute-start.8 = (bf16[3,512,128]{2,1,0:T(8,128)(2,1)}, bf16[3,512,128]{2,1,0:T(8,128)(2,1)S(1)}, u32[]{:S(2)}, u32[]{:S(2)}) collective-permute-start(bf16[3,512,128]{2,1,0:T(8,128)(2,1)} %bitcast.152), channel_id=1, source_target_pairs={{0,2},{1,3},{4,6},{5,7},{8,10},{9,11},{12,14},{13,15},{16,18},{17,... | collective-permute-start | bytes 1179656 | tf_op jit(solution)/shard_map/ppermute | solution.py:482
  51.3 24.5 %collective-permute-start.9 = (bf16[3,512,128]{2,1,0:T(8,128)(2,1)}, bf16[3,512,128]{2,1,0:T(8,128)(2,1)S(1)}, u32[]{:S(2)}, u32[]{:S(2)}) collective-permute-start(bf16[3,512,128]{2,1,0:T(8,128)(2,1)} %bitcast.153), channel_id=1, source_target_pairs={{0,1},{1,2},{2,3},{4,5},{5,6},{6,7},{8,9},{9,10},{10,11},{12,13},{... | collective-permute-start | bytes 1179656 | tf_op jit(solution)/shard_map/ppermute | solution.py:482
  60.1 15.7 %copy-start = (bf16[3,512,128]{2,1,0:T(8,128)(2,1)}, bf16[3,512,128]{2,1,0:T(8,128)(2,1)S(1)}, u32[]{:S(2)}) copy-start(bf16[3,512,128]{2,1,0:T(8,128)(2,1)S(1)} %collective-permute-done.7.rest_0_) | copy-start | bytes 1179652
  129.7 9.6 %collective-permute-start.10 = (bf16[4,4,160,512]{3,2,1,0:T(8,128)(2,1)}, bf16[4,4,160,512]{3,2,1,0:T(8,128)(2,1)S(1)}, u32[]{:S(2)}, u32[]{:S(2)}) collective-permute-start(bf16[4,4,160,512]{3,2,1,0:T(8,128)(2,1)} %dynamic-slice_bitcast_fusion), channel_id=1, source_target_pairs={{0,4},{4,0},{8,12},{12,8},{16,20},{20,16},{24,28},{28,24},{1,5},{5... | collective-permute-start | bytes 7864328 | tf_op jit(solution)/shard_map/ppermute | solution.py:476
  135.4 19.9 %collective-permute-start.11 = (bf16[1,512,128]{2,1,0:T(8,128)(2,1)}, bf16[1,512,128]{2,1,0:T(8,128)(2,1)S(1)}, u32[]{:S(2)}, u32[]{:S(2)}) collective-permute-start(bf16[1,512,128]{2,1,0:T(8,128)(2,1)} %get-tuple-element.66), channel_id=1, source_target_pairs={{1,0},{2,1},{3,2},{5,4},{6,5},{7,6},{9,8},{10,9},{11,10},{13,12},{... | collective-permute-start | bytes 393224 | tf_op jit(solution)/shard_map/ppermute | solution.py:482
  136.7 19.9 %collective-permute-start.12 = (bf16[1,512,128]{2,1,0:T(8,128)(2,1)}, bf16[1,512,128]{2,1,0:T(8,128)(2,1)S(1)}, u32[]{:S(2)}, u32[]{:S(2)}) collective-permute-start(bf16[1,512,128]{2,1,0:T(8,128)(2,1)} %get-tuple-element.67), channel_id=1, source_target_pairs={{2,0},{3,1},{6,4},{7,5},{10,8},{11,9},{14,12},{15,13},{18,16},{19,... | collective-permute-start | bytes 393224 | tf_op jit(solution)/shard_map/ppermute | solution.py:482
  138.0 25.2 %collective-permute-start.13 = (bf16[1,512,128]{2,1,0:T(8,128)(2,1)}, bf16[1,512,128]{2,1,0:T(8,128)(2,1)S(1)}, u32[]{:S(2)}, u32[]{:S(2)}) collective-permute-start(bf16[1,512,128]{2,1,0:T(8,128)(2,1)} %get-tuple-element.68), channel_id=1, source_target_pairs={{3,0},{7,4},{11,8},{15,12},{19,16},{23,20},{27,24},{31,28}} | collective-permute-start | bytes 393224 | tf_op jit(solution)/shard_map/ppermute | solution.py:482
  152.6 13.9 %collective-permute-start.17 = (bf16[1,512,128]{2,1,0:T(8,128)(2,1)}, bf16[1,512,128]{2,1,0:T(8,128)(2,1)S(1)}, u32[]{:S(2)}, u32[]{:S(2)}) collective-permute-start(bf16[1,512,128]{2,1,0:T(8,128)(2,1)} %get-tuple-element.74), channel_id=1, source_target_pairs={{1,0},{2,1},{3,2},{5,4},{6,5},{7,6},{9,8},{10,9},{11,10},{13,12},{... | collective-permute-start | bytes 393224 | tf_op jit(solution)/shard_map/ppermute | solution.py:482
  154.0 23.0 %collective-permute-start.18 = (bf16[1,512,128]{2,1,0:T(8,128)(2,1)}, bf16[1,512,128]{2,1,0:T(8,128)(2,1)S(1)}, u32[]{:S(2)}, u32[]{:S(2)}) collective-permute-start(bf16[1,512,128]{2,1,0:T(8,128)(2,1)} %get-tuple-element.75), channel_id=1, source_target_pairs={{2,0},{3,1},{6,4},{7,5},{10,8},{11,9},{14,12},{15,13},{18,16},{19,... | collective-permute-start | bytes 393224 | tf_op jit(solution)/shard_map/ppermute | solution.py:482
  155.3 20.4 %copy-start.6 = (bf16[1,512,128]{2,1,0:T(8,128)(2,1)}, bf16[1,512,128]{2,1,0:T(8,128)(2,1)S(1)}, u32[]{:S(2)}) copy-start(bf16[1,512,128]{2,1,0:T(8,128)(2,1)S(1)} %collective-permute-done.11) | copy-start | bytes 393220
  155.3 41.5 %collective-permute-start.19 = (bf16[1,512,128]{2,1,0:T(8,128)(2,1)}, bf16[1,512,128]{2,1,0:T(8,128)(2,1)S(1)}, u32[]{:S(2)}, u32[]{:S(2)}) collective-permute-start(bf16[1,512,128]{2,1,0:T(8,128)(2,1)} %get-tuple-element.76), channel_id=1, source_target_pairs={{3,0},{7,4},{11,8},{15,12},{19,16},{23,20},{27,24},{31,28}} | collective-permute-start | bytes 393224 | tf_op jit(solution)/shard_map/ppermute | solution.py:482
  156.6 19.1 %copy-start.7 = (bf16[1,512,128]{2,1,0:T(8,128)(2,1)}, bf16[1,512,128]{2,1,0:T(8,128)(2,1)S(1)}, u32[]{:S(2)}) copy-start(bf16[1,512,128]{2,1,0:T(8,128)(2,1)S(1)} %collective-permute-done.12) | copy-start | bytes 393220
  156.6 40.2 %collective-permute-start.14 = (bf16[1,512,128]{2,1,0:T(8,128)(2,1)}, bf16[1,512,128]{2,1,0:T(8,128)(2,1)S(1)}, u32[]{:S(2)}, u32[]{:S(2)}) collective-permute-start(bf16[1,512,128]{2,1,0:T(8,128)(2,1)} %get-tuple-element.70), channel_id=1, source_target_pairs={{1,0},{2,1},{3,2},{5,4},{6,5},{7,6},{9,8},{10,9},{11,10},{13,12},{... | collective-permute-start | bytes 393224 | tf_op jit(solution)/shard_map/ppermute | solution.py:482
  163.2 4.8 %copy-start.8 = (bf16[1,512,128]{2,1,0:T(8,128)(2,1)}, bf16[1,512,128]{2,1,0:T(8,128)(2,1)S(1)}, u32[]{:S(2)}) copy-start(bf16[1,512,128]{2,1,0:T(8,128)(2,1)S(1)} %collective-permute-done.13) | copy-start | bytes 393220
  163.2 33.6 %collective-permute-start.15 = (bf16[1,512,128]{2,1,0:T(8,128)(2,1)}, bf16[1,512,128]{2,1,0:T(8,128)(2,1)S(1)}, u32[]{:S(2)}, u32[]{:S(2)}) collective-permute-start(bf16[1,512,128]{2,1,0:T(8,128)(2,1)} %get-tuple-element.71), channel_id=1, source_target_pairs={{2,0},{3,1},{6,4},{7,5},{10,8},{11,9},{14,12},{15,13},{18,16},{19,... | collective-permute-start | bytes 393224 | tf_op jit(solution)/shard_map/ppermute | solution.py:482
  166.5 30.3 %collective-permute-start.16 = (bf16[1,512,128]{2,1,0:T(8,128)(2,1)}, bf16[1,512,128]{2,1,0:T(8,128)(2,1)S(1)}, u32[]{:S(2)}, u32[]{:S(2)}) collective-permute-start(bf16[1,512,128]{2,1,0:T(8,128)(2,1)} %get-tuple-element.72), channel_id=1, source_target_pairs={{3,0},{7,4},{11,8},{15,12},{19,16},{23,20},{27,24},{31,28}} | collective-permute-start | bytes 393224 | tf_op jit(solution)/shard_map/ppermute | solution.py:482
  177.0 19.9 %copy-start.10 = (bf16[1,512,128]{2,1,0:T(8,128)(2,1)}, bf16[1,512,128]{2,1,0:T(8,128)(2,1)S(1)}, u32[]{:S(2)}) copy-start(bf16[1,512,128]{2,1,0:T(8,128)(2,1)S(1)} %collective-permute-done.18) | copy-start | bytes 393220
  177.0 70.1 %collective-permute-start.36 = (bf16[4,2,80,512]{3,2,1,0:T(8,128)(2,1)S(1)}, bf16[4,2,80,512]{3,2,1,0:T(8,128)(2,1)}, u32[]{:S(2)}, u32[]{:S(2)}) collective-permute-start(bf16[4,2,80,512]{3,2,1,0:T(8,128)(2,1)S(1)} %dynamic-slice_bitcast_fusion.1), channel_id=1, source_target_pairs={{0,2},{1,3},{2,0},{3,1},{4,6},{5,7},{6,4},{7,5},{8,10},{9,11},{10,... | collective-permute-start | bytes 1966088 | tf_op jit(solution)/shard_map/ppermute | solution.py:476
  197.6 12.9 %copy-start.3 = (bf16[512,512]{1,0:T(8,128)(2,1)S(1)}, bf16[512,512]{1,0:T(8,128)(2,1)}, u32[]{:S(2)}) copy-start(bf16[512,512]{1,0:T(8,128)(2,1)} %get-tuple-element.79) | copy-start | bytes 1572868
  207.6 3.0 %collective-permute-start.20 = (bf16[4,4,16,256]{3,2,1,0:T(8,128)(2,1)S(1)}, bf16[4,4,16,256]{3,2,1,0:T(8,128)(2,1)S(1)}, u32[]{:S(2)}, u32[]{:S(2)}) collective-permute-start(bf16[4,4,16,256]{3,2,1,0:T(8,128)(2,1)S(1)} %dynamic-slice_bitcast_fusion.5), channel_id=1, source_target_pairs={{0,4},{4,0},{8,12},{12,8},{16,20},{20,16},{24,28},{28,24},{1,5},{5... | collective-permute-start | bytes 393224 | tf_op jit(solution)/shard_map/ppermute | solution.py:476
  208.6 41.4 %collective-permute-start.34 = (bf16[4,2,80,512]{3,2,1,0:T(8,128)(2,1)}, bf16[4,2,80,512]{3,2,1,0:T(8,128)(2,1)}, u32[]{:S(2)}, u32[]{:S(2)}) collective-permute-start(bf16[4,2,80,512]{3,2,1,0:T(8,128)(2,1)} %dynamic-slice_bitcast_fusion.2), channel_id=1, source_target_pairs={{0,1},{1,0},{2,3},{3,2},{4,5},{5,4},{6,7},{7,6},{8,9},{9,8},{10,11... | collective-permute-start | bytes 1966088 | tf_op jit(solution)/shard_map/ppermute | solution.py:476
  210.6 1.6 collective-permute-start.27
  210.7 16.3 %collective-permute-start.21 = (bf16[4,16,256]{2,1,0:T(8,128)(2,1)S(1)}, bf16[4,16,256]{2,1,0:T(8,128)(2,1)S(1)}, u32[]{:S(2)}, u32[]{:S(2)}) collective-permute-start(bf16[4,16,256]{2,1,0:T(8,128)(2,1)S(1)} %get-tuple-element.178), channel_id=1, source_target_pairs={{0,1},{1,0},{2,3},{3,2},{4,5},{5,4},{6,7},{7,6},{8,9},{9,8},{10,11... | collective-permute-start | bytes 98312 | tf_op jit(solution)/shard_map/ppermute | solution.py:476
  211.1 15.9 %collective-permute-start.22 = (bf16[4,16,256]{2,1,0:T(8,128)(2,1)S(1)}, bf16[4,16,256]{2,1,0:T(8,128)(2,1)S(1)}, u32[]{:S(2)}, u32[]{:S(2)}) collective-permute-start(bf16[4,16,256]{2,1,0:T(8,128)(2,1)S(1)} %get-tuple-element.180), channel_id=1, source_target_pairs={{0,2},{1,3},{2,0},{3,1},{4,6},{5,7},{6,4},{7,5},{8,10},{9,11},{10,... | collective-permute-start | bytes 98312 | tf_op jit(solution)/shard_map/ppermute | solution.py:476
  212.2 14.8 %collective-permute-start.23 = (bf16[4,16,256]{2,1,0:T(8,128)(2,1)S(1)}, bf16[4,16,256]{2,1,0:T(8,128)(2,1)S(1)}, u32[]{:S(2)}, u32[]{:S(2)}) collective-permute-start(bf16[4,16,256]{2,1,0:T(8,128)(2,1)S(1)} %get-tuple-element.179), channel_id=1, source_target_pairs={{0,3},{1,2},{2,1},{3,0},{4,7},{5,6},{6,5},{7,4},{8,11},{9,10},{10,... | collective-permute-start | bytes 98312 | tf_op jit(solution)/shard_map/ppermute | solution.py:476
  227.1 8.6 %collective-permute-start.24 = (bf16[16,256]{1,0:T(8,128)(2,1)S(1)}, bf16[16,256]{1,0:T(8,128)(2,1)S(1)}, u32[]{:S(2)}, u32[]{:S(2)}) collective-permute-start(bf16[16,256]{1,0:T(8,128)(2,1)S(1)} %get-tuple-element.186), channel_id=1, source_target_pairs={{0,8},{4,12},{8,0},{12,4},{16,24},{20,28},{24,16},{28,20},{1,9},{5... | collective-permute-start | bytes 24584 | tf_op jit(solution)/shard_map/ppermute | solution.py:476
  229.9 7.7 %collective-permute-start.25 = (bf16[16,256]{1,0:T(8,128)(2,1)S(1)}, bf16[16,256]{1,0:T(8,128)(2,1)S(1)}, u32[]{:S(2)}, u32[]{:S(2)}) collective-permute-start(bf16[16,256]{1,0:T(8,128)(2,1)S(1)} %get-tuple-element.188), channel_id=1, source_target_pairs={{0,16},{4,20},{8,24},{12,28},{16,0},{20,4},{24,8},{28,12},{1,17},{... | collective-permute-start | bytes 24584 | tf_op jit(solution)/shard_map/ppermute | solution.py:476
  235.0 5.4 %collective-permute-start.26 = (bf16[16,256]{1,0:T(8,128)(2,1)S(1)}, bf16[16,256]{1,0:T(8,128)(2,1)S(1)}, u32[]{:S(2)}, u32[]{:S(2)}) collective-permute-start(bf16[16,256]{1,0:T(8,128)(2,1)S(1)} %get-tuple-element.187), channel_id=1, source_target_pairs={{0,24},{4,28},{8,16},{12,20},{16,8},{20,12},{24,0},{28,4},{1,25},{... | collective-permute-start | bytes 24584 | tf_op jit(solution)/shard_map/ppermute | solution.py:476
  235.7 9.9 %collective-permute-start.28 = (bf16[4,16,512]{2,1,0:T(8,128)(2,1)}, bf16[4,16,512]{2,1,0:T(8,128)(2,1)}, u32[]{:S(2)}, u32[]{:S(2)}) collective-permute-start(bf16[4,16,512]{2,1,0:T(8,128)(2,1)} %get-tuple-element.175), channel_id=1, source_target_pairs={{0,1},{1,0},{2,3},{3,2},{4,5},{5,4},{6,7},{7,6},{8,9},{9,8},{10,11... | collective-permute-start | bytes 196616 | tf_op jit(solution)/shard_map/ppermute | solution.py:476
  237.6 8.0 %collective-permute-start.29 = (bf16[4,16,512]{2,1,0:T(8,128)(2,1)}, bf16[4,16,512]{2,1,0:T(8,128)(2,1)}, u32[]{:S(2)}, u32[]{:S(2)}) collective-permute-start(bf16[4,16,512]{2,1,0:T(8,128)(2,1)} %get-tuple-element.177), channel_id=1, source_target_pairs={{0,2},{1,3},{2,0},{3,1},{4,6},{5,7},{6,4},{7,5},{8,10},{9,11},{10,... | collective-permute-start | bytes 196616 | tf_op jit(solution)/shard_map/ppermute | solution.py:476
  240.4 5.7 %collective-permute-start.30 = (bf16[4,16,512]{2,1,0:T(8,128)(2,1)}, bf16[4,16,512]{2,1,0:T(8,128)(2,1)}, u32[]{:S(2)}, u32[]{:S(2)}) collective-permute-start(bf16[4,16,512]{2,1,0:T(8,128)(2,1)} %get-tuple-element.176), channel_id=1, source_target_pairs={{0,3},{1,2},{2,1},{3,0},{4,7},{5,6},{6,5},{7,4},{8,11},{9,10},{10,... | collective-permute-start | bytes 196616 | tf_op jit(solution)/shard_map/ppermute | solution.py:476
  248.3 9.2 %collective-permute-start.37 = (bf16[4,80,512]{2,1,0:T(8,128)(2,1)S(1)}, bf16[4,80,512]{2,1,0:T(8,128)(2,1)S(1)}, u32[]{:S(2)}, u32[]{:S(2)}) collective-permute-start(bf16[4,80,512]{2,1,0:T(8,128)(2,1)S(1)} %dynamic-slice_bitcast_fusion.3), channel_id=1, source_target_pairs={{0,1},{1,0},{2,3},{3,2},{4,5},{5,4},{6,7},{7,6},{8,9},{9,8},{10,11... | collective-permute-start | bytes 983048 | tf_op jit(solution)/shard_map/ppermute | solution.py:476
  251.2 7.1 %collective-permute-start.35 = (bf16[4,80,512]{2,1,0:T(8,128)(2,1)S(1)}, bf16[4,80,512]{2,1,0:T(8,128)(2,1)S(1)}, u32[]{:S(2)}, u32[]{:S(2)}) collective-permute-start(bf16[4,80,512]{2,1,0:T(8,128)(2,1)S(1)} %dynamic-slice_bitcast_fusion.4), channel_id=1, source_target_pairs={{0,2},{1,3},{2,0},{3,1},{4,6},{5,7},{6,4},{7,5},{8,10},{9,11},{10,... | collective-permute-start | bytes 983048 | tf_op jit(solution)/shard_map/ppermute | solution.py:476
  253.1 7.1 %collective-permute-start.31 = (bf16[16,512]{1,0:T(8,128)(2,1)S(1)}, bf16[16,512]{1,0:T(8,128)(2,1)S(1)}, u32[]{:S(2)}, u32[]{:S(2)}) collective-permute-start(bf16[16,512]{1,0:T(8,128)(2,1)S(1)} %get-tuple-element.183), channel_id=1, source_target_pairs={{0,8},{4,12},{8,0},{12,4},{16,24},{20,28},{24,16},{28,20},{1,9},{5... | collective-permute-start | bytes 49160 | tf_op jit(solution)/shard_map/ppermute | solution.py:476
  253.1 9.8 %collective-permute-start.32 = (bf16[16,512]{1,0:T(8,128)(2,1)S(1)}, bf16[16,512]{1,0:T(8,128)(2,1)S(1)}, u32[]{:S(2)}, u32[]{:S(2)}) collective-permute-start(bf16[16,512]{1,0:T(8,128)(2,1)S(1)} %get-tuple-element.185), channel_id=1, source_target_pairs={{0,16},{4,20},{8,24},{12,28},{16,0},{20,4},{24,8},{28,12},{1,17},{... | collective-permute-start | bytes 49160 | tf_op jit(solution)/shard_map/ppermute | solution.py:476
  253.8 9.2 %collective-permute-start.33 = (bf16[16,512]{1,0:T(8,128)(2,1)S(1)}, bf16[16,512]{1,0:T(8,128)(2,1)S(1)}, u32[]{:S(2)}, u32[]{:S(2)}) collective-permute-start(bf16[16,512]{1,0:T(8,128)(2,1)S(1)} %get-tuple-element.184), channel_id=1, source_target_pairs={{0,24},{4,28},{8,16},{12,20},{16,8},{20,12},{24,0},{28,4},{1,25},{... | collective-permute-start | bytes 49160 | tf_op jit(solution)/shard_map/ppermute | solution.py:476
  258.5 7.6 %collective-permute-start.38 = (bf16[160,512]{1,0:T(8,128)(2,1)S(1)}, bf16[160,512]{1,0:T(8,128)(2,1)S(1)}, u32[]{:S(2)}, u32[]{:S(2)}) collective-permute-start(bf16[160,512]{1,0:T(8,128)(2,1)S(1)} %get-tuple-element.163), channel_id=1, source_target_pairs={{0,8},{4,12},{8,0},{12,4},{16,24},{20,28},{24,16},{28,20},{1,9},{5... | collective-permute-start | bytes 491528 | tf_op jit(solution)/shard_map/ppermute | solution.py:476
  258.5 11.7 %collective-permute-start.39 = (bf16[160,512]{1,0:T(8,128)(2,1)S(1)}, bf16[160,512]{1,0:T(8,128)(2,1)S(1)}, u32[]{:S(2)}, u32[]{:S(2)}) collective-permute-start(bf16[160,512]{1,0:T(8,128)(2,1)S(1)} %get-tuple-element.164), channel_id=1, source_target_pairs={{0,16},{4,20},{8,24},{12,28},{16,0},{20,4},{24,8},{28,12},{1,17},{... | collective-permute-start | bytes 491528 | tf_op jit(solution)/shard_map/ppermute | solution.py:476
  260.2 10.0 %collective-permute-start.40 = (bf16[160,512]{1,0:T(8,128)(2,1)S(1)}, bf16[160,512]{1,0:T(8,128)(2,1)S(1)}, u32[]{:S(2)}, u32[]{:S(2)}) collective-permute-start(bf16[160,512]{1,0:T(8,128)(2,1)S(1)} %get-tuple-element.165), channel_id=1, source_target_pairs={{0,24},{4,28},{8,16},{12,20},{16,8},{20,12},{24,0},{28,4},{1,25},{... | collective-permute-start | bytes 491528 | tf_op jit(solution)/shard_map/ppermute | solution.py:476
  (9 other events, 10.6 us)
Sparse Core Ops, SparseCore 0:
  12.5 69.3 all-gather.2

commit v3 on v2

v3 whole, which is shorter than its diff:
```python
import functools

import jax
import jax.numpy as jnp
from jax import lax
from jax.experimental import pallas as pl
from jax.experimental.pallas import tpu as pltpu
from jax.sharding import PartitionSpec as P

EPS = 1e-05
LANES = 128
MIB = 1024 * 1024
BF16 = jnp.bfloat16
F32 = jnp.float32


def call_params():
    return pltpu.CompilerParams(vmem_limit_bytes=56 * MIB)


def cost(flops, bytes_accessed, transcendentals=0):
    return pl.CostEstimate(
        flops=int(flops), bytes_accessed=int(bytes_accessed), transcendentals=int(transcendentals)
    )


def dot_nn(left, right):
    return lax.dot_general(left, right, (((1,), (0,)), ((), ())), preferred_element_type=F32)


def dot_nt(left, right):
    return lax.dot_general(left, right, (((1,), (1,)), ((), ())), preferred_element_type=F32)


def lanes_of(rows, width):
    return lax.broadcasted_iota(jnp.int32, (rows, width), 1)


def fold_matrix(width, head, shift):
    source = lax.broadcasted_iota(jnp.int32, (width, LANES), 0)
    target = lax.broadcasted_iota(jnp.int32, (width, LANES), 1)
    return jnp.where(target == shift + lax.rem(source, head), 1.0, 0.0).astype(BF16)


def unfold_matrix(width, head, shift):
    source = lax.broadcasted_iota(jnp.int32, (LANES, width), 1)
    target = lax.broadcasted_iota(jnp.int32, (LANES, width), 0)
    return jnp.where(target == shift + lax.rem(source, head), 1.0, 0.0).astype(BF16)


def rows_of(columns, picked):
    row = lax.broadcasted_iota(jnp.int32, (8, LANES), 0)
    lane = lax.broadcasted_iota(jnp.int32, (8, LANES), 1)
    chosen = jnp.zeros((8, LANES), F32)
    for at, column in enumerate(picked):
        chosen = jnp.where((row == at) & (lane == column), 1.0, chosen)
    return dot_nt(chosen.astype(BF16), columns)


def normalize(values):
    centered = values - jnp.mean(values, -1, keepdims=True)
    inv_dev = lax.rsqrt(jnp.mean(centered * centered, -1, keepdims=True) + EPS)
    return centered * inv_dev, inv_dev


def norm_back(grad, gain, normed, inv_dev):
    scaled = grad * gain
    return inv_dev * (
        scaled
        - jnp.mean(scaled, -1, keepdims=True)
        - normed * jnp.mean(scaled * normed, -1, keepdims=True)
    )


def pack_kernel(query_ref, kv_ref, router_ref, down_ref, up_ref, out_ref, *rest):
    *vector_refs, up_bias_ref, first_ref, second_ref = rest
    own_rows, width = query_ref.shape
    first_ref[:, :width] = query_ref[...]
    first_ref[:, width : width + LANES] = kv_ref[...]
    rows = [router_ref[...].astype(F32)]
    rows += [ref[...].astype(F32).reshape(1, own_rows) for ref in vector_refs]
    bias = up_bias_ref[...].astype(F32).reshape(1, up_bias_ref.shape[0])
    rows += [
        bias[:, at * own_rows : (at + 1) * own_rows] for at in range(bias.shape[1] // own_rows)
    ]
    count = router_ref.shape[0] + len(rows) - 1
    rows.append(jnp.zeros((32 - count, own_rows), F32))
    rows = jnp.concatenate(rows, 0).astype(BF16)
    row = lax.broadcasted_iota(jnp.int32, (32, LANES), 0)
    lane = lax.broadcasted_iota(jnp.int32, (32, LANES), 1)
    chosen = jnp.where(lane == row, 1.0, 0.0).astype(BF16)
    turned = lax.dot_general(rows, chosen, (((0,), (0,)), ((), ())), preferred_element_type=F32)
    first_ref[:, width + LANES :] = turned.astype(BF16)
    ff_rows = down_ref.shape[0]
    second_ref[:ff_rows] = down_ref[...]
    blocks = up_ref.shape[1] // width
    for at in range(blocks):
        low = ff_rows + at * own_rows
        second_ref[low : low + own_rows] = up_ref[:, at * width : (at + 1) * width]
    second_ref[ff_rows + blocks * own_rows :] = out_ref[...]


def in_order(place_ref, parts, put):
    z_me, core_me, seq_me = place_ref[0], place_ref[1], place_ref[2]
    for core, part in enumerate(parts):
        for seq in range(part.shape[0]):
            for z in range(part.shape[1]):
                dp_at = (z_me ^ z) * 2 + (core_me ^ core)
                put(dp_at * part.shape[0] + (seq_me ^ seq), part[seq, z])


def keyval_kernel(experts, head, place_ref, x_ref, mine_ref, mate_ref, *rest):
    hidden_ref, kv_ref, weight_ref, blocks_ref = rest

    @pl.when(pl.program_id(0) == 0)
    def _():
        def put(device, block):
            blocks_ref[device] = block

        in_order(place_ref, (mine_ref, mate_ref), put)
        weight_ref[...] = blocks_ref[...].reshape(weight_ref.shape)

    inner = experts * head
    vectors = rows_of(weight_ref[:, inner + LANES :], (experts, experts + 1))
    normed, _ = normalize(x_ref[...].astype(F32))
    hidden = (normed * vectors[0:1] + vectors[1:2]).astype(BF16)
    hidden_ref[...] = hidden
    kv_ref[...] = dot_nn(hidden, weight_ref[:, inner : inner + LANES]).astype(BF16)


def query_kernel(experts, head, hidden_ref, routes_ref, weight_ref, q_ref, gate_ref):
    inner = experts * head
    hidden = hidden_ref[...]
    rows = hidden.shape[0]
    logits = dot_nn(hidden, weight_ref[:, inner + LANES :])
    lane = lanes_of(rows, LANES)
    first, second = routes_ref[:, 0:1], routes_ref[:, 1:2]
    logit_one = jnp.sum(jnp.where(lane == first, logits, 0.0), -1, keepdims=True)
    logit_two = jnp.sum(jnp.where(lane == second, logits, 0.0), -1, keepdims=True)
    peak = jnp.maximum(logit_one, logit_two)
    exp_one = jnp.exp(logit_one - peak)
    exp_two = jnp.exp(logit_two - peak)
    total = exp_one + exp_two
    gates = jnp.where(lane == 0, exp_one / total, jnp.where(lane == 1, exp_two / total, 0.0))
    gates = jnp.where(lane == 2, first.astype(F32), gates)
    gate_ref[...] = jnp.where(lane == 3, second.astype(F32), gates)
    queries = (dot_nn(hidden, weight_ref[:, :inner]) * (head**-0.5)).astype(BF16)
    owner = lax.div(lanes_of(rows, inner), head)
    fold = fold_matrix(inner, head, 0)
    zero = jnp.zeros_like(queries)
    q_ref[0] = dot_nn(jnp.where(owner == first, queries, zero), fold).astype(BF16)
    q_ref[1] = dot_nn(jnp.where(owner == second, queries, zero), fold).astype(BF16)


def masked(scores, start, key_at, query_at=None):
    keys = key_at + lax.broadcasted_iota(jnp.int32, scores.shape, 0)
    seen = keys >= start
    if query_at is not None:
        lane = lax.broadcasted_iota(jnp.int32, (1, scores.shape[1]), 1)
        seen = seen & (keys <= query_at + lax.rem(lane, scores.shape[1] // 2))
    return jnp.where(seen, scores, -1e30)


def by_halves(ref):
    half = ref.shape[1] // 2
    return [
        jnp.concatenate([ref[0, at * half : (at + 1) * half], ref[1, at * half : (at + 1) * half]], 0)
        for at in range(2)
    ]


def from_halves(ref, groups):
    half = ref.shape[1] // 2
    for at, group in enumerate(groups):
        ref[0, at * half : (at + 1) * half] = group[:half]
        ref[1, at * half : (at + 1) * half] = group[half:]


def row_halves(row):
    half = row.shape[1] // 2
    return [
        jnp.concatenate([row[:, at * half : (at + 1) * half]] * 2, 1) for at in range(2)
    ]


def over_pieces(step, bounds_ref, seq, reach, local):
    low = jnp.minimum(bounds_ref[seq] // local, reach - 1)

    def body(at, carry):
        step(at)
        return carry

    lax.fori_loop(low, reach - 1, body, 0)


def attend_kernel(reach, head, bounds_ref, q_ref, start_ref, *rest):
    pieces = rest[:reach]
    mixed_ref, lse_ref, kv_buf, peak_ref, total_ref, acc_ref = rest[reach:]
    seq = pl.program_id(0)
    local = pieces[0].shape[1]
    half = local // 2
    for at in range(reach - 1):
        kv_buf[at] = pieces[at][0]
    queries = by_halves(q_ref)
    starts = row_halves(start_ref[0])
    peak_ref[...] = jnp.full_like(peak_ref, -1e30)
    total_ref[...] = jnp.zeros_like(total_ref)
    acc_ref[...] = jnp.zeros_like(acc_ref)

    def turned_values(keyval):
        return keyval.T[head:]

    def accumulate(group, scores, values):
        old = peak_ref[group : group + 1]
        peak = jnp.maximum(old, jnp.max(scores, 0, keepdims=True))
        fade = jnp.exp(old - peak)
        expo = jnp.exp(scores - peak)
        total_ref[group : group + 1] = total_ref[group : group + 1] * fade + jnp.sum(
            expo, 0, keepdims=True
        )
        acc_ref[group] = acc_ref[group] * fade + dot_nn(values, expo.astype(BF16))
        peak_ref[group : group + 1] = peak

    def step(at):
        keyval = kv_buf[at]
        values = turned_values(keyval)
        for group in range(2):
            scores = masked(dot_nt(keyval, queries[group]), starts[group], at * local)
            accumulate(group, scores, values)

    over_pieces(step, bounds_ref, seq, reach, local)
    own = pieces[reach - 1][0]
    own_at = (reach - 1) * local
    values = turned_values(own)
    for group in range(2):
        keys = half * (group + 1)
        scores = masked(
            dot_nt(own[:keys], queries[group]), starts[group], own_at, own_at + group * half
        )
        accumulate(group, scores, values[:, :keys])
    groups = []
    for group in range(2):
        mixed = acc_ref[group] / total_ref[group : group + 1]
        groups.append(jnp.concatenate([jnp.zeros_like(mixed), mixed], 0).T)
    from_halves(mixed_ref, groups)
    lse_ref[0] = peak_ref[...] + jnp.log(total_ref[...])


def mid_kernel(
    experts,
    head,
    x_ref,
    dy_ref,
    gate_ref,
    mixed_ref,
    vector_ref,
    core_ref,
    down_ref,
    up_ref,
    wo_ref,
    out_ref,
    grad_mid_ref,
    grad_mixed_ref,
    side_ref,
    *rest,
):
    *grads_refs, acc_out, acc_up, acc_down, acc_vec, acc_upb, branch_ref, gsec_ref = rest
    step, last = pl.program_id(0), pl.num_programs(0) - 1
    rows, width = x_ref.shape
    inner = experts * head
    owners, own_rows = wo_ref.shape[:2]
    ff_rows = down_ref.shape[1]
    ff = owners * ff_rows
    blocks = ff // width

    @pl.when(step == 0)
    def _():
        acc_out[...] = jnp.zeros_like(acc_out)
        acc_up[...] = jnp.zeros_like(acc_up)
        acc_down[...] = jnp.zeros_like(acc_down)
        acc_vec[...] = jnp.zeros_like(acc_vec)
        acc_upb[...] = jnp.zeros_like(acc_upb)

    gain, shift = vector_ref[1:2, :width], vector_ref[2:3, :width]
    down_bias = vector_ref[3:4, :width]
    gate_one, gate_two = gate_ref[:, 0:1], gate_ref[:, 1:2]
    first, second = gate_ref[:, 2:3].astype(jnp.int32), gate_ref[:, 3:4].astype(jnp.int32)
    owner = lax.div(lanes_of(rows, inner), head)
    unfold = unfold_matrix(inner, head, head)
    fold = fold_matrix(inner, head, head)
    wo = wo_ref[...].reshape(inner, width)
    mixed_one, mixed_two = mixed_ref[0], mixed_ref[1]
    routed_one = dot_nn((gate_one * mixed_one).astype(BF16), unfold)
    routed_two = dot_nn((gate_two * mixed_two).astype(BF16), unfold)
    routed = jnp.where(
        owner == first, routed_one, jnp.where(owner == second, routed_two, 0.0)
    )
    routed = routed.astype(BF16)
    middle = x_ref[...].astype(F32) + dot_nn(routed, wo)
    normed, inv_dev = normalize(middle)
    second_low = (normed * gain + shift).astype(BF16)
    second_t = second_low.T
    dy = dy_ref[...]
    dy_wide = dy.astype(F32)
    dy_t = dy.T
    branch_ref[...] = middle + down_bias
    gsec_ref[...] = jnp.zeros_like(gsec_ref)
    per_block = width // ff_rows if owners > 1 else 1

    def down_block(at):
        if owners > 1:
            return down_ref[at * per_block : (at + 1) * per_block].reshape(width, width)
        return down_ref[0, at * width : (at + 1) * width, :]

    def up_block(at):
        return up_ref[:, at * own_rows : (at + 1) * own_rows, :].reshape(width, width)

    def ahead(at):
        lo = at * width
        pre_act = dot_nn(second_low, up_block(at)) + vector_ref[0:1, lo : lo + width]
        return pre_act, dot_nt(dy, down_block(at)).astype(BF16)

    ready = ahead(0)
    for at in range(blocks):
        lo = at * width
        pre_act, grad_active = ready
        if at + 1 < blocks:
            ready = ahead(at + 1)
        sigma = jax.nn.sigmoid(pre_act)
        active = (pre_act * sigma).astype(BF16)
        slope = sigma * (1.0 + pre_act * (1.0 - sigma))
        grad_low = (grad_active.astype(F32) * slope).astype(BF16)
        branch_ref[...] += dot_nn(active, down_block(at))
        gsec_ref[...] += dot_nt(grad_low, up_block(at))
        acc_down[:, lo : lo + width] += dot_nn(dy_t, active)
        acc_up[:, lo : lo + width] += dot_nn(second_t, grad_low)
        acc_upb[8:9, lo : lo + width] += jnp.sum(grad_low.astype(F32), 0, keepdims=True)

    out_ref[...] = branch_ref[...].astype(BF16)
    gsec = gsec_ref[...]
    acc_vec[0:1] += jnp.sum(gsec * normed, 0, keepdims=True)
    acc_vec[1:2] += jnp.sum(gsec, 0, keepdims=True)
    acc_vec[2:3] += jnp.sum(dy_wide, 0, keepdims=True)
    grad_mid = dy_wide + norm_back(gsec, gain, normed, inv_dev)
    grad_mid_ref[...] = grad_mid
    grad_att = grad_mid.astype(BF16)
    acc_out[...] += dot_nn(routed.T, grad_att)
    grad_routed = dot_nt(grad_att, wo).astype(BF16)
    zero = jnp.zeros_like(grad_routed)
    picked_one = dot_nn(jnp.where(owner == first, grad_routed, zero), fold)
    picked_two = dot_nn(jnp.where(owner == second, grad_routed, zero), fold)
    grad_mixed_one = (gate_one * picked_one).astype(BF16)
    grad_mixed_two = (gate_two * picked_two).astype(BF16)
    grad_mixed_ref[0] = grad_mixed_one
    grad_mixed_ref[1] = grad_mixed_two
    inner_one = jnp.sum(grad_mixed_one.astype(F32) * mixed_one, -1, keepdims=True)
    inner_two = jnp.sum(grad_mixed_two.astype(F32) * mixed_two, -1, keepdims=True)
    grad_one = jnp.sum(picked_one * mixed_one, -1, keepdims=True)
    grad_two = jnp.sum(picked_two * mixed_two, -1, keepdims=True)
    common = gate_one * grad_one + gate_two * grad_two
    lane = lanes_of(rows, LANES)
    side = jnp.where(lane == first, gate_one * (grad_one - common), 0.0)
    side = jnp.where(lane == second, gate_two * (grad_two - common), side)
    side = jnp.where(lane == head, inner_one, side)
    side = jnp.where(lane == head + 1, inner_two, side)
    side = jnp.where(lane == head + 2, first.astype(F32), side)
    side_ref[...] = jnp.where(lane == head + 3, second.astype(F32), side)

    @pl.when(step == last)
    def _():
        up_at, out_at = ff_rows, ff_rows + blocks * own_rows

        def leave(value, columns, row, count, group):
            if owners == 1:
                grads_refs[0][0, row : row + value.shape[0], columns] = value
                return
            keep_ref, send_ref = grads_refs
            seqs = keep_ref.shape[1]
            parts = value.reshape(value.shape[0] // (2 * seqs * count), 2, seqs, count, -1)
            planes = parts.shape[0]
            other = core_ref[0] == 1
            low, high = parts[:, 0], parts[:, 1]
            where = (slice(group * planes, (group + 1) * planes), slice(None), slice(row, row + count), columns)
            keep_ref[where] = jnp.where(other, high, low)
            send_ref[where] = jnp.where(other, low, high)

        everything = slice(None)
        for at in range(blocks):
            lo = at * width
            turned = acc_down[:, lo : lo + width].T.astype(BF16)
            leave(turned, everything, lo if owners == 1 else 0, ff_rows, at)
            leave(
                acc_up[:, lo : lo + width].astype(BF16),
                everything,
                up_at + at * own_rows,
                own_rows,
                0,
            )
        leave(acc_out[...].astype(BF16), everything, out_at, own_rows, 0)
        vectors_turned = acc_vec[...].T
        extra = acc_upb[...].T
        if owners > 1:
            extra = extra.reshape(owners, blocks, own_rows, LANES)
        for at in range(blocks):
            if owners > 1:
                part = extra[:, at].reshape(width, LANES)
            else:
                part = extra[at * width : (at + 1) * width]
            if at == 0:
                part = part + vectors_turned
            columns = slice(at * LANES, (at + 1) * LANES)
            leave(part.astype(BF16), columns, out_at + own_rows, own_rows, 0)


def attend_back_kernel(
    reach, head, first_seq, chained, bounds_ref, q_ref, grad_ref, side_ref, lse_ref, start_ref, *rest
):
    pieces = rest[:reach]
    rest = rest[reach + chained :]
    grad_q_ref, leave_ref, kv_buf, acc_kv, acc_q = rest
    seq = first_seq + pl.program_id(0)
    local = pieces[0].shape[1]
    half = local // 2
    for at in range(reach - 1):
        kv_buf[at] = pieces[at][0]
    acc_kv[...] = jnp.zeros_like(acc_kv)
    acc_q[...] = jnp.zeros_like(acc_q)
    queries = by_halves(q_ref)
    grads = by_halves(grad_ref)
    side = side_ref[...].T
    inner_rows = [side[head + at : head + at + 1] for at in range(2)]
    starts = row_halves(start_ref[0])
    inners = [
        jnp.concatenate([row[:, at * half : (at + 1) * half] for row in inner_rows], 1)
        for at in range(2)
    ]
    log_sums = [lse_ref[0, at : at + 1] for at in range(2)]

    def one_group(group, keyval, keys_turned, mask):
        scores = mask(dot_nt(keyval, queries[group]))
        probs = jnp.exp(scores - log_sums[group])
        grad_probs = dot_nt(keyval, grads[group])
        grad_scores = (probs * (grad_probs - inners[group])).astype(BF16)
        acc_q[group] += dot_nn(keys_turned, grad_scores)
        return dot_nn(grad_scores, queries[group]) + dot_nn(probs.astype(BF16), grads[group])

    def turned_keys(keyval):
        return keyval.T[:head]

    def step(at):
        keyval = kv_buf[at]
        turned = turned_keys(keyval)
        added = []
        for group in range(2):

            def mask(scores):
                return masked(scores, starts[group], at * local)

            added.append(one_group(group, keyval, turned, mask))
        acc_kv[at] += added[0] + added[1]

    over_pieces(step, bounds_ref, seq, reach, local)
    own = pieces[reach - 1][0]
    own_at = (reach - 1) * local
    turned = turned_keys(own)
    for group in range(2):
        keys = half * (group + 1)
        added = one_group(
            group,
            own[:keys],
            turned[:, :keys],
            lambda scores: masked(scores, starts[group], own_at, own_at + group * half),
        )
        acc_kv[reach - 1, :keys] += added
    groups = []
    for group in range(2):
        grad_q = acc_q[group] * (head**-0.5)
        groups.append(jnp.concatenate([grad_q, jnp.zeros_like(grad_q)], 0).T.astype(BF16))
    from_halves(grad_q_ref, groups)
    shards = leave_ref.shape[0]
    me = bounds_ref[bounds_ref.shape[0] - 1]
    for at in range(shards):

        @pl.when((at > me) | (at <= me - reach))
        def _():
            leave_ref[at, 0] = jnp.zeros((local, LANES), BF16)

    for at in range(reach):
        target = me - (reach - 1) + at

        @pl.when(target >= 0)
        def _():
            leave_ref[target, 0] = acc_kv[at].astype(BF16)


def query_grad_kernel(
    experts,
    head,
    hidden_ref,
    grad_q_ref,
    grad_logit_ref,
    weight_ref,
    partial_ref,
    d_query_ref,
    d_router_ref,
    acc_query,
    acc_router,
):
    step, last = pl.program_id(0), pl.num_programs(0) - 1
    rows, width = hidden_ref.shape
    inner = experts * head

    @pl.when(step == 0)
    def _():
        acc_query[...] = jnp.zeros_like(acc_query)
        acc_router[...] = jnp.zeros_like(acc_router)

    side = grad_logit_ref[...]
    first = side[:, head + 2 : head + 3].astype(jnp.int32)
    second = side[:, head + 3 : head + 4].astype(jnp.int32)
    owner = lax.div(lanes_of(rows, inner), head)
    unfold = unfold_matrix(inner, head, 0)
    grad_queries = jnp.where(
        owner == first,
        dot_nn(grad_q_ref[0], unfold),
        jnp.where(owner == second, dot_nn(grad_q_ref[1], unfold), 0.0),
    ).astype(BF16)
    grad_logits = jnp.where(lanes_of(rows, LANES) < experts, side, 0.0)
    logit_high = grad_logits.astype(BF16)
    logit_low = (grad_logits - logit_high.astype(F32)).astype(BF16)
    router = weight_ref[:, inner + LANES :]
    partial_ref[...] = (
        dot_nt(grad_queries, weight_ref[:, :inner])
        + dot_nt(logit_high, router)
        + dot_nt(logit_low, router)
    )
    hidden_t = hidden_ref[...].T
    acc_query[...] += dot_nn(hidden_t, grad_queries)
    acc_router[...] += dot_nn(hidden_t, logit_high) + dot_nn(hidden_t, logit_low)

    @pl.when(step == last)
    def _():
        d_query_ref[...] = acc_query[...].astype(BF16)
        d_router_ref[...] = acc_router[...]


def last_kernel(
    experts,
    head,
    parts,
    core_ref,
    x_ref,
    hidden_ref,
    partial_ref,
    grad_mid_ref,
    query_ref,
    router_ref,
    weight_ref,
    *rest,
):
    pieces = rest[: len(parts)]
    grad_in_ref, *leaving, acc_kv, acc_vec, summed_ref = rest[len(parts) :]
    step, last = pl.program_id(0), pl.num_programs(0) - 1
    rows, width = x_ref.shape
    inner = experts * head

    @pl.when(step == 0)
    def _():
        acc_kv[...] = jnp.zeros_like(acc_kv)
        acc_vec[...] = jnp.zeros_like(acc_vec)

    for piece, (low, high) in zip(pieces, parts):

        @pl.when((step >= low) & (step < high))
        def _():
            per_step = piece.shape[1] // (high - low)
            base = (step - low) * per_step
            summed = piece[0, pl.ds(base, per_step)].astype(F32)
            for at in range(1, piece.shape[0]):
                summed = summed + piece[at, pl.ds(base, per_step)].astype(F32)
            summed_ref[...] = summed.astype(BF16).reshape(summed_ref.shape)

    gain = rows_of(weight_ref[:, inner + LANES :], (experts,))[0:1]
    normed, inv_dev = normalize(x_ref[...].astype(F32))
    grad_keyvals = summed_ref[...]
    grad_hidden = partial_ref[...] + dot_nt(grad_keyvals, weight_ref[:, inner : inner + LANES])
    grad_in_ref[...] = grad_mid_ref[...] + norm_back(grad_hidden, gain, normed, inv_dev)
    hidden_t = hidden_ref[...].T
    acc_kv[...] += dot_nn(hidden_t, grad_keyvals)
    acc_vec[experts : experts + 1] += jnp.sum(grad_hidden * normed, 0, keepdims=True)
    acc_vec[experts + 1 : experts + 2] += jnp.sum(grad_hidden, 0, keepdims=True)

    @pl.when(step == last)
    def _():
        extra = router_ref[...] + acc_vec[...].T
        for value, low in (
            (query_ref[...], 0),
            (acc_kv[...].astype(BF16), inner),
            (extra.astype(BF16), inner + LANES),
        ):
            columns = slice(low, low + value.shape[1])
            if len(leaving) == 1:
                leaving[0][:, columns] = value
                continue
            keep_ref, send_ref = leaving
            planes, seqs, own_rows = keep_ref.shape[:3]
            by_core = value.reshape(planes, 2, seqs, own_rows, value.shape[1])
            other = core_ref[0] == 1
            keep_ref[:, :, :, columns] = jnp.where(other, by_core[:, 1], by_core[:, 0])
            send_ref[:, :, :, columns] = jnp.where(other, by_core[:, 0], by_core[:, 1])


def finish_second_kernel(total_ref, down_ref, up_ref, out_ref, up_bias_ref, *vector_refs):
    ff_rows, width = down_ref.shape
    own_rows, ff = up_ref.shape
    blocks = ff // width
    down_ref[...] = total_ref[:ff_rows].astype(F32)
    for at in range(blocks):
        low = ff_rows + at * own_rows
        up_ref[:, at * width : (at + 1) * width] = total_ref[low : low + own_rows].astype(F32)
    low = ff_rows + blocks * own_rows
    out_ref[...] = total_ref[low : low + own_rows].astype(F32)
    turned = total_ref[low + own_rows :].astype(F32).T
    up_bias_ref[...] = jnp.concatenate([turned[at * LANES + 8] for at in range(blocks)], 0)
    for at, ref in enumerate(vector_refs):
        ref[...] = turned[at]


def finish_first_kernel(count, *refs):
    query_ref, kv_ref, router_ref, gain_ref, bias_ref = refs[count:]
    total = refs[0][...].astype(F32)
    for ref in refs[1:count]:
        total = total + ref[...].astype(F32)
    inner, pair, experts = query_ref.shape[1], kv_ref.shape[1], router_ref.shape[0]
    query_ref[...] = total[:, :inner]
    kv_ref[...] = total[:, inner : inner + pair]
    turned = total[:, inner + LANES :].T
    router_ref[...] = turned[:experts]
    gain_ref[...] = turned[experts]
    bias_ref[...] = turned[experts + 1]


def whole_spec(shape):
    zeros = (0,) * len(shape)
    return pl.BlockSpec(shape, lambda *_: zeros, pipeline_mode=pl.Buffered(1))


def row_spec(rows, columns):
    return pl.BlockSpec((rows, columns), lambda i, *_: (i, 0))


def pair_spec(rows):
    return pl.BlockSpec((2, rows, LANES), lambda i, *_: (0, i, 0))


def swapped(value, axis, mask):
    count = lax.axis_size(axis)
    return lax.ppermute(value, axis, [(at, at ^ mask) for at in range(count)])


def passed_along(value, axis, steps):
    count = lax.axis_size(axis)
    leading, last = (max(0, -steps), min(count, count - steps))
    return lax.ppermute(value, axis, [(source, source + steps) for source in range(leading, last)])


def spread(shard):
    dp, seq = lax.axis_size("dp"), lax.axis_size("seq")
    along = [shard] + [swapped(shard, "dp", 2 * at) for at in range(1, dp // 2)]
    held = jnp.stack(along)
    held = jnp.stack([held] + [swapped(held, "seq", at) for at in range(1, seq)])
    return held, swapped(held, "dp", 1)


def at_index(value, index, dim):
    return lax.dynamic_index_in_dim(value, index, dim, keepdims=False)


def core_halved(value):
    core = lax.axis_index("dp") % 2
    return at_index(value, core, 1) + swapped(at_index(value, 1 - core, 1), "dp", 1)


def summed_direct(value, dim, axis, scale):
    me = lax.axis_index(axis) // scale
    total = at_index(value, me, dim).astype(F32)
    for at in range(1, value.shape[dim]):
        total = total + swapped(at_index(value, me ^ at, dim), axis, at * scale).astype(F32)
    return total


def together(*values):
    return lax.optimization_barrier(values)


def on_device(
    block_in,
    routes,
    segments,
    cotangent,
    ln1_gain,
    ln1_bias,
    query_weight,
    kv_weight,
    router_weight,
    out_weight,
    ln2_gain,
    ln2_bias,
    up_weight,
    up_bias,
    down_weight,
    down_bias,
):
    micro_count, seq_count, local_len, width = block_in.shape
    full_len = segments.shape[2]
    experts = router_weight.shape[1]
    head = kv_weight.shape[1] // 2
    inner = experts * head
    ff = up_weight.shape[1]
    dp, shards = lax.axis_size("dp"), lax.axis_size("seq")
    devices = dp * shards
    own_rows, ff_rows, blocks = width // devices, ff // devices, ff // width
    aligned = own_rows % 16 == 0
    batch = micro_count * seq_count
    rows_all = batch * local_len
    tile = seq_count * local_len
    longest = full_len * 3 // 4
    reach = min(shards, (longest - 2) // local_len + 2)
    own_shard = lax.axis_index("seq")
    start_pos = own_shard * local_len

    def padded(value, columns):
        return jnp.pad(value, ((0, 0), (0, columns - value.shape[1])))

    a_cols = inner + 2 * LANES
    if aligned:
        packed_a, packed_b = pl.pallas_call(
            pack_kernel,
            out_shape=[
                jax.ShapeDtypeStruct((own_rows, a_cols), BF16),
                jax.ShapeDtypeStruct((ff_rows + (blocks + 1) * own_rows, width), BF16),
            ],
            compiler_params=call_params(),
            name="pack",
        )(
            query_weight,
            kv_weight,
            router_weight.T,
            down_weight,
            up_weight,
            out_weight,
            ln1_gain,
            ln1_bias,
            ln2_gain,
            ln2_bias,
            down_bias,
            up_bias,
        )
    else:
        rows = jnp.concatenate([ln1_gain, ln1_bias, ln2_gain, ln2_bias, down_bias, up_bias])
        rows = rows.reshape(5 + blocks, own_rows)
        extra = padded(jnp.concatenate([router_weight, rows.T], 1), LANES)
        packed_a = jnp.concatenate([query_weight, kv_weight, extra], 1)
        packed_b = jnp.concatenate(
            [down_weight]
            + [up_weight[:, at * width : (at + 1) * width] for at in range(blocks)]
            + [out_weight],
            0,
        )
    mine_a, mate_a = spread(packed_a)
    place = jnp.stack(
        [lax.axis_index("dp") // 2, lax.axis_index("dp") % 2, lax.axis_index("seq")]
    ).astype(jnp.int32)
    place_a = place
    if not aligned:
        held = jnp.moveaxis(jnp.stack([mine_a, mate_a]), 2, 0)
        for dim, at in ((0, 0), (1, 1), (2, 2)):
            order = jnp.arange(held.shape[dim], dtype=jnp.int32) ^ place[at]
            held = jnp.take(held, order, axis=dim)
        held = held.reshape(2, width // 2, a_cols)
        mine_a, mate_a = held[:1, None], held[1:, None]
        place_a = jnp.zeros_like(place)
    group_b = lax.all_gather(packed_b, ("dp", "seq"), axis=0, tiled=False)
    up_at, out_at = ff_rows, ff_rows + blocks * own_rows
    if aligned:
        nb, rb, fb = devices, own_rows, ff_rows
        weights = [group_b, group_b, group_b]
        weight_specs = [
            pl.BlockSpec((nb, ff_rows, width), lambda *_: (0, 0, 0), pipeline_mode=pl.Buffered(1)),
            pl.BlockSpec(
                (nb, blocks * own_rows, width), lambda *_: (0, 1, 0), pipeline_mode=pl.Buffered(1)
            ),
            pl.BlockSpec(
                (nb, own_rows, width),
                lambda *_: (0, out_at // own_rows, 0),
                pipeline_mode=pl.Buffered(1),
            ),
        ]
    else:
        nb, rb, fb = 1, width, ff
        up_all = group_b[:, up_at:out_at].reshape(devices, blocks, own_rows, width)
        weights = [
            group_b[:, :ff_rows].reshape(1, ff, width),
            jnp.moveaxis(up_all, 0, 1).reshape(1, ff, width),
            group_b[:, out_at:].reshape(1, width, width),
        ]
        weight_specs = [whole_spec(value.shape) for value in weights]

    tokens = block_in.reshape(rows_all, width)
    grad_out = cotangent.reshape(rows_all, width)
    route_rows = routes.reshape(rows_all, 2)

    seg_rows = segments.reshape(batch, full_len)
    seg_local = lax.dynamic_slice_in_dim(seg_rows, start_pos, local_len, 1)
    doc_start = jnp.sum(
        (seg_rows[:, None, :] < seg_local[:, :, None]).astype(jnp.int32), -1, dtype=jnp.int32
    )
    doc_start = jnp.maximum(doc_start - (own_shard - (reach - 1)) * local_len, 0)
    bounds = jnp.concatenate([doc_start[:, 0], own_shard.reshape(1).astype(jnp.int32)])
    starts = doc_start.reshape(batch, 1, local_len)

    steps = micro_count
    hidden, keyvals, group_a = pl.pallas_call(
        functools.partial(keyval_kernel, experts, head),
        grid=(steps,),
        in_specs=[
            pl.BlockSpec(memory_space=pltpu.SMEM),
            row_spec(tile, width),
            whole_spec(mine_a.shape),
            whole_spec(mate_a.shape),
        ],
        out_specs=[row_spec(tile, width), row_spec(tile, LANES), whole_spec((width, a_cols))],
        out_shape=[
            jax.ShapeDtypeStruct((rows_all, width), BF16),
            jax.ShapeDtypeStruct((rows_all, LANES), BF16),
            jax.ShapeDtypeStruct((width, a_cols), BF16),
        ],
        scratch_shapes=[
            pltpu.VMEM((2 * mine_a.shape[0] * mine_a.shape[1],) + mine_a.shape[2:], BF16)
        ],
        compiler_params=call_params(),
        cost_estimate=cost(2 * rows_all * width * LANES, rows_all * width * 4),
        name="keyval",
    )(place_a, tokens, mine_a, mate_a)

    own_pieces = keyvals.reshape(batch, local_len, LANES)
    pieces = [own_pieces] + [passed_along(own_pieces, "seq", back) for back in range(1, reach)]
    pieces = pieces[::-1]

    queries, gates = pl.pallas_call(
        functools.partial(query_kernel, experts, head),
        grid=(steps,),
        in_specs=[row_spec(tile, width), row_spec(tile, 2), whole_spec((width, a_cols))],
        out_specs=[pair_spec(tile), row_spec(tile, LANES)],
        out_shape=[
            jax.ShapeDtypeStruct((2, rows_all, LANES), BF16),
            jax.ShapeDtypeStruct((rows_all, LANES), F32),
        ],
        compiler_params=call_params(),
        cost_estimate=cost(2 * rows_all * width * (a_cols + 512), rows_all * width * 4),
        name="query",
    )(hidden, route_rows, group_a)

    columns = group_a[:, inner + LANES :].astype(F32)
    small = jnp.pad(columns[:, experts + 2 : experts + 5].T, ((0, 4), (0, ff - width)))
    up_row = columns[:, experts + 5 : experts + 5 + blocks]
    up_row = jnp.swapaxes(up_row.reshape(devices, own_rows, blocks), 1, 2).reshape(1, ff)
    vectors = jnp.concatenate([up_row, small], 0)

    piece_spec = pl.BlockSpec((1, local_len, LANES), lambda b, *_: (b, 0, 0))
    q_spec = pl.BlockSpec((2, local_len, LANES), lambda b, *_: (0, b, 0))
    start_spec = pl.BlockSpec((1, 1, local_len), lambda b, *_: (b, 0, 0))
    lse_spec = pl.BlockSpec((1, 2, local_len), lambda b, *_: (b, 0, 0))
    pairs = rows_all * full_len
    mixed, lse = pl.pallas_call(
        functools.partial(attend_kernel, reach, head),
        grid_spec=pltpu.PrefetchScalarGridSpec(
            num_scalar_prefetch=1,
            grid=(batch,),
            in_specs=[q_spec, start_spec] + [piece_spec] * reach,
            out_specs=[q_spec, lse_spec],
            scratch_shapes=[
                pltpu.VMEM((reach, local_len, LANES), BF16),
                pltpu.VMEM((2, local_len), F32),
                pltpu.VMEM((2, local_len), F32),
                pltpu.VMEM((2, head, local_len), F32),
            ],
        ),
        out_shape=[
            jax.ShapeDtypeStruct((2, rows_all, LANES), F32),
            jax.ShapeDtypeStruct((batch, 2, local_len), F32),
        ],
        compiler_params=call_params(),
        cost_estimate=cost(4 * pairs * LANES, rows_all * LANES * 16, pairs),
        name="attend",
    )(bounds, queries, starts, *pieces)

    grad_rows = ff_rows + (blocks + 2) * own_rows if aligned else ff + (blocks + 2) * width
    core_index = (lax.axis_index("dp") % 2).reshape(1).astype(jnp.int32)
    if aligned:
        leaving = [(dp // 2, shards, grad_rows, width)] * 2
    else:
        leaving = [(nb, grad_rows, width)]
    block_out, grad_mid, grad_mixed, side, *grads_b = pl.pallas_call(
        functools.partial(mid_kernel, experts, head),
        grid=(steps,),
        in_specs=[
            row_spec(tile, width),
            row_spec(tile, width),
            row_spec(tile, LANES),
            pair_spec(tile),
            whole_spec((8, ff)),
            pl.BlockSpec(memory_space=pltpu.SMEM),
        ]
        + weight_specs,
        out_specs=[
            row_spec(tile, width),
            row_spec(tile, width),
            pair_spec(tile),
            row_spec(tile, LANES),
        ]
        + [whole_spec(shape) for shape in leaving],
        out_shape=[
            jax.ShapeDtypeStruct((rows_all, width), BF16),
            jax.ShapeDtypeStruct((rows_all, width), F32),
            jax.ShapeDtypeStruct((2, rows_all, LANES), BF16),
            jax.ShapeDtypeStruct((rows_all, LANES), F32),
        ]
        + [jax.ShapeDtypeStruct(shape, BF16) for shape in leaving],
        scratch_shapes=[
            pltpu.VMEM((inner, width), F32),
            pltpu.VMEM((width, ff), F32),
            pltpu.VMEM((width, ff), F32),
            pltpu.VMEM((LANES, width), F32),
            pltpu.VMEM((LANES, ff), F32),
            pltpu.VMEM((tile, width), F32),
            pltpu.VMEM((tile, width), F32),
        ],
        compiler_params=call_params(),
        cost_estimate=cost(6 * rows_all * width * (2 * ff + width), rows_all * width * 16),
        name="mid",
    )(tokens, grad_out, gates, mixed, vectors, core_index, *weights)

    if not aligned:
        parts = grads_b[0][0]
        down_part = parts[:ff].reshape(devices, ff_rows, width)
        up_part = parts[ff : 2 * ff].reshape(blocks, devices, own_rows, width)
        up_part = jnp.moveaxis(up_part, 0, 1).reshape(devices, blocks * own_rows, width)
        out_part = parts[2 * ff : 2 * ff + width].reshape(devices, own_rows, width)
        tail = parts[2 * ff + width :]
        rows_up = tail.reshape(width, blocks, LANES)[:, :, 8].T.reshape(devices, own_rows, blocks)
        rows_vec = tail[:, :8].reshape(devices, own_rows, 8)
        rows_up = jnp.moveaxis(rows_up.reshape(devices, blocks, own_rows), 1, 2)
        tail = jnp.zeros((devices, own_rows, blocks, LANES), BF16)
        tail = tail.at[:, :, :, 8].set(rows_up).at[:, :, 0, :8].set(rows_vec)
        tail = tail.reshape(devices, own_rows, width)
        packed = jnp.concatenate([down_part, up_part, out_part, tail], 1)
        packed = packed.reshape((dp // 2, 2, shards) + packed.shape[1:])
        grads_b = [at_index(packed, core_index[0], 1), at_index(packed, 1 - core_index[0], 1)]

    keep, send = grads_b
    bits = shards.bit_length() - 1
    order = [1 << at for at in range(bits)]
    orders = (order, order[bits // 2 :] + order[: bits // 2])
    half_rows = keep.shape[2] // 2
    remaining = [list(reversed(order)), list(reversed(order))]
    halves = [None, None]
    arriving = swapped(send, "dp", 1)

    def core_step():
        held = keep + arriving
        held = held.reshape((dp // 2,) + (2,) * bits + held.shape[2:])
        halves[0] = held[..., :half_rows, :]
        halves[1] = held[..., half_rows:, :]

    leave_spec = pl.BlockSpec((shards, 1, local_len, LANES), lambda b, *_: (0, b, 0, 0))

    def send_halves(stage):
        for part in range(2):
            mask = orders[part][stage]
            dim = 1 + remaining[part].index(mask)
            remaining[part].remove(mask)
            bit = (own_shard // mask) % 2
            halves[part] = at_index(halves[part], bit, dim), at_index(halves[part], 1 - bit, dim)
        return [swapped(halves[part][1], "seq", orders[part][stage]) for part in range(2)]

    core_step()
    pending = send_halves(0)
    stage = 1
    bounds_now, *kept = together(bounds, halves[0][0], halves[1][0])
    grad_queries = None
    returned = []
    splits = [0, max(1, micro_count - 1), micro_count] if micro_count > 1 else [0, 1]
    for micro, stop in zip(splits[:-1], splits[1:]):
        count = (stop - micro) * seq_count

        def at_micro(block, dims, base=micro * seq_count):
            if dims == "b":
                return pl.BlockSpec(block, lambda b, *_: (base + b, 0, 0))
            return pl.BlockSpec(block, lambda b, *_: (0, base + b, 0))

        q_at = at_micro((2, local_len, LANES), "q")
        in_specs = [
            q_at,
            q_at,
            pl.BlockSpec(
                (local_len, LANES), lambda b, *_, base=micro * seq_count: (base + b, 0)
            ),
            at_micro((1, 2, local_len), "b"),
            at_micro((1, 1, local_len), "b"),
        ]
        in_specs += [at_micro((1, local_len, LANES), "b")] * reach
        operands = [queries, grad_mixed, side, lse, starts, *pieces]
        aliases = {}
        if micro:
            in_specs.append(pl.BlockSpec(memory_space=pl.ANY))
            operands.append(grad_queries)
            aliases = {len(operands): 0}
        grad_queries, leave = pl.pallas_call(
            functools.partial(
                attend_back_kernel, reach, head, micro * seq_count, int(micro > 0)
            ),
            grid_spec=pltpu.PrefetchScalarGridSpec(
                num_scalar_prefetch=1,
                grid=(count,),
                in_specs=in_specs,
                out_specs=[q_at, leave_spec],
                scratch_shapes=[
                    pltpu.VMEM((reach, local_len, LANES), BF16),
                    pltpu.VMEM((reach, local_len, LANES), F32),
                    pltpu.VMEM((2, head, local_len), F32),
                ],
            ),
            out_shape=[
                jax.ShapeDtypeStruct((2, rows_all, LANES), BF16),
                jax.ShapeDtypeStruct((shards, count, local_len, LANES), BF16),
            ],
            input_output_aliases=aliases,
            compiler_params=call_params(),
            cost_estimate=cost(
                10 * pairs * LANES * count // batch,
                count * local_len * LANES * 32,
                pairs * count // batch,
            ),
            name="attend_back",
        )(bounds_now, *operands)
        returned.append(lax.all_to_all(leave, "seq", 0, 0, tiled=True))
        if micro == 0 and stage < bits:
            pending[0], pending[1], grad_queries = together(*pending, grad_queries)
            halves[0], halves[1] = kept[0] + pending[0], kept[1] + pending[1]
            pending = send_halves(stage)
            stage += 1
            bounds_now, *kept = together(bounds, halves[0][0], halves[1][0])

    pending[0], pending[1], grad_queries = together(*pending, grad_queries)
    halves[0], halves[1] = kept[0] + pending[0], kept[1] + pending[1]
    while stage < bits:
        pending = send_halves(stage)
        halves[0], halves[1] = halves[0][0] + pending[0], halves[1][0] + pending[1]
        stage += 1
    own_b = jnp.concatenate(halves, 1)
    z_me = lax.axis_index("dp") // 2
    z_bits = (dp // 2).bit_length() - 1
    own_b = own_b.reshape((2,) * z_bits + own_b.shape[1:])
    z_stage = 0

    def z_split(value):
        bit = (z_me >> z_stage) & 1
        dim = z_bits - 1 - z_stage
        return at_index(value, bit, dim), at_index(value, 1 - bit, dim)

    arriving_b = None
    if z_bits:
        kept_b, send_b = z_split(own_b)
        side, kept_b = together(side, kept_b)
        arriving_b = swapped(send_b, "dp", 2)
        z_stage = 1
    partial_hidden, d_query, d_router = pl.pallas_call(
        functools.partial(query_grad_kernel, experts, head),
        grid=(steps,),
        in_specs=[
            row_spec(tile, width),
            pair_spec(tile),
            row_spec(tile, LANES),
            whole_spec((width, a_cols)),
        ],
        out_specs=[
            row_spec(tile, width),
            whole_spec((width, inner)),
            whole_spec((width, LANES)),
        ],
        out_shape=[
            jax.ShapeDtypeStruct((rows_all, width), F32),
            jax.ShapeDtypeStruct((width, inner), BF16),
            jax.ShapeDtypeStruct((width, LANES), F32),
        ],
        scratch_shapes=[pltpu.VMEM((width, inner), F32), pltpu.VMEM((width, LANES), F32)],
        compiler_params=call_params(),
        cost_estimate=cost(4 * rows_all * width * a_cols, rows_all * width * 12),
        name="query_grad",
    )(hidden, grad_queries, side, group_a)
    if z_bits > 1:
        arriving_b, partial_hidden = together(arriving_b, partial_hidden)
        kept_b, send_b = z_split(kept_b + arriving_b)
        partial_hidden, kept_b = together(partial_hidden, kept_b)
        arriving_b = swapped(send_b, "dp", 4)
        z_stage = 2
    if aligned:
        small_shapes = [(dp // 2, shards, own_rows, a_cols)] * 2
    else:
        small_shapes = [(width, a_cols)]
    grad_in, *small = pl.pallas_call(
        functools.partial(last_kernel, experts, head, tuple(zip(splits[:-1], splits[1:]))),
        grid=(steps,),
        in_specs=[
            pl.BlockSpec(memory_space=pltpu.SMEM),
            row_spec(tile, width),
            row_spec(tile, width),
            row_spec(tile, width),
            row_spec(tile, width),
            whole_spec((width, inner)),
            whole_spec((width, LANES)),
            whole_spec((width, a_cols)),
        ]
        + [whole_spec(piece.shape) for piece in returned],
        out_specs=[row_spec(tile, width)] + [whole_spec(shape) for shape in small_shapes],
        out_shape=[
            jax.ShapeDtypeStruct((rows_all, width), F32),
        ]
        + [jax.ShapeDtypeStruct(shape, BF16) for shape in small_shapes],
        scratch_shapes=[
            pltpu.VMEM((width, LANES), F32),
            pltpu.VMEM((LANES, width), F32),
            pltpu.VMEM((tile, LANES), BF16),
        ],
        compiler_params=call_params(),
        cost_estimate=cost(4 * rows_all * width * LANES, rows_all * width * 16),
        name="last",
    )(core_index, tokens, hidden, partial_hidden, grad_mid, d_query, d_router, group_a, *returned)
    if not aligned:
        by_core = small[0].reshape(dp // 2, 2, shards, own_rows, a_cols)
        small = [at_index(by_core, core_index[0], 1), at_index(by_core, 1 - core_index[0], 1)]
    keep_small, send_small = small
    if arriving_b is not None:
        send_small, arriving_b = together(send_small, arriving_b)
        own_b = kept_b + arriving_b
    while z_stage < z_bits:
        kept_b, send_b = z_split(own_b)
        own_b = kept_b + swapped(send_b, "dp", 2 << z_stage)
        z_stage += 1
    held = keep_small + swapped(send_small, "dp", 1)
    held = summed_direct(held, 1, "seq", 1).astype(BF16)
    ends = [at_index(held, z_me, 0)]
    ends += [swapped(at_index(held, z_me ^ at, 0), "dp", 2 * at) for at in range(1, dp // 2)]

    out_at_b, tail_at = ff_rows + blocks * own_rows, ff_rows + (blocks + 1) * own_rows
    if aligned:
        vector_shape = jax.ShapeDtypeStruct((own_rows,), F32)
        grad_down, grad_up, grad_out_weight, grad_up_bias, *second_vectors = pl.pallas_call(
            finish_second_kernel,
            out_shape=[
                jax.ShapeDtypeStruct((ff_rows, width), F32),
                jax.ShapeDtypeStruct((own_rows, ff), F32),
                jax.ShapeDtypeStruct((own_rows, width), F32),
                jax.ShapeDtypeStruct((ff_rows,), F32),
            ]
            + [vector_shape] * 3,
            compiler_params=call_params(),
            name="finish_second",
        )(own_b)
        grad_query, grad_kv, grad_router, *first_vectors = pl.pallas_call(
            functools.partial(finish_first_kernel, len(ends)),
            out_shape=[
                jax.ShapeDtypeStruct((own_rows, inner), F32),
                jax.ShapeDtypeStruct((own_rows, 2 * head), F32),
                jax.ShapeDtypeStruct((experts, own_rows), F32),
            ]
            + [vector_shape] * 2,
            compiler_params=call_params(),
            name="finish_first",
        )(*ends)
        grad_router = grad_router.T
    else:
        own_b = own_b.astype(F32)
        total = sum([piece.astype(F32) for piece in ends])
        ends = own_b[tail_at:]
        grad_up = jnp.concatenate(
            [
                own_b[ff_rows + at * own_rows : ff_rows + (at + 1) * own_rows]
                for at in range(blocks)
            ],
            1,
        )
        grad_up_bias = jnp.concatenate([ends[:, at * LANES + 8] for at in range(blocks)])
        grad_down, grad_out_weight = own_b[:ff_rows], own_b[out_at_b:tail_at]
        second_vectors = [ends[:, at] for at in range(3)]
        grad_query, grad_kv = total[:, :inner], total[:, inner : inner + 2 * head]
        total = total[:, inner + LANES :]
        grad_router = total[:, :experts]
        first_vectors = [total[:, experts], total[:, experts + 1]]
    return (
        block_out.reshape(block_in.shape),
        grad_in.reshape(block_in.shape),
        first_vectors[0],
        first_vectors[1],
        grad_query,
        grad_kv,
        grad_router,
        grad_out_weight,
        second_vectors[0],
        second_vectors[1],
        grad_up,
        grad_up_bias,
        grad_down,
        second_vectors[2],
    )


def solution(mesh):
    rows = P(("dp", "seq"), None)
    vector = P(("dp", "seq"))
    data = P(None, "dp", "seq", None)
    weights = (
        vector,
        vector,
        rows,
        rows,
        rows,
        rows,
        vector,
        vector,
        rows,
        vector,
        rows,
        vector,
    )
    return jax.shard_map(
        on_device,
        mesh=mesh,
        in_specs=(data, data, P(None, "dp", None), data) + weights,
        out_specs=(data, data) + weights,
        check_vma=False,
    )
```

time: 286 us -> 228 us (0.80); the launches traced: 281 us -> 227 us
  starting transfers between devices: 79 us -> 47 us
  local copies, waits for them, and re-layouts: 26.8 us -> 11 us
    ppermute x29 -> x21, starting transfers between devices: 60.8 us -> 24.4 us  [swapped(): return lax.ppermute(value, axis, [(at, at ^ mask) for at in range(count)])]
    ppermute x12 -> x3, waiting for transfers between devices: 28.4 us -> 7.97 us  [passed_along(): lax.ppermute(value, axis, [(source, source + steps) for source in range(l...]
    all_to_all x0 -> x2, starting transfers between devices: none -> 16.3 us  [on_device(): returned.append(lax.all_to_all(leave, 'seq', 0, 0, tiled=True))]
    all_gather x1, waiting for transfers between devices: 0.01 us -> 14.4 us  [on_device(): group_b = lax.all_gather(packed_b, ('dp', 'seq'), axis=0, tiled=False)]
    ppermute x12 -> x3, starting transfers between devices: 18.1 us -> 6.19 us  [passed_along(): lax.ppermute(value, axis, [(source, source + steps) for source in range(l...]
    unnamed x41 -> x25, local copies, waits for them, and re-layouts: 9.5 us -> 4.92 us
    ppermute x29 -> x21, waiting for transfers between devices: 29.5 us -> 33.3 us  [swapped(): return lax.ppermute(value, axis, [(at, at ^ mask) for at in range(count)])]
    slice x8 -> x2, local copies, waits for them, and re-layouts: 3.66 us -> 0.24 us  [the longest x1 0.24 us: core_step(): halves[1] = held[..., half_rows:, :]]
  transfers between devices with their start and end apart: 42 -> 27, of which waited for: 17 -> 15; matrix products, arithmetic and copies ran while one was open for 9% -> 6% of each run, Pallas kernels for 17% -> 20%
where the time goes in v3:
time: 228 us; the launch traced here: 227 us
  Pallas kernels  88.7 us (39%)
  waiting for transfers between devices  55.7 us (24%)
  starting transfers between devices  47 us (21%)
  between operations  14.4 us (6%)
  local copies, waits for them, and re-layouts  11 us (5%)
  other arithmetic  10.3 us (5%)
    pallas_call x1, Pallas kernels, on_device(): pl.pallas_call(functools.partial(mid_kernel, experts, head), grid=(steps,...  39.3 us
    ppermute x21, waiting for transfers between devices, swapped(): return lax.ppermute(value, axis, [(at, at ^ mask) for at in range(count)])  33.3 us
    ppermute x21, starting transfers between devices, swapped(): return lax.ppermute(value, axis, [(at, at ^ mask) for at in range(count)])  24.4 us
    all_to_all x2, starting transfers between devices, on_device(): returned.append(lax.all_to_all(leave, 'seq', 0, 0, tiled=True))  16.3 us
    all_gather x1, waiting for transfers between devices, on_device(): group_b = lax.all_gather(packed_b, ('dp', 'seq'), axis=0, tiled=False)  14.4 us
    pallas_call x2, Pallas kernels, on_device(): pl.pallas_call(functools.partial(attend_back_kernel, reach, head, micro *...  10.8 us
    pallas_call x1, Pallas kernels, on_device(): pl.pallas_call(functools.partial(last_kernel, experts, head, tuple(zip(sp...  9.17 us
    ppermute x3, waiting for transfers between devices, passed_along(): lax.ppermute(value, axis, [(source, source + steps) for source in range(l...  7.97 us
  transfers between devices with their start and end apart: 27, of which 15 were waited for; matrix products, arithmetic and copies ran while one was open for 6% of the time, Pallas kernels for 20%

profile of v3, /device:TPU:0, one launch (start us, length us, event | category | flops | bytes accessed | tf_op | source)
XLA Modules:
  0.0 227.2 jit_solution(16741732439031856738)
XLA Ops:
  7.2 1.8 pack.1
  9.1 3.1 %collective-permute-start = (bf16[16,768]{1,0:T(8,128)(2,1)}, bf16[16,768]{1,0:T(8,128)(2,1)S(1)}, u32[]{:S(2)}, u32[]{:S(2)}) collective-permute-start(bf16[16,768]{1,0:T(8,128)(2,1)} %get-tuple-element.71), channel_id=1, source_target_pairs={{0,8},{4,12},{8,0},{12,4},{16,24},{20,28},{24,16},{28,20},{1,9},{5... | collective-permute-start | bytes 73736 | tf_op jit(solution)/shard_map/ppermute | solution.py:658
  12.2 2.6 %collective-permute-start.1 = (bf16[16,768]{1,0:T(8,128)(2,1)}, bf16[16,768]{1,0:T(8,128)(2,1)S(1)}, u32[]{:S(2)}, u32[]{:S(2)}) collective-permute-start(bf16[16,768]{1,0:T(8,128)(2,1)} %get-tuple-element.71), channel_id=1, source_target_pairs={{0,16},{4,20},{8,24},{12,28},{16,0},{20,4},{24,8},{28,12},{1,17},{... | collective-permute-start | bytes 73736 | tf_op jit(solution)/shard_map/ppermute | solution.py:658
  16.3 1.2 collective-permute-done.1
  17.5 3.1 %collective-permute-done.2 = bf16[16,768]{1,0:T(8,128)(2,1)S(1)} collective-permute-done((bf16[16,768]{1,0:T(8,128)(2,1)}, bf16[16,768]{1,0:T(8,128)(2,1)S(1)}, u32[]{:S(2)}, u32[]{:S(2)}) %collective-permute-start.2) | collective-permute-done | bytes 24608 | tf_op jit(solution)/shard_map/ppermute | solution.py:658
  21.4 1.6 collective-permute-start.3
  22.9 1.5 collective-permute-start.4
  24.9 1.5 convert_reduce_fusion
  26.5 1.3 collective-permute-done.3
  27.9 2.0 collective-permute-done.5
  30.2 1.2 copy.48
  34.0 4.8 %keyval.1 = (bf16[1536,512]{1,0:T(8,128)(2,1)}, bf16[1536,128]{1,0:T(8,128)(2,1)}, bf16[512,768]{1,0:T(8,128)(2,1)}) custom-call(s32[3]{0:T(128)} %pad_add_fusion.place_ref, bf16[1536,512]{1,0:T(8,128)(2,1)} %bitcast.88, bf16[4,4,16,768]{3,2,1,0:T(8,128)(2,1)} %copy-done.2, bf16[4,4,16,768]{3,2,1,0:T(8,128)(2,1)} %copy-done.3), custom_call_target="tpu_custom_call" | custom-call | flops 201326592 | bytes 3145728 | tf_op jit(solution)/shard_map/keyval/pallas_call | solution.py:823
  38.8 2.4 %collective-permute-start.7 = (bf16[3,512,128]{2,1,0:T(8,128)(2,1)}, bf16[3,512,128]{2,1,0:T(8,128)(2,1)S(1)}, u32[]{:S(2)}, u32[]{:S(2)}) collective-permute-start(bf16[3,512,128]{2,1,0:T(8,128)(2,1)} %bitcast.109), channel_id=1, source_target_pairs={{0,3},{4,7},{8,11},{12,15},{16,19},{20,23},{24,27},{28,31}} | collective-permute-start | bytes 1179656 | tf_op jit(solution)/shard_map/ppermute | solution.py:664
  41.2 1.3 collective-permute-start.8
  42.5 2.5 %collective-permute-start.9 = (bf16[3,512,128]{2,1,0:T(8,128)(2,1)}, bf16[3,512,128]{2,1,0:T(8,128)(2,1)S(1)}, u32[]{:S(2)}, u32[]{:S(2)}) collective-permute-start(bf16[3,512,128]{2,1,0:T(8,128)(2,1)} %bitcast.111), channel_id=1, source_target_pairs={{0,1},{1,2},{2,3},{4,5},{5,6},{6,7},{8,9},{9,10},{10,11},{12,13},{... | collective-permute-start | bytes 1179656 | tf_op jit(solution)/shard_map/ppermute | solution.py:664
  45.0 1.4 copy.49
  46.7 5.5 %query.1 = (bf16[2,1536,128]{2,1,0:T(8,128)(2,1)}, f32[1536,128]{1,0:T(8,128)}) custom-call(bf16[1536,512]{1,0:T(8,128)(2,1)} %get-tuple-element.72.hidden_ref, s32[1536,2]{1,0:T(8,128)} %bitcast.92, bf16[512,768]{1,0:T(8,128)(2,1)} %get-tuple-element.73.weight_ref), custom_call_target="tpu_custom_call" | custom-call | flops 2013265920 | bytes 3145728 | tf_op jit(solution)/shard_map/query/pallas_call | solution.py:850
  52.8 7.4 %collective-permute-done.8.rest_1_ = bf16[3,512,128]{2,1,0:T(8,128)(2,1)S(1)} collective-permute-done((bf16[3,512,128]{2,1,0:T(8,128)(2,1)}, bf16[3,512,128]{2,1,0:T(8,128)(2,1)S(1)}, u32[]{:S(2)}, u32[]{:S(2)}) %collective-permute-start.8) | collective-permute-done | bytes 393248 | tf_op jit(solution)/shard_map/ppermute | solution.py:664
  61.6 6.6 %attend.1 = (f32[2,1536,128]{2,1,0:T(8,128)}, f32[3,2,512]{2,1,0:T(2,128)}) custom-call(s32[4]{0:T(128)} %pad_add_fusion.1.bounds_ref, bf16[2,1536,128]{2,1,0:T(8,128)(2,1)} %get-tuple-element.75.q_ref, s32[3,1,512]{2,1,0:T(1,128)} %max.18.start_ref, bf16[3,512,128]{2,1,0:T(8,128)(2,1)} %copy-done.8, bf16[3,512,128]{2,1,0:T(8,128)(2,1)} %copy-done.9, ...), custom_call_target="tpu_custom_call" | custom-call | flops 1610612736 | bytes 3145728 | tf_op jit(solution)/shard_map/attend/pallas_call | solution.py:875
  68.2 14.4 %all-gather.3.cloned.1.call-done = bf16[4608,512]{1,0:T(8,128)(2,1)} async-done(((bf16[144,512]{1,0:T(8,128)(2,1)}), bf16[4608,512]{1,0:T(8,128)(2,1)}) %all-gather.3.cloned.1.call-update) | async-done | bytes 4718608 | tf_op jit(solution)/shard_map/all_gather | solution.py:783
  82.6 39.3 %mid.1 = (bf16[1536,512]{1,0:T(8,128)(2,1)}, f32[1536,512]{1,0:T(8,128)}, bf16[2,1536,128]{2,1,0:T(8,128)(2,1)}, f32[1536,128]{1,0:T(8,128)}, bf16[4,4,160,512]{...) custom-call(bf16[1536,512]{1,0:T(8,128)(2,1)} %bitcast.89, bf16[1536,512]{1,0:T(8,128)(2,1)} %bitcast.108, ...), custom_call_target="tpu_custom_call" | custom-call | flops 21743271936 | bytes 12582912 | tf_op jit(solution)/shard_map/mid/pallas_call | solution.py:904
  122.2 4.9 %collective-permute-done.10 = bf16[4,4,160,512]{3,2,1,0:T(8,128)(2,1)S(1)} collective-permute-done((bf16[4,4,160,512]{3,2,1,0:T(8,128)(2,1)}, bf16[4,4,160,512]{3,2,1,0:T(8,128)(2,1)S(1)}, u32[]{:S(2)}, u32[]{:S(2)}) %collective-permute-start.10) | collective-permute-done | bytes 2621472 | tf_op jit(solution)/shard_map/ppermute | solution.py:658
  127.1 2.5 %add.120 = bf16[4,4,160,512]{3,2,1,0:T(8,128)(2,1)S(1)} add(bf16[4,4,160,512]{3,2,1,0:T(8,128)(2,1)} %get-tuple-element.80, bf16[4,4,160,512]{3,2,1,0:T(8,128)(2,1)S(1)} %collective-permute-done.10) | non-fusion elementwise | flops 1310720 | bytes 7864320 | tf_op jit(solution)/shard_map/add | solution.py:971
  130.8 1.5 collective-permute-start.12
  132.3 1.0 dynamic-slice_bitcast_fusion.1
  133.9 6.3 %attend_back.2 = (bf16[2,1536,128]{2,1,0:T(8,128)(2,1)}, bf16[4,2,512,128]{3,2,1,0:T(8,128)(2,1)}) custom-call(s32[4]{0:T(128)} %pad_add_fusion.1.bounds_ref, bf16[2,1536,128]{2,1,0:T(8,128)(2,1)} %get-tuple-element.75.q_ref, bf16[2,1536,128]{2,1,0:T(8,128)(2,1)} %get-tuple-element.84.grad_ref, f32[1536,128]{1,0:T(8,128)} %get-tuple-element.99.side_ref.grad_logit_ref, ...), custom_call_target="tpu_custom_call" | custom-call | flops 2684354560 | bytes 4194304 | tf_op jit(solution)/shard_map/attend_back/pallas_call | solution.py:1019
  140.2 12.6 %all-to-all-start = ((bf16[4,2,512,128]{3,2,1,0:T(8,128)(2,1)}), bf16[4,2,512,128]{3,2,1,0:T(8,128)(2,1)S(1)}, u32[]{:S(2)}, u32[]{:S(2)}) async-start(bf16[4,2,512,128]{3,2,1,0:T(8,128)(2,1)} %get-tuple-element.108), calls=%async_computation | async-start | bytes 2097152 | tf_op jit(solution)/shard_map/all_to_all | solution.py:1047
  152.7 1.3 add.127
  154.3 2.1 collective-permute-start.13
  156.4 1.5 collective-permute-start.14
  157.9 4.6 %attend_back.3 = (bf16[2,1536,128]{2,1,0:T(8,128)(2,1)}, bf16[4,1,512,128]{3,2,1,0:T(8,128)(2,1)}) custom-call(s32[4]{0:T(128)} %pad_add_fusion.1.bounds_ref, bf16[2,1536,128]{2,1,0:T(8,128)(2,1)} %get-tuple-element.75.q_ref, bf16[2,1536,128]{2,1,0:T(8,128)(2,1)} %get-tuple-element.84.grad_ref, ...), custom_call_target="tpu_custom_call", output_to_operand_aliasing={{0}: (10, {})} | custom-call | flops 1342177280 | bytes 2097152 | tf_op jit(solution)/shard_map/attend_back/pallas_call | solution.py:1019
  162.4 10.8 %collective-permute-done.13 = bf16[4,80,512]{2,1,0:T(8,128)(2,1)S(1)} collective-permute-done((bf16[4,80,512]{2,1,0:T(8,128)(2,1)S(1)}, bf16[4,80,512]{2,1,0:T(8,128)(2,1)S(1)}, u32[]{:S(2)}, u32[]{:S(2)}) %collective-permute-start.13) | collective-permute-done | bytes 327712 | tf_op jit(solution)/shard_map/ppermute | solution.py:658
  173.6 3.7 %all-to-all-start.1 = ((bf16[4,1,512,128]{3,2,1,0:T(8,128)(2,1)}), bf16[4,1,512,128]{3,2,1,0:T(8,128)(2,1)S(1)}, u32[]{:S(2)}, u32[]{:S(2)}) async-start(bf16[4,1,512,128]{3,2,1,0:T(8,128)(2,1)} %get-tuple-element.109), calls=%async_computation.1 | async-start | bytes 1048576 | tf_op jit(solution)/shard_map/all_to_all | solution.py:1047
  177.4 7.5 %query_grad.1 = (f32[1536,512]{1,0:T(8,128)}, bf16[512,512]{1,0:T(8,128)(2,1)}, f32[512,128]{1,0:T(8,128)}) custom-call(bf16[1536,512]{1,0:T(8,128)(2,1)} %get-tuple-element.72.hidden_ref, bf16[2,1536,128]{2,1,0:T(8,128)(2,1)} %get-tuple-element.98.grad_q_ref, f32[1536,128]{1,0:T(8,128)} %get-tuple-element.99.side_ref.grad_logit_ref, ...), custom_call_target="tpu_custom_call" | custom-call | flops 2415919104 | bytes 9437184 | tf_op jit(solution)/shard_map/query_grad/pallas_call | solution.py:1078
  185.1 1.1 collective-permute-start.16
  187.0 9.2 %last.1 = (f32[1536,512]{1,0:T(8,128)}, bf16[4,4,16,768]{3,2,1,0:T(8,128)(2,1)}, bf16[4,4,16,768]{3,2,1,0:T(8,128)(2,1)}) custom-call(s32[1]{0:T(128)} %bitcast.3.core_ref, bf16[1536,512]{1,0:T(8,128)(2,1)} %bitcast.90, bf16[1536,512]{1,0:T(8,128)(2,1)} %get-tuple-element.72.hidden_ref, f32[1536,512]{1,0:T(8,128)} %get-tuple-element.104.partial_ref, ...), custom_call_target="tpu_custom_call" | custom-call | flops 402653184 | bytes 12582912 | tf_op jit(solution)/shard_map/last/pallas_call | solution.py:1112
  196.3 1.9 collective-permute-done.17
  198.2 1.1 add.136
  199.3 1.8 collective-permute-start.18
  201.1 1.5 collective-permute-start.19
  202.8 1.4 collective-permute-done.18
  204.2 2.6 %collective-permute-done.19 = bf16[4,16,768]{2,1,0:T(8,128)(2,1)S(1)} collective-permute-done((bf16[4,16,768]{2,1,0:T(8,128)(2,1)S(1)}, bf16[4,16,768]{2,1,0:T(8,128)(2,1)S(1)}, u32[]{:S(2)}, u32[]{:S(2)}) %collective-permute-start.19) | collective-permute-done | bytes 98336 | tf_op jit(solution)/shard_map/ppermute | solution.py:658
  206.8 1.2 collective-permute-done.20
  208.7 1.0 collective-permute-start.21
  209.7 2.9 %collective-permute-start.22 = (bf16[16,768]{1,0:T(8,128)(2,1)S(1)}, bf16[16,768]{1,0:T(8,128)(2,1)S(1)}, u32[]{:S(2)}, u32[]{:S(2)}) collective-permute-start(bf16[16,768]{1,0:T(8,128)(2,1)S(1)} %get-tuple-element.202), channel_id=1, source_target_pairs={{0,16},{4,20},{8,24},{12,28},{16,0},{20,4},{24,8},{28,12},{1,17},{... | collective-permute-start | bytes 73736 | tf_op jit(solution)/shard_map/ppermute | solution.py:658
  213.8 1.7 finish_second.1
  215.6 2.7 %collective-permute-done.23.refs_3_ = bf16[16,768]{1,0:T(8,128)(2,1)S(1)} collective-permute-done((bf16[16,768]{1,0:T(8,128)(2,1)S(1)}, bf16[16,768]{1,0:T(8,128)(2,1)S(1)}, u32[]{:S(2)}, u32[]{:S(2)}) %collective-permute-start.23) | collective-permute-done | bytes 24608 | tf_op jit(solution)/shard_map/ppermute | solution.py:658
  218.9 1.5 finish_first.1
  (78 shorter events, 14.6 us)
Async XLA Ops:
  7.2 23.0 %copy-start.7 = (s32[3,1,512,2]{2,3,1,0:T(2,128)S(1)}, s32[3,1,512,2]{2,3,1,0:T(2,128)}, u32[]{:S(2)}) copy-start(s32[3,1,512,2]{2,3,1,0:T(2,128)} %param.17) | copy-start | bytes 36868
  7.2 75.4 %all-gather.3.cloned.1.call-start = ((), (), s32[]{:S(2)}) async-start(), calls=%async_computation.2 | async-start | bytes 4866048 | tf_op jit(solution)/shard_map/all_gather | solution.py:783
  9.1 7.1 %collective-permute-start = (bf16[16,768]{1,0:T(8,128)(2,1)}, bf16[16,768]{1,0:T(8,128)(2,1)S(1)}, u32[]{:S(2)}, u32[]{:S(2)}) collective-permute-start(bf16[16,768]{1,0:T(8,128)(2,1)} %get-tuple-element.71), channel_id=1, source_target_pairs={{0,8},{4,12},{8,0},{12,4},{16,24},{20,28},{24,16},{28,20},{1,9},{5... | collective-permute-start | bytes 73736 | tf_op jit(solution)/shard_map/ppermute | solution.py:658
  12.2 5.3 %collective-permute-start.1 = (bf16[16,768]{1,0:T(8,128)(2,1)}, bf16[16,768]{1,0:T(8,128)(2,1)S(1)}, u32[]{:S(2)}, u32[]{:S(2)}) collective-permute-start(bf16[16,768]{1,0:T(8,128)(2,1)} %get-tuple-element.71), channel_id=1, source_target_pairs={{0,16},{4,20},{8,24},{12,28},{16,0},{20,4},{24,8},{28,12},{1,17},{... | collective-permute-start | bytes 73736 | tf_op jit(solution)/shard_map/ppermute | solution.py:658
  14.8 5.8 %collective-permute-start.2 = (bf16[16,768]{1,0:T(8,128)(2,1)}, bf16[16,768]{1,0:T(8,128)(2,1)S(1)}, u32[]{:S(2)}, u32[]{:S(2)}) collective-permute-start(bf16[16,768]{1,0:T(8,128)(2,1)} %get-tuple-element.71), channel_id=1, source_target_pairs={{0,24},{4,28},{8,16},{12,20},{16,8},{20,12},{24,0},{28,4},{1,25},{... | collective-permute-start | bytes 73736 | tf_op jit(solution)/shard_map/ppermute | solution.py:658
  21.4 6.4 %collective-permute-start.3 = (bf16[4,16,768]{2,1,0:T(8,128)(2,1)S(1)}, bf16[4,16,768]{2,1,0:T(8,128)(2,1)S(1)}, u32[]{:S(2)}, u32[]{:S(2)}) collective-permute-start(bf16[4,16,768]{2,1,0:T(8,128)(2,1)S(1)} %get-tuple-element.206), channel_id=1, source_target_pairs={{0,1},{1,0},{2,3},{3,2},{4,5},{5,4},{6,7},{7,6},{8,9},{9,8},{10,11... | collective-permute-start | bytes 294920 | tf_op jit(solution)/shard_map/ppermute | solution.py:658
  22.9 5.0 %collective-permute-start.4 = (bf16[4,16,768]{2,1,0:T(8,128)(2,1)S(1)}, bf16[4,16,768]{2,1,0:T(8,128)(2,1)S(1)}, u32[]{:S(2)}, u32[]{:S(2)}) collective-permute-start(bf16[4,16,768]{2,1,0:T(8,128)(2,1)S(1)} %get-tuple-element.206), channel_id=1, source_target_pairs={{0,2},{1,3},{2,0},{3,1},{4,6},{5,7},{6,4},{7,5},{8,10},{9,11},{10,... | collective-permute-start | bytes 294920 | tf_op jit(solution)/shard_map/ppermute | solution.py:658
  24.5 5.5 %collective-permute-start.5 = (bf16[4,16,768]{2,1,0:T(8,128)(2,1)S(1)}, bf16[4,16,768]{2,1,0:T(8,128)(2,1)S(1)}, u32[]{:S(2)}, u32[]{:S(2)}) collective-permute-start(bf16[4,16,768]{2,1,0:T(8,128)(2,1)S(1)} %get-tuple-element.206), channel_id=1, source_target_pairs={{0,3},{1,2},{2,1},{3,0},{4,7},{5,6},{6,5},{7,4},{8,11},{9,10},{10,... | collective-permute-start | bytes 294920 | tf_op jit(solution)/shard_map/ppermute | solution.py:658
  30.0 3.2 %copy-start.2 = (bf16[4,4,16,768]{3,2,1,0:T(8,128)(2,1)}, bf16[4,4,16,768]{3,2,1,0:T(8,128)(2,1)S(1)}, u32[]{:S(2)}) copy-start(bf16[4,4,16,768]{3,2,1,0:T(8,128)(2,1)S(1)} %pad_maximum_fusion.1.mine_ref) | copy-start | bytes 1179652
  30.0 3.2 %collective-permute-start.6 = (bf16[4,4,16,768]{3,2,1,0:T(8,128)(2,1)S(1)}, bf16[4,4,16,768]{3,2,1,0:T(8,128)(2,1)S(1)}, u32[]{:S(2)}, u32[]{:S(2)}) collective-permute-start(bf16[4,4,16,768]{3,2,1,0:T(8,128)(2,1)S(1)} %pad_maximum_fusion.1.mine_ref), channel_id=1, source_target_pairs={{0,4},{4,0},{8,12},{12,8},{16,20},{20,16},{24,28},{28,24},{1,5},{5... | collective-permute-start | bytes 1179656 | tf_op jit(solution)/shard_map/ppermute | solution.py:658
  33.2 0.8 copy-start.3
  38.8 14.0 %collective-permute-start.7 = (bf16[3,512,128]{2,1,0:T(8,128)(2,1)}, bf16[3,512,128]{2,1,0:T(8,128)(2,1)S(1)}, u32[]{:S(2)}, u32[]{:S(2)}) collective-permute-start(bf16[3,512,128]{2,1,0:T(8,128)(2,1)} %bitcast.109), channel_id=1, source_target_pairs={{0,3},{4,7},{8,11},{12,15},{16,19},{20,23},{24,27},{28,31}} | collective-permute-start | bytes 1179656 | tf_op jit(solution)/shard_map/ppermute | solution.py:664
  41.2 19.0 %collective-permute-start.8 = (bf16[3,512,128]{2,1,0:T(8,128)(2,1)}, bf16[3,512,128]{2,1,0:T(8,128)(2,1)S(1)}, u32[]{:S(2)}, u32[]{:S(2)}) collective-permute-start(bf16[3,512,128]{2,1,0:T(8,128)(2,1)} %bitcast.110), channel_id=1, source_target_pairs={{0,2},{1,3},{4,6},{5,7},{8,10},{9,11},{12,14},{13,15},{16,18},{17,... | collective-permute-start | bytes 1179656 | tf_op jit(solution)/shard_map/ppermute | solution.py:664
  42.5 18.3 %collective-permute-start.9 = (bf16[3,512,128]{2,1,0:T(8,128)(2,1)}, bf16[3,512,128]{2,1,0:T(8,128)(2,1)S(1)}, u32[]{:S(2)}, u32[]{:S(2)}) collective-permute-start(bf16[3,512,128]{2,1,0:T(8,128)(2,1)} %bitcast.111), channel_id=1, source_target_pairs={{0,1},{1,2},{2,3},{4,5},{5,6},{6,7},{8,9},{9,10},{10,11},{12,13},{... | collective-permute-start | bytes 1179656 | tf_op jit(solution)/shard_map/ppermute | solution.py:664
  52.8 8.0 %copy-start.8 = (bf16[3,512,128]{2,1,0:T(8,128)(2,1)}, bf16[3,512,128]{2,1,0:T(8,128)(2,1)S(1)}, u32[]{:S(2)}) copy-start(bf16[3,512,128]{2,1,0:T(8,128)(2,1)S(1)} %collective-permute-done.7.rest_0_) | copy-start | bytes 1179652
  60.2 0.8 copy-start.9
  60.8 0.7 copy-start.10
  121.9 5.2 %collective-permute-start.10 = (bf16[4,4,160,512]{3,2,1,0:T(8,128)(2,1)}, bf16[4,4,160,512]{3,2,1,0:T(8,128)(2,1)S(1)}, u32[]{:S(2)}, u32[]{:S(2)}) collective-permute-start(bf16[4,4,160,512]{3,2,1,0:T(8,128)(2,1)} %get-tuple-element.81), channel_id=1, source_target_pairs={{0,4},{4,0},{8,12},{12,8},{16,20},{20,16},{24,28},{28,24},{1,5},{5... | collective-permute-start | bytes 7864328 | tf_op jit(solution)/shard_map/ppermute | solution.py:658
  130.8 21.9 %collective-permute-start.12 = (bf16[4,2,80,512]{3,2,1,0:T(8,128)(2,1)}, bf16[4,2,80,512]{3,2,1,0:T(8,128)(2,1)S(1)}, u32[]{:S(2)}, u32[]{:S(2)}) collective-permute-start(bf16[4,2,80,512]{3,2,1,0:T(8,128)(2,1)} %get-tuple-element.186), channel_id=1, source_target_pairs={{0,2},{1,3},{2,0},{3,1},{4,6},{5,7},{6,4},{7,5},{8,10},{9,11},{10,... | collective-permute-start | bytes 1966088 | tf_op jit(solution)/shard_map/ppermute | solution.py:658
  133.3 19.4 %collective-permute-start.11 = (bf16[4,2,80,512]{3,2,1,0:T(8,128)(2,1)}, bf16[4,2,80,512]{3,2,1,0:T(8,128)(2,1)}, u32[]{:S(2)}, u32[]{:S(2)}) collective-permute-start(bf16[4,2,80,512]{3,2,1,0:T(8,128)(2,1)} %get-tuple-element.188), channel_id=1, source_target_pairs={{0,1},{1,0},{2,3},{3,2},{4,5},{5,4},{6,7},{7,6},{8,9},{9,8},{10,11... | collective-permute-start | bytes 1966088 | tf_op jit(solution)/shard_map/ppermute | solution.py:658
  140.2 33.4 %all-to-all-start = ((bf16[4,2,512,128]{3,2,1,0:T(8,128)(2,1)}), bf16[4,2,512,128]{3,2,1,0:T(8,128)(2,1)S(1)}, u32[]{:S(2)}, u32[]{:S(2)}) async-start(bf16[4,2,512,128]{3,2,1,0:T(8,128)(2,1)} %get-tuple-element.108), calls=%async_computation | async-start | bytes 2097152 | tf_op jit(solution)/shard_map/all_to_all | solution.py:1047
  154.3 18.9 %collective-permute-start.13 = (bf16[4,80,512]{2,1,0:T(8,128)(2,1)S(1)}, bf16[4,80,512]{2,1,0:T(8,128)(2,1)S(1)}, u32[]{:S(2)}, u32[]{:S(2)}) collective-permute-start(bf16[4,80,512]{2,1,0:T(8,128)(2,1)S(1)} %get-tuple-element.208), channel_id=1, source_target_pairs={{0,2},{1,3},{2,0},{3,1},{4,6},{5,7},{6,4},{7,5},{8,10},{9,11},{10,... | collective-permute-start | bytes 983048 | tf_op jit(solution)/shard_map/ppermute | solution.py:658
  156.4 16.8 %collective-permute-start.14 = (bf16[4,80,512]{2,1,0:T(8,128)(2,1)S(1)}, bf16[4,80,512]{2,1,0:T(8,128)(2,1)S(1)}, u32[]{:S(2)}, u32[]{:S(2)}) collective-permute-start(bf16[4,80,512]{2,1,0:T(8,128)(2,1)S(1)} %get-tuple-element.192), channel_id=1, source_target_pairs={{0,1},{1,0},{2,3},{3,2},{4,5},{5,4},{6,7},{7,6},{8,9},{9,8},{10,11... | collective-permute-start | bytes 983048 | tf_op jit(solution)/shard_map/ppermute | solution.py:658
  173.5 11.4 %collective-permute-start.15 = (bf16[2,160,512]{2,1,0:T(8,128)(2,1)S(1)}, bf16[2,160,512]{2,1,0:T(8,128)(2,1)S(1)}, u32[]{:S(2)}, u32[]{:S(2)}) collective-permute-start(bf16[2,160,512]{2,1,0:T(8,128)(2,1)S(1)} %get-tuple-element.191), channel_id=1, source_target_pairs={{0,8},{4,12},{8,0},{12,4},{16,24},{20,28},{24,16},{28,20},{1,9},{5... | collective-permute-start | bytes 983048 | tf_op jit(solution)/shard_map/ppermute | solution.py:658
  173.6 11.3 %copy-start = (bf16[4,2,512,128]{3,2,1,0:T(8,128)(2,1)}, bf16[4,2,512,128]{3,2,1,0:T(8,128)(2,1)S(1)}, u32[]{:S(2)}) copy-start(bf16[4,2,512,128]{3,2,1,0:T(8,128)(2,1)S(1)} %all-to-all-done.rest_0_) | copy-start | bytes 3145732
  173.6 12.5 %all-to-all-start.1 = ((bf16[4,1,512,128]{3,2,1,0:T(8,128)(2,1)}), bf16[4,1,512,128]{3,2,1,0:T(8,128)(2,1)S(1)}, u32[]{:S(2)}, u32[]{:S(2)}) async-start(bf16[4,1,512,128]{3,2,1,0:T(8,128)(2,1)} %get-tuple-element.109), calls=%async_computation.1 | async-start | bytes 1048576 | tf_op jit(solution)/shard_map/all_to_all | solution.py:1047
  185.1 11.1 %collective-permute-start.16 = (bf16[160,512]{1,0:T(8,128)(2,1)S(1)}, bf16[160,512]{1,0:T(8,128)(2,1)S(1)}, u32[]{:S(2)}, u32[]{:S(2)}) collective-permute-start(bf16[160,512]{1,0:T(8,128)(2,1)S(1)} %get-tuple-element.199), channel_id=1, source_target_pairs={{0,16},{4,20},{8,24},{12,28},{16,0},{20,4},{24,8},{28,12},{1,17},{... | collective-permute-start | bytes 491528 | tf_op jit(solution)/shard_map/ppermute | solution.py:658
  186.2 0.8 copy-start.1
  196.2 2.0 collective-permute-start.17
  199.3 4.9 %collective-permute-start.18 = (bf16[4,16,768]{2,1,0:T(8,128)(2,1)S(1)}, bf16[4,16,768]{2,1,0:T(8,128)(2,1)S(1)}, u32[]{:S(2)}, u32[]{:S(2)}) collective-permute-start(bf16[4,16,768]{2,1,0:T(8,128)(2,1)S(1)} %get-tuple-element.196), channel_id=1, source_target_pairs={{0,1},{1,0},{2,3},{3,2},{4,5},{5,4},{6,7},{7,6},{8,9},{9,8},{10,11... | collective-permute-start | bytes 294920 | tf_op jit(solution)/shard_map/ppermute | solution.py:658
  201.1 5.7 %collective-permute-start.19 = (bf16[4,16,768]{2,1,0:T(8,128)(2,1)S(1)}, bf16[4,16,768]{2,1,0:T(8,128)(2,1)S(1)}, u32[]{:S(2)}, u32[]{:S(2)}) collective-permute-start(bf16[4,16,768]{2,1,0:T(8,128)(2,1)S(1)} %get-tuple-element.198), channel_id=1, source_target_pairs={{0,2},{1,3},{2,0},{3,1},{4,6},{5,7},{6,4},{7,5},{8,10},{9,11},{10,... | collective-permute-start | bytes 294920 | tf_op jit(solution)/shard_map/ppermute | solution.py:658
  202.5 5.5 %collective-permute-start.20 = (bf16[4,16,768]{2,1,0:T(8,128)(2,1)S(1)}, bf16[4,16,768]{2,1,0:T(8,128)(2,1)S(1)}, u32[]{:S(2)}, u32[]{:S(2)}) collective-permute-start(bf16[4,16,768]{2,1,0:T(8,128)(2,1)S(1)} %get-tuple-element.197), channel_id=1, source_target_pairs={{0,3},{1,2},{2,1},{3,0},{4,7},{5,6},{6,5},{7,4},{8,11},{9,10},{10,... | collective-permute-start | bytes 294920 | tf_op jit(solution)/shard_map/ppermute | solution.py:658
  208.7 6.8 %collective-permute-start.21 = (bf16[16,768]{1,0:T(8,128)(2,1)S(1)}, bf16[16,768]{1,0:T(8,128)(2,1)S(1)}, u32[]{:S(2)}, u32[]{:S(2)}) collective-permute-start(bf16[16,768]{1,0:T(8,128)(2,1)S(1)} %get-tuple-element.203), channel_id=1, source_target_pairs={{0,8},{4,12},{8,0},{12,4},{16,24},{20,28},{24,16},{28,20},{1,9},{5... | collective-permute-start | bytes 73736 | tf_op jit(solution)/shard_map/ppermute | solution.py:658
  209.7 5.9 %collective-permute-start.22 = (bf16[16,768]{1,0:T(8,128)(2,1)S(1)}, bf16[16,768]{1,0:T(8,128)(2,1)S(1)}, u32[]{:S(2)}, u32[]{:S(2)}) collective-permute-start(bf16[16,768]{1,0:T(8,128)(2,1)S(1)} %get-tuple-element.202), channel_id=1, source_target_pairs={{0,16},{4,20},{8,24},{12,28},{16,0},{20,4},{24,8},{28,12},{1,17},{... | collective-permute-start | bytes 73736 | tf_op jit(solution)/shard_map/ppermute | solution.py:658
  212.6 5.6 %collective-permute-start.23 = (bf16[16,768]{1,0:T(8,128)(2,1)S(1)}, bf16[16,768]{1,0:T(8,128)(2,1)S(1)}, u32[]{:S(2)}, u32[]{:S(2)}) collective-permute-start(bf16[16,768]{1,0:T(8,128)(2,1)S(1)} %get-tuple-element.201), channel_id=1, source_target_pairs={{0,24},{4,28},{8,16},{12,20},{16,8},{20,12},{24,0},{28,4},{1,25},{... | collective-permute-start | bytes 73736 | tf_op jit(solution)/shard_map/ppermute | solution.py:658
  215.6 2.7 %copy-start.4 = (bf16[16,768]{1,0:T(8,128)(2,1)}, bf16[16,768]{1,0:T(8,128)(2,1)S(1)}, u32[]{:S(2)}) copy-start(bf16[16,768]{1,0:T(8,128)(2,1)S(1)} %collective-permute-done.21.refs_1_) | copy-start | bytes 73732
  215.6 2.7 %copy-start.5 = (bf16[16,768]{1,0:T(8,128)(2,1)}, bf16[16,768]{1,0:T(8,128)(2,1)S(1)}, u32[]{:S(2)}) copy-start(bf16[16,768]{1,0:T(8,128)(2,1)S(1)} %collective-permute-done.22.refs_2_) | copy-start | bytes 73732
  218.2 0.6 copy-start.6
Sparse Core Ops, SparseCore 0:
  10.9 71.5 all-gather.2

commit v4 on v3

--- a/solution.py
+++ b/solution.py
@@ -959,35 +959,43 @@
         grads_b = [at_index(packed, core_index[0], 1), at_index(packed, 1 - core_index[0], 1)]
 
     keep, send = grads_b
-    bits = shards.bit_length() - 1
-    order = [1 << at for at in range(bits)]
-    orders = (order, order[bits // 2 :] + order[: bits // 2])
-    half_rows = keep.shape[2] // 2
-    remaining = [list(reversed(order)), list(reversed(order))]
-    halves = [None, None]
-    arriving = swapped(send, "dp", 1)
-
-    def core_step():
-        held = keep + arriving
-        held = held.reshape((dp // 2,) + (2,) * bits + held.shape[2:])
-        halves[0] = held[..., :half_rows, :]
-        halves[1] = held[..., half_rows:, :]
+    bits, z_bits = shards.bit_length() - 1, (dp // 2).bit_length() - 1
+    along_x = [("seq", 1 << at) for at in range(bits // 2)]
+    along_y = [("seq", 1 << at) for at in range(bits // 2, bits)]
+    along_z = [("dp", 2 << at) for at in range(z_bits)]
+    near, far = along_z[:1], along_z[1:]
+    dims = along_z[::-1] + along_y[::-1] + along_x[::-1]
+    orders = [along_x + along_y + near, along_y + near + along_x, near + along_x + along_y]
+    third = -(-keep.shape[2] // 24) * 8 if keep.shape[2] % 8 == 0 else -(-keep.shape[2] // 3)
+    cuts = [0, third, 2 * third, keep.shape[2]]
+    held = keep + swapped(send, "dp", 1)
+    held = held.reshape((2,) * len(dims) + held.shape[2:])
+    parts = [
+        (held[..., low:high, :], dims, order)
+        for low, high, order in zip(cuts[:-1], cuts[1:], orders)
+    ]
+
+    def send_parts(parts):
+        stays, arrives = [], []
+        for value, left, order in parts:
+            axis, mask = order[0]
+            dim, bit = left.index(order[0]), (lax.axis_index(axis) // mask) % 2
+            left = left[:dim] + left[dim + 1 :]
+            stays.append((at_index(value, bit, dim), left, order[1:]))
+            arrives.append(swapped(at_index(value, 1 - bit, dim), axis, mask))
+        return stays, arrives
+
+    def behind(parts, other):
+        *values, other = together(*[value for value, _, _ in parts], other)
+        return [(value,) + part[1:] for value, part in zip(values, parts)], other
+
+    def joined(parts, arrives):
+        return [(part[0] + piece,) + part[1:] for part, piece in zip(parts, arrives)]
 
     leave_spec = pl.BlockSpec((shards, 1, local_len, LANES), lambda b, *_: (0, b, 0, 0))
 
-    def send_halves(stage):
-        for part in range(2):
-            mask = orders[part][stage]
-            dim = 1 + remaining[part].index(mask)
-            remaining[part].remove(mask)
-            bit = (own_shard // mask) % 2
-            halves[part] = at_index(halves[part], bit, dim), at_index(halves[part], 1 - bit, dim)
-        return [swapped(halves[part][1], "seq", orders[part][stage]) for part in range(2)]
-
-    core_step()
-    pending = send_halves(0)
-    stage = 1
-    bounds_now, *kept = together(bounds, halves[0][0], halves[1][0])
+    parts, arrives = send_parts(parts)
+    parts, bounds_now = behind(parts, bounds)
     grad_queries = None
     returned = []
     splits = [0, max(1, micro_count - 1), micro_count] if micro_count > 1 else [0, 1]
@@ -1045,36 +1053,14 @@
             name="attend_back",
         )(bounds_now, *operands)
         returned.append(lax.all_to_all(leave, "seq", 0, 0, tiled=True))
-        if micro == 0 and stage < bits:
-            pending[0], pending[1], grad_queries = together(*pending, grad_queries)
-            halves[0], halves[1] = kept[0] + pending[0], kept[1] + pending[1]
-            pending = send_halves(stage)
-            stage += 1
-            bounds_now, *kept = together(bounds, halves[0][0], halves[1][0])
-
-    pending[0], pending[1], grad_queries = together(*pending, grad_queries)
-    halves[0], halves[1] = kept[0] + pending[0], kept[1] + pending[1]
-    while stage < bits:
-        pending = send_halves(stage)
-        halves[0], halves[1] = halves[0][0] + pending[0], halves[1][0] + pending[1]
-        stage += 1
-    own_b = jnp.concatenate(halves, 1)
-    z_me = lax.axis_index("dp") // 2
-    z_bits = (dp // 2).bit_length() - 1
-    own_b = own_b.reshape((2,) * z_bits + own_b.shape[1:])
-    z_stage = 0
-
-    def z_split(value):
-        bit = (z_me >> z_stage) & 1
-        dim = z_bits - 1 - z_stage
-        return at_index(value, bit, dim), at_index(value, 1 - bit, dim)
-
-    arriving_b = None
-    if z_bits:
-        kept_b, send_b = z_split(own_b)
-        side, kept_b = together(side, kept_b)
-        arriving_b = swapped(send_b, "dp", 2)
-        z_stage = 1
+        if parts[0][2]:
+            *arrives, grad_queries = together(*arrives, grad_queries)
+            parts, arrives = send_parts(joined(parts, arrives))
+            if stop < micro_count:
+                parts, bounds_now = behind(parts, bounds)
+            else:
+                parts, side = behind(parts, side)
+
     partial_hidden, d_query, d_router = pl.pallas_call(
         functools.partial(query_grad_kernel, experts, head),
         grid=(steps,),
@@ -1099,12 +1085,13 @@
         cost_estimate=cost(4 * rows_all * width * a_cols, rows_all * width * 12),
         name="query_grad",
     )(hidden, grad_queries, side, group_a)
-    if z_bits > 1:
-        arriving_b, partial_hidden = together(arriving_b, partial_hidden)
-        kept_b, send_b = z_split(kept_b + arriving_b)
-        partial_hidden, kept_b = together(partial_hidden, kept_b)
-        arriving_b = swapped(send_b, "dp", 4)
-        z_stage = 2
+    *arrives, partial_hidden = together(*arrives, partial_hidden)
+    parts = joined(parts, arrives)
+    while parts[0][2]:
+        parts = joined(*send_parts(parts))
+    whole = jnp.concatenate([value for value, _, _ in parts], -2)
+    parts, arrives = send_parts([(whole, parts[0][1], far)])
+    parts, partial_hidden = behind(parts, partial_hidden)
     if aligned:
         small_shapes = [(dp // 2, shards, own_rows, a_cols)] * 2
     else:
@@ -1141,15 +1128,14 @@
         by_core = small[0].reshape(dp // 2, 2, shards, own_rows, a_cols)
         small = [at_index(by_core, core_index[0], 1), at_index(by_core, 1 - core_index[0], 1)]
     keep_small, send_small = small
-    if arriving_b is not None:
-        send_small, arriving_b = together(send_small, arriving_b)
-        own_b = kept_b + arriving_b
-    while z_stage < z_bits:
-        kept_b, send_b = z_split(own_b)
-        own_b = kept_b + swapped(send_b, "dp", 2 << z_stage)
-        z_stage += 1
+    *arrives, send_small = together(*arrives, send_small)
+    parts = joined(parts, arrives)
+    while parts[0][2]:
+        parts = joined(*send_parts(parts))
+    own_b = parts[0][0]
     held = keep_small + swapped(send_small, "dp", 1)
     held = summed_direct(held, 1, "seq", 1).astype(BF16)
+    z_me = lax.axis_index("dp") // 2
     ends = [at_index(held, z_me, 0)]
     ends += [swapped(at_index(held, z_me ^ at, 0), "dp", 2 * at) for at in range(1, dp // 2)]
 

time: 228 us -> 227 us (level)
  waiting for transfers between devices: 55.7 us -> 46.5 us
  starting transfers between devices: 47 us -> 52.5 us
    ppermute x21 -> x25, starting transfers between devices: 24.4 us -> 33.2 us  [swapped(): return lax.ppermute(value, axis, [(at, at ^ mask) for at in range(count)])]
    ppermute x21 -> x25, waiting for transfers between devices: 33.3 us -> 25.9 us  [swapped(): return lax.ppermute(value, axis, [(at, at ^ mask) for at in range(count)])]
    all_to_all x2, starting transfers between devices: 16.3 us -> 13 us  [on_device(): returned.append(lax.all_to_all(leave, 'seq', 0, 0, tiled=True))]
    add x7 -> x11, other arithmetic: 4.96 us -> 6.87 us  [the longest x10 4.33 us: joined(): part[0] + piece]
    unnamed x25 -> x23, local copies, waits for them, and re-layouts: 4.92 us -> 5.78 us
  transfers between devices with their start and end apart: 27 -> 31, of which waited for: 15 -> 14; matrix products, arithmetic and copies ran while one was open for 6% -> 7% of each run, Pallas kernels for 20% -> 20%
where the time goes in v4:
time: 227 us; the launch traced here: 225 us
  Pallas kernels  88.4 us (39%)
  starting transfers between devices  52.5 us (23%)
  waiting for transfers between devices  46.5 us (20%)
  between operations  14.5 us (6%)
  other arithmetic  12.2 us (5%)
  local copies, waits for them, and re-layouts  11 us (5%)
    pallas_call x1, Pallas kernels, on_device(): pl.pallas_call(functools.partial(mid_kernel, experts, head), grid=(steps,...  39.3 us
    ppermute x25, starting transfers between devices, swapped(): return lax.ppermute(value, axis, [(at, at ^ mask) for at in range(count)])  33.2 us
    ppermute x25, waiting for transfers between devices, swapped(): return lax.ppermute(value, axis, [(at, at ^ mask) for at in range(count)])  25.9 us
    all_gather x1, waiting for transfers between devices, on_device(): group_b = lax.all_gather(packed_b, ('dp', 'seq'), axis=0, tiled=False)  13.2 us
    all_to_all x2, starting transfers between devices, on_device(): returned.append(lax.all_to_all(leave, 'seq', 0, 0, tiled=True))  13 us
    pallas_call x2, Pallas kernels, on_device(): pl.pallas_call(functools.partial(attend_back_kernel, reach, head, micro *...  10.8 us
    pallas_call x1, Pallas kernels, on_device(): pl.pallas_call(functools.partial(last_kernel, experts, head, tuple(zip(sp...  9.16 us
    pallas_call x1, Pallas kernels, on_device(): pl.pallas_call(functools.partial(query_grad_kernel, experts, head), grid=...  7.56 us
  transfers between devices with their start and end apart: 31, of which 14 were waited for; matrix products, arithmetic and copies ran while one was open for 7% of the time, Pallas kernels for 20%

profile of v4, /device:TPU:0, one launch (start us, length us, event | category | flops | bytes accessed | tf_op | source)
XLA Modules:
  0.0 225.2 jit_solution(9191956980654402986)
XLA Ops:
  7.2 1.8 pack.1
  9.1 3.1 %collective-permute-start = (bf16[16,768]{1,0:T(8,128)(2,1)}, bf16[16,768]{1,0:T(8,128)(2,1)S(1)}, u32[]{:S(2)}, u32[]{:S(2)}) collective-permute-start(bf16[16,768]{1,0:T(8,128)(2,1)} %get-tuple-element.79), channel_id=1, source_target_pairs={{0,8},{4,12},{8,0},{12,4},{16,24},{20,28},{24,16},{28,20},{1,9},{5... | collective-permute-start | bytes 73736 | tf_op jit(solution)/shard_map/ppermute | solution.py:658
  12.2 2.6 %collective-permute-start.1 = (bf16[16,768]{1,0:T(8,128)(2,1)}, bf16[16,768]{1,0:T(8,128)(2,1)S(1)}, u32[]{:S(2)}, u32[]{:S(2)}) collective-permute-start(bf16[16,768]{1,0:T(8,128)(2,1)} %get-tuple-element.79), channel_id=1, source_target_pairs={{0,16},{4,20},{8,24},{12,28},{16,0},{20,4},{24,8},{28,12},{1,17},{... | collective-permute-start | bytes 73736 | tf_op jit(solution)/shard_map/ppermute | solution.py:658
  16.2 1.2 collective-permute-done.1
  17.5 3.1 %collective-permute-done.2 = bf16[16,768]{1,0:T(8,128)(2,1)S(1)} collective-permute-done((bf16[16,768]{1,0:T(8,128)(2,1)}, bf16[16,768]{1,0:T(8,128)(2,1)S(1)}, u32[]{:S(2)}, u32[]{:S(2)}) %collective-permute-start.2) | collective-permute-done | bytes 24608 | tf_op jit(solution)/shard_map/ppermute | solution.py:658
  21.4 1.6 collective-permute-start.3
  22.9 1.5 collective-permute-start.4
  24.9 1.5 convert_reduce_fusion
  26.5 1.3 collective-permute-done.3
  27.9 2.0 collective-permute-done.5
  30.1 1.9 copy.53
  34.7 4.7 %keyval.1 = (bf16[1536,512]{1,0:T(8,128)(2,1)}, bf16[1536,128]{1,0:T(8,128)(2,1)}, bf16[512,768]{1,0:T(8,128)(2,1)}) custom-call(s32[3]{0:T(128)} %pad_add_fusion.place_ref, bf16[1536,512]{1,0:T(8,128)(2,1)} %bitcast.102, bf16[4,4,16,768]{3,2,1,0:T(8,128)(2,1)} %copy-done.2, bf16[4,4,16,768]{3,2,1,0:T(8,128)(2,1)} %copy-done.3), custom_call_target="tpu_custom_call" | custom-call | flops 201326592 | bytes 3145728 | tf_op jit(solution)/shard_map/keyval/pallas_call | solution.py:823
  39.5 2.4 %collective-permute-start.7 = (bf16[3,512,128]{2,1,0:T(8,128)(2,1)}, bf16[3,512,128]{2,1,0:T(8,128)(2,1)S(1)}, u32[]{:S(2)}, u32[]{:S(2)}) collective-permute-start(bf16[3,512,128]{2,1,0:T(8,128)(2,1)} %bitcast.128), channel_id=1, source_target_pairs={{0,3},{4,7},{8,11},{12,15},{16,19},{20,23},{24,27},{28,31}} | collective-permute-start | bytes 1179656 | tf_op jit(solution)/shard_map/ppermute | solution.py:664
  41.9 1.3 collective-permute-start.8
  43.2 2.5 %collective-permute-start.9 = (bf16[3,512,128]{2,1,0:T(8,128)(2,1)}, bf16[3,512,128]{2,1,0:T(8,128)(2,1)S(1)}, u32[]{:S(2)}, u32[]{:S(2)}) collective-permute-start(bf16[3,512,128]{2,1,0:T(8,128)(2,1)} %bitcast.130), channel_id=1, source_target_pairs={{0,1},{1,2},{2,3},{4,5},{5,6},{6,7},{8,9},{9,10},{10,11},{12,13},{... | collective-permute-start | bytes 1179656 | tf_op jit(solution)/shard_map/ppermute | solution.py:664
  45.7 1.4 copy.54
  47.4 5.5 %query.1 = (bf16[2,1536,128]{2,1,0:T(8,128)(2,1)}, f32[1536,128]{1,0:T(8,128)}) custom-call(bf16[1536,512]{1,0:T(8,128)(2,1)} %get-tuple-element.80.hidden_ref, s32[1536,2]{1,0:T(8,128)} %bitcast.107, bf16[512,768]{1,0:T(8,128)(2,1)} %get-tuple-element.81.weight_ref), custom_call_target="tpu_custom_call" | custom-call | flops 2013265920 | bytes 3145728 | tf_op jit(solution)/shard_map/query/pallas_call | solution.py:850
  53.5 7.3 %collective-permute-done.8.rest_1_ = bf16[3,512,128]{2,1,0:T(8,128)(2,1)S(1)} collective-permute-done((bf16[3,512,128]{2,1,0:T(8,128)(2,1)}, bf16[3,512,128]{2,1,0:T(8,128)(2,1)S(1)}, u32[]{:S(2)}, u32[]{:S(2)}) %collective-permute-start.8) | collective-permute-done | bytes 393248 | tf_op jit(solution)/shard_map/ppermute | solution.py:664
  61.8 6.3 %attend.1 = (f32[2,1536,128]{2,1,0:T(8,128)}, f32[3,2,512]{2,1,0:T(2,128)}) custom-call(s32[4]{0:T(128)} %pad_add_fusion.1.bounds_ref, bf16[2,1536,128]{2,1,0:T(8,128)(2,1)} %get-tuple-element.83.q_ref, s32[3,1,512]{2,1,0:T(1,128)} %max.18.start_ref, bf16[3,512,128]{2,1,0:T(8,128)(2,1)} %copy-done.7, bf16[3,512,128]{2,1,0:T(8,128)(2,1)} %copy-done.8, ...), custom_call_target="tpu_custom_call" | custom-call | flops 1610612736 | bytes 3145728 | tf_op jit(solution)/shard_map/attend/pallas_call | solution.py:875
  68.1 13.2 %all-gather.3.cloned.1.call-done = bf16[4608,512]{1,0:T(8,128)(2,1)} async-done(((bf16[144,512]{1,0:T(8,128)(2,1)}), bf16[4608,512]{1,0:T(8,128)(2,1)}) %all-gather.3.cloned.1.call-update) | async-done | bytes 4718608 | tf_op jit(solution)/shard_map/all_gather | solution.py:783
  81.3 39.3 %mid.1 = (bf16[1536,512]{1,0:T(8,128)(2,1)}, f32[1536,512]{1,0:T(8,128)}, bf16[2,1536,128]{2,1,0:T(8,128)(2,1)}, f32[1536,128]{1,0:T(8,128)}, bf16[4,4,160,512]{...) custom-call(bf16[1536,512]{1,0:T(8,128)(2,1)} %bitcast.103, bf16[1536,512]{1,0:T(8,128)(2,1)} %bitcast.127, ...), custom_call_target="tpu_custom_call" | custom-call | flops 21743271936 | bytes 12582912 | tf_op jit(solution)/shard_map/mid/pallas_call | solution.py:904
  120.9 4.9 %collective-permute-done.10 = bf16[4,4,160,512]{3,2,1,0:T(8,128)(2,1)S(1)} collective-permute-done((bf16[4,4,160,512]{3,2,1,0:T(8,128)(2,1)}, bf16[4,4,160,512]{3,2,1,0:T(8,128)(2,1)S(1)}, u32[]{:S(2)}, u32[]{:S(2)}) %collective-permute-start.10) | collective-permute-done | bytes 2621472 | tf_op jit(solution)/shard_map/ppermute | solution.py:658
  125.8 2.5 %add.155 = bf16[4,4,160,512]{3,2,1,0:T(8,128)(2,1)S(1)} add(bf16[4,4,160,512]{3,2,1,0:T(8,128)(2,1)} %get-tuple-element.88, bf16[4,4,160,512]{3,2,1,0:T(8,128)(2,1)S(1)} %collective-permute-done.10) | non-fusion elementwise | flops 1310720 | bytes 7864320 | tf_op jit(solution)/shard_map/add | solution.py:971
  128.7 1.6 collective-permute-start.12
  132.2 1.5 collective-permute-start.13
  133.7 6.3 %attend_back.2 = (bf16[2,1536,128]{2,1,0:T(8,128)(2,1)}, bf16[4,2,512,128]{3,2,1,0:T(8,128)(2,1)}) custom-call(s32[4]{0:T(128)} %pad_add_fusion.1.bounds_ref, bf16[2,1536,128]{2,1,0:T(8,128)(2,1)} %get-tuple-element.83.q_ref, bf16[2,1536,128]{2,1,0:T(8,128)(2,1)} %get-tuple-element.92.grad_ref, f32[1536,128]{1,0:T(8,128)} %get-tuple-element.112.side_ref.grad_logit_ref, ...), custom_call_target="tpu_custom_call" | custom-call | flops 2684354560 | bytes 4194304 | tf_op jit(solution)/shard_map/attend_back/pallas_call | solution.py:1027
  139.9 9.3 %all-to-all-start = ((bf16[4,2,512,128]{3,2,1,0:T(8,128)(2,1)}), bf16[4,2,512,128]{3,2,1,0:T(8,128)(2,1)S(1)}, u32[]{:S(2)}, u32[]{:S(2)}) async-start(bf16[4,2,512,128]{3,2,1,0:T(8,128)(2,1)} %get-tuple-element.124), calls=%async_computation | async-start | bytes 2097152 | tf_op jit(solution)/shard_map/all_to_all | solution.py:1055
  149.3 1.1 add.166
  150.5 1.8 collective-permute-start.15
  152.3 1.1 add.165
  153.5 2.1 collective-permute-start.14
  156.8 1.5 collective-permute-start.16
  158.4 4.5 %attend_back.3 = (bf16[2,1536,128]{2,1,0:T(8,128)(2,1)}, bf16[4,1,512,128]{3,2,1,0:T(8,128)(2,1)}) custom-call(s32[4]{0:T(128)} %pad_add_fusion.1.bounds_ref, bf16[2,1536,128]{2,1,0:T(8,128)(2,1)} %get-tuple-element.83.q_ref, bf16[2,1536,128]{2,1,0:T(8,128)(2,1)} %get-tuple-element.92.grad_ref, ...), custom_call_target="tpu_custom_call", output_to_operand_aliasing={{0}: (10, {})} | custom-call | flops 1342177280 | bytes 2097152 | tf_op jit(solution)/shard_map/attend_back/pallas_call | solution.py:1027
  162.9 5.4 %collective-permute-done.16 = bf16[2,2,48,512]{3,2,0,1:T(8,128)(2,1)S(1)} collective-permute-done((bf16[2,2,48,512]{3,2,0,1:T(8,128)(2,1)S(1)}, bf16[2,2,48,512]{3,2,0,1:T(8,128)(2,1)S(1)}, u32[]{:S(2)}, u32[]{:S(2)}) %collective-permute-start.16) | collective-permute-done | bytes 196640 | tf_op jit(solution)/shard_map/ppermute | solution.py:658
  170.2 1.2 collective-permute-start.18
  171.4 3.7 %all-to-all-start.1 = ((bf16[4,1,512,128]{3,2,1,0:T(8,128)(2,1)}), bf16[4,1,512,128]{3,2,1,0:T(8,128)(2,1)S(1)}, u32[]{:S(2)}, u32[]{:S(2)}) async-start(bf16[4,1,512,128]{3,2,1,0:T(8,128)(2,1)} %get-tuple-element.125), calls=%async_computation.1 | async-start | bytes 1048576 | tf_op jit(solution)/shard_map/all_to_all | solution.py:1055
  175.1 7.6 %query_grad.1 = (f32[1536,512]{1,0:T(8,128)}, bf16[512,512]{1,0:T(8,128)(2,1)}, f32[512,128]{1,0:T(8,128)}) custom-call(bf16[1536,512]{1,0:T(8,128)(2,1)} %get-tuple-element.80.hidden_ref, bf16[2,1536,128]{2,1,0:T(8,128)(2,1)} %get-tuple-element.111.grad_q_ref, f32[1536,128]{1,0:T(8,128)} %get-tuple-element.112.side_ref.grad_logit_ref, ...), custom_call_target="tpu_custom_call" | custom-call | flops 2415919104 | bytes 9437184 | tf_op jit(solution)/shard_map/query_grad/pallas_call | solution.py:1064
  182.9 4.0 %collective-permute-start.20 = (bf16[160,512]{1,0:T(8,128)(2,1)S(1)}, bf16[160,512]{1,0:T(8,128)(2,1)S(1)}, u32[]{:S(2)}, u32[]{:S(2)}) collective-permute-start(bf16[160,512]{1,0:T(8,128)(2,1)S(1)} %get-tuple-element.203), channel_id=1, source_target_pairs={{0,16},{4,20},{8,24},{12,28},{16,0},{20,4},{24,8},{28,12},{1,17},{... | collective-permute-start | bytes 491528 | tf_op jit(solution)/shard_map/ppermute | solution.py:658
  187.7 9.2 %last.1 = (f32[1536,512]{1,0:T(8,128)}, bf16[4,4,16,768]{3,2,1,0:T(8,128)(2,1)}, bf16[4,4,16,768]{3,2,1,0:T(8,128)(2,1)}) custom-call(s32[1]{0:T(128)} %bitcast.3.core_ref, bf16[1536,512]{1,0:T(8,128)(2,1)} %bitcast.104, bf16[1536,512]{1,0:T(8,128)(2,1)} %get-tuple-element.80.hidden_ref, f32[1536,512]{1,0:T(8,128)} %get-tuple-element.120.partial_ref, ...), custom_call_target="tpu_custom_call" | custom-call | flops 402653184 | bytes 12582912 | tf_op jit(solution)/shard_map/last/pallas_call | solution.py:1099
  196.9 1.9 collective-permute-done.21
  200.0 1.8 collective-permute-start.22
  201.7 1.5 collective-permute-start.23
  203.5 1.4 collective-permute-done.22
  204.9 2.6 %collective-permute-done.23 = bf16[4,16,768]{2,1,0:T(8,128)(2,1)S(1)} collective-permute-done((bf16[4,16,768]{2,1,0:T(8,128)(2,1)S(1)}, bf16[4,16,768]{2,1,0:T(8,128)(2,1)S(1)}, u32[]{:S(2)}, u32[]{:S(2)}) %collective-permute-start.23) | collective-permute-done | bytes 98336 | tf_op jit(solution)/shard_map/ppermute | solution.py:658
  207.5 1.2 collective-permute-done.24
  210.4 3.3 %collective-permute-start.27 = (bf16[16,768]{1,0:T(8,128)(2,1)S(1)}, bf16[16,768]{1,0:T(8,128)(2,1)S(1)}, u32[]{:S(2)}, u32[]{:S(2)}) collective-permute-start(bf16[16,768]{1,0:T(8,128)(2,1)S(1)} %get-tuple-element.211), channel_id=1, source_target_pairs={{0,24},{4,28},{8,16},{12,20},{16,8},{20,12},{24,0},{28,4},{1,25},{... | collective-permute-start | bytes 73736 | tf_op jit(solution)/shard_map/ppermute | solution.py:658
  214.5 1.7 finish_second.1
  216.8 1.5 finish_first.1
  (99 shorter events, 18.7 us)
Async XLA Ops:
  7.2 74.1 %all-gather.3.cloned.1.call-start = ((), (), s32[]{:S(2)}) async-start(), calls=%async_computation.2 | async-start | bytes 4866048 | tf_op jit(solution)/shard_map/all_gather | solution.py:783
  9.1 7.1 %collective-permute-start = (bf16[16,768]{1,0:T(8,128)(2,1)}, bf16[16,768]{1,0:T(8,128)(2,1)S(1)}, u32[]{:S(2)}, u32[]{:S(2)}) collective-permute-start(bf16[16,768]{1,0:T(8,128)(2,1)} %get-tuple-element.79), channel_id=1, source_target_pairs={{0,8},{4,12},{8,0},{12,4},{16,24},{20,28},{24,16},{28,20},{1,9},{5... | collective-permute-start | bytes 73736 | tf_op jit(solution)/shard_map/ppermute | solution.py:658
  12.2 5.3 %collective-permute-start.1 = (bf16[16,768]{1,0:T(8,128)(2,1)}, bf16[16,768]{1,0:T(8,128)(2,1)S(1)}, u32[]{:S(2)}, u32[]{:S(2)}) collective-permute-start(bf16[16,768]{1,0:T(8,128)(2,1)} %get-tuple-element.79), channel_id=1, source_target_pairs={{0,16},{4,20},{8,24},{12,28},{16,0},{20,4},{24,8},{28,12},{1,17},{... | collective-permute-start | bytes 73736 | tf_op jit(solution)/shard_map/ppermute | solution.py:658
  14.8 5.8 %collective-permute-start.2 = (bf16[16,768]{1,0:T(8,128)(2,1)}, bf16[16,768]{1,0:T(8,128)(2,1)S(1)}, u32[]{:S(2)}, u32[]{:S(2)}) collective-permute-start(bf16[16,768]{1,0:T(8,128)(2,1)} %get-tuple-element.79), channel_id=1, source_target_pairs={{0,24},{4,28},{8,16},{12,20},{16,8},{20,12},{24,0},{28,4},{1,25},{... | collective-permute-start | bytes 73736 | tf_op jit(solution)/shard_map/ppermute | solution.py:658
  21.4 6.4 %collective-permute-start.3 = (bf16[4,16,768]{2,1,0:T(8,128)(2,1)S(1)}, bf16[4,16,768]{2,1,0:T(8,128)(2,1)S(1)}, u32[]{:S(2)}, u32[]{:S(2)}) collective-permute-start(bf16[4,16,768]{2,1,0:T(8,128)(2,1)S(1)} %get-tuple-element.216), channel_id=1, source_target_pairs={{0,1},{1,0},{2,3},{3,2},{4,5},{5,4},{6,7},{7,6},{8,9},{9,8},{10,11... | collective-permute-start | bytes 294920 | tf_op jit(solution)/shard_map/ppermute | solution.py:658
  22.9 5.0 %collective-permute-start.4 = (bf16[4,16,768]{2,1,0:T(8,128)(2,1)S(1)}, bf16[4,16,768]{2,1,0:T(8,128)(2,1)S(1)}, u32[]{:S(2)}, u32[]{:S(2)}) collective-permute-start(bf16[4,16,768]{2,1,0:T(8,128)(2,1)S(1)} %get-tuple-element.216), channel_id=1, source_target_pairs={{0,2},{1,3},{2,0},{3,1},{4,6},{5,7},{6,4},{7,5},{8,10},{9,11},{10,... | collective-permute-start | bytes 294920 | tf_op jit(solution)/shard_map/ppermute | solution.py:658
  24.4 5.5 %collective-permute-start.5 = (bf16[4,16,768]{2,1,0:T(8,128)(2,1)S(1)}, bf16[4,16,768]{2,1,0:T(8,128)(2,1)S(1)}, u32[]{:S(2)}, u32[]{:S(2)}) collective-permute-start(bf16[4,16,768]{2,1,0:T(8,128)(2,1)S(1)} %get-tuple-element.216), channel_id=1, source_target_pairs={{0,3},{1,2},{2,1},{3,0},{4,7},{5,6},{6,5},{7,4},{8,11},{9,10},{10,... | collective-permute-start | bytes 294920 | tf_op jit(solution)/shard_map/ppermute | solution.py:658
  30.0 3.9 %copy-start.2 = (bf16[4,4,16,768]{3,2,1,0:T(8,128)(2,1)}, bf16[4,4,16,768]{3,2,1,0:T(8,128)(2,1)S(1)}, u32[]{:S(2)}) copy-start(bf16[4,4,16,768]{3,2,1,0:T(8,128)(2,1)S(1)} %pad_maximum_fusion.mine_ref) | copy-start | bytes 1179652
  30.0 3.9 %collective-permute-start.6 = (bf16[4,4,16,768]{3,2,1,0:T(8,128)(2,1)S(1)}, bf16[4,4,16,768]{3,2,1,0:T(8,128)(2,1)S(1)}, u32[]{:S(2)}, u32[]{:S(2)}) collective-permute-start(bf16[4,4,16,768]{3,2,1,0:T(8,128)(2,1)S(1)} %pad_maximum_fusion.mine_ref), channel_id=1, source_target_pairs={{0,4},{4,0},{8,12},{12,8},{16,20},{20,16},{24,28},{28,24},{1,5},{5... | collective-permute-start | bytes 1179656 | tf_op jit(solution)/shard_map/ppermute | solution.py:658
  33.9 0.8 copy-start.3
  39.5 14.1 %collective-permute-start.7 = (bf16[3,512,128]{2,1,0:T(8,128)(2,1)}, bf16[3,512,128]{2,1,0:T(8,128)(2,1)S(1)}, u32[]{:S(2)}, u32[]{:S(2)}) collective-permute-start(bf16[3,512,128]{2,1,0:T(8,128)(2,1)} %bitcast.128), channel_id=1, source_target_pairs={{0,3},{4,7},{8,11},{12,15},{16,19},{20,23},{24,27},{28,31}} | collective-permute-start | bytes 1179656 | tf_op jit(solution)/shard_map/ppermute | solution.py:664
  41.9 19.0 %collective-permute-start.8 = (bf16[3,512,128]{2,1,0:T(8,128)(2,1)}, bf16[3,512,128]{2,1,0:T(8,128)(2,1)S(1)}, u32[]{:S(2)}, u32[]{:S(2)}) collective-permute-start(bf16[3,512,128]{2,1,0:T(8,128)(2,1)} %bitcast.129), channel_id=1, source_target_pairs={{0,2},{1,3},{4,6},{5,7},{8,10},{9,11},{12,14},{13,15},{16,18},{17,... | collective-permute-start | bytes 1179656 | tf_op jit(solution)/shard_map/ppermute | solution.py:664
  43.2 17.7 %collective-permute-start.9 = (bf16[3,512,128]{2,1,0:T(8,128)(2,1)}, bf16[3,512,128]{2,1,0:T(8,128)(2,1)S(1)}, u32[]{:S(2)}, u32[]{:S(2)}) collective-permute-start(bf16[3,512,128]{2,1,0:T(8,128)(2,1)} %bitcast.130), channel_id=1, source_target_pairs={{0,1},{1,2},{2,3},{4,5},{5,6},{6,7},{8,9},{9,10},{10,11},{12,13},{... | collective-permute-start | bytes 1179656 | tf_op jit(solution)/shard_map/ppermute | solution.py:664
  53.5 7.4 %copy-start.7 = (bf16[3,512,128]{2,1,0:T(8,128)(2,1)}, bf16[3,512,128]{2,1,0:T(8,128)(2,1)S(1)}, u32[]{:S(2)}) copy-start(bf16[3,512,128]{2,1,0:T(8,128)(2,1)S(1)} %collective-permute-done.7.rest_0_) | copy-start | bytes 1179652
  60.9 0.7 copy-start.8
  60.9 0.9 copy-start.9
  120.6 5.2 %collective-permute-start.10 = (bf16[4,4,160,512]{3,2,1,0:T(8,128)(2,1)}, bf16[4,4,160,512]{3,2,1,0:T(8,128)(2,1)S(1)}, u32[]{:S(2)}, u32[]{:S(2)}) collective-permute-start(bf16[4,4,160,512]{3,2,1,0:T(8,128)(2,1)} %get-tuple-element.89), channel_id=1, source_target_pairs={{0,4},{4,0},{8,12},{12,8},{16,20},{20,16},{24,28},{28,24},{1,5},{5... | collective-permute-start | bytes 7864328 | tf_op jit(solution)/shard_map/ppermute | solution.py:658
  128.7 20.6 %collective-permute-start.12 = (bf16[2,2,2,56,512]{4,3,2,1,0:T(8,128)(2,1)S(1)}, bf16[2,2,2,56,512]{4,3,2,1,0:T(8,128)(2,1)}, u32[]{:S(2)}, u32[]{:S(2)}) collective-permute-start(bf16[2,2,2,56,512]{4,3,2,1,0:T(8,128)(2,1)S(1)} %get-tuple-element.188), channel_id=1, source_target_pairs={{0,2},{1,3},{2,0},{3,1},{4,6},{5,7},{6,4},{7,5},{8,10},{9,11},{10,... | collective-permute-start | bytes 1376264 | tf_op jit(solution)/shard_map/ppermute | solution.py:658
  130.4 18.9 %collective-permute-start.11 = (bf16[2,2,2,56,512]{4,3,2,1,0:T(8,128)(2,1)S(1)}, bf16[2,2,2,56,512]{4,3,2,1,0:T(8,128)(2,1)}, u32[]{:S(2)}, u32[]{:S(2)}) collective-permute-start(bf16[2,2,2,56,512]{4,3,2,1,0:T(8,128)(2,1)S(1)} %get-tuple-element.190), channel_id=1, source_target_pairs={{0,1},{1,0},{2,3},{3,2},{4,5},{5,4},{6,7},{7,6},{8,9},{9,8},{10,11... | collective-permute-start | bytes 1376264 | tf_op jit(solution)/shard_map/ppermute | solution.py:658
  132.2 17.1 %collective-permute-start.13 = (bf16[2,2,2,48,512]{4,3,2,1,0:T(8,128)(2,1)}, bf16[2,2,2,48,512]{4,3,2,1,0:T(8,128)(2,1)}, u32[]{:S(2)}, u32[]{:S(2)}) collective-permute-start(bf16[2,2,2,48,512]{4,3,2,1,0:T(8,128)(2,1)} %get-tuple-element.192), channel_id=1, source_target_pairs={{0,8},{4,12},{8,0},{12,4},{16,24},{20,28},{24,16},{28,20},{1,9},{5... | collective-permute-start | bytes 1179656 | tf_op jit(solution)/shard_map/ppermute | solution.py:658
  139.9 31.4 %all-to-all-start = ((bf16[4,2,512,128]{3,2,1,0:T(8,128)(2,1)}), bf16[4,2,512,128]{3,2,1,0:T(8,128)(2,1)S(1)}, u32[]{:S(2)}, u32[]{:S(2)}) async-start(bf16[4,2,512,128]{3,2,1,0:T(8,128)(2,1)} %get-tuple-element.124), calls=%async_computation | async-start | bytes 2097152 | tf_op jit(solution)/shard_map/all_to_all | solution.py:1055
  150.5 17.9 %collective-permute-start.15 = (bf16[2,2,56,512]{3,2,0,1:T(8,128)(2,1)S(1)}, bf16[2,2,56,512]{3,2,0,1:T(8,128)(2,1)S(1)}, u32[]{:S(2)}, u32[]{:S(2)}) collective-permute-start(bf16[2,2,56,512]{3,2,0,1:T(8,128)(2,1)S(1)} %bitcast.110), channel_id=1, source_target_pairs={{0,8},{4,12},{8,0},{12,4},{16,24},{20,28},{24,16},{28,20},{1,9},{5... | collective-permute-start | bytes 688136 | tf_op jit(solution)/shard_map/ppermute | solution.py:658
  153.5 15.5 %collective-permute-start.14 = (bf16[2,2,56,512]{3,2,0,1:T(8,128)(2,1)S(1)}, bf16[2,2,56,512]{3,2,0,1:T(8,128)(2,1)S(1)}, u32[]{:S(2)}, u32[]{:S(2)}) collective-permute-start(bf16[2,2,56,512]{3,2,0,1:T(8,128)(2,1)S(1)} %bitcast.111), channel_id=1, source_target_pairs={{0,2},{1,3},{2,0},{3,1},{4,6},{5,7},{6,4},{7,5},{8,10},{9,11},{10,... | collective-permute-start | bytes 688136 | tf_op jit(solution)/shard_map/ppermute | solution.py:658
  156.8 11.6 %collective-permute-start.16 = (bf16[2,2,48,512]{3,2,0,1:T(8,128)(2,1)S(1)}, bf16[2,2,48,512]{3,2,0,1:T(8,128)(2,1)S(1)}, u32[]{:S(2)}, u32[]{:S(2)}) collective-permute-start(bf16[2,2,48,512]{3,2,0,1:T(8,128)(2,1)S(1)} %bitcast.112), channel_id=1, source_target_pairs={{0,1},{1,0},{2,3},{3,2},{4,5},{5,4},{6,7},{7,6},{8,9},{9,8},{10,11... | collective-permute-start | bytes 589832 | tf_op jit(solution)/shard_map/ppermute | solution.py:658
  169.3 13.4 %collective-permute-start.19 = (bf16[2,48,512]{2,1,0:T(8,128)(2,1)S(1)}, bf16[2,48,512]{2,1,0:T(8,128)(2,1)S(1)}, u32[]{:S(2)}, u32[]{:S(2)}) collective-permute-start(bf16[2,48,512]{2,1,0:T(8,128)(2,1)S(1)} %get-tuple-element.209), channel_id=1, source_target_pairs={{0,2},{1,3},{2,0},{3,1},{4,6},{5,7},{6,4},{7,5},{8,10},{9,11},{10,... | collective-permute-start | bytes 294920 | tf_op jit(solution)/shard_map/ppermute | solution.py:658
  170.2 12.5 %collective-permute-start.17 = (bf16[2,56,512]{2,1,0:T(8,128)(2,1)S(1)}, bf16[2,56,512]{2,1,0:T(8,128)(2,1)S(1)}, u32[]{:S(2)}, u32[]{:S(2)}) collective-permute-start(bf16[2,56,512]{2,1,0:T(8,128)(2,1)S(1)} %get-tuple-element.218), channel_id=1, source_target_pairs={{0,8},{4,12},{8,0},{12,4},{16,24},{20,28},{24,16},{28,20},{1,9},{5... | collective-permute-start | bytes 344072 | tf_op jit(solution)/shard_map/ppermute | solution.py:658
  170.2 12.5 %collective-permute-start.18 = (bf16[2,56,512]{2,1,0:T(8,128)(2,1)S(1)}, bf16[2,56,512]{2,1,0:T(8,128)(2,1)S(1)}, u32[]{:S(2)}, u32[]{:S(2)}) collective-permute-start(bf16[2,56,512]{2,1,0:T(8,128)(2,1)S(1)} %get-tuple-element.205), channel_id=1, source_target_pairs={{0,1},{1,0},{2,3},{3,2},{4,5},{5,4},{6,7},{7,6},{8,9},{9,8},{10,11... | collective-permute-start | bytes 344072 | tf_op jit(solution)/shard_map/ppermute | solution.py:658
  171.4 11.3 %copy-start = (bf16[4,2,512,128]{3,2,1,0:T(8,128)(2,1)}, bf16[4,2,512,128]{3,2,1,0:T(8,128)(2,1)S(1)}, u32[]{:S(2)}) copy-start(bf16[4,2,512,128]{3,2,1,0:T(8,128)(2,1)S(1)} %all-to-all-done.rest_0_) | copy-start | bytes 3145732
  171.4 15.5 %all-to-all-start.1 = ((bf16[4,1,512,128]{3,2,1,0:T(8,128)(2,1)}), bf16[4,1,512,128]{3,2,1,0:T(8,128)(2,1)S(1)}, u32[]{:S(2)}, u32[]{:S(2)}) async-start(bf16[4,1,512,128]{3,2,1,0:T(8,128)(2,1)} %get-tuple-element.125), calls=%async_computation.1 | async-start | bytes 1048576 | tf_op jit(solution)/shard_map/all_to_all | solution.py:1055
  182.9 13.9 %collective-permute-start.20 = (bf16[160,512]{1,0:T(8,128)(2,1)S(1)}, bf16[160,512]{1,0:T(8,128)(2,1)S(1)}, u32[]{:S(2)}, u32[]{:S(2)}) collective-permute-start(bf16[160,512]{1,0:T(8,128)(2,1)S(1)} %get-tuple-element.203), channel_id=1, source_target_pairs={{0,16},{4,20},{8,24},{12,28},{16,0},{20,4},{24,8},{28,12},{1,17},{... | collective-permute-start | bytes 491528 | tf_op jit(solution)/shard_map/ppermute | solution.py:658
  186.9 0.8 copy-start.1
  196.8 2.0 collective-permute-start.21
  200.0 4.9 %collective-permute-start.22 = (bf16[4,16,768]{2,1,0:T(8,128)(2,1)S(1)}, bf16[4,16,768]{2,1,0:T(8,128)(2,1)S(1)}, u32[]{:S(2)}, u32[]{:S(2)}) collective-permute-start(bf16[4,16,768]{2,1,0:T(8,128)(2,1)S(1)} %get-tuple-element.198), channel_id=1, source_target_pairs={{0,1},{1,0},{2,3},{3,2},{4,5},{5,4},{6,7},{7,6},{8,9},{9,8},{10,11... | collective-permute-start | bytes 294920 | tf_op jit(solution)/shard_map/ppermute | solution.py:658
  201.7 5.7 %collective-permute-start.23 = (bf16[4,16,768]{2,1,0:T(8,128)(2,1)S(1)}, bf16[4,16,768]{2,1,0:T(8,128)(2,1)S(1)}, u32[]{:S(2)}, u32[]{:S(2)}) collective-permute-start(bf16[4,16,768]{2,1,0:T(8,128)(2,1)S(1)} %get-tuple-element.200), channel_id=1, source_target_pairs={{0,2},{1,3},{2,0},{3,1},{4,6},{5,7},{6,4},{7,5},{8,10},{9,11},{10,... | collective-permute-start | bytes 294920 | tf_op jit(solution)/shard_map/ppermute | solution.py:658
  203.2 5.5 %collective-permute-start.24 = (bf16[4,16,768]{2,1,0:T(8,128)(2,1)S(1)}, bf16[4,16,768]{2,1,0:T(8,128)(2,1)S(1)}, u32[]{:S(2)}, u32[]{:S(2)}) collective-permute-start(bf16[4,16,768]{2,1,0:T(8,128)(2,1)S(1)} %get-tuple-element.199), channel_id=1, source_target_pairs={{0,3},{1,2},{2,1},{3,0},{4,7},{5,6},{6,5},{7,4},{8,11},{9,10},{10,... | collective-permute-start | bytes 294920 | tf_op jit(solution)/shard_map/ppermute | solution.py:658
  209.4 6.8 %collective-permute-start.25 = (bf16[16,768]{1,0:T(8,128)(2,1)S(1)}, bf16[16,768]{1,0:T(8,128)(2,1)S(1)}, u32[]{:S(2)}, u32[]{:S(2)}) collective-permute-start(bf16[16,768]{1,0:T(8,128)(2,1)S(1)} %get-tuple-element.213), channel_id=1, source_target_pairs={{0,8},{4,12},{8,0},{12,4},{16,24},{20,28},{24,16},{28,20},{1,9},{5... | collective-permute-start | bytes 73736 | tf_op jit(solution)/shard_map/ppermute | solution.py:658
  210.0 6.2 %collective-permute-start.26 = (bf16[16,768]{1,0:T(8,128)(2,1)S(1)}, bf16[16,768]{1,0:T(8,128)(2,1)S(1)}, u32[]{:S(2)}, u32[]{:S(2)}) collective-permute-start(bf16[16,768]{1,0:T(8,128)(2,1)S(1)} %get-tuple-element.212), channel_id=1, source_target_pairs={{0,16},{4,20},{8,24},{12,28},{16,0},{20,4},{24,8},{28,12},{1,17},{... | collective-permute-start | bytes 73736 | tf_op jit(solution)/shard_map/ppermute | solution.py:658
  210.4 5.8 %collective-permute-start.27 = (bf16[16,768]{1,0:T(8,128)(2,1)S(1)}, bf16[16,768]{1,0:T(8,128)(2,1)S(1)}, u32[]{:S(2)}, u32[]{:S(2)}) collective-permute-start(bf16[16,768]{1,0:T(8,128)(2,1)S(1)} %get-tuple-element.211), channel_id=1, source_target_pairs={{0,24},{4,28},{8,16},{12,20},{16,8},{20,12},{24,0},{28,4},{1,25},{... | collective-permute-start | bytes 73736 | tf_op jit(solution)/shard_map/ppermute | solution.py:658
  216.2 0.6 copy-start.4
  216.2 0.6 copy-start.5
  216.2 0.6 copy-start.6
Sparse Core Ops, SparseCore 0:
  10.9 70.3 all-gather.2

commit v5 on v4

--- a/solution.py
+++ b/solution.py
@@ -14,8 +14,12 @@
 F32 = jnp.float32
 
 
-def call_params():
-    return pltpu.CompilerParams(vmem_limit_bytes=56 * MIB)
+def call_params(mib=56):
+    return pltpu.CompilerParams(vmem_limit_bytes=mib * MIB)
+
+
+def in_hbm(*values):
+    return [pltpu.with_memory_space_constraint(value, pltpu.HBM) for value in values]
 
 
 def cost(flops, bytes_accessed, transcendentals=0):
@@ -246,6 +250,25 @@
     lse_ref[0] = peak_ref[...] + jnp.log(total_ref[...])
 
 
+def summed_by(values, chosen):
+    matrix = jnp.where(chosen, 1.0, 0.0).astype(BF16)
+    high = values.astype(BF16)
+    low = (values - high.astype(F32)).astype(BF16)
+    return dot_nn(high, matrix) + dot_nn(low, matrix)
+
+
+def mid_scratch(rows_all, width, ff, weights, leaving):
+    return (
+        [pltpu.VMEM((rows_all, ff), BF16)] * 2
+        + [pltpu.VMEM((width, rows_all), BF16)] * 3
+        + [pltpu.VMEM((rows_all, width), BF16)]
+        + [pltpu.VMEM((LANES, width), F32), pltpu.VMEM((LANES, ff), F32)]
+        + [pltpu.VMEM(weights, BF16)]
+        + [pltpu.VMEM(shape, BF16) for shape in leaving]
+        + [pltpu.SemaphoreType.DMA((3,)), pltpu.SemaphoreType.DMA((2 + 4 * ff // width,))]
+    )
+
+
 def mid_kernel(
     experts,
     head,
@@ -255,31 +278,43 @@
     mixed_ref,
     vector_ref,
     core_ref,
-    down_ref,
-    up_ref,
-    wo_ref,
+    weight_ref,
     out_ref,
     grad_mid_ref,
     grad_mixed_ref,
     side_ref,
     *rest,
 ):
-    *grads_refs, acc_out, acc_up, acc_down, acc_vec, acc_upb, branch_ref, gsec_ref = rest
+    owners = weight_ref.shape[0]
+    count = 2 if owners > 1 else 1
+    leaving, rest = rest[:count], rest[count:]
+    active_ref, grad_ref, dy_t_ref, second_t_ref, routed_t_ref, att_ref = rest[:6]
+    acc_vec, acc_upb, kept_ref = rest[6:9]
+    staged, (in_sems, out_sems) = rest[9 : 9 + count], rest[9 + count :]
     step, last = pl.program_id(0), pl.num_programs(0) - 1
     rows, width = x_ref.shape
     inner = experts * head
-    owners, own_rows = wo_ref.shape[:2]
-    ff_rows = down_ref.shape[1]
-    ff = owners * ff_rows
+    own_rows = width // owners
+    ff = active_ref.shape[1]
+    ff_rows = ff // owners
     blocks = ff // width
+    up_at, out_at = ff_rows, ff_rows + blocks * own_rows
+
+    spans = ((out_at, out_at + own_rows), (0, ff_rows), (up_at, out_at))
+    loads = [
+        pltpu.make_async_copy(
+            weight_ref.at[:, low:high, :], kept_ref.at[:, low:high, :], in_sems.at[at]
+        )
+        for at, (low, high) in enumerate(spans)
+    ]
 
     @pl.when(step == 0)
     def _():
-        acc_out[...] = jnp.zeros_like(acc_out)
-        acc_up[...] = jnp.zeros_like(acc_up)
-        acc_down[...] = jnp.zeros_like(acc_down)
+        for load in loads:
+            load.start()
         acc_vec[...] = jnp.zeros_like(acc_vec)
         acc_upb[...] = jnp.zeros_like(acc_upb)
+        loads[0].wait()
 
     gain, shift = vector_ref[1:2, :width], vector_ref[2:3, :width]
     down_bias = vector_ref[3:4, :width]
@@ -288,7 +323,7 @@
     owner = lax.div(lanes_of(rows, inner), head)
     unfold = unfold_matrix(inner, head, head)
     fold = fold_matrix(inner, head, head)
-    wo = wo_ref[...].reshape(inner, width)
+    wo = kept_ref[:, out_at : out_at + own_rows, :].reshape(inner, width)
     mixed_one, mixed_two = mixed_ref[0], mixed_ref[1]
     routed_one = dot_nn((gate_one * mixed_one).astype(BF16), unfold)
     routed_two = dot_nn((gate_two * mixed_two).astype(BF16), unfold)
@@ -299,21 +334,28 @@
     middle = x_ref[...].astype(F32) + dot_nn(routed, wo)
     normed, inv_dev = normalize(middle)
     second_low = (normed * gain + shift).astype(BF16)
-    second_t = second_low.T
     dy = dy_ref[...]
     dy_wide = dy.astype(F32)
-    dy_t = dy.T
-    branch_ref[...] = middle + down_bias
-    gsec_ref[...] = jnp.zeros_like(gsec_ref)
+    here = pl.ds(pl.multiple_of(step * rows, rows), rows)
+    second_t_ref[:, here] = second_low.T
+    dy_t_ref[:, here] = dy.T
+    routed_t_ref[:, here] = routed.T
     per_block = width // ff_rows if owners > 1 else 1
+
+    @pl.when(step == 0)
+    def _():
+        loads[1].wait()
+        loads[2].wait()
 
     def down_block(at):
         if owners > 1:
-            return down_ref[at * per_block : (at + 1) * per_block].reshape(width, width)
-        return down_ref[0, at * width : (at + 1) * width, :]
+            block = kept_ref[at * per_block : (at + 1) * per_block, :ff_rows, :]
+            return block.reshape(width, width)
+        return kept_ref[0, at * width : (at + 1) * width, :]
 
     def up_block(at):
-        return up_ref[:, at * own_rows : (at + 1) * own_rows, :].reshape(width, width)
+        low = up_at + at * own_rows
+        return kept_ref[:, low : low + own_rows, :].reshape(width, width)
 
     def ahead(at):
         lo = at * width
@@ -330,21 +372,21 @@
         active = (pre_act * sigma).astype(BF16)
         slope = sigma * (1.0 + pre_act * (1.0 - sigma))
         grad_low = (grad_active.astype(F32) * slope).astype(BF16)
-        branch_ref[...] += dot_nn(active, down_block(at))
-        gsec_ref[...] += dot_nt(grad_low, up_block(at))
-        acc_down[:, lo : lo + width] += dot_nn(dy_t, active)
-        acc_up[:, lo : lo + width] += dot_nn(second_t, grad_low)
+        active_ref[here, lo : lo + width] = active
+        grad_ref[here, lo : lo + width] = grad_low
         acc_upb[8:9, lo : lo + width] += jnp.sum(grad_low.astype(F32), 0, keepdims=True)
 
-    out_ref[...] = branch_ref[...].astype(BF16)
-    gsec = gsec_ref[...]
+    down_all = jnp.concatenate([down_block(at) for at in range(blocks)], 0)
+    up_all = jnp.concatenate([up_block(at) for at in range(blocks)], 1)
+    out_ref[...] = (middle + down_bias + dot_nn(active_ref[here, :], down_all)).astype(BF16)
+    gsec = dot_nt(grad_ref[here, :], up_all)
     acc_vec[0:1] += jnp.sum(gsec * normed, 0, keepdims=True)
     acc_vec[1:2] += jnp.sum(gsec, 0, keepdims=True)
     acc_vec[2:3] += jnp.sum(dy_wide, 0, keepdims=True)
     grad_mid = dy_wide + norm_back(gsec, gain, normed, inv_dev)
-    grad_mid_ref[...] = grad_mid
     grad_att = grad_mid.astype(BF16)
-    acc_out[...] += dot_nn(routed.T, grad_att)
+    grad_mid_ref[...] = grad_att
+    att_ref[here, :] = grad_att
     grad_routed = dot_nt(grad_att, wo).astype(BF16)
     zero = jnp.zeros_like(grad_routed)
     picked_one = dot_nn(jnp.where(owner == first, grad_routed, zero), fold)
@@ -353,50 +395,105 @@
     grad_mixed_two = (gate_two * picked_two).astype(BF16)
     grad_mixed_ref[0] = grad_mixed_one
     grad_mixed_ref[1] = grad_mixed_two
-    inner_one = jnp.sum(grad_mixed_one.astype(F32) * mixed_one, -1, keepdims=True)
-    inner_two = jnp.sum(grad_mixed_two.astype(F32) * mixed_two, -1, keepdims=True)
-    grad_one = jnp.sum(picked_one * mixed_one, -1, keepdims=True)
-    grad_two = jnp.sum(picked_two * mixed_two, -1, keepdims=True)
+    spread_one = lax.broadcasted_iota(jnp.int32, (2 * LANES, 2 * LANES), 0) // LANES
+    spread_two = lax.broadcasted_iota(jnp.int32, (2 * LANES, 2 * LANES), 1) // LANES
+    sums = summed_by(
+        jnp.concatenate([picked_one * mixed_one, picked_two * mixed_two], 1),
+        spread_one == spread_two,
+    )
+    grad_one, grad_two = sums[:, :LANES], sums[:, LANES:]
+    source = lax.broadcasted_iota(jnp.int32, (2 * LANES, LANES), 0) // LANES
+    target = lax.broadcasted_iota(jnp.int32, (2 * LANES, LANES), 1)
+    inners = summed_by(
+        jnp.concatenate(
+            [grad_mixed_one.astype(F32) * mixed_one, grad_mixed_two.astype(F32) * mixed_two], 1
+        ),
+        target == head + source,
+    )
     common = gate_one * grad_one + gate_two * grad_two
     lane = lanes_of(rows, LANES)
-    side = jnp.where(lane == first, gate_one * (grad_one - common), 0.0)
+    side = jnp.where(lane == first, gate_one * (grad_one - common), inners)
     side = jnp.where(lane == second, gate_two * (grad_two - common), side)
-    side = jnp.where(lane == head, inner_one, side)
-    side = jnp.where(lane == head + 1, inner_two, side)
-    side = jnp.where(lane == head + 2, first.astype(F32), side)
-    side_ref[...] = jnp.where(lane == head + 3, second.astype(F32), side)
+    side = jnp.where(lane == head + 2, gate_ref[:, 2:3], side)
+    side_ref[...] = jnp.where(lane == head + 3, gate_ref[:, 3:4], side)
 
     @pl.when(step == last)
     def _():
-        up_at, out_at = ff_rows, ff_rows + blocks * own_rows
-
-        def leave(value, columns, row, count, group):
+        leaves = []
+
+        def put(value, columns, row, count, group):
             if owners == 1:
-                grads_refs[0][0, row : row + value.shape[0], columns] = value
+                staged[0][0, row : row + value.shape[0], columns] = value
                 return
-            keep_ref, send_ref = grads_refs
-            seqs = keep_ref.shape[1]
-            parts = value.reshape(value.shape[0] // (2 * seqs * count), 2, seqs, count, -1)
-            planes = parts.shape[0]
+            seqs = staged[0].shape[1]
+            by_core = value.reshape(value.shape[0] // (2 * seqs * count), 2, seqs, count, -1)
+            planes = by_core.shape[0]
             other = core_ref[0] == 1
-            low, high = parts[:, 0], parts[:, 1]
-            where = (slice(group * planes, (group + 1) * planes), slice(None), slice(row, row + count), columns)
-            keep_ref[where] = jnp.where(other, high, low)
-            send_ref[where] = jnp.where(other, low, high)
+            low, high = by_core[:, 0], by_core[:, 1]
+            where = (slice(group * planes, (group + 1) * planes), slice(None), slice(row, row + count))
+            staged[0][where + (columns,)] = jnp.where(other, high, low)
+            staged[1][where + (columns,)] = jnp.where(other, low, high)
+
+        def leave(where):
+            for source, target in zip(staged, leaving):
+                copy = pltpu.make_async_copy(
+                    source.at[where], target.at[where], out_sems.at[len(leaves)]
+                )
+                copy.start()
+                leaves.append(copy)
 
         everything = slice(None)
-        for at in range(blocks):
-            lo = at * width
-            turned = acc_down[:, lo : lo + width].T.astype(BF16)
-            leave(turned, everything, lo if owners == 1 else 0, ff_rows, at)
-            leave(
-                acc_up[:, lo : lo + width].astype(BF16),
-                everything,
-                up_at + at * own_rows,
-                own_rows,
-                0,
-            )
-        leave(acc_out[...].astype(BF16), everything, out_at, own_rows, 0)
+
+        def weight_block(at, carry):
+            columns = pl.ds(pl.multiple_of(at * width, width), width)
+            turned = dot_nn(dy_t_ref[...], active_ref[:, columns]).T.astype(BF16)
+            straight = dot_nn(second_t_ref[...], grad_ref[:, columns]).astype(BF16)
+            low = up_at + at * own_rows
+            if owners == 1:
+                staged[0][0, pl.ds(at * width, width), :] = turned
+                staged[0][0, pl.ds(low, width), :] = straight
+                return carry
+            seqs = staged[0].shape[1]
+            other = core_ref[0] == 1
+            for value, rows_each, planes in ((turned, ff_rows, 1), (straight, own_rows, blocks)):
+                by_core = value.reshape(-1, 2, seqs, rows_each, width)
+                first_half, second_half = by_core[:, 0], by_core[:, 1]
+                if planes == 1:
+                    count = by_core.shape[0]
+                    where = (pl.ds(at * count, count), everything, slice(0, ff_rows))
+                else:
+                    low = pl.multiple_of(up_at + at * own_rows, own_rows)
+                    where = (everything, everything, pl.ds(low, own_rows))
+                staged[0][where] = jnp.where(other, second_half, first_half)
+                staged[1][where] = jnp.where(other, first_half, second_half)
+                for copy in block_copies(at, planes > 1):
+                    copy.start()
+            return carry
+
+        def block_copies(at, straight):
+            count = staged[0].shape[0] // blocks
+            if straight:
+                low = pl.multiple_of(up_at + at * own_rows, own_rows)
+                where = (everything, everything, pl.ds(low, own_rows))
+            else:
+                where = (pl.ds(at * count, count), everything, slice(0, ff_rows))
+            base = 2 + 4 * at + 2 * int(straight)
+            return [
+                pltpu.make_async_copy(source.at[where], target.at[where], out_sems.at[base + side])
+                for side, (source, target) in enumerate(zip(staged, leaving))
+            ]
+
+        def block_waits(at, carry):
+            for straight in (False, True):
+                for copy in block_copies(at, straight):
+                    copy.wait()
+            return carry
+
+        lax.fori_loop(0, blocks, weight_block, 0)
+        if owners == 1:
+            leave((slice(0, 1), slice(0, out_at)))
+        d_out = dot_nn(routed_t_ref[...], att_ref[...])
+        put(d_out.astype(BF16), everything, out_at, own_rows, 0)
         vectors_turned = acc_vec[...].T
         extra = acc_upb[...].T
         if owners > 1:
@@ -409,7 +506,13 @@
             if at == 0:
                 part = part + vectors_turned
             columns = slice(at * LANES, (at + 1) * LANES)
-            leave(part.astype(BF16), columns, out_at + own_rows, own_rows, 0)
+            put(part.astype(BF16), columns, out_at + own_rows, own_rows, 0)
+        ending = slice(out_at, out_at + 2 * own_rows)
+        leave((slice(0, 1), ending) if owners == 1 else (everything, everything, ending))
+        for copy in leaves:
+            copy.wait()
+        if owners > 1:
+            lax.fori_loop(0, blocks, block_waits, 0)
 
 
 def attend_back_kernel(
@@ -533,7 +636,7 @@
         dot_nt(grad_queries, weight_ref[:, :inner])
         + dot_nt(logit_high, router)
         + dot_nt(logit_low, router)
-    )
+    ).astype(BF16)
     hidden_t = hidden_ref[...].T
     acc_query[...] += dot_nn(hidden_t, grad_queries)
     acc_router[...] += dot_nn(hidden_t, logit_high) + dot_nn(hidden_t, logit_low)
@@ -583,8 +686,8 @@
     gain = rows_of(weight_ref[:, inner + LANES :], (experts,))[0:1]
     normed, inv_dev = normalize(x_ref[...].astype(F32))
     grad_keyvals = summed_ref[...]
-    grad_hidden = partial_ref[...] + dot_nt(grad_keyvals, weight_ref[:, inner : inner + LANES])
-    grad_in_ref[...] = grad_mid_ref[...] + norm_back(grad_hidden, gain, normed, inv_dev)
+    grad_hidden = partial_ref[...].astype(F32) + dot_nt(grad_keyvals, weight_ref[:, inner : inner + LANES])
+    grad_in_ref[...] = grad_mid_ref[...].astype(F32) + norm_back(grad_hidden, gain, normed, inv_dev)
     hidden_t = hidden_ref[...].T
     acc_kv[...] += dot_nn(hidden_t, grad_keyvals)
     acc_vec[experts : experts + 1] += jnp.sum(grad_hidden * normed, 0, keepdims=True)
@@ -783,28 +886,17 @@
     group_b = lax.all_gather(packed_b, ("dp", "seq"), axis=0, tiled=False)
     up_at, out_at = ff_rows, ff_rows + blocks * own_rows
     if aligned:
-        nb, rb, fb = devices, own_rows, ff_rows
-        weights = [group_b, group_b, group_b]
-        weight_specs = [
-            pl.BlockSpec((nb, ff_rows, width), lambda *_: (0, 0, 0), pipeline_mode=pl.Buffered(1)),
-            pl.BlockSpec(
-                (nb, blocks * own_rows, width), lambda *_: (0, 1, 0), pipeline_mode=pl.Buffered(1)
-            ),
-            pl.BlockSpec(
-                (nb, own_rows, width),
-                lambda *_: (0, out_at // own_rows, 0),
-                pipeline_mode=pl.Buffered(1),
-            ),
-        ]
+        weights = group_b
     else:
-        nb, rb, fb = 1, width, ff
         up_all = group_b[:, up_at:out_at].reshape(devices, blocks, own_rows, width)
-        weights = [
-            group_b[:, :ff_rows].reshape(1, ff, width),
-            jnp.moveaxis(up_all, 0, 1).reshape(1, ff, width),
-            group_b[:, out_at:].reshape(1, width, width),
-        ]
-        weight_specs = [whole_spec(value.shape) for value in weights]
+        weights = jnp.concatenate(
+            [
+                group_b[:, :ff_rows].reshape(ff, width),
+                jnp.moveaxis(up_all, 0, 1).reshape(ff, width),
+                group_b[:, out_at:].reshape(width, width),
+            ],
+            0,
+        )[None]
 
     tokens = block_in.reshape(rows_all, width)
     grad_out = cotangent.reshape(rows_all, width)
@@ -900,7 +992,7 @@
     if aligned:
         leaving = [(dp // 2, shards, grad_rows, width)] * 2
     else:
-        leaving = [(nb, grad_rows, width)]
+        leaving = [(1, grad_rows, width)]
     block_out, grad_mid, grad_mixed, side, *grads_b = pl.pallas_call(
         functools.partial(mid_kernel, experts, head),
         grid=(steps,),
@@ -912,34 +1004,26 @@
             whole_spec((8, ff)),
             pl.BlockSpec(memory_space=pltpu.SMEM),
         ]
-        + weight_specs,
+        + [pl.BlockSpec(memory_space=pl.ANY)],
         out_specs=[
             row_spec(tile, width),
             row_spec(tile, width),
             pair_spec(tile),
             row_spec(tile, LANES),
         ]
-        + [whole_spec(shape) for shape in leaving],
+        + [pl.BlockSpec(memory_space=pl.ANY)] * len(leaving),
         out_shape=[
             jax.ShapeDtypeStruct((rows_all, width), BF16),
-            jax.ShapeDtypeStruct((rows_all, width), F32),
+            jax.ShapeDtypeStruct((rows_all, width), BF16),
             jax.ShapeDtypeStruct((2, rows_all, LANES), BF16),
             jax.ShapeDtypeStruct((rows_all, LANES), F32),
         ]
         + [jax.ShapeDtypeStruct(shape, BF16) for shape in leaving],
-        scratch_shapes=[
-            pltpu.VMEM((inner, width), F32),
-            pltpu.VMEM((width, ff), F32),
-            pltpu.VMEM((width, ff), F32),
-            pltpu.VMEM((LANES, width), F32),
-            pltpu.VMEM((LANES, ff), F32),
-            pltpu.VMEM((tile, width), F32),
-            pltpu.VMEM((tile, width), F32),
-        ],
+        scratch_shapes=mid_scratch(rows_all, width, ff, weights.shape, leaving),
         compiler_params=call_params(),
         cost_estimate=cost(6 * rows_all * width * (2 * ff + width), rows_all * width * 16),
         name="mid",
-    )(tokens, grad_out, gates, mixed, vectors, core_index, *weights)
+    )(tokens, grad_out, gates, mixed, vectors, core_index, weights)
 
     if not aligned:
         parts = grads_b[0][0]
@@ -1018,7 +1102,7 @@
             at_micro((1, 1, local_len), "b"),
         ]
         in_specs += [at_micro((1, local_len, LANES), "b")] * reach
-        operands = [queries, grad_mixed, side, lse, starts, *pieces]
+        operands = in_hbm(queries, grad_mixed, side, lse, starts, *pieces)
         aliases = {}
         if micro:
             in_specs.append(pl.BlockSpec(memory_space=pl.ANY))
@@ -1040,11 +1124,11 @@
                 ],
             ),
             out_shape=[
-                jax.ShapeDtypeStruct((2, rows_all, LANES), BF16),
+                pltpu.HBM((2, rows_all, LANES), BF16),
                 jax.ShapeDtypeStruct((shards, count, local_len, LANES), BF16),
             ],
             input_output_aliases=aliases,
-            compiler_params=call_params(),
+            compiler_params=call_params(28),
             cost_estimate=cost(
                 10 * pairs * LANES * count // batch,
                 count * local_len * LANES * 32,
@@ -1076,22 +1160,22 @@
             whole_spec((width, LANES)),
         ],
         out_shape=[
-            jax.ShapeDtypeStruct((rows_all, width), F32),
-            jax.ShapeDtypeStruct((width, inner), BF16),
-            jax.ShapeDtypeStruct((width, LANES), F32),
+            jax.ShapeDtypeStruct((rows_all, width), BF16),
+            pltpu.HBM((width, inner), BF16),
+            pltpu.HBM((width, LANES), F32),
         ],
         scratch_shapes=[pltpu.VMEM((width, inner), F32), pltpu.VMEM((width, LANES), F32)],
-        compiler_params=call_params(),
+        compiler_params=call_params(28),
         cost_estimate=cost(4 * rows_all * width * a_cols, rows_all * width * 12),
         name="query_grad",
-    )(hidden, grad_queries, side, group_a)
-    *arrives, partial_hidden = together(*arrives, partial_hidden)
+    )(*in_hbm(hidden, grad_queries, side, group_a))
+    *arrives, d_router = together(*arrives, d_router)
     parts = joined(parts, arrives)
     while parts[0][2]:
         parts = joined(*send_parts(parts))
     whole = jnp.concatenate([value for value, _, _ in parts], -2)
     parts, arrives = send_parts([(whole, parts[0][1], far)])
-    parts, partial_hidden = behind(parts, partial_hidden)
+    parts, d_router = behind(parts, d_router)
     if aligned:
         small_shapes = [(dp // 2, shards, own_rows, a_cols)] * 2
     else:
@@ -1120,10 +1204,16 @@
             pltpu.VMEM((LANES, width), F32),
             pltpu.VMEM((tile, LANES), BF16),
         ],
-        compiler_params=call_params(),
+        compiler_params=call_params(28),
         cost_estimate=cost(4 * rows_all * width * LANES, rows_all * width * 16),
         name="last",
-    )(core_index, tokens, hidden, partial_hidden, grad_mid, d_query, d_router, group_a, *returned)
+    )(
+        core_index,
+        *in_hbm(tokens, hidden),
+        partial_hidden,
+        *in_hbm(grad_mid, d_query, d_router, group_a),
+        *returned,
+    )
     if not aligned:
         by_core = small[0].reshape(dp // 2, 2, shards, own_rows, a_cols)
         small = [at_index(by_core, core_index[0], 1), at_index(by_core, 1 - core_index[0], 1)]

time: 227 us -> 227 us (level)
  Pallas kernels: 88.4 us -> 84.7 us
  other arithmetic: 12.2 us -> 14.8 us
    ppermute x25, starting transfers between devices: 33.2 us -> 28 us  [swapped(): return lax.ppermute(value, axis, [(at, at ^ mask) for at in range(count)])]
    add x10, other arithmetic: 4.33 us -> 7.95 us  [joined(): part[0] + piece]
    all_to_all x2, starting transfers between devices: 13 us -> 16.3 us  [on_device(): returned.append(lax.all_to_all(leave, 'seq', 0, 0, tiled=True))]
    ppermute x25, waiting for transfers between devices: 25.9 us -> 28.4 us  [swapped(): return lax.ppermute(value, axis, [(at, at ^ mask) for at in range(count)])]
  transfers between devices with their start and end apart: 31 -> 31, of which waited for: 14 -> 16; matrix products, arithmetic and copies ran while one was open for 7% -> 9% of each run, Pallas kernels for 20% -> 19%
where the time goes in v5:
time: 227 us; the launch traced here: 225 us
  Pallas kernels  84.7 us (37%)
  starting transfers between devices  50.5 us (22%)
  waiting for transfers between devices  48.6 us (21%)
  other arithmetic  14.8 us (7%)
  between operations  14.5 us (6%)
  local copies, waits for them, and re-layouts  12.3 us (5%)
    pallas_call x1, Pallas kernels, on_device(): pl.pallas_call(functools.partial(mid_kernel, experts, head), grid=(steps,...  37.8 us
    ppermute x25, waiting for transfers between devices, swapped(): return lax.ppermute(value, axis, [(at, at ^ mask) for at in range(count)])  28.4 us
    ppermute x25, starting transfers between devices, swapped(): return lax.ppermute(value, axis, [(at, at ^ mask) for at in range(count)])  28 us
    all_to_all x2, starting transfers between devices, on_device(): returned.append(lax.all_to_all(leave, 'seq', 0, 0, tiled=True))  16.3 us
    all_gather x1, waiting for transfers between devices, on_device(): group_b = lax.all_gather(packed_b, ('dp', 'seq'), axis=0, tiled=False)  12.9 us
    pallas_call x2, Pallas kernels, on_device(): pl.pallas_call(functools.partial(attend_back_kernel, reach, head, micro *...  10.6 us
    add x10, other arithmetic, joined(): part[0] + piece  7.95 us
    pallas_call x1, Pallas kernels, on_device(): pl.pallas_call(functools.partial(last_kernel, experts, head, tuple(zip(sp...  7.3 us
  transfers between devices with their start and end apart: 31, of which 16 were waited for; matrix products, arithmetic and copies ran while one was open for 9% of the time, Pallas kernels for 19%

profile of v5, /device:TPU:0, one launch (start us, length us, event | category | flops | bytes accessed | tf_op | source)
XLA Modules:
  0.0 225.3 jit_solution(1143192354590994497)
XLA Ops:
  7.2 1.8 pack.1
  9.1 3.1 %collective-permute-start = (bf16[16,768]{1,0:T(8,128)(2,1)}, bf16[16,768]{1,0:T(8,128)(2,1)S(1)}, u32[]{:S(2)}, u32[]{:S(2)}) collective-permute-start(bf16[16,768]{1,0:T(8,128)(2,1)} %get-tuple-element.79), channel_id=1, source_target_pairs={{0,8},{4,12},{8,0},{12,4},{16,24},{20,28},{24,16},{28,20},{1,9},{5... | collective-permute-start | bytes 73736 | tf_op jit(solution)/shard_map/ppermute | solution.py:761
  12.2 2.6 %collective-permute-start.1 = (bf16[16,768]{1,0:T(8,128)(2,1)}, bf16[16,768]{1,0:T(8,128)(2,1)S(1)}, u32[]{:S(2)}, u32[]{:S(2)}) collective-permute-start(bf16[16,768]{1,0:T(8,128)(2,1)} %get-tuple-element.79), channel_id=1, source_target_pairs={{0,16},{4,20},{8,24},{12,28},{16,0},{20,4},{24,8},{28,12},{1,17},{... | collective-permute-start | bytes 73736 | tf_op jit(solution)/shard_map/ppermute | solution.py:761
  16.2 1.2 collective-permute-done.1
  17.5 3.1 %collective-permute-done.2 = bf16[16,768]{1,0:T(8,128)(2,1)S(1)} collective-permute-done((bf16[16,768]{1,0:T(8,128)(2,1)}, bf16[16,768]{1,0:T(8,128)(2,1)S(1)}, u32[]{:S(2)}, u32[]{:S(2)}) %collective-permute-start.2) | collective-permute-done | bytes 24608 | tf_op jit(solution)/shard_map/ppermute | solution.py:761
  21.4 1.6 collective-permute-start.3
  22.9 1.5 collective-permute-start.4
  24.9 1.5 convert_reduce_fusion
  26.5 1.3 collective-permute-done.3
  27.9 2.0 collective-permute-done.5
  30.1 1.9 copy.53
  34.7 4.8 %keyval.1 = (bf16[1536,512]{1,0:T(8,128)(2,1)}, bf16[1536,128]{1,0:T(8,128)(2,1)}, bf16[512,768]{1,0:T(8,128)(2,1)}) custom-call(s32[3]{0:T(128)} %pad_add_fusion.place_ref, bf16[1536,512]{1,0:T(8,128)(2,1)} %bitcast.102, bf16[4,4,16,768]{3,2,1,0:T(8,128)(2,1)} %copy-done.1, bf16[4,4,16,768]{3,2,1,0:T(8,128)(2,1)} %copy-done.3), custom_call_target="tpu_custom_call" | custom-call | flops 201326592 | bytes 3145728 | tf_op jit(solution)/shard_map/keyval/pallas_call | solution.py:915
  39.5 2.4 %collective-permute-start.7 = (bf16[3,512,128]{2,1,0:T(8,128)(2,1)}, bf16[3,512,128]{2,1,0:T(8,128)(2,1)S(1)}, u32[]{:S(2)}, u32[]{:S(2)}) collective-permute-start(bf16[3,512,128]{2,1,0:T(8,128)(2,1)} %bitcast.126), channel_id=1, source_target_pairs={{0,3},{4,7},{8,11},{12,15},{16,19},{20,23},{24,27},{28,31}} | collective-permute-start | bytes 1179656 | tf_op jit(solution)/shard_map/ppermute | solution.py:767
  41.9 1.3 collective-permute-start.8
  43.3 2.5 %collective-permute-start.9 = (bf16[3,512,128]{2,1,0:T(8,128)(2,1)}, bf16[3,512,128]{2,1,0:T(8,128)(2,1)S(1)}, u32[]{:S(2)}, u32[]{:S(2)}) collective-permute-start(bf16[3,512,128]{2,1,0:T(8,128)(2,1)} %bitcast.128), channel_id=1, source_target_pairs={{0,1},{1,2},{2,3},{4,5},{5,6},{6,7},{8,9},{9,10},{10,11},{12,13},{... | collective-permute-start | bytes 1179656 | tf_op jit(solution)/shard_map/ppermute | solution.py:767
  45.7 1.4 copy.54
  47.5 5.7 %query.1 = (bf16[2,1536,128]{2,1,0:T(8,128)(2,1)}, f32[1536,128]{1,0:T(8,128)}) custom-call(bf16[1536,512]{1,0:T(8,128)(2,1)} %get-tuple-element.80.hidden_ref, s32[1536,2]{1,0:T(8,128)} %bitcast.107, bf16[512,768]{1,0:T(8,128)(2,1)} %get-tuple-element.81.weight_ref), custom_call_target="tpu_custom_call" | custom-call | flops 2013265920 | bytes 3145728 | tf_op jit(solution)/shard_map/query/pallas_call | solution.py:942
  53.8 7.2 %collective-permute-done.8.rest_1_ = bf16[3,512,128]{2,1,0:T(8,128)(2,1)S(1)} collective-permute-done((bf16[3,512,128]{2,1,0:T(8,128)(2,1)}, bf16[3,512,128]{2,1,0:T(8,128)(2,1)S(1)}, u32[]{:S(2)}, u32[]{:S(2)}) %collective-permute-start.8) | collective-permute-done | bytes 393248 | tf_op jit(solution)/shard_map/ppermute | solution.py:767
  61.9 6.3 %attend.1 = (f32[2,1536,128]{2,1,0:T(8,128)}, f32[3,2,512]{2,1,0:T(2,128)}) custom-call(s32[4]{0:T(128)} %pad_add_fusion.1.bounds_ref, bf16[2,1536,128]{2,1,0:T(8,128)(2,1)} %get-tuple-element.83.q_ref, s32[3,1,512]{2,1,0:T(1,128)} %max.18.start_ref, bf16[3,512,128]{2,1,0:T(8,128)(2,1)} %copy-done.7, bf16[3,512,128]{2,1,0:T(8,128)(2,1)} %copy-done.8, ...), custom_call_target="tpu_custom_call" | custom-call | flops 1610612736 | bytes 3145728 | tf_op jit(solution)/shard_map/attend/pallas_call | solution.py:967
  68.2 12.9 %all-gather.3.cloned.1.call-done = bf16[4608,512]{1,0:T(8,128)(2,1)} async-done(((bf16[144,512]{1,0:T(8,128)(2,1)}), bf16[4608,512]{1,0:T(8,128)(2,1)}) %all-gather.3.cloned.1.call-update) | async-done | bytes 4718608 | tf_op jit(solution)/shard_map/all_gather | solution.py:886
  81.1 37.8 %mid.1 = (bf16[1536,512]{1,0:T(8,128)(2,1)}, bf16[1536,512]{1,0:T(8,128)(2,1)}, bf16[2,1536,128]{2,1,0:T(8,128)(2,1)}, f32[1536,128]{1,0:T(8,128)}, bf16[4,4,160...) custom-call(bf16[1536,512]{1,0:T(8,128)(2,1)} %bitcast.103, bf16[1536,512]{1,0:T(8,128)(2,1)} %bitcast.125, ...), custom_call_target="tpu_custom_call" | custom-call | flops 21743271936 | bytes 12582912 | tf_op jit(solution)/shard_map/mid/pallas_call | solution.py:996
  119.3 4.8 %collective-permute-done.10 = bf16[4,4,160,512]{3,2,1,0:T(8,128)(2,1)S(1)} collective-permute-done((bf16[4,4,160,512]{3,2,1,0:T(8,128)(2,1)}, bf16[4,4,160,512]{3,2,1,0:T(8,128)(2,1)S(1)}, u32[]{:S(2)}, u32[]{:S(2)}) %collective-permute-start.10) | collective-permute-done | bytes 2621472 | tf_op jit(solution)/shard_map/ppermute | solution.py:761
  124.1 2.5 %add.155 = bf16[4,4,160,512]{3,2,1,0:T(8,128)(2,1)S(1)} add(bf16[4,4,160,512]{3,2,1,0:T(8,128)(2,1)} %get-tuple-element.88, bf16[4,4,160,512]{3,2,1,0:T(8,128)(2,1)S(1)} %collective-permute-done.10) | non-fusion elementwise | flops 1310720 | bytes 7864320 | tf_op jit(solution)/shard_map/add | solution.py:1055
  127.0 1.5 collective-permute-start.12
  130.1 1.9 collective-permute-start.13
  132.0 6.2 %attend_back.2 = (bf16[2,1536,128]{2,1,0:T(8,128)(2,1)}, bf16[4,2,512,128]{3,2,1,0:T(8,128)(2,1)}) custom-call(s32[4]{0:T(128)S(1)} %copy-done, bf16[2,1536,128]{2,1,0:T(8,128)(2,1)} %get-tuple-element.83.q_ref, bf16[2,1536,128]{2,1,0:T(8,128)(2,1)} %get-tuple-element.92.grad_ref, f32[1536,128]{1,0:T(8,128)} %get-tuple-element.111.side_ref.grad_logit_ref, ...), custom_call_target="tpu_custom_call" | custom-call | flops 2684354560 | bytes 4194304 | tf_op jit(solution)/shard_map/attend_back/pallas_call | solution.py:1111
  138.2 12.6 %all-to-all-start = ((bf16[4,2,512,128]{3,2,1,0:T(8,128)(2,1)}), bf16[4,2,512,128]{3,2,1,0:T(8,128)(2,1)S(1)}, u32[]{:S(2)}, u32[]{:S(2)}) async-start(bf16[4,2,512,128]{3,2,1,0:T(8,128)(2,1)} %get-tuple-element.124), calls=%async_computation | async-start | bytes 2097152 | tf_op jit(solution)/shard_map/all_to_all | solution.py:1139
  150.8 1.1 add.166
  152.1 1.1 add.165
  153.3 2.1 collective-permute-start.14
  156.5 1.5 collective-permute-start.16
  158.1 4.4 %attend_back.3 = (bf16[2,1536,128]{2,1,0:T(8,128)(2,1)}, bf16[4,1,512,128]{3,2,1,0:T(8,128)(2,1)}) custom-call(s32[4]{0:T(128)S(1)} %copy-done, bf16[2,1536,128]{2,1,0:T(8,128)(2,1)} %get-tuple-element.83.q_ref, bf16[2,1536,128]{2,1,0:T(8,128)(2,1)} %get-tuple-element.92.grad_ref, ...), custom_call_target="tpu_custom_call", output_to_operand_aliasing={{0}: (10, {})} | custom-call | flops 1342177280 | bytes 2097152 | tf_op jit(solution)/shard_map/attend_back/pallas_call | solution.py:1111
  162.6 5.6 %collective-permute-done.16 = bf16[2,2,48,512]{3,2,0,1:T(8,128)(2,1)S(1)} collective-permute-done((bf16[2,2,48,512]{3,2,0,1:T(8,128)(2,1)S(1)}, bf16[2,2,48,512]{3,2,0,1:T(8,128)(2,1)S(1)}, u32[]{:S(2)}, u32[]{:S(2)}) %collective-permute-start.16) | collective-permute-done | bytes 196640 | tf_op jit(solution)/shard_map/ppermute | solution.py:761
  171.2 1.2 collective-permute-start.18
  172.5 3.7 %all-to-all-start.1 = ((bf16[4,1,512,128]{3,2,1,0:T(8,128)(2,1)}), bf16[4,1,512,128]{3,2,1,0:T(8,128)(2,1)S(1)}, u32[]{:S(2)}, u32[]{:S(2)}) async-start(bf16[4,1,512,128]{3,2,1,0:T(8,128)(2,1)} %get-tuple-element.125), calls=%async_computation.1 | async-start | bytes 1048576 | tf_op jit(solution)/shard_map/all_to_all | solution.py:1139
  176.2 7.2 %query_grad.1 = (bf16[1536,512]{1,0:T(8,128)(2,1)S(1)}, bf16[512,512]{1,0:T(8,128)(2,1)}, f32[512,128]{1,0:T(8,128)}) custom-call(bf16[1536,512]{1,0:T(8,128)(2,1)} %get-tuple-element.80.hidden_ref, bf16[2,1536,128]{2,1,0:T(8,128)(2,1)} %get-tuple-element.104.grad_q_ref, f32[1536,128]{1,0:T(8,128)} %get-tuple-element.111.side_ref.grad_logit_ref, ...), custom_call_target="tpu_custom_call" | custom-call | flops 2415919104 | bytes 9437184 | tf_op jit(solution)/shard_map/query_grad/pallas_call | solution.py:1148
  187.6 7.3 %last.1 = (f32[1536,512]{1,0:T(8,128)}, bf16[4,4,16,768]{3,2,1,0:T(8,128)(2,1)S(1)}, bf16[4,4,16,768]{3,2,1,0:T(8,128)(2,1)}) custom-call(s32[1]{0:T(128)} %bitcast.3.core_ref, bf16[1536,512]{1,0:T(8,128)(2,1)} %bitcast.104, bf16[1536,512]{1,0:T(8,128)(2,1)} %get-tuple-element.80.hidden_ref, bf16[1536,512]{1,0:T(8,128)(2,1)S(1)} %get-tuple-element.112.partial_ref, ...), custom_call_target="tpu_custom_call" | custom-call | flops 402653184 | bytes 12582912 | tf_op jit(solution)/shard_map/last/pallas_call | solution.py:1183
  195.5 1.9 collective-permute-done.21
  197.6 1.5 collective-permute-start.22
  199.1 1.5 collective-permute-start.23
  201.1 1.3 collective-permute-done.22
  202.5 2.4 %collective-permute-done.23 = bf16[4,16,768]{2,1,0:T(8,128)(2,1)S(1)} collective-permute-done((bf16[4,16,768]{2,1,0:T(8,128)(2,1)S(1)}, bf16[4,16,768]{2,1,0:T(8,128)(2,1)S(1)}, u32[]{:S(2)}, u32[]{:S(2)}) %collective-permute-start.23) | collective-permute-done | bytes 98336 | tf_op jit(solution)/shard_map/ppermute | solution.py:761
  204.8 1.2 collective-permute-done.24
  207.9 2.9 %collective-permute-start.26 = (bf16[16,768]{1,0:T(8,128)(2,1)S(1)}, bf16[16,768]{1,0:T(8,128)(2,1)S(1)}, u32[]{:S(2)}, u32[]{:S(2)}) collective-permute-start(bf16[16,768]{1,0:T(8,128)(2,1)S(1)} %get-tuple-element.212), channel_id=1, source_target_pairs={{0,16},{4,20},{8,24},{12,28},{16,0},{20,4},{24,8},{28,12},{1,17},{... | collective-permute-start | bytes 73736 | tf_op jit(solution)/shard_map/ppermute | solution.py:761
  211.2 1.6 add.189.total_ref
  212.8 1.7 finish_second.1
  214.5 1.9 collective-permute-done.27.refs_3_
  217.0 1.5 finish_first.1
  (99 shorter events, 22.4 us)
Async XLA Ops:
  7.2 73.9 %all-gather.3.cloned.1.call-start = ((), (), s32[]{:S(2)}) async-start(), calls=%async_computation.2 | async-start | bytes 4866048 | tf_op jit(solution)/shard_map/all_gather | solution.py:886
  9.1 7.1 %collective-permute-start = (bf16[16,768]{1,0:T(8,128)(2,1)}, bf16[16,768]{1,0:T(8,128)(2,1)S(1)}, u32[]{:S(2)}, u32[]{:S(2)}) collective-permute-start(bf16[16,768]{1,0:T(8,128)(2,1)} %get-tuple-element.79), channel_id=1, source_target_pairs={{0,8},{4,12},{8,0},{12,4},{16,24},{20,28},{24,16},{28,20},{1,9},{5... | collective-permute-start | bytes 73736 | tf_op jit(solution)/shard_map/ppermute | solution.py:761
  12.2 5.3 %collective-permute-start.1 = (bf16[16,768]{1,0:T(8,128)(2,1)}, bf16[16,768]{1,0:T(8,128)(2,1)S(1)}, u32[]{:S(2)}, u32[]{:S(2)}) collective-permute-start(bf16[16,768]{1,0:T(8,128)(2,1)} %get-tuple-element.79), channel_id=1, source_target_pairs={{0,16},{4,20},{8,24},{12,28},{16,0},{20,4},{24,8},{28,12},{1,17},{... | collective-permute-start | bytes 73736 | tf_op jit(solution)/shard_map/ppermute | solution.py:761
  14.8 5.8 %collective-permute-start.2 = (bf16[16,768]{1,0:T(8,128)(2,1)}, bf16[16,768]{1,0:T(8,128)(2,1)S(1)}, u32[]{:S(2)}, u32[]{:S(2)}) collective-permute-start(bf16[16,768]{1,0:T(8,128)(2,1)} %get-tuple-element.79), channel_id=1, source_target_pairs={{0,24},{4,28},{8,16},{12,20},{16,8},{20,12},{24,0},{28,4},{1,25},{... | collective-permute-start | bytes 73736 | tf_op jit(solution)/shard_map/ppermute | solution.py:761
  21.4 6.4 %collective-permute-start.3 = (bf16[4,16,768]{2,1,0:T(8,128)(2,1)S(1)}, bf16[4,16,768]{2,1,0:T(8,128)(2,1)S(1)}, u32[]{:S(2)}, u32[]{:S(2)}) collective-permute-start(bf16[4,16,768]{2,1,0:T(8,128)(2,1)S(1)} %get-tuple-element.216), channel_id=1, source_target_pairs={{0,1},{1,0},{2,3},{3,2},{4,5},{5,4},{6,7},{7,6},{8,9},{9,8},{10,11... | collective-permute-start | bytes 294920 | tf_op jit(solution)/shard_map/ppermute | solution.py:761
  22.9 5.0 %collective-permute-start.4 = (bf16[4,16,768]{2,1,0:T(8,128)(2,1)S(1)}, bf16[4,16,768]{2,1,0:T(8,128)(2,1)S(1)}, u32[]{:S(2)}, u32[]{:S(2)}) collective-permute-start(bf16[4,16,768]{2,1,0:T(8,128)(2,1)S(1)} %get-tuple-element.216), channel_id=1, source_target_pairs={{0,2},{1,3},{2,0},{3,1},{4,6},{5,7},{6,4},{7,5},{8,10},{9,11},{10,... | collective-permute-start | bytes 294920 | tf_op jit(solution)/shard_map/ppermute | solution.py:761
  24.4 5.5 %collective-permute-start.5 = (bf16[4,16,768]{2,1,0:T(8,128)(2,1)S(1)}, bf16[4,16,768]{2,1,0:T(8,128)(2,1)S(1)}, u32[]{:S(2)}, u32[]{:S(2)}) collective-permute-start(bf16[4,16,768]{2,1,0:T(8,128)(2,1)S(1)} %get-tuple-element.216), channel_id=1, source_target_pairs={{0,3},{1,2},{2,1},{3,0},{4,7},{5,6},{6,5},{7,4},{8,11},{9,10},{10,... | collective-permute-start | bytes 294920 | tf_op jit(solution)/shard_map/ppermute | solution.py:761
  30.0 3.9 %copy-start.1 = (bf16[4,4,16,768]{3,2,1,0:T(8,128)(2,1)}, bf16[4,4,16,768]{3,2,1,0:T(8,128)(2,1)S(1)}, u32[]{:S(2)}) copy-start(bf16[4,4,16,768]{3,2,1,0:T(8,128)(2,1)S(1)} %pad_maximum_fusion.mine_ref) | copy-start | bytes 1179652
  30.0 3.9 %collective-permute-start.6 = (bf16[4,4,16,768]{3,2,1,0:T(8,128)(2,1)S(1)}, bf16[4,4,16,768]{3,2,1,0:T(8,128)(2,1)S(1)}, u32[]{:S(2)}, u32[]{:S(2)}) collective-permute-start(bf16[4,4,16,768]{3,2,1,0:T(8,128)(2,1)S(1)} %pad_maximum_fusion.mine_ref), channel_id=1, source_target_pairs={{0,4},{4,0},{8,12},{12,8},{16,20},{20,16},{24,28},{28,24},{1,5},{5... | collective-permute-start | bytes 1179656 | tf_op jit(solution)/shard_map/ppermute | solution.py:761
  33.9 0.7 copy-start.3
  39.5 14.2 %collective-permute-start.7 = (bf16[3,512,128]{2,1,0:T(8,128)(2,1)}, bf16[3,512,128]{2,1,0:T(8,128)(2,1)S(1)}, u32[]{:S(2)}, u32[]{:S(2)}) collective-permute-start(bf16[3,512,128]{2,1,0:T(8,128)(2,1)} %bitcast.126), channel_id=1, source_target_pairs={{0,3},{4,7},{8,11},{12,15},{16,19},{20,23},{24,27},{28,31}} | collective-permute-start | bytes 1179656 | tf_op jit(solution)/shard_map/ppermute | solution.py:767
  41.9 19.0 %collective-permute-start.8 = (bf16[3,512,128]{2,1,0:T(8,128)(2,1)}, bf16[3,512,128]{2,1,0:T(8,128)(2,1)S(1)}, u32[]{:S(2)}, u32[]{:S(2)}) collective-permute-start(bf16[3,512,128]{2,1,0:T(8,128)(2,1)} %bitcast.127), channel_id=1, source_target_pairs={{0,2},{1,3},{4,6},{5,7},{8,10},{9,11},{12,14},{13,15},{16,18},{17,... | collective-permute-start | bytes 1179656 | tf_op jit(solution)/shard_map/ppermute | solution.py:767
  43.3 17.7 %collective-permute-start.9 = (bf16[3,512,128]{2,1,0:T(8,128)(2,1)}, bf16[3,512,128]{2,1,0:T(8,128)(2,1)S(1)}, u32[]{:S(2)}, u32[]{:S(2)}) collective-permute-start(bf16[3,512,128]{2,1,0:T(8,128)(2,1)} %bitcast.128), channel_id=1, source_target_pairs={{0,1},{1,2},{2,3},{4,5},{5,6},{6,7},{8,9},{9,10},{10,11},{12,13},{... | collective-permute-start | bytes 1179656 | tf_op jit(solution)/shard_map/ppermute | solution.py:767
  53.8 7.2 %copy-start.7 = (bf16[3,512,128]{2,1,0:T(8,128)(2,1)}, bf16[3,512,128]{2,1,0:T(8,128)(2,1)S(1)}, u32[]{:S(2)}) copy-start(bf16[3,512,128]{2,1,0:T(8,128)(2,1)S(1)} %collective-permute-done.7.rest_0_) | copy-start | bytes 1179652
  60.9 0.7 copy-start.8
  60.9 0.9 copy-start.9
  118.9 5.2 %collective-permute-start.10 = (bf16[4,4,160,512]{3,2,1,0:T(8,128)(2,1)}, bf16[4,4,160,512]{3,2,1,0:T(8,128)(2,1)S(1)}, u32[]{:S(2)}, u32[]{:S(2)}) collective-permute-start(bf16[4,4,160,512]{3,2,1,0:T(8,128)(2,1)} %get-tuple-element.89), channel_id=1, source_target_pairs={{0,4},{4,0},{8,12},{12,8},{16,20},{20,16},{24,28},{28,24},{1,5},{5... | collective-permute-start | bytes 7864328 | tf_op jit(solution)/shard_map/ppermute | solution.py:761
  126.9 5.1 %copy-start = (s32[4]{0:T(128)S(1)}, s32[4]{0:T(128)}, u32[]{:S(2)}) copy-start(s32[4]{0:T(128)} %pad_add_fusion.1.bounds_ref) | copy-start | bytes 52
  127.0 23.7 %collective-permute-start.12 = (bf16[2,2,2,56,512]{4,3,2,1,0:T(8,128)(2,1)S(1)}, bf16[2,2,2,56,512]{4,3,2,1,0:T(8,128)(2,1)}, u32[]{:S(2)}, u32[]{:S(2)}) collective-permute-start(bf16[2,2,2,56,512]{4,3,2,1,0:T(8,128)(2,1)S(1)} %get-tuple-element.188), channel_id=1, source_target_pairs={{0,2},{1,3},{2,0},{3,1},{4,6},{5,7},{6,4},{7,5},{8,10},{9,11},{10,... | collective-permute-start | bytes 1376264 | tf_op jit(solution)/shard_map/ppermute | solution.py:761
  128.6 22.1 %collective-permute-start.11 = (bf16[2,2,2,56,512]{4,3,2,1,0:T(8,128)(2,1)S(1)}, bf16[2,2,2,56,512]{4,3,2,1,0:T(8,128)(2,1)}, u32[]{:S(2)}, u32[]{:S(2)}) collective-permute-start(bf16[2,2,2,56,512]{4,3,2,1,0:T(8,128)(2,1)S(1)} %get-tuple-element.190), channel_id=1, source_target_pairs={{0,1},{1,0},{2,3},{3,2},{4,5},{5,4},{6,7},{7,6},{8,9},{9,8},{10,11... | collective-permute-start | bytes 1376264 | tf_op jit(solution)/shard_map/ppermute | solution.py:761
  130.1 20.7 %collective-permute-start.13 = (bf16[2,2,2,48,512]{4,3,2,1,0:T(8,128)(2,1)}, bf16[2,2,2,48,512]{4,3,2,1,0:T(8,128)(2,1)}, u32[]{:S(2)}, u32[]{:S(2)}) collective-permute-start(bf16[2,2,2,48,512]{4,3,2,1,0:T(8,128)(2,1)} %get-tuple-element.192), channel_id=1, source_target_pairs={{0,8},{4,12},{8,0},{12,4},{16,24},{20,28},{24,16},{28,20},{1,9},{5... | collective-permute-start | bytes 1179656 | tf_op jit(solution)/shard_map/ppermute | solution.py:761
  138.2 34.3 %all-to-all-start = ((bf16[4,2,512,128]{3,2,1,0:T(8,128)(2,1)}), bf16[4,2,512,128]{3,2,1,0:T(8,128)(2,1)S(1)}, u32[]{:S(2)}, u32[]{:S(2)}) async-start(bf16[4,2,512,128]{3,2,1,0:T(8,128)(2,1)} %get-tuple-element.124), calls=%async_computation | async-start | bytes 2097152 | tf_op jit(solution)/shard_map/all_to_all | solution.py:1139
  152.0 16.2 %collective-permute-start.15 = (bf16[2,2,56,512]{3,2,0,1:T(8,128)(2,1)S(1)}, bf16[2,2,56,512]{3,2,0,1:T(8,128)(2,1)S(1)}, u32[]{:S(2)}, u32[]{:S(2)}) collective-permute-start(bf16[2,2,56,512]{3,2,0,1:T(8,128)(2,1)S(1)} %bitcast.110), channel_id=1, source_target_pairs={{0,8},{4,12},{8,0},{12,4},{16,24},{20,28},{24,16},{28,20},{1,9},{5... | collective-permute-start | bytes 688136 | tf_op jit(solution)/shard_map/ppermute | solution.py:761
  153.3 15.6 %collective-permute-start.14 = (bf16[2,2,56,512]{3,2,0,1:T(8,128)(2,1)S(1)}, bf16[2,2,56,512]{3,2,0,1:T(8,128)(2,1)S(1)}, u32[]{:S(2)}, u32[]{:S(2)}) collective-permute-start(bf16[2,2,56,512]{3,2,0,1:T(8,128)(2,1)S(1)} %bitcast.111), channel_id=1, source_target_pairs={{0,2},{1,3},{2,0},{3,1},{4,6},{5,7},{6,4},{7,5},{8,10},{9,11},{10,... | collective-permute-start | bytes 688136 | tf_op jit(solution)/shard_map/ppermute | solution.py:761
  156.5 11.7 %collective-permute-start.16 = (bf16[2,2,48,512]{3,2,0,1:T(8,128)(2,1)S(1)}, bf16[2,2,48,512]{3,2,0,1:T(8,128)(2,1)S(1)}, u32[]{:S(2)}, u32[]{:S(2)}) collective-permute-start(bf16[2,2,48,512]{3,2,0,1:T(8,128)(2,1)S(1)} %bitcast.112), channel_id=1, source_target_pairs={{0,1},{1,0},{2,3},{3,2},{4,5},{5,4},{6,7},{7,6},{8,9},{9,8},{10,11... | collective-permute-start | bytes 589832 | tf_op jit(solution)/shard_map/ppermute | solution.py:761
  170.4 13.0 %collective-permute-start.19 = (bf16[2,48,512]{2,1,0:T(8,128)(2,1)}, bf16[2,48,512]{2,1,0:T(8,128)(2,1)}, u32[]{:S(2)}, u32[]{:S(2)}) collective-permute-start(bf16[2,48,512]{2,1,0:T(8,128)(2,1)} %get-tuple-element.209), channel_id=1, source_target_pairs={{0,2},{1,3},{2,0},{3,1},{4,6},{5,7},{6,4},{7,5},{8,10},{9,11},{10,... | collective-permute-start | bytes 294920 | tf_op jit(solution)/shard_map/ppermute | solution.py:761
  171.2 12.2 %collective-permute-start.17 = (bf16[2,56,512]{2,1,0:T(8,128)(2,1)}, bf16[2,56,512]{2,1,0:T(8,128)(2,1)}, u32[]{:S(2)}, u32[]{:S(2)}) collective-permute-start(bf16[2,56,512]{2,1,0:T(8,128)(2,1)} %get-tuple-element.218), channel_id=1, source_target_pairs={{0,8},{4,12},{8,0},{12,4},{16,24},{20,28},{24,16},{28,20},{1,9},{5... | collective-permute-start | bytes 344072 | tf_op jit(solution)/shard_map/ppermute | solution.py:761
  171.2 12.2 %collective-permute-start.18 = (bf16[2,56,512]{2,1,0:T(8,128)(2,1)}, bf16[2,56,512]{2,1,0:T(8,128)(2,1)}, u32[]{:S(2)}, u32[]{:S(2)}) collective-permute-start(bf16[2,56,512]{2,1,0:T(8,128)(2,1)} %get-tuple-element.205), channel_id=1, source_target_pairs={{0,1},{1,0},{2,3},{3,2},{4,5},{5,4},{6,7},{7,6},{8,9},{9,8},{10,11... | collective-permute-start | bytes 344072 | tf_op jit(solution)/shard_map/ppermute | solution.py:761
  172.5 15.1 %all-to-all-start.1 = ((bf16[4,1,512,128]{3,2,1,0:T(8,128)(2,1)}), bf16[4,1,512,128]{3,2,1,0:T(8,128)(2,1)S(1)}, u32[]{:S(2)}, u32[]{:S(2)}) async-start(bf16[4,1,512,128]{3,2,1,0:T(8,128)(2,1)} %get-tuple-element.125), calls=%async_computation.1 | async-start | bytes 1048576 | tf_op jit(solution)/shard_map/all_to_all | solution.py:1139
  187.0 8.5 %collective-permute-start.20 = (bf16[160,512]{1,0:T(8,128)(2,1)}, bf16[160,512]{1,0:T(8,128)(2,1)}, u32[]{:S(2)}, u32[]{:S(2)}) collective-permute-start(bf16[160,512]{1,0:T(8,128)(2,1)} %get-tuple-element.203), channel_id=1, source_target_pairs={{0,16},{4,20},{8,24},{12,28},{16,0},{20,4},{24,8},{28,12},{1,17},{... | collective-permute-start | bytes 491528 | tf_op jit(solution)/shard_map/ppermute | solution.py:761
  194.9 16.3 %copy-start.2 = (bf16[160,512]{1,0:T(8,128)(2,1)S(1)}, bf16[160,512]{1,0:T(8,128)(2,1)}, u32[]{:S(2)}) copy-start(bf16[160,512]{1,0:T(8,128)(2,1)} %get-tuple-element.135) | copy-start | bytes 491524
  195.5 1.9 collective-permute-start.21
  197.6 4.9 %collective-permute-start.22 = (bf16[4,16,768]{2,1,0:T(8,128)(2,1)S(1)}, bf16[4,16,768]{2,1,0:T(8,128)(2,1)S(1)}, u32[]{:S(2)}, u32[]{:S(2)}) collective-permute-start(bf16[4,16,768]{2,1,0:T(8,128)(2,1)S(1)} %get-tuple-element.198), channel_id=1, source_target_pairs={{0,1},{1,0},{2,3},{3,2},{4,5},{5,4},{6,7},{7,6},{8,9},{9,8},{10,11... | collective-permute-start | bytes 294920 | tf_op jit(solution)/shard_map/ppermute | solution.py:761
  199.1 5.7 %collective-permute-start.23 = (bf16[4,16,768]{2,1,0:T(8,128)(2,1)S(1)}, bf16[4,16,768]{2,1,0:T(8,128)(2,1)S(1)}, u32[]{:S(2)}, u32[]{:S(2)}) collective-permute-start(bf16[4,16,768]{2,1,0:T(8,128)(2,1)S(1)} %get-tuple-element.200), channel_id=1, source_target_pairs={{0,2},{1,3},{2,0},{3,1},{4,6},{5,7},{6,4},{7,5},{8,10},{9,11},{10,... | collective-permute-start | bytes 294920 | tf_op jit(solution)/shard_map/ppermute | solution.py:761
  200.6 5.5 %collective-permute-start.24 = (bf16[4,16,768]{2,1,0:T(8,128)(2,1)S(1)}, bf16[4,16,768]{2,1,0:T(8,128)(2,1)S(1)}, u32[]{:S(2)}, u32[]{:S(2)}) collective-permute-start(bf16[4,16,768]{2,1,0:T(8,128)(2,1)S(1)} %get-tuple-element.199), channel_id=1, source_target_pairs={{0,3},{1,2},{2,1},{3,0},{4,7},{5,6},{6,5},{7,4},{8,11},{9,10},{10,... | collective-permute-start | bytes 294920 | tf_op jit(solution)/shard_map/ppermute | solution.py:761
  206.8 7.7 %collective-permute-start.25 = (bf16[16,768]{1,0:T(8,128)(2,1)S(1)}, bf16[16,768]{1,0:T(8,128)(2,1)S(1)}, u32[]{:S(2)}, u32[]{:S(2)}) collective-permute-start(bf16[16,768]{1,0:T(8,128)(2,1)S(1)} %get-tuple-element.213), channel_id=1, source_target_pairs={{0,8},{4,12},{8,0},{12,4},{16,24},{20,28},{24,16},{28,20},{1,9},{5... | collective-permute-start | bytes 73736 | tf_op jit(solution)/shard_map/ppermute | solution.py:761
  207.9 6.6 %collective-permute-start.26 = (bf16[16,768]{1,0:T(8,128)(2,1)S(1)}, bf16[16,768]{1,0:T(8,128)(2,1)S(1)}, u32[]{:S(2)}, u32[]{:S(2)}) collective-permute-start(bf16[16,768]{1,0:T(8,128)(2,1)S(1)} %get-tuple-element.212), channel_id=1, source_target_pairs={{0,16},{4,20},{8,24},{12,28},{16,0},{20,4},{24,8},{28,12},{1,17},{... | collective-permute-start | bytes 73736 | tf_op jit(solution)/shard_map/ppermute | solution.py:761
  210.8 5.6 %collective-permute-start.27 = (bf16[16,768]{1,0:T(8,128)(2,1)S(1)}, bf16[16,768]{1,0:T(8,128)(2,1)S(1)}, u32[]{:S(2)}, u32[]{:S(2)}) collective-permute-start(bf16[16,768]{1,0:T(8,128)(2,1)S(1)} %get-tuple-element.211), channel_id=1, source_target_pairs={{0,24},{4,28},{8,16},{12,20},{16,8},{20,12},{24,0},{28,4},{1,25},{... | collective-permute-start | bytes 73736 | tf_op jit(solution)/shard_map/ppermute | solution.py:761
  214.5 2.0 copy-start.4
  214.5 1.9 copy-start.5
  216.4 0.6 copy-start.6
Sparse Core Ops, SparseCore 0:
  10.9 70.1 all-gather.2

commit v6 on v5

--- a/solution.py
+++ b/solution.py
@@ -713,17 +713,18 @@
             send_ref[:, :, :, columns] = jnp.where(other, by_core[:, 0], by_core[:, 1])
 
 
-def finish_second_kernel(total_ref, down_ref, up_ref, out_ref, up_bias_ref, *vector_refs):
+def finish_second_kernel(kept_ref, last_ref, down_ref, up_ref, out_ref, up_bias_ref, *vector_refs):
     ff_rows, width = down_ref.shape
     own_rows, ff = up_ref.shape
     blocks = ff // width
-    down_ref[...] = total_ref[:ff_rows].astype(F32)
+    total = kept_ref[...].astype(F32) + last_ref[...].astype(F32)
+    down_ref[...] = total[:ff_rows]
     for at in range(blocks):
         low = ff_rows + at * own_rows
-        up_ref[:, at * width : (at + 1) * width] = total_ref[low : low + own_rows].astype(F32)
+        up_ref[:, at * width : (at + 1) * width] = total[low : low + own_rows]
     low = ff_rows + blocks * own_rows
-    out_ref[...] = total_ref[low : low + own_rows].astype(F32)
-    turned = total_ref[low + own_rows :].astype(F32).T
+    out_ref[...] = total[low : low + own_rows]
+    turned = total[low + own_rows :].T
     up_bias_ref[...] = jnp.concatenate([turned[at * LANES + 8] for at in range(blocks)], 0)
     for at, ref in enumerate(vector_refs):
         ref[...] = turned[at]
@@ -1106,7 +1107,7 @@
         aliases = {}
         if micro:
             in_specs.append(pl.BlockSpec(memory_space=pl.ANY))
-            operands.append(grad_queries)
+            operands += in_hbm(grad_queries)
             aliases = {len(operands): 0}
         grad_queries, leave = pl.pallas_call(
             functools.partial(
@@ -1161,8 +1162,8 @@
         ],
         out_shape=[
             jax.ShapeDtypeStruct((rows_all, width), BF16),
-            pltpu.HBM((width, inner), BF16),
-            pltpu.HBM((width, LANES), F32),
+            jax.ShapeDtypeStruct((width, inner), BF16),
+            jax.ShapeDtypeStruct((width, LANES), F32),
         ],
         scratch_shapes=[pltpu.VMEM((width, inner), F32), pltpu.VMEM((width, LANES), F32)],
         compiler_params=call_params(28),
@@ -1211,18 +1212,18 @@
         core_index,
         *in_hbm(tokens, hidden),
         partial_hidden,
-        *in_hbm(grad_mid, d_query, d_router, group_a),
-        *returned,
+        *in_hbm(grad_mid, d_query),
+        d_router,
+        *in_hbm(group_a, *returned),
     )
     if not aligned:
         by_core = small[0].reshape(dp // 2, 2, shards, own_rows, a_cols)
         small = [at_index(by_core, core_index[0], 1), at_index(by_core, 1 - core_index[0], 1)]
     keep_small, send_small = small
     *arrives, send_small = together(*arrives, send_small)
-    parts = joined(parts, arrives)
     while parts[0][2]:
-        parts = joined(*send_parts(parts))
-    own_b = parts[0][0]
+        parts, arrives = send_parts(joined(parts, arrives))
+    own_b = (parts[0][0], arrives[0])
     held = keep_small + swapped(send_small, "dp", 1)
     held = summed_direct(held, 1, "seq", 1).astype(BF16)
     z_me = lax.axis_index("dp") // 2
@@ -1243,7 +1244,7 @@
             + [vector_shape] * 3,
             compiler_params=call_params(),
             name="finish_second",
-        )(own_b)
+        )(*own_b)
         grad_query, grad_kv, grad_router, *first_vectors = pl.pallas_call(
             functools.partial(finish_first_kernel, len(ends)),
             out_shape=[
@@ -1257,7 +1258,7 @@
         )(*ends)
         grad_router = grad_router.T
     else:
-        own_b = own_b.astype(F32)
+        own_b = own_b[0].astype(F32) + own_b[1].astype(F32)
         total = sum([piece.astype(F32) for piece in ends])
         ends = own_b[tail_at:]
         grad_up = jnp.concatenate(

time: 227 us -> 222 us (0.978)
  other arithmetic: 14.8 us -> 10.5 us
  waiting for transfers between devices: 48.6 us -> 44.9 us
  starting transfers between devices: 50.5 us -> 54.1 us
    ppermute x25, starting transfers between devices: 28 us -> 34.9 us  [swapped(): return lax.ppermute(value, axis, [(at, at ^ mask) for at in range(count)])]
    add x10 -> x9, other arithmetic: 7.95 us -> 3.64 us  [joined(): part[0] + piece]
    ppermute x25, waiting for transfers between devices: 28.4 us -> 24.6 us  [swapped(): return lax.ppermute(value, axis, [(at, at ^ mask) for at in range(count)])]
    all_to_all x2, starting transfers between devices: 16.3 us -> 13 us  [on_device(): returned.append(lax.all_to_all(leave, 'seq', 0, 0, tiled=True))]
    unnamed x23 -> x29, local copies, waits for them, and re-layouts: 4.96 us -> 7.55 us
  transfers between devices with their start and end apart: 31 -> 31, of which waited for: 16 -> 15; matrix products, arithmetic and copies ran while one was open for 9% -> 7% of each run, Pallas kernels for 19% -> 19%
where the time goes in v6:
time: 222 us
  Pallas kernels  84.1 us (38%)
  starting transfers between devices  54.1 us (24%)
  waiting for transfers between devices  44.9 us (20%)
  between operations  14.5 us (7%)
  local copies, waits for them, and re-layouts  13.5 us (6%)
  other arithmetic  10.5 us (5%)
    pallas_call x1, Pallas kernels, on_device(): pl.pallas_call(functools.partial(mid_kernel, experts, head), grid=(steps,...  37.8 us
    ppermute x25, starting transfers between devices, swapped(): return lax.ppermute(value, axis, [(at, at ^ mask) for at in range(count)])  34.9 us
    ppermute x25, waiting for transfers between devices, swapped(): return lax.ppermute(value, axis, [(at, at ^ mask) for at in range(count)])  24.6 us
    all_gather x1, waiting for transfers between devices, on_device(): group_b = lax.all_gather(packed_b, ('dp', 'seq'), axis=0, tiled=False)  13.1 us
    all_to_all x2, starting transfers between devices, on_device(): returned.append(lax.all_to_all(leave, 'seq', 0, 0, tiled=True))  13 us
    pallas_call x2, Pallas kernels, on_device(): pl.pallas_call(functools.partial(attend_back_kernel, reach, head, micro *...  10.6 us
    pallas_call x1, Pallas kernels, on_device(): pl.pallas_call(functools.partial(last_kernel, experts, head, tuple(zip(sp...  7.57 us
    unnamed x29, local copies, waits for them, and re-layouts  7.55 us
  transfers between devices with their start and end apart: 31, of which 15 were waited for; matrix products, arithmetic and copies ran while one was open for 7% of the time, Pallas kernels for 19%

profile of v6, /device:TPU:0, one launch (start us, length us, event | category | flops | bytes accessed | tf_op | source)
XLA Modules:
  0.0 221.6 jit_solution(4529509120036475076)
XLA Ops:
  7.2 1.8 pack.1
  9.1 3.1 %collective-permute-start = (bf16[16,768]{1,0:T(8,128)(2,1)}, bf16[16,768]{1,0:T(8,128)(2,1)S(1)}, u32[]{:S(2)}, u32[]{:S(2)}) collective-permute-start(bf16[16,768]{1,0:T(8,128)(2,1)} %get-tuple-element.79), channel_id=1, source_target_pairs={{0,8},{4,12},{8,0},{12,4},{16,24},{20,28},{24,16},{28,20},{1,9},{5... | collective-permute-start | bytes 73736 | tf_op jit(solution)/shard_map/ppermute | solution.py:762
  12.2 2.6 %collective-permute-start.1 = (bf16[16,768]{1,0:T(8,128)(2,1)}, bf16[16,768]{1,0:T(8,128)(2,1)S(1)}, u32[]{:S(2)}, u32[]{:S(2)}) collective-permute-start(bf16[16,768]{1,0:T(8,128)(2,1)} %get-tuple-element.79), channel_id=1, source_target_pairs={{0,16},{4,20},{8,24},{12,28},{16,0},{20,4},{24,8},{28,12},{1,17},{... | collective-permute-start | bytes 73736 | tf_op jit(solution)/shard_map/ppermute | solution.py:762
  16.2 1.2 collective-permute-done.1
  17.5 3.1 %collective-permute-done.2 = bf16[16,768]{1,0:T(8,128)(2,1)S(1)} collective-permute-done((bf16[16,768]{1,0:T(8,128)(2,1)}, bf16[16,768]{1,0:T(8,128)(2,1)S(1)}, u32[]{:S(2)}, u32[]{:S(2)}) %collective-permute-start.2) | collective-permute-done | bytes 24608 | tf_op jit(solution)/shard_map/ppermute | solution.py:762
  21.4 1.6 collective-permute-start.3
  22.9 1.5 collective-permute-start.4
  24.9 1.5 convert_reduce_fusion
  26.5 1.3 collective-permute-done.3
  27.9 2.0 collective-permute-done.5
  30.1 1.9 copy.53
  34.7 4.8 %keyval.1 = (bf16[1536,512]{1,0:T(8,128)(2,1)}, bf16[1536,128]{1,0:T(8,128)(2,1)}, bf16[512,768]{1,0:T(8,128)(2,1)}) custom-call(s32[3]{0:T(128)} %pad_add_fusion.place_ref, bf16[1536,512]{1,0:T(8,128)(2,1)} %bitcast.102, bf16[4,4,16,768]{3,2,1,0:T(8,128)(2,1)} %copy-done.4, bf16[4,4,16,768]{3,2,1,0:T(8,128)(2,1)} %copy-done.5), custom_call_target="tpu_custom_call" | custom-call | flops 201326592 | bytes 3145728 | tf_op jit(solution)/shard_map/keyval/pallas_call | solution.py:916
  39.5 2.4 %collective-permute-start.7 = (bf16[3,512,128]{2,1,0:T(8,128)(2,1)}, bf16[3,512,128]{2,1,0:T(8,128)(2,1)S(1)}, u32[]{:S(2)}, u32[]{:S(2)}) collective-permute-start(bf16[3,512,128]{2,1,0:T(8,128)(2,1)} %bitcast.126), channel_id=1, source_target_pairs={{0,3},{4,7},{8,11},{12,15},{16,19},{20,23},{24,27},{28,31}} | collective-permute-start | bytes 1179656 | tf_op jit(solution)/shard_map/ppermute | solution.py:768
  41.9 1.3 collective-permute-start.8
  43.2 2.5 %collective-permute-start.9 = (bf16[3,512,128]{2,1,0:T(8,128)(2,1)}, bf16[3,512,128]{2,1,0:T(8,128)(2,1)S(1)}, u32[]{:S(2)}, u32[]{:S(2)}) collective-permute-start(bf16[3,512,128]{2,1,0:T(8,128)(2,1)} %bitcast.128), channel_id=1, source_target_pairs={{0,1},{1,2},{2,3},{4,5},{5,6},{6,7},{8,9},{9,10},{10,11},{12,13},{... | collective-permute-start | bytes 1179656 | tf_op jit(solution)/shard_map/ppermute | solution.py:768
  45.7 1.4 copy.54
  47.4 5.6 %query.1 = (bf16[2,1536,128]{2,1,0:T(8,128)(2,1)}, f32[1536,128]{1,0:T(8,128)}) custom-call(bf16[1536,512]{1,0:T(8,128)(2,1)} %get-tuple-element.80.hidden_ref, s32[1536,2]{1,0:T(8,128)} %bitcast.107, bf16[512,768]{1,0:T(8,128)(2,1)} %get-tuple-element.81.weight_ref), custom_call_target="tpu_custom_call" | custom-call | flops 2013265920 | bytes 3145728 | tf_op jit(solution)/shard_map/query/pallas_call | solution.py:943
  53.7 7.2 %collective-permute-done.8.rest_1_ = bf16[3,512,128]{2,1,0:T(8,128)(2,1)S(1)} collective-permute-done((bf16[3,512,128]{2,1,0:T(8,128)(2,1)}, bf16[3,512,128]{2,1,0:T(8,128)(2,1)S(1)}, u32[]{:S(2)}, u32[]{:S(2)}) %collective-permute-start.8) | collective-permute-done | bytes 393248 | tf_op jit(solution)/shard_map/ppermute | solution.py:768
  61.8 6.4 %attend.1 = (f32[2,1536,128]{2,1,0:T(8,128)}, f32[3,2,512]{2,1,0:T(2,128)}) custom-call(s32[4]{0:T(128)} %pad_add_fusion.1.bounds_ref, bf16[2,1536,128]{2,1,0:T(8,128)(2,1)} %get-tuple-element.83.q_ref, s32[3,1,512]{2,1,0:T(1,128)} %max.18.start_ref, bf16[3,512,128]{2,1,0:T(8,128)(2,1)} %copy-done.10, bf16[3,512,128]{2,1,0:T(8,128)(2,1)} %copy-done.11, ...), custom_call_target="tpu_custom_call" | custom-call | flops 1610612736 | bytes 3145728 | tf_op jit(solution)/shard_map/attend/pallas_call | solution.py:968
  68.2 13.1 %all-gather.3.cloned.1.call-done = bf16[4608,512]{1,0:T(8,128)(2,1)} async-done(((bf16[144,512]{1,0:T(8,128)(2,1)}), bf16[4608,512]{1,0:T(8,128)(2,1)}) %all-gather.3.cloned.1.call-update) | async-done | bytes 4718608 | tf_op jit(solution)/shard_map/all_gather | solution.py:887
  81.3 37.8 %mid.1 = (bf16[1536,512]{1,0:T(8,128)(2,1)}, bf16[1536,512]{1,0:T(8,128)(2,1)}, bf16[2,1536,128]{2,1,0:T(8,128)(2,1)}, f32[1536,128]{1,0:T(8,128)}, bf16[4,4,160...) custom-call(bf16[1536,512]{1,0:T(8,128)(2,1)} %bitcast.103, bf16[1536,512]{1,0:T(8,128)(2,1)} %bitcast.125, ...), custom_call_target="tpu_custom_call" | custom-call | flops 21743271936 | bytes 12582912 | tf_op jit(solution)/shard_map/mid/pallas_call | solution.py:997
  119.4 4.8 %collective-permute-done.10 = bf16[4,4,160,512]{3,2,1,0:T(8,128)(2,1)S(1)} collective-permute-done((bf16[4,4,160,512]{3,2,1,0:T(8,128)(2,1)}, bf16[4,4,160,512]{3,2,1,0:T(8,128)(2,1)S(1)}, u32[]{:S(2)}, u32[]{:S(2)}) %collective-permute-start.10) | collective-permute-done | bytes 2621472 | tf_op jit(solution)/shard_map/ppermute | solution.py:762
  124.2 2.5 %add.152 = bf16[4,4,160,512]{3,2,1,0:T(8,128)(2,1)S(1)} add(bf16[4,4,160,512]{3,2,1,0:T(8,128)(2,1)} %get-tuple-element.88, bf16[4,4,160,512]{3,2,1,0:T(8,128)(2,1)S(1)} %collective-permute-done.10) | non-fusion elementwise | flops 1310720 | bytes 7864320 | tf_op jit(solution)/shard_map/add | solution.py:1056
  127.2 1.6 collective-permute-start.12
  130.2 1.9 collective-permute-start.13
  132.1 6.2 %attend_back.2 = (bf16[2,1536,128]{2,1,0:T(8,128)(2,1)}, bf16[4,2,512,128]{3,2,1,0:T(8,128)(2,1)}) custom-call(s32[4]{0:T(128)S(1)} %copy-done.1, bf16[2,1536,128]{2,1,0:T(8,128)(2,1)} %get-tuple-element.83.q_ref, bf16[2,1536,128]{2,1,0:T(8,128)(2,1)} %get-tuple-element.92.grad_ref, f32[1536,128]{1,0:T(8,128)} %get-tuple-element.111.side_ref.grad_logit_ref, ...), custom_call_target="tpu_custom_call" | custom-call | flops 2684354560 | bytes 4194304 | tf_op jit(solution)/shard_map/attend_back/pallas_call | solution.py:1112
  138.3 9.3 %all-to-all-start = ((bf16[4,2,512,128]{3,2,1,0:T(8,128)(2,1)}), bf16[4,2,512,128]{3,2,1,0:T(8,128)(2,1)S(1)}, u32[]{:S(2)}, u32[]{:S(2)}) async-start(bf16[4,2,512,128]{3,2,1,0:T(8,128)(2,1)} %get-tuple-element.124), calls=%async_computation | async-start | bytes 2097152 | tf_op jit(solution)/shard_map/all_to_all | solution.py:1140
  147.6 1.1 add.163
  148.8 3.5 %collective-permute-start.15 = (bf16[2,2,56,512]{3,2,0,1:T(8,128)(2,1)S(1)}, bf16[2,2,56,512]{3,2,0,1:T(8,128)(2,1)S(1)}, u32[]{:S(2)}, u32[]{:S(2)}) collective-permute-start(bf16[2,2,56,512]{3,2,0,1:T(8,128)(2,1)S(1)} %bitcast.110), channel_id=1, source_target_pairs={{0,8},{4,12},{8,0},{12,4},{16,24},{20,28},{24,16},{28,20},{1,9},{5... | collective-permute-start | bytes 688136 | tf_op jit(solution)/shard_map/ppermute | solution.py:762
  152.3 1.1 add.162
  153.5 2.1 collective-permute-start.14
  156.8 1.5 collective-permute-start.16
  158.4 4.4 %attend_back.3 = (bf16[2,1536,128]{2,1,0:T(8,128)(2,1)}, bf16[4,1,512,128]{3,2,1,0:T(8,128)(2,1)}) custom-call(s32[4]{0:T(128)S(1)} %copy-done.1, bf16[2,1536,128]{2,1,0:T(8,128)(2,1)} %get-tuple-element.83.q_ref, bf16[2,1536,128]{2,1,0:T(8,128)(2,1)} %get-tuple-element.92.grad_ref, ...), custom_call_target="tpu_custom_call", output_to_operand_aliasing={{0}: (10, {})} | custom-call | flops 1342177280 | bytes 2097152 | tf_op jit(solution)/shard_map/attend_back/pallas_call | solution.py:1112
  162.8 3.9 %collective-permute-done.16 = bf16[2,2,48,512]{3,2,0,1:T(8,128)(2,1)S(1)} collective-permute-done((bf16[2,2,48,512]{3,2,0,1:T(8,128)(2,1)S(1)}, bf16[2,2,48,512]{3,2,0,1:T(8,128)(2,1)S(1)}, u32[]{:S(2)}, u32[]{:S(2)}) %collective-permute-start.16) | collective-permute-done | bytes 196640 | tf_op jit(solution)/shard_map/ppermute | solution.py:762
  168.8 1.2 collective-permute-start.18
  171.0 3.7 %all-to-all-start.1 = ((bf16[4,1,512,128]{3,2,1,0:T(8,128)(2,1)}), bf16[4,1,512,128]{3,2,1,0:T(8,128)(2,1)S(1)}, u32[]{:S(2)}, u32[]{:S(2)}) async-start(bf16[4,1,512,128]{3,2,1,0:T(8,128)(2,1)} %get-tuple-element.125), calls=%async_computation.1 | async-start | bytes 1048576 | tf_op jit(solution)/shard_map/all_to_all | solution.py:1140
  174.8 6.3 %query_grad.1 = (bf16[1536,512]{1,0:T(8,128)(2,1)S(1)}, bf16[512,512]{1,0:T(8,128)(2,1)S(1)}, f32[512,128]{1,0:T(8,128)S(1)}) custom-call(bf16[1536,512]{1,0:T(8,128)(2,1)} %get-tuple-element.80.hidden_ref, bf16[2,1536,128]{2,1,0:T(8,128)(2,1)} %get-tuple-element.104.grad_q_ref, f32[1536,128]{1,0:T(8,128)} %get-tuple-element.111.side_ref.grad_logit_ref, ...), custom_call_target="tpu_custom_call" | custom-call | flops 2415919104 | bytes 9437184 | tf_op jit(solution)/shard_map/query_grad/pallas_call | solution.py:1149
  182.7 3.6 %collective-permute-start.20 = (bf16[160,512]{1,0:T(8,128)(2,1)S(1)}, bf16[160,512]{1,0:T(8,128)(2,1)S(1)}, u32[]{:S(2)}, u32[]{:S(2)}) collective-permute-start(bf16[160,512]{1,0:T(8,128)(2,1)S(1)} %get-tuple-element.203), channel_id=1, source_target_pairs={{0,16},{4,20},{8,24},{12,28},{16,0},{20,4},{24,8},{28,12},{1,17},{... | collective-permute-start | bytes 491528 | tf_op jit(solution)/shard_map/ppermute | solution.py:762
  187.1 7.6 %last.1 = (f32[1536,512]{1,0:T(8,128)}, bf16[4,4,16,768]{3,2,1,0:T(8,128)(2,1)S(1)}, bf16[4,4,16,768]{3,2,1,0:T(8,128)(2,1)S(1)}) custom-call(s32[1]{0:T(128)} %bitcast.3.core_ref, bf16[1536,512]{1,0:T(8,128)(2,1)} %bitcast.104, bf16[1536,512]{1,0:T(8,128)(2,1)} %get-tuple-element.80.hidden_ref, bf16[1536,512]{1,0:T(8,128)(2,1)S(1)} %get-tuple-element.112.partial_ref, ...), custom_call_target="tpu_custom_call" | custom-call | flops 402653184 | bytes 12582912 | tf_op jit(solution)/shard_map/last/pallas_call | solution.py:1184
  194.8 1.7 collective-permute-done.21
  196.6 1.8 collective-permute-start.22
  198.4 1.5 collective-permute-start.23
  200.2 1.4 collective-permute-done.22
  201.5 2.6 %collective-permute-done.23 = bf16[4,16,768]{2,1,0:T(8,128)(2,1)S(1)} collective-permute-done((bf16[4,16,768]{2,1,0:T(8,128)(2,1)S(1)}, bf16[4,16,768]{2,1,0:T(8,128)(2,1)S(1)}, u32[]{:S(2)}, u32[]{:S(2)}) %collective-permute-start.23) | collective-permute-done | bytes 98336 | tf_op jit(solution)/shard_map/ppermute | solution.py:762
  204.1 1.2 collective-permute-done.24
  207.1 3.3 %collective-permute-start.27 = (bf16[16,768]{1,0:T(8,128)(2,1)S(1)}, bf16[16,768]{1,0:T(8,128)(2,1)S(1)}, u32[]{:S(2)}, u32[]{:S(2)}) collective-permute-start(bf16[16,768]{1,0:T(8,128)(2,1)S(1)} %get-tuple-element.211), channel_id=1, source_target_pairs={{0,24},{4,28},{8,16},{12,20},{16,8},{20,12},{24,0},{28,4},{1,25},{... | collective-permute-start | bytes 73736 | tf_op jit(solution)/shard_map/ppermute | solution.py:762
  210.5 1.8 finish_second.1
  213.3 1.5 finish_first.1
  (104 shorter events, 19.8 us)
Async XLA Ops:
  7.2 74.1 %all-gather.3.cloned.1.call-start = ((), (), s32[]{:S(2)}) async-start(), calls=%async_computation.2 | async-start | bytes 4866048 | tf_op jit(solution)/shard_map/all_gather | solution.py:887
  9.1 7.1 %collective-permute-start = (bf16[16,768]{1,0:T(8,128)(2,1)}, bf16[16,768]{1,0:T(8,128)(2,1)S(1)}, u32[]{:S(2)}, u32[]{:S(2)}) collective-permute-start(bf16[16,768]{1,0:T(8,128)(2,1)} %get-tuple-element.79), channel_id=1, source_target_pairs={{0,8},{4,12},{8,0},{12,4},{16,24},{20,28},{24,16},{28,20},{1,9},{5... | collective-permute-start | bytes 73736 | tf_op jit(solution)/shard_map/ppermute | solution.py:762
  12.2 5.3 %collective-permute-start.1 = (bf16[16,768]{1,0:T(8,128)(2,1)}, bf16[16,768]{1,0:T(8,128)(2,1)S(1)}, u32[]{:S(2)}, u32[]{:S(2)}) collective-permute-start(bf16[16,768]{1,0:T(8,128)(2,1)} %get-tuple-element.79), channel_id=1, source_target_pairs={{0,16},{4,20},{8,24},{12,28},{16,0},{20,4},{24,8},{28,12},{1,17},{... | collective-permute-start | bytes 73736 | tf_op jit(solution)/shard_map/ppermute | solution.py:762
  14.8 5.8 %collective-permute-start.2 = (bf16[16,768]{1,0:T(8,128)(2,1)}, bf16[16,768]{1,0:T(8,128)(2,1)S(1)}, u32[]{:S(2)}, u32[]{:S(2)}) collective-permute-start(bf16[16,768]{1,0:T(8,128)(2,1)} %get-tuple-element.79), channel_id=1, source_target_pairs={{0,24},{4,28},{8,16},{12,20},{16,8},{20,12},{24,0},{28,4},{1,25},{... | collective-permute-start | bytes 73736 | tf_op jit(solution)/shard_map/ppermute | solution.py:762
  21.4 6.4 %collective-permute-start.3 = (bf16[4,16,768]{2,1,0:T(8,128)(2,1)S(1)}, bf16[4,16,768]{2,1,0:T(8,128)(2,1)S(1)}, u32[]{:S(2)}, u32[]{:S(2)}) collective-permute-start(bf16[4,16,768]{2,1,0:T(8,128)(2,1)S(1)} %get-tuple-element.216), channel_id=1, source_target_pairs={{0,1},{1,0},{2,3},{3,2},{4,5},{5,4},{6,7},{7,6},{8,9},{9,8},{10,11... | collective-permute-start | bytes 294920 | tf_op jit(solution)/shard_map/ppermute | solution.py:762
  22.9 5.0 %collective-permute-start.4 = (bf16[4,16,768]{2,1,0:T(8,128)(2,1)S(1)}, bf16[4,16,768]{2,1,0:T(8,128)(2,1)S(1)}, u32[]{:S(2)}, u32[]{:S(2)}) collective-permute-start(bf16[4,16,768]{2,1,0:T(8,128)(2,1)S(1)} %get-tuple-element.216), channel_id=1, source_target_pairs={{0,2},{1,3},{2,0},{3,1},{4,6},{5,7},{6,4},{7,5},{8,10},{9,11},{10,... | collective-permute-start | bytes 294920 | tf_op jit(solution)/shard_map/ppermute | solution.py:762
  24.4 5.5 %collective-permute-start.5 = (bf16[4,16,768]{2,1,0:T(8,128)(2,1)S(1)}, bf16[4,16,768]{2,1,0:T(8,128)(2,1)S(1)}, u32[]{:S(2)}, u32[]{:S(2)}) collective-permute-start(bf16[4,16,768]{2,1,0:T(8,128)(2,1)S(1)} %get-tuple-element.216), channel_id=1, source_target_pairs={{0,3},{1,2},{2,1},{3,0},{4,7},{5,6},{6,5},{7,4},{8,11},{9,10},{10,... | collective-permute-start | bytes 294920 | tf_op jit(solution)/shard_map/ppermute | solution.py:762
  30.0 3.9 %copy-start.4 = (bf16[4,4,16,768]{3,2,1,0:T(8,128)(2,1)}, bf16[4,4,16,768]{3,2,1,0:T(8,128)(2,1)S(1)}, u32[]{:S(2)}) copy-start(bf16[4,4,16,768]{3,2,1,0:T(8,128)(2,1)S(1)} %pad_maximum_fusion.mine_ref) | copy-start | bytes 1179652
  30.0 3.9 %collective-permute-start.6 = (bf16[4,4,16,768]{3,2,1,0:T(8,128)(2,1)S(1)}, bf16[4,4,16,768]{3,2,1,0:T(8,128)(2,1)S(1)}, u32[]{:S(2)}, u32[]{:S(2)}) collective-permute-start(bf16[4,4,16,768]{3,2,1,0:T(8,128)(2,1)S(1)} %pad_maximum_fusion.mine_ref), channel_id=1, source_target_pairs={{0,4},{4,0},{8,12},{12,8},{16,20},{20,16},{24,28},{28,24},{1,5},{5... | collective-permute-start | bytes 1179656 | tf_op jit(solution)/shard_map/ppermute | solution.py:762
  33.9 0.8 copy-start.5
  39.5 14.2 %collective-permute-start.7 = (bf16[3,512,128]{2,1,0:T(8,128)(2,1)}, bf16[3,512,128]{2,1,0:T(8,128)(2,1)S(1)}, u32[]{:S(2)}, u32[]{:S(2)}) collective-permute-start(bf16[3,512,128]{2,1,0:T(8,128)(2,1)} %bitcast.126), channel_id=1, source_target_pairs={{0,3},{4,7},{8,11},{12,15},{16,19},{20,23},{24,27},{28,31}} | collective-permute-start | bytes 1179656 | tf_op jit(solution)/shard_map/ppermute | solution.py:768
  41.9 19.0 %collective-permute-start.8 = (bf16[3,512,128]{2,1,0:T(8,128)(2,1)}, bf16[3,512,128]{2,1,0:T(8,128)(2,1)S(1)}, u32[]{:S(2)}, u32[]{:S(2)}) collective-permute-start(bf16[3,512,128]{2,1,0:T(8,128)(2,1)} %bitcast.127), channel_id=1, source_target_pairs={{0,2},{1,3},{4,6},{5,7},{8,10},{9,11},{12,14},{13,15},{16,18},{17,... | collective-permute-start | bytes 1179656 | tf_op jit(solution)/shard_map/ppermute | solution.py:768
  43.2 17.7 %collective-permute-start.9 = (bf16[3,512,128]{2,1,0:T(8,128)(2,1)}, bf16[3,512,128]{2,1,0:T(8,128)(2,1)S(1)}, u32[]{:S(2)}, u32[]{:S(2)}) collective-permute-start(bf16[3,512,128]{2,1,0:T(8,128)(2,1)} %bitcast.128), channel_id=1, source_target_pairs={{0,1},{1,2},{2,3},{4,5},{5,6},{6,7},{8,9},{9,10},{10,11},{12,13},{... | collective-permute-start | bytes 1179656 | tf_op jit(solution)/shard_map/ppermute | solution.py:768
  53.7 7.2 %copy-start.10 = (bf16[3,512,128]{2,1,0:T(8,128)(2,1)}, bf16[3,512,128]{2,1,0:T(8,128)(2,1)S(1)}, u32[]{:S(2)}) copy-start(bf16[3,512,128]{2,1,0:T(8,128)(2,1)S(1)} %collective-permute-done.7.rest_0_) | copy-start | bytes 1179652
  60.9 0.8 copy-start.11
  60.9 0.9 copy-start.12
  119.0 5.2 %collective-permute-start.10 = (bf16[4,4,160,512]{3,2,1,0:T(8,128)(2,1)}, bf16[4,4,160,512]{3,2,1,0:T(8,128)(2,1)S(1)}, u32[]{:S(2)}, u32[]{:S(2)}) collective-permute-start(bf16[4,4,160,512]{3,2,1,0:T(8,128)(2,1)} %get-tuple-element.89), channel_id=1, source_target_pairs={{0,4},{4,0},{8,12},{12,8},{16,20},{20,16},{24,28},{28,24},{1,5},{5... | collective-permute-start | bytes 7864328 | tf_op jit(solution)/shard_map/ppermute | solution.py:762
  127.1 5.1 %copy-start.1 = (s32[4]{0:T(128)S(1)}, s32[4]{0:T(128)}, u32[]{:S(2)}) copy-start(s32[4]{0:T(128)} %pad_add_fusion.1.bounds_ref) | copy-start | bytes 52
  127.2 20.4 %collective-permute-start.12 = (bf16[2,2,2,56,512]{4,3,2,1,0:T(8,128)(2,1)S(1)}, bf16[2,2,2,56,512]{4,3,2,1,0:T(8,128)(2,1)}, u32[]{:S(2)}, u32[]{:S(2)}) collective-permute-start(bf16[2,2,2,56,512]{4,3,2,1,0:T(8,128)(2,1)S(1)} %get-tuple-element.188), channel_id=1, source_target_pairs={{0,2},{1,3},{2,0},{3,1},{4,6},{5,7},{6,4},{7,5},{8,10},{9,11},{10,... | collective-permute-start | bytes 1376264 | tf_op jit(solution)/shard_map/ppermute | solution.py:762
  128.8 18.8 %collective-permute-start.11 = (bf16[2,2,2,56,512]{4,3,2,1,0:T(8,128)(2,1)S(1)}, bf16[2,2,2,56,512]{4,3,2,1,0:T(8,128)(2,1)}, u32[]{:S(2)}, u32[]{:S(2)}) collective-permute-start(bf16[2,2,2,56,512]{4,3,2,1,0:T(8,128)(2,1)S(1)} %get-tuple-element.190), channel_id=1, source_target_pairs={{0,1},{1,0},{2,3},{3,2},{4,5},{5,4},{6,7},{7,6},{8,9},{9,8},{10,11... | collective-permute-start | bytes 1376264 | tf_op jit(solution)/shard_map/ppermute | solution.py:762
  130.2 17.3 %collective-permute-start.13 = (bf16[2,2,2,48,512]{4,3,2,1,0:T(8,128)(2,1)}, bf16[2,2,2,48,512]{4,3,2,1,0:T(8,128)(2,1)}, u32[]{:S(2)}, u32[]{:S(2)}) collective-permute-start(bf16[2,2,2,48,512]{4,3,2,1,0:T(8,128)(2,1)} %get-tuple-element.192), channel_id=1, source_target_pairs={{0,8},{4,12},{8,0},{12,4},{16,24},{20,28},{24,16},{28,20},{1,9},{5... | collective-permute-start | bytes 1179656 | tf_op jit(solution)/shard_map/ppermute | solution.py:762
  138.3 31.7 %all-to-all-start = ((bf16[4,2,512,128]{3,2,1,0:T(8,128)(2,1)}), bf16[4,2,512,128]{3,2,1,0:T(8,128)(2,1)S(1)}, u32[]{:S(2)}, u32[]{:S(2)}) async-start(bf16[4,2,512,128]{3,2,1,0:T(8,128)(2,1)} %get-tuple-element.124), calls=%async_computation | async-start | bytes 2097152 | tf_op jit(solution)/shard_map/all_to_all | solution.py:1140
  148.8 17.9 %collective-permute-start.15 = (bf16[2,2,56,512]{3,2,0,1:T(8,128)(2,1)S(1)}, bf16[2,2,56,512]{3,2,0,1:T(8,128)(2,1)S(1)}, u32[]{:S(2)}, u32[]{:S(2)}) collective-permute-start(bf16[2,2,56,512]{3,2,0,1:T(8,128)(2,1)S(1)} %bitcast.110), channel_id=1, source_target_pairs={{0,8},{4,12},{8,0},{12,4},{16,24},{20,28},{24,16},{28,20},{1,9},{5... | collective-permute-start | bytes 688136 | tf_op jit(solution)/shard_map/ppermute | solution.py:762
  153.5 13.8 %collective-permute-start.14 = (bf16[2,2,56,512]{3,2,0,1:T(8,128)(2,1)S(1)}, bf16[2,2,56,512]{3,2,0,1:T(8,128)(2,1)S(1)}, u32[]{:S(2)}, u32[]{:S(2)}) collective-permute-start(bf16[2,2,56,512]{3,2,0,1:T(8,128)(2,1)S(1)} %bitcast.111), channel_id=1, source_target_pairs={{0,2},{1,3},{2,0},{3,1},{4,6},{5,7},{6,4},{7,5},{8,10},{9,11},{10,... | collective-permute-start | bytes 688136 | tf_op jit(solution)/shard_map/ppermute | solution.py:762
  156.8 9.9 %collective-permute-start.16 = (bf16[2,2,48,512]{3,2,0,1:T(8,128)(2,1)S(1)}, bf16[2,2,48,512]{3,2,0,1:T(8,128)(2,1)S(1)}, u32[]{:S(2)}, u32[]{:S(2)}) collective-permute-start(bf16[2,2,48,512]{3,2,0,1:T(8,128)(2,1)S(1)} %bitcast.112), channel_id=1, source_target_pairs={{0,1},{1,0},{2,3},{3,2},{4,5},{5,4},{6,7},{7,6},{8,9},{9,8},{10,11... | collective-permute-start | bytes 589832 | tf_op jit(solution)/shard_map/ppermute | solution.py:762
  167.6 14.2 %collective-permute-start.19 = (bf16[2,48,512]{2,1,0:T(8,128)(2,1)S(1)}, bf16[2,48,512]{2,1,0:T(8,128)(2,1)S(1)}, u32[]{:S(2)}, u32[]{:S(2)}) collective-permute-start(bf16[2,48,512]{2,1,0:T(8,128)(2,1)S(1)} %get-tuple-element.209), channel_id=1, source_target_pairs={{0,2},{1,3},{2,0},{3,1},{4,6},{5,7},{6,4},{7,5},{8,10},{9,11},{10,... | collective-permute-start | bytes 294920 | tf_op jit(solution)/shard_map/ppermute | solution.py:762
  168.5 13.3 %collective-permute-start.17 = (bf16[2,56,512]{2,1,0:T(8,128)(2,1)S(1)}, bf16[2,56,512]{2,1,0:T(8,128)(2,1)S(1)}, u32[]{:S(2)}, u32[]{:S(2)}) collective-permute-start(bf16[2,56,512]{2,1,0:T(8,128)(2,1)S(1)} %get-tuple-element.218), channel_id=1, source_target_pairs={{0,8},{4,12},{8,0},{12,4},{16,24},{20,28},{24,16},{28,20},{1,9},{5... | collective-permute-start | bytes 344072 | tf_op jit(solution)/shard_map/ppermute | solution.py:762
  168.8 13.1 %collective-permute-start.18 = (bf16[2,56,512]{2,1,0:T(8,128)(2,1)S(1)}, bf16[2,56,512]{2,1,0:T(8,128)(2,1)S(1)}, u32[]{:S(2)}, u32[]{:S(2)}) collective-permute-start(bf16[2,56,512]{2,1,0:T(8,128)(2,1)S(1)} %get-tuple-element.205), channel_id=1, source_target_pairs={{0,1},{1,0},{2,3},{3,2},{4,5},{5,4},{6,7},{7,6},{8,9},{9,8},{10,11... | collective-permute-start | bytes 344072 | tf_op jit(solution)/shard_map/ppermute | solution.py:762
  170.0 1.0 copy-start.2
  171.0 15.3 %all-to-all-start.1 = ((bf16[4,1,512,128]{3,2,1,0:T(8,128)(2,1)}), bf16[4,1,512,128]{3,2,1,0:T(8,128)(2,1)S(1)}, u32[]{:S(2)}, u32[]{:S(2)}) async-start(bf16[4,1,512,128]{3,2,1,0:T(8,128)(2,1)} %get-tuple-element.125), calls=%async_computation.1 | async-start | bytes 1048576 | tf_op jit(solution)/shard_map/all_to_all | solution.py:1140
  181.1 0.8 copy-start
  182.7 12.0 %collective-permute-start.20 = (bf16[160,512]{1,0:T(8,128)(2,1)S(1)}, bf16[160,512]{1,0:T(8,128)(2,1)S(1)}, u32[]{:S(2)}, u32[]{:S(2)}) collective-permute-start(bf16[160,512]{1,0:T(8,128)(2,1)S(1)} %get-tuple-element.203), channel_id=1, source_target_pairs={{0,16},{4,20},{8,24},{12,28},{16,0},{20,4},{24,8},{28,12},{1,17},{... | collective-permute-start | bytes 491528 | tf_op jit(solution)/shard_map/ppermute | solution.py:762
  186.3 0.8 copy-start.3
  194.7 15.8 %copy-start.6 = (bf16[160,512]{1,0:T(8,128)(2,1)}, bf16[160,512]{1,0:T(8,128)(2,1)S(1)}, u32[]{:S(2)}) copy-start(bf16[160,512]{1,0:T(8,128)(2,1)S(1)} %collective-permute-done.20.last_ref) | copy-start | bytes 491524
  194.7 1.8 collective-permute-start.21
  196.6 4.9 %collective-permute-start.22 = (bf16[4,16,768]{2,1,0:T(8,128)(2,1)S(1)}, bf16[4,16,768]{2,1,0:T(8,128)(2,1)S(1)}, u32[]{:S(2)}, u32[]{:S(2)}) collective-permute-start(bf16[4,16,768]{2,1,0:T(8,128)(2,1)S(1)} %get-tuple-element.198), channel_id=1, source_target_pairs={{0,1},{1,0},{2,3},{3,2},{4,5},{5,4},{6,7},{7,6},{8,9},{9,8},{10,11... | collective-permute-start | bytes 294920 | tf_op jit(solution)/shard_map/ppermute | solution.py:762
  198.4 5.7 %collective-permute-start.23 = (bf16[4,16,768]{2,1,0:T(8,128)(2,1)S(1)}, bf16[4,16,768]{2,1,0:T(8,128)(2,1)S(1)}, u32[]{:S(2)}, u32[]{:S(2)}) collective-permute-start(bf16[4,16,768]{2,1,0:T(8,128)(2,1)S(1)} %get-tuple-element.200), channel_id=1, source_target_pairs={{0,2},{1,3},{2,0},{3,1},{4,6},{5,7},{6,4},{7,5},{8,10},{9,11},{10,... | collective-permute-start | bytes 294920 | tf_op jit(solution)/shard_map/ppermute | solution.py:762
  199.9 5.5 %collective-permute-start.24 = (bf16[4,16,768]{2,1,0:T(8,128)(2,1)S(1)}, bf16[4,16,768]{2,1,0:T(8,128)(2,1)S(1)}, u32[]{:S(2)}, u32[]{:S(2)}) collective-permute-start(bf16[4,16,768]{2,1,0:T(8,128)(2,1)S(1)} %get-tuple-element.199), channel_id=1, source_target_pairs={{0,3},{1,2},{2,1},{3,0},{4,7},{5,6},{6,5},{7,4},{8,11},{9,10},{10,... | collective-permute-start | bytes 294920 | tf_op jit(solution)/shard_map/ppermute | solution.py:762
  206.1 6.2 %collective-permute-start.25 = (bf16[16,768]{1,0:T(8,128)(2,1)S(1)}, bf16[16,768]{1,0:T(8,128)(2,1)S(1)}, u32[]{:S(2)}, u32[]{:S(2)}) collective-permute-start(bf16[16,768]{1,0:T(8,128)(2,1)S(1)} %get-tuple-element.213), channel_id=1, source_target_pairs={{0,8},{4,12},{8,0},{12,4},{16,24},{20,28},{24,16},{28,20},{1,9},{5... | collective-permute-start | bytes 73736 | tf_op jit(solution)/shard_map/ppermute | solution.py:762
  206.1 6.2 %collective-permute-start.26 = (bf16[16,768]{1,0:T(8,128)(2,1)S(1)}, bf16[16,768]{1,0:T(8,128)(2,1)S(1)}, u32[]{:S(2)}, u32[]{:S(2)}) collective-permute-start(bf16[16,768]{1,0:T(8,128)(2,1)S(1)} %get-tuple-element.212), channel_id=1, source_target_pairs={{0,16},{4,20},{8,24},{12,28},{16,0},{20,4},{24,8},{28,12},{1,17},{... | collective-permute-start | bytes 73736 | tf_op jit(solution)/shard_map/ppermute | solution.py:762
  207.1 5.6 %collective-permute-start.27 = (bf16[16,768]{1,0:T(8,128)(2,1)S(1)}, bf16[16,768]{1,0:T(8,128)(2,1)S(1)}, u32[]{:S(2)}, u32[]{:S(2)}) collective-permute-start(bf16[16,768]{1,0:T(8,128)(2,1)S(1)} %get-tuple-element.211), channel_id=1, source_target_pairs={{0,24},{4,28},{8,16},{12,20},{16,8},{20,12},{24,0},{28,4},{1,25},{... | collective-permute-start | bytes 73736 | tf_op jit(solution)/shard_map/ppermute | solution.py:762
  212.3 0.6 copy-start.7
  212.3 0.6 copy-start.8
  212.7 0.6 copy-start.9
Sparse Core Ops, SparseCore 0:
  10.9 70.3 all-gather.2

commit v7 on v6

--- a/solution.py
+++ b/solution.py
@@ -363,6 +363,8 @@
         return pre_act, dot_nt(dy, down_block(at)).astype(BF16)
 
     ready = ahead(0)
+    branch = middle + down_bias
+    gsec = jnp.zeros_like(middle)
     for at in range(blocks):
         lo = at * width
         pre_act, grad_active = ready
@@ -374,12 +376,11 @@
         grad_low = (grad_active.astype(F32) * slope).astype(BF16)
         active_ref[here, lo : lo + width] = active
         grad_ref[here, lo : lo + width] = grad_low
+        branch = branch + dot_nn(active, down_block(at))
+        gsec = gsec + dot_nt(grad_low, up_block(at))
         acc_upb[8:9, lo : lo + width] += jnp.sum(grad_low.astype(F32), 0, keepdims=True)
 
-    down_all = jnp.concatenate([down_block(at) for at in range(blocks)], 0)
-    up_all = jnp.concatenate([up_block(at) for at in range(blocks)], 1)
-    out_ref[...] = (middle + down_bias + dot_nn(active_ref[here, :], down_all)).astype(BF16)
-    gsec = dot_nt(grad_ref[here, :], up_all)
+    out_ref[...] = branch.astype(BF16)
     acc_vec[0:1] += jnp.sum(gsec * normed, 0, keepdims=True)
     acc_vec[1:2] += jnp.sum(gsec, 0, keepdims=True)
     acc_vec[2:3] += jnp.sum(dy_wide, 0, keepdims=True)

time: 222 us -> 223 us (level)
    ppermute x25, starting transfers between devices: 34.9 us -> 31.5 us  [swapped(): return lax.ppermute(value, axis, [(at, at ^ mask) for at in range(count)])]
    all_to_all x2, starting transfers between devices: 13 us -> 16.1 us  [on_device(): returned.append(lax.all_to_all(leave, 'seq', 0, 0, tiled=True))]
where the time goes in v7:
time: 223 us; the launch traced here: 222 us
  Pallas kernels  83.4 us (37%)
  starting transfers between devices  53.8 us (24%)
  waiting for transfers between devices  45.7 us (20%)
  between operations  14.5 us (7%)
  local copies, waits for them, and re-layouts  13.5 us (6%)
  other arithmetic  10.5 us (5%)
    pallas_call x1, Pallas kernels, on_device(): pl.pallas_call(functools.partial(mid_kernel, experts, head), grid=(steps,...  37 us
    ppermute x25, starting transfers between devices, swapped(): return lax.ppermute(value, axis, [(at, at ^ mask) for at in range(count)])  31.5 us
    ppermute x25, waiting for transfers between devices, swapped(): return lax.ppermute(value, axis, [(at, at ^ mask) for at in range(count)])  25.2 us
    all_to_all x2, starting transfers between devices, on_device(): returned.append(lax.all_to_all(leave, 'seq', 0, 0, tiled=True))  16.1 us
    all_gather x1, waiting for transfers between devices, on_device(): group_b = lax.all_gather(packed_b, ('dp', 'seq'), axis=0, tiled=False)  13.1 us
    pallas_call x2, Pallas kernels, on_device(): pl.pallas_call(functools.partial(attend_back_kernel, reach, head, micro *...  10.8 us
    pallas_call x1, Pallas kernels, on_device(): pl.pallas_call(functools.partial(last_kernel, experts, head, tuple(zip(sp...  7.56 us
    unnamed x29, local copies, waits for them, and re-layouts  7.55 us
  transfers between devices with their start and end apart: 31, of which 15 were waited for; matrix products, arithmetic and copies ran while one was open for 7% of the time, Pallas kernels for 19%

profile of v7, /device:TPU:0, one launch (start us, length us, event | category | flops | bytes accessed | tf_op | source)
XLA Modules:
  0.0 221.5 jit_solution(3500110014707687351)
XLA Ops:
  7.2 1.8 pack.1
  9.1 3.1 %collective-permute-start = (bf16[16,768]{1,0:T(8,128)(2,1)}, bf16[16,768]{1,0:T(8,128)(2,1)S(1)}, u32[]{:S(2)}, u32[]{:S(2)}) collective-permute-start(bf16[16,768]{1,0:T(8,128)(2,1)} %get-tuple-element.79), channel_id=1, source_target_pairs={{0,8},{4,12},{8,0},{12,4},{16,24},{20,28},{24,16},{28,20},{1,9},{5... | collective-permute-start | bytes 73736 | tf_op jit(solution)/shard_map/ppermute | solution.py:763
  12.2 2.6 %collective-permute-start.1 = (bf16[16,768]{1,0:T(8,128)(2,1)}, bf16[16,768]{1,0:T(8,128)(2,1)S(1)}, u32[]{:S(2)}, u32[]{:S(2)}) collective-permute-start(bf16[16,768]{1,0:T(8,128)(2,1)} %get-tuple-element.79), channel_id=1, source_target_pairs={{0,16},{4,20},{8,24},{12,28},{16,0},{20,4},{24,8},{28,12},{1,17},{... | collective-permute-start | bytes 73736 | tf_op jit(solution)/shard_map/ppermute | solution.py:763
  16.2 1.2 collective-permute-done.1
  17.5 3.1 %collective-permute-done.2 = bf16[16,768]{1,0:T(8,128)(2,1)S(1)} collective-permute-done((bf16[16,768]{1,0:T(8,128)(2,1)}, bf16[16,768]{1,0:T(8,128)(2,1)S(1)}, u32[]{:S(2)}, u32[]{:S(2)}) %collective-permute-start.2) | collective-permute-done | bytes 24608 | tf_op jit(solution)/shard_map/ppermute | solution.py:763
  21.4 1.6 collective-permute-start.3
  22.9 1.5 collective-permute-start.4
  24.9 1.5 convert_reduce_fusion
  26.5 1.3 collective-permute-done.3
  27.9 2.0 collective-permute-done.5
  30.1 1.9 copy.53
  34.7 4.8 %keyval.1 = (bf16[1536,512]{1,0:T(8,128)(2,1)}, bf16[1536,128]{1,0:T(8,128)(2,1)}, bf16[512,768]{1,0:T(8,128)(2,1)}) custom-call(s32[3]{0:T(128)} %pad_add_fusion.place_ref, bf16[1536,512]{1,0:T(8,128)(2,1)} %bitcast.102, bf16[4,4,16,768]{3,2,1,0:T(8,128)(2,1)} %copy-done.4, bf16[4,4,16,768]{3,2,1,0:T(8,128)(2,1)} %copy-done.5), custom_call_target="tpu_custom_call" | custom-call | flops 201326592 | bytes 3145728 | tf_op jit(solution)/shard_map/keyval/pallas_call | solution.py:917
  39.5 2.4 %collective-permute-start.7 = (bf16[3,512,128]{2,1,0:T(8,128)(2,1)}, bf16[3,512,128]{2,1,0:T(8,128)(2,1)S(1)}, u32[]{:S(2)}, u32[]{:S(2)}) collective-permute-start(bf16[3,512,128]{2,1,0:T(8,128)(2,1)} %bitcast.126), channel_id=1, source_target_pairs={{0,3},{4,7},{8,11},{12,15},{16,19},{20,23},{24,27},{28,31}} | collective-permute-start | bytes 1179656 | tf_op jit(solution)/shard_map/ppermute | solution.py:769
  41.9 1.3 collective-permute-start.8
  43.2 2.5 %collective-permute-start.9 = (bf16[3,512,128]{2,1,0:T(8,128)(2,1)}, bf16[3,512,128]{2,1,0:T(8,128)(2,1)S(1)}, u32[]{:S(2)}, u32[]{:S(2)}) collective-permute-start(bf16[3,512,128]{2,1,0:T(8,128)(2,1)} %bitcast.128), channel_id=1, source_target_pairs={{0,1},{1,2},{2,3},{4,5},{5,6},{6,7},{8,9},{9,10},{10,11},{12,13},{... | collective-permute-start | bytes 1179656 | tf_op jit(solution)/shard_map/ppermute | solution.py:769
  45.7 1.4 copy.54
  47.4 5.5 %query.1 = (bf16[2,1536,128]{2,1,0:T(8,128)(2,1)}, f32[1536,128]{1,0:T(8,128)}) custom-call(bf16[1536,512]{1,0:T(8,128)(2,1)} %get-tuple-element.80.hidden_ref, s32[1536,2]{1,0:T(8,128)} %bitcast.107, bf16[512,768]{1,0:T(8,128)(2,1)} %get-tuple-element.81.weight_ref), custom_call_target="tpu_custom_call" | custom-call | flops 2013265920 | bytes 3145728 | tf_op jit(solution)/shard_map/query/pallas_call | solution.py:944
  53.5 7.4 %collective-permute-done.8.rest_1_ = bf16[3,512,128]{2,1,0:T(8,128)(2,1)S(1)} collective-permute-done((bf16[3,512,128]{2,1,0:T(8,128)(2,1)}, bf16[3,512,128]{2,1,0:T(8,128)(2,1)S(1)}, u32[]{:S(2)}, u32[]{:S(2)}) %collective-permute-start.8) | collective-permute-done | bytes 393248 | tf_op jit(solution)/shard_map/ppermute | solution.py:769
  61.8 6.4 %attend.1 = (f32[2,1536,128]{2,1,0:T(8,128)}, f32[3,2,512]{2,1,0:T(2,128)}) custom-call(s32[4]{0:T(128)} %pad_add_fusion.1.bounds_ref, bf16[2,1536,128]{2,1,0:T(8,128)(2,1)} %get-tuple-element.83.q_ref, s32[3,1,512]{2,1,0:T(1,128)} %max.18.start_ref, bf16[3,512,128]{2,1,0:T(8,128)(2,1)} %copy-done.10, bf16[3,512,128]{2,1,0:T(8,128)(2,1)} %copy-done.11, ...), custom_call_target="tpu_custom_call" | custom-call | flops 1610612736 | bytes 3145728 | tf_op jit(solution)/shard_map/attend/pallas_call | solution.py:969
  68.2 13.1 %all-gather.3.cloned.1.call-done = bf16[4608,512]{1,0:T(8,128)(2,1)} async-done(((bf16[144,512]{1,0:T(8,128)(2,1)}), bf16[4608,512]{1,0:T(8,128)(2,1)}) %all-gather.3.cloned.1.call-update) | async-done | bytes 4718608 | tf_op jit(solution)/shard_map/all_gather | solution.py:888
  81.3 37.0 %mid.1 = (bf16[1536,512]{1,0:T(8,128)(2,1)}, bf16[1536,512]{1,0:T(8,128)(2,1)}, bf16[2,1536,128]{2,1,0:T(8,128)(2,1)}, f32[1536,128]{1,0:T(8,128)}, bf16[4,4,160...) custom-call(bf16[1536,512]{1,0:T(8,128)(2,1)} %bitcast.103, bf16[1536,512]{1,0:T(8,128)(2,1)} %bitcast.125, ...), custom_call_target="tpu_custom_call" | custom-call | flops 21743271936 | bytes 12582912 | tf_op jit(solution)/shard_map/mid/pallas_call | solution.py:998
  118.7 4.9 %collective-permute-done.10 = bf16[4,4,160,512]{3,2,1,0:T(8,128)(2,1)S(1)} collective-permute-done((bf16[4,4,160,512]{3,2,1,0:T(8,128)(2,1)}, bf16[4,4,160,512]{3,2,1,0:T(8,128)(2,1)S(1)}, u32[]{:S(2)}, u32[]{:S(2)}) %collective-permute-start.10) | collective-permute-done | bytes 2621472 | tf_op jit(solution)/shard_map/ppermute | solution.py:763
  123.5 2.5 %add.152 = bf16[4,4,160,512]{3,2,1,0:T(8,128)(2,1)S(1)} add(bf16[4,4,160,512]{3,2,1,0:T(8,128)(2,1)} %get-tuple-element.88, bf16[4,4,160,512]{3,2,1,0:T(8,128)(2,1)S(1)} %collective-permute-done.10) | non-fusion elementwise | flops 1310720 | bytes 7864320 | tf_op jit(solution)/shard_map/add | solution.py:1057
  126.5 1.5 collective-permute-start.12
  129.5 1.9 collective-permute-start.13
  131.4 6.4 %attend_back.2 = (bf16[2,1536,128]{2,1,0:T(8,128)(2,1)}, bf16[4,2,512,128]{3,2,1,0:T(8,128)(2,1)}) custom-call(s32[4]{0:T(128)S(1)} %copy-done.1, bf16[2,1536,128]{2,1,0:T(8,128)(2,1)} %get-tuple-element.83.q_ref, bf16[2,1536,128]{2,1,0:T(8,128)(2,1)} %get-tuple-element.92.grad_ref, f32[1536,128]{1,0:T(8,128)} %get-tuple-element.111.side_ref.grad_logit_ref, ...), custom_call_target="tpu_custom_call" | custom-call | flops 2684354560 | bytes 4194304 | tf_op jit(solution)/shard_map/attend_back/pallas_call | solution.py:1113
  137.8 12.6 %all-to-all-start = ((bf16[4,2,512,128]{3,2,1,0:T(8,128)(2,1)}), bf16[4,2,512,128]{3,2,1,0:T(8,128)(2,1)S(1)}, u32[]{:S(2)}, u32[]{:S(2)}) async-start(bf16[4,2,512,128]{3,2,1,0:T(8,128)(2,1)} %get-tuple-element.124), calls=%async_computation | async-start | bytes 2097152 | tf_op jit(solution)/shard_map/all_to_all | solution.py:1141
  150.4 1.1 add.163
  151.8 1.1 add.162
  153.1 2.1 collective-permute-start.14
  156.3 1.5 collective-permute-start.16
  157.9 4.4 %attend_back.3 = (bf16[2,1536,128]{2,1,0:T(8,128)(2,1)}, bf16[4,1,512,128]{3,2,1,0:T(8,128)(2,1)}) custom-call(s32[4]{0:T(128)S(1)} %copy-done.1, bf16[2,1536,128]{2,1,0:T(8,128)(2,1)} %get-tuple-element.83.q_ref, bf16[2,1536,128]{2,1,0:T(8,128)(2,1)} %get-tuple-element.92.grad_ref, ...), custom_call_target="tpu_custom_call", output_to_operand_aliasing={{0}: (10, {})} | custom-call | flops 1342177280 | bytes 2097152 | tf_op jit(solution)/shard_map/attend_back/pallas_call | solution.py:1113
  162.3 3.9 %collective-permute-done.16 = bf16[2,2,48,512]{3,2,0,1:T(8,128)(2,1)S(1)} collective-permute-done((bf16[2,2,48,512]{3,2,0,1:T(8,128)(2,1)S(1)}, bf16[2,2,48,512]{3,2,0,1:T(8,128)(2,1)S(1)}, u32[]{:S(2)}, u32[]{:S(2)}) %collective-permute-start.16) | collective-permute-done | bytes 196640 | tf_op jit(solution)/shard_map/ppermute | solution.py:763
  168.4 1.7 collective-permute-start.18
  171.1 3.5 %all-to-all-start.1 = ((bf16[4,1,512,128]{3,2,1,0:T(8,128)(2,1)}), bf16[4,1,512,128]{3,2,1,0:T(8,128)(2,1)S(1)}, u32[]{:S(2)}, u32[]{:S(2)}) async-start(bf16[4,1,512,128]{3,2,1,0:T(8,128)(2,1)} %get-tuple-element.125), calls=%async_computation.1 | async-start | bytes 1048576 | tf_op jit(solution)/shard_map/all_to_all | solution.py:1141
  174.6 6.3 %query_grad.1 = (bf16[1536,512]{1,0:T(8,128)(2,1)S(1)}, bf16[512,512]{1,0:T(8,128)(2,1)S(1)}, f32[512,128]{1,0:T(8,128)S(1)}) custom-call(bf16[1536,512]{1,0:T(8,128)(2,1)} %get-tuple-element.80.hidden_ref, bf16[2,1536,128]{2,1,0:T(8,128)(2,1)} %get-tuple-element.104.grad_q_ref, f32[1536,128]{1,0:T(8,128)} %get-tuple-element.111.side_ref.grad_logit_ref, ...), custom_call_target="tpu_custom_call" | custom-call | flops 2415919104 | bytes 9437184 | tf_op jit(solution)/shard_map/query_grad/pallas_call | solution.py:1150
  182.6 3.0 %collective-permute-start.20 = (bf16[160,512]{1,0:T(8,128)(2,1)S(1)}, bf16[160,512]{1,0:T(8,128)(2,1)S(1)}, u32[]{:S(2)}, u32[]{:S(2)}) collective-permute-start(bf16[160,512]{1,0:T(8,128)(2,1)S(1)} %get-tuple-element.203), channel_id=1, source_target_pairs={{0,16},{4,20},{8,24},{12,28},{16,0},{20,4},{24,8},{28,12},{1,17},{... | collective-permute-start | bytes 491528 | tf_op jit(solution)/shard_map/ppermute | solution.py:763
  186.4 7.6 %last.1 = (f32[1536,512]{1,0:T(8,128)}, bf16[4,4,16,768]{3,2,1,0:T(8,128)(2,1)S(1)}, bf16[4,4,16,768]{3,2,1,0:T(8,128)(2,1)S(1)}) custom-call(s32[1]{0:T(128)} %bitcast.3.core_ref, bf16[1536,512]{1,0:T(8,128)(2,1)} %bitcast.104, bf16[1536,512]{1,0:T(8,128)(2,1)} %get-tuple-element.80.hidden_ref, bf16[1536,512]{1,0:T(8,128)(2,1)S(1)} %get-tuple-element.112.partial_ref, ...), custom_call_target="tpu_custom_call" | custom-call | flops 402653184 | bytes 12582912 | tf_op jit(solution)/shard_map/last/pallas_call | solution.py:1185
  194.0 1.7 collective-permute-done.21
  195.9 2.0 collective-permute-start.22
  197.9 1.5 collective-permute-start.23
  199.4 1.6 collective-permute-done.22
  201.0 2.6 %collective-permute-done.23 = bf16[4,16,768]{2,1,0:T(8,128)(2,1)S(1)} collective-permute-done((bf16[4,16,768]{2,1,0:T(8,128)(2,1)S(1)}, bf16[4,16,768]{2,1,0:T(8,128)(2,1)S(1)}, u32[]{:S(2)}, u32[]{:S(2)}) %collective-permute-start.23) | collective-permute-done | bytes 98336 | tf_op jit(solution)/shard_map/ppermute | solution.py:763
  203.6 1.2 collective-permute-done.24
  205.6 1.4 collective-permute-start.26
  207.0 3.0 %collective-permute-start.27 = (bf16[16,768]{1,0:T(8,128)(2,1)S(1)}, bf16[16,768]{1,0:T(8,128)(2,1)S(1)}, u32[]{:S(2)}, u32[]{:S(2)}) collective-permute-start(bf16[16,768]{1,0:T(8,128)(2,1)S(1)} %get-tuple-element.211), channel_id=1, source_target_pairs={{0,24},{4,28},{8,16},{12,20},{16,8},{20,12},{24,0},{28,4},{1,25},{... | collective-permute-start | bytes 73736 | tf_op jit(solution)/shard_map/ppermute | solution.py:763
  209.9 1.8 finish_second.1
  213.2 1.5 finish_first.1
  (104 shorter events, 19.3 us)
Async XLA Ops:
  7.2 74.1 %all-gather.3.cloned.1.call-start = ((), (), s32[]{:S(2)}) async-start(), calls=%async_computation.2 | async-start | bytes 4866048 | tf_op jit(solution)/shard_map/all_gather | solution.py:888
  9.1 7.1 %collective-permute-start = (bf16[16,768]{1,0:T(8,128)(2,1)}, bf16[16,768]{1,0:T(8,128)(2,1)S(1)}, u32[]{:S(2)}, u32[]{:S(2)}) collective-permute-start(bf16[16,768]{1,0:T(8,128)(2,1)} %get-tuple-element.79), channel_id=1, source_target_pairs={{0,8},{4,12},{8,0},{12,4},{16,24},{20,28},{24,16},{28,20},{1,9},{5... | collective-permute-start | bytes 73736 | tf_op jit(solution)/shard_map/ppermute | solution.py:763
  12.2 5.3 %collective-permute-start.1 = (bf16[16,768]{1,0:T(8,128)(2,1)}, bf16[16,768]{1,0:T(8,128)(2,1)S(1)}, u32[]{:S(2)}, u32[]{:S(2)}) collective-permute-start(bf16[16,768]{1,0:T(8,128)(2,1)} %get-tuple-element.79), channel_id=1, source_target_pairs={{0,16},{4,20},{8,24},{12,28},{16,0},{20,4},{24,8},{28,12},{1,17},{... | collective-permute-start | bytes 73736 | tf_op jit(solution)/shard_map/ppermute | solution.py:763
  14.8 5.8 %collective-permute-start.2 = (bf16[16,768]{1,0:T(8,128)(2,1)}, bf16[16,768]{1,0:T(8,128)(2,1)S(1)}, u32[]{:S(2)}, u32[]{:S(2)}) collective-permute-start(bf16[16,768]{1,0:T(8,128)(2,1)} %get-tuple-element.79), channel_id=1, source_target_pairs={{0,24},{4,28},{8,16},{12,20},{16,8},{20,12},{24,0},{28,4},{1,25},{... | collective-permute-start | bytes 73736 | tf_op jit(solution)/shard_map/ppermute | solution.py:763
  21.4 6.4 %collective-permute-start.3 = (bf16[4,16,768]{2,1,0:T(8,128)(2,1)S(1)}, bf16[4,16,768]{2,1,0:T(8,128)(2,1)S(1)}, u32[]{:S(2)}, u32[]{:S(2)}) collective-permute-start(bf16[4,16,768]{2,1,0:T(8,128)(2,1)S(1)} %get-tuple-element.216), channel_id=1, source_target_pairs={{0,1},{1,0},{2,3},{3,2},{4,5},{5,4},{6,7},{7,6},{8,9},{9,8},{10,11... | collective-permute-start | bytes 294920 | tf_op jit(solution)/shard_map/ppermute | solution.py:763
  22.9 5.0 %collective-permute-start.4 = (bf16[4,16,768]{2,1,0:T(8,128)(2,1)S(1)}, bf16[4,16,768]{2,1,0:T(8,128)(2,1)S(1)}, u32[]{:S(2)}, u32[]{:S(2)}) collective-permute-start(bf16[4,16,768]{2,1,0:T(8,128)(2,1)S(1)} %get-tuple-element.216), channel_id=1, source_target_pairs={{0,2},{1,3},{2,0},{3,1},{4,6},{5,7},{6,4},{7,5},{8,10},{9,11},{10,... | collective-permute-start | bytes 294920 | tf_op jit(solution)/shard_map/ppermute | solution.py:763
  24.4 5.5 %collective-permute-start.5 = (bf16[4,16,768]{2,1,0:T(8,128)(2,1)S(1)}, bf16[4,16,768]{2,1,0:T(8,128)(2,1)S(1)}, u32[]{:S(2)}, u32[]{:S(2)}) collective-permute-start(bf16[4,16,768]{2,1,0:T(8,128)(2,1)S(1)} %get-tuple-element.216), channel_id=1, source_target_pairs={{0,3},{1,2},{2,1},{3,0},{4,7},{5,6},{6,5},{7,4},{8,11},{9,10},{10,... | collective-permute-start | bytes 294920 | tf_op jit(solution)/shard_map/ppermute | solution.py:763
  30.0 3.9 %copy-start.4 = (bf16[4,4,16,768]{3,2,1,0:T(8,128)(2,1)}, bf16[4,4,16,768]{3,2,1,0:T(8,128)(2,1)S(1)}, u32[]{:S(2)}) copy-start(bf16[4,4,16,768]{3,2,1,0:T(8,128)(2,1)S(1)} %pad_maximum_fusion.mine_ref) | copy-start | bytes 1179652
  30.0 3.9 %collective-permute-start.6 = (bf16[4,4,16,768]{3,2,1,0:T(8,128)(2,1)S(1)}, bf16[4,4,16,768]{3,2,1,0:T(8,128)(2,1)S(1)}, u32[]{:S(2)}, u32[]{:S(2)}) collective-permute-start(bf16[4,4,16,768]{3,2,1,0:T(8,128)(2,1)S(1)} %pad_maximum_fusion.mine_ref), channel_id=1, source_target_pairs={{0,4},{4,0},{8,12},{12,8},{16,20},{20,16},{24,28},{28,24},{1,5},{5... | collective-permute-start | bytes 1179656 | tf_op jit(solution)/shard_map/ppermute | solution.py:763
  33.9 0.8 copy-start.5
  39.5 14.0 %collective-permute-start.7 = (bf16[3,512,128]{2,1,0:T(8,128)(2,1)}, bf16[3,512,128]{2,1,0:T(8,128)(2,1)S(1)}, u32[]{:S(2)}, u32[]{:S(2)}) collective-permute-start(bf16[3,512,128]{2,1,0:T(8,128)(2,1)} %bitcast.126), channel_id=1, source_target_pairs={{0,3},{4,7},{8,11},{12,15},{16,19},{20,23},{24,27},{28,31}} | collective-permute-start | bytes 1179656 | tf_op jit(solution)/shard_map/ppermute | solution.py:769
  41.9 19.0 %collective-permute-start.8 = (bf16[3,512,128]{2,1,0:T(8,128)(2,1)}, bf16[3,512,128]{2,1,0:T(8,128)(2,1)S(1)}, u32[]{:S(2)}, u32[]{:S(2)}) collective-permute-start(bf16[3,512,128]{2,1,0:T(8,128)(2,1)} %bitcast.127), channel_id=1, source_target_pairs={{0,2},{1,3},{4,6},{5,7},{8,10},{9,11},{12,14},{13,15},{16,18},{17,... | collective-permute-start | bytes 1179656 | tf_op jit(solution)/shard_map/ppermute | solution.py:769
  43.2 17.7 %collective-permute-start.9 = (bf16[3,512,128]{2,1,0:T(8,128)(2,1)}, bf16[3,512,128]{2,1,0:T(8,128)(2,1)S(1)}, u32[]{:S(2)}, u32[]{:S(2)}) collective-permute-start(bf16[3,512,128]{2,1,0:T(8,128)(2,1)} %bitcast.128), channel_id=1, source_target_pairs={{0,1},{1,2},{2,3},{4,5},{5,6},{6,7},{8,9},{9,10},{10,11},{12,13},{... | collective-permute-start | bytes 1179656 | tf_op jit(solution)/shard_map/ppermute | solution.py:769
  53.5 7.4 %copy-start.10 = (bf16[3,512,128]{2,1,0:T(8,128)(2,1)}, bf16[3,512,128]{2,1,0:T(8,128)(2,1)S(1)}, u32[]{:S(2)}) copy-start(bf16[3,512,128]{2,1,0:T(8,128)(2,1)S(1)} %collective-permute-done.7.rest_0_) | copy-start | bytes 1179652
  60.9 0.8 copy-start.11
  60.9 0.9 copy-start.12
  118.3 5.2 %collective-permute-start.10 = (bf16[4,4,160,512]{3,2,1,0:T(8,128)(2,1)}, bf16[4,4,160,512]{3,2,1,0:T(8,128)(2,1)S(1)}, u32[]{:S(2)}, u32[]{:S(2)}) collective-permute-start(bf16[4,4,160,512]{3,2,1,0:T(8,128)(2,1)} %get-tuple-element.89), channel_id=1, source_target_pairs={{0,4},{4,0},{8,12},{12,8},{16,20},{20,16},{24,28},{28,24},{1,5},{5... | collective-permute-start | bytes 7864328 | tf_op jit(solution)/shard_map/ppermute | solution.py:763
  126.4 5.1 %copy-start.1 = (s32[4]{0:T(128)S(1)}, s32[4]{0:T(128)}, u32[]{:S(2)}) copy-start(s32[4]{0:T(128)} %pad_add_fusion.1.bounds_ref) | copy-start | bytes 52
  126.5 23.9 %collective-permute-start.12 = (bf16[2,2,2,56,512]{4,3,2,1,0:T(8,128)(2,1)S(1)}, bf16[2,2,2,56,512]{4,3,2,1,0:T(8,128)(2,1)}, u32[]{:S(2)}, u32[]{:S(2)}) collective-permute-start(bf16[2,2,2,56,512]{4,3,2,1,0:T(8,128)(2,1)S(1)} %get-tuple-element.188), channel_id=1, source_target_pairs={{0,2},{1,3},{2,0},{3,1},{4,6},{5,7},{6,4},{7,5},{8,10},{9,11},{10,... | collective-permute-start | bytes 1376264 | tf_op jit(solution)/shard_map/ppermute | solution.py:763
  128.1 22.3 %collective-permute-start.11 = (bf16[2,2,2,56,512]{4,3,2,1,0:T(8,128)(2,1)S(1)}, bf16[2,2,2,56,512]{4,3,2,1,0:T(8,128)(2,1)}, u32[]{:S(2)}, u32[]{:S(2)}) collective-permute-start(bf16[2,2,2,56,512]{4,3,2,1,0:T(8,128)(2,1)S(1)} %get-tuple-element.190), channel_id=1, source_target_pairs={{0,1},{1,0},{2,3},{3,2},{4,5},{5,4},{6,7},{7,6},{8,9},{9,8},{10,11... | collective-permute-start | bytes 1376264 | tf_op jit(solution)/shard_map/ppermute | solution.py:763
  129.5 20.9 %collective-permute-start.13 = (bf16[2,2,2,48,512]{4,3,2,1,0:T(8,128)(2,1)}, bf16[2,2,2,48,512]{4,3,2,1,0:T(8,128)(2,1)}, u32[]{:S(2)}, u32[]{:S(2)}) collective-permute-start(bf16[2,2,2,48,512]{4,3,2,1,0:T(8,128)(2,1)} %get-tuple-element.192), channel_id=1, source_target_pairs={{0,8},{4,12},{8,0},{12,4},{16,24},{20,28},{24,16},{28,20},{1,9},{5... | collective-permute-start | bytes 1179656 | tf_op jit(solution)/shard_map/ppermute | solution.py:763
  137.8 32.3 %all-to-all-start = ((bf16[4,2,512,128]{3,2,1,0:T(8,128)(2,1)}), bf16[4,2,512,128]{3,2,1,0:T(8,128)(2,1)S(1)}, u32[]{:S(2)}, u32[]{:S(2)}) async-start(bf16[4,2,512,128]{3,2,1,0:T(8,128)(2,1)} %get-tuple-element.124), calls=%async_computation | async-start | bytes 2097152 | tf_op jit(solution)/shard_map/all_to_all | solution.py:1141
  151.6 14.6 %collective-permute-start.15 = (bf16[2,2,56,512]{3,2,0,1:T(8,128)(2,1)S(1)}, bf16[2,2,56,512]{3,2,0,1:T(8,128)(2,1)S(1)}, u32[]{:S(2)}, u32[]{:S(2)}) collective-permute-start(bf16[2,2,56,512]{3,2,0,1:T(8,128)(2,1)S(1)} %bitcast.110), channel_id=1, source_target_pairs={{0,8},{4,12},{8,0},{12,4},{16,24},{20,28},{24,16},{28,20},{1,9},{5... | collective-permute-start | bytes 688136 | tf_op jit(solution)/shard_map/ppermute | solution.py:763
  153.1 13.8 %collective-permute-start.14 = (bf16[2,2,56,512]{3,2,0,1:T(8,128)(2,1)S(1)}, bf16[2,2,56,512]{3,2,0,1:T(8,128)(2,1)S(1)}, u32[]{:S(2)}, u32[]{:S(2)}) collective-permute-start(bf16[2,2,56,512]{3,2,0,1:T(8,128)(2,1)S(1)} %bitcast.111), channel_id=1, source_target_pairs={{0,2},{1,3},{2,0},{3,1},{4,6},{5,7},{6,4},{7,5},{8,10},{9,11},{10,... | collective-permute-start | bytes 688136 | tf_op jit(solution)/shard_map/ppermute | solution.py:763
  156.3 9.9 %collective-permute-start.16 = (bf16[2,2,48,512]{3,2,0,1:T(8,128)(2,1)S(1)}, bf16[2,2,48,512]{3,2,0,1:T(8,128)(2,1)S(1)}, u32[]{:S(2)}, u32[]{:S(2)}) collective-permute-start(bf16[2,2,48,512]{3,2,0,1:T(8,128)(2,1)S(1)} %bitcast.112), channel_id=1, source_target_pairs={{0,1},{1,0},{2,3},{3,2},{4,5},{5,4},{6,7},{7,6},{8,9},{9,8},{10,11... | collective-permute-start | bytes 589832 | tf_op jit(solution)/shard_map/ppermute | solution.py:763
  167.1 14.6 %collective-permute-start.19 = (bf16[2,48,512]{2,1,0:T(8,128)(2,1)S(1)}, bf16[2,48,512]{2,1,0:T(8,128)(2,1)S(1)}, u32[]{:S(2)}, u32[]{:S(2)}) collective-permute-start(bf16[2,48,512]{2,1,0:T(8,128)(2,1)S(1)} %get-tuple-element.209), channel_id=1, source_target_pairs={{0,2},{1,3},{2,0},{3,1},{4,6},{5,7},{6,4},{7,5},{8,10},{9,11},{10,... | collective-permute-start | bytes 294920 | tf_op jit(solution)/shard_map/ppermute | solution.py:763
  168.0 13.7 %collective-permute-start.17 = (bf16[2,56,512]{2,1,0:T(8,128)(2,1)S(1)}, bf16[2,56,512]{2,1,0:T(8,128)(2,1)S(1)}, u32[]{:S(2)}, u32[]{:S(2)}) collective-permute-start(bf16[2,56,512]{2,1,0:T(8,128)(2,1)S(1)} %get-tuple-element.218), channel_id=1, source_target_pairs={{0,8},{4,12},{8,0},{12,4},{16,24},{20,28},{24,16},{28,20},{1,9},{5... | collective-permute-start | bytes 344072 | tf_op jit(solution)/shard_map/ppermute | solution.py:763
  168.4 13.3 %collective-permute-start.18 = (bf16[2,56,512]{2,1,0:T(8,128)(2,1)S(1)}, bf16[2,56,512]{2,1,0:T(8,128)(2,1)S(1)}, u32[]{:S(2)}, u32[]{:S(2)}) collective-permute-start(bf16[2,56,512]{2,1,0:T(8,128)(2,1)S(1)} %get-tuple-element.205), channel_id=1, source_target_pairs={{0,1},{1,0},{2,3},{3,2},{4,5},{5,4},{6,7},{7,6},{8,9},{9,8},{10,11... | collective-permute-start | bytes 344072 | tf_op jit(solution)/shard_map/ppermute | solution.py:763
  170.1 1.0 copy-start.2
  171.1 14.4 %all-to-all-start.1 = ((bf16[4,1,512,128]{3,2,1,0:T(8,128)(2,1)}), bf16[4,1,512,128]{3,2,1,0:T(8,128)(2,1)S(1)}, u32[]{:S(2)}, u32[]{:S(2)}) async-start(bf16[4,1,512,128]{3,2,1,0:T(8,128)(2,1)} %get-tuple-element.125), calls=%async_computation.1 | async-start | bytes 1048576 | tf_op jit(solution)/shard_map/all_to_all | solution.py:1141
  180.9 0.8 copy-start
  182.6 11.4 %collective-permute-start.20 = (bf16[160,512]{1,0:T(8,128)(2,1)S(1)}, bf16[160,512]{1,0:T(8,128)(2,1)S(1)}, u32[]{:S(2)}, u32[]{:S(2)}) collective-permute-start(bf16[160,512]{1,0:T(8,128)(2,1)S(1)} %get-tuple-element.203), channel_id=1, source_target_pairs={{0,16},{4,20},{8,24},{12,28},{16,0},{20,4},{24,8},{28,12},{1,17},{... | collective-permute-start | bytes 491528 | tf_op jit(solution)/shard_map/ppermute | solution.py:763
  185.6 0.8 copy-start.3
  193.9 16.0 %copy-start.6 = (bf16[160,512]{1,0:T(8,128)(2,1)}, bf16[160,512]{1,0:T(8,128)(2,1)S(1)}, u32[]{:S(2)}) copy-start(bf16[160,512]{1,0:T(8,128)(2,1)S(1)} %collective-permute-done.20.last_ref) | copy-start | bytes 491524
  193.9 1.8 collective-permute-start.21
  195.9 5.2 %collective-permute-start.22 = (bf16[4,16,768]{2,1,0:T(8,128)(2,1)S(1)}, bf16[4,16,768]{2,1,0:T(8,128)(2,1)S(1)}, u32[]{:S(2)}, u32[]{:S(2)}) collective-permute-start(bf16[4,16,768]{2,1,0:T(8,128)(2,1)S(1)} %get-tuple-element.198), channel_id=1, source_target_pairs={{0,1},{1,0},{2,3},{3,2},{4,5},{5,4},{6,7},{7,6},{8,9},{9,8},{10,11... | collective-permute-start | bytes 294920 | tf_op jit(solution)/shard_map/ppermute | solution.py:763
  197.9 5.7 %collective-permute-start.23 = (bf16[4,16,768]{2,1,0:T(8,128)(2,1)S(1)}, bf16[4,16,768]{2,1,0:T(8,128)(2,1)S(1)}, u32[]{:S(2)}, u32[]{:S(2)}) collective-permute-start(bf16[4,16,768]{2,1,0:T(8,128)(2,1)S(1)} %get-tuple-element.200), channel_id=1, source_target_pairs={{0,2},{1,3},{2,0},{3,1},{4,6},{5,7},{6,4},{7,5},{8,10},{9,11},{10,... | collective-permute-start | bytes 294920 | tf_op jit(solution)/shard_map/ppermute | solution.py:763
  199.4 5.5 %collective-permute-start.24 = (bf16[4,16,768]{2,1,0:T(8,128)(2,1)S(1)}, bf16[4,16,768]{2,1,0:T(8,128)(2,1)S(1)}, u32[]{:S(2)}, u32[]{:S(2)}) collective-permute-start(bf16[4,16,768]{2,1,0:T(8,128)(2,1)S(1)} %get-tuple-element.199), channel_id=1, source_target_pairs={{0,3},{1,2},{2,1},{3,0},{4,7},{5,6},{6,5},{7,4},{8,11},{9,10},{10,... | collective-permute-start | bytes 294920 | tf_op jit(solution)/shard_map/ppermute | solution.py:763
  205.6 6.2 %collective-permute-start.25 = (bf16[16,768]{1,0:T(8,128)(2,1)S(1)}, bf16[16,768]{1,0:T(8,128)(2,1)S(1)}, u32[]{:S(2)}, u32[]{:S(2)}) collective-permute-start(bf16[16,768]{1,0:T(8,128)(2,1)S(1)} %get-tuple-element.213), channel_id=1, source_target_pairs={{0,8},{4,12},{8,0},{12,4},{16,24},{20,28},{24,16},{28,20},{1,9},{5... | collective-permute-start | bytes 73736 | tf_op jit(solution)/shard_map/ppermute | solution.py:763
  205.6 6.2 %collective-permute-start.26 = (bf16[16,768]{1,0:T(8,128)(2,1)S(1)}, bf16[16,768]{1,0:T(8,128)(2,1)S(1)}, u32[]{:S(2)}, u32[]{:S(2)}) collective-permute-start(bf16[16,768]{1,0:T(8,128)(2,1)S(1)} %get-tuple-element.212), channel_id=1, source_target_pairs={{0,16},{4,20},{8,24},{12,28},{16,0},{20,4},{24,8},{28,12},{1,17},{... | collective-permute-start | bytes 73736 | tf_op jit(solution)/shard_map/ppermute | solution.py:763
  207.0 5.6 %collective-permute-start.27 = (bf16[16,768]{1,0:T(8,128)(2,1)S(1)}, bf16[16,768]{1,0:T(8,128)(2,1)S(1)}, u32[]{:S(2)}, u32[]{:S(2)}) collective-permute-start(bf16[16,768]{1,0:T(8,128)(2,1)S(1)} %get-tuple-element.211), channel_id=1, source_target_pairs={{0,24},{4,28},{8,16},{12,20},{16,8},{20,12},{24,0},{28,4},{1,25},{... | collective-permute-start | bytes 73736 | tf_op jit(solution)/shard_map/ppermute | solution.py:763
  211.8 0.8 copy-start.7
  211.8 0.8 copy-start.8
  212.6 0.6 copy-start.9
Sparse Core Ops, SparseCore 0:
  10.9 70.3 all-gather.2
